TPU v7x, 32 devices: a whole 2x2x4 slice. The times are simulated.
32 devices in a mesh: dp: 4 (over y, x), mp: 8 (over z, core).
Axes of the slice: x: 2, y: 2, z: 4, core: 2. Of those that a mesh axis runs over, the one named last changes fastest.
Arguments:
- tokens: bfloat16 [8192, 1024], P(('mp', 'dp')), may hold values from -6 to 6
- cotangent: bfloat16 [8192, 1024], P(('mp', 'dp')), may hold values from -6 to 6
- domain_ids: int32 [8, 1], P('mp'), may hold values from 0 to 3
- domain_weight: float32 [4], replicated, may hold values from 0.5 to 2
- gains: float32 [2, 1024], replicated, may hold values from 0.5 to 1.5
- gain_mom: float32 [2, 1024], P(None, 'dp'), may hold values from -256 to 256
- factor_w: float32 [1024, 800], P('dp'), may hold values from -0.25 to 0.25
- factor_mom: float32 [1024, 800], P('dp'), may hold values from -160 to 160
- out_w: float32 [1024, 1024], P('dp'), may hold values from -0.75 to 0.75
- out_mom: float32 [1024, 1024], P('dp'), may hold values from -160 to 160
- gate_up_w: float32 [2, 1024, 2816], P(None, 'dp', 'mp'), may hold values from -0.1875 to 0.1875
- gate_up_mom: float32 [2, 1024, 2816], P(None, 'dp', 'mp'), may hold values from -160 to 160
- down_w: float32 [2816, 1024], P('mp', 'dp'), may hold values from -0.109375 to 0.109375
- down_mom: float32 [2816, 1024], P('mp', 'dp'), may hold values from -160 to 160
Outputs:
- block_out: bfloat16 [8192, 1024], P(('mp', 'dp'))
- input_grad: float32 [8192, 1024], P(('mp', 'dp'))
- gain_grad: float32 [2, 1024], P(None, 'dp')
- new_gains: float32 [2, 1024], P(None, 'dp')
- new_gain_mom: float32 [2, 1024], P(None, 'dp')
- new_factor_mom: float32 [1024, 800], P('dp')
- new_factor_w: float32 [1024, 800], P('dp')
- new_out_mom: float32 [1024, 1024], P('dp')
- new_out_w: float32 [1024, 1024], P('dp')
- new_gate_up_mom: float32 [2, 1024, 2816], P(None, 'dp', 'mp')
- new_gate_up_w: float32 [2, 1024, 2816], P(None, 'dp', 'mp')
- new_down_mom: float32 [2816, 1024], P('mp', 'dp')
- new_down_w: float32 [2816, 1024], P('mp', 'dp')
Inputs may be any that keep to these rules, and one draw needn't show every extreme that they name: `domain_ids`: every domain is named by at least one sequence.
All inputs are finite; a program needn't handle non-finite values.
Results may differ from a plain program's by a relative error of at most 0.013.
The roundings to bfloat16 on the way count: a program that leaves them out, or rounds other values in their place, can miss the bound.
Values may be sent and summed in bfloat16 or wider, within the bound.
No kernel may reach another device: no remote copies, remote signals or barrier semaphores. Data moves between devices by JAX's collectives and lax.ppermute only.
A program may use at most 384 MiB of HBM per device.

v0:
```python
import math

import jax
import jax.numpy as jnp
from jax import lax
from jax.sharding import PartitionSpec as P

D = 1024
HEADS = 16
HEAD_DIM = 64
RANK_Q = 6
RANK_KV = 2
FF = 2816
BLOCK = 512
NS_STEPS = 5


EPS = 1e-06
NS_EPS = 1e-07
MOMENTUM = 0.5
LEARN = 0.2
LEARN_VEC = 0.002
COEF_A = 3.4445
COEF_B = -4.775
COEF_C = 2.0315
NEG = -1e30
HIGH_PRECISION = lax.Precision.HIGHEST


def product(left_mat, right_mat):
    return jnp.dot(left_mat, right_mat, preferred_element_type=jnp.float32)


def product_tn(left_mat, right_mat):
    return lax.dot_general(
        left_mat, right_mat, (((0,), (0,)), ((), ())), preferred_element_type=jnp.float32
    )


def product_nt(left_mat, right_mat):
    return lax.dot_general(
        left_mat, right_mat, (((1,), (1,)), ((), ())), preferred_element_type=jnp.float32
    )


def exact(left_mat, right_mat):
    return jnp.dot(left_mat, right_mat, precision=HIGH_PRECISION)


def exact_tn(left_mat, right_mat):
    return lax.dot_general(left_mat, right_mat, (((0,), (0,)), ((), ())), precision=HIGH_PRECISION)


def exact_nt(left_mat, right_mat):
    return lax.dot_general(left_mat, right_mat, (((1,), (1,)), ((), ())), precision=HIGH_PRECISION)


def normalize(values):
    row_scale = lax.rsqrt(jnp.mean(values * values, axis=-1, keepdims=True) + EPS)
    return (values * row_scale, row_scale)


def norm_back(grad_in, normed, row_scale, gain):
    scaled = grad_in * gain
    inner_sum = jnp.mean(scaled * normed, axis=-1, keepdims=True)
    return (row_scale * (scaled - normed * inner_sum), jnp.sum(grad_in * normed, axis=0))


def factor_widths():
    return [
        RANK_Q * HEADS,
        RANK_KV * HEADS,
        RANK_KV * HEADS,
        RANK_Q * HEAD_DIM,
        RANK_KV * HEAD_DIM,
        RANK_KV * HEAD_DIM,
    ]


def split_blocks(matrix):
    pieces = []
    offset = 0
    for block_width in factor_widths():
        pieces.append(matrix[..., offset : offset + block_width])
        offset = offset + block_width
    return pieces


def compose(heads_part, dims_part, rank):
    row_count = heads_part.shape[0]
    left_part = heads_part.reshape(row_count, rank, HEADS)
    right_part = dims_part.reshape(row_count, rank, HEAD_DIM)
    return (
        jnp.einsum("trh,trd->thd", left_part, right_part, precision=HIGH_PRECISION) / rank
    ).astype(jnp.bfloat16)


def compose_back(grad_in, heads_part, dims_part, rank):
    row_count = grad_in.shape[0]
    left_part = heads_part.reshape(row_count, rank, HEADS)
    right_part = dims_part.reshape(row_count, rank, HEAD_DIM)
    d_left = jnp.einsum("thd,trd->trh", grad_in, right_part, precision=HIGH_PRECISION) / rank
    d_right = jnp.einsum("thd,trh->trd", grad_in, left_part, precision=HIGH_PRECISION) / rank
    return (d_left.reshape(row_count, rank * HEADS), d_right.reshape(row_count, rank * HEAD_DIM))


def block_scores(query_block, key_vecs, block_index, block_rows):
    scores = jnp.einsum(
        "qhd,khd->hqk", query_block, key_vecs, preferred_element_type=jnp.float32
    ) * HEAD_DIM ** (-0.5)
    rows_here = lax.broadcasted_iota(jnp.int32, scores.shape, 1) + block_index * block_rows
    cols_here = lax.broadcasted_iota(jnp.int32, scores.shape, 2)
    return jnp.where(cols_here <= rows_here, scores, NEG)


def attend_seq(queries, key_vecs, values):
    length = queries.shape[0]
    block_rows = min(BLOCK, length)
    outputs = []
    totals = []
    for block_index in range(length // block_rows):
        key_reach = (block_index + 1) * block_rows
        scores = block_scores(
            queries[block_index * block_rows : key_reach],
            key_vecs[:key_reach],
            block_index,
            block_rows,
        )
        row_max = jnp.max(scores, axis=-1, keepdims=True)
        weights = jnp.exp(scores - row_max)
        row_total = jnp.sum(weights, axis=-1, keepdims=True)
        probability = (weights / row_total).astype(jnp.bfloat16)
        outputs.append(
            jnp.einsum(
                "hqk,khd->qhd", probability, values[:key_reach], preferred_element_type=jnp.float32
            )
        )
        totals.append(row_max + jnp.log(row_total))
    return (jnp.concatenate(outputs, axis=0), jnp.concatenate(totals, axis=1))


def attend_back(queries, key_vecs, values, totals, d_attn):
    length = queries.shape[0]
    block_rows = min(BLOCK, length)
    factor_scale = HEAD_DIM ** (-0.5)
    d_queries = []
    d_keys = jnp.zeros(key_vecs.shape, jnp.float32)
    d_values = jnp.zeros(values.shape, jnp.float32)
    for block_index in range(length // block_rows):
        key_reach = (block_index + 1) * block_rows
        query_block = queries[block_index * block_rows : key_reach]
        grad_block = d_attn[block_index * block_rows : key_reach]
        scores = block_scores(query_block, key_vecs[:key_reach], block_index, block_rows)
        probability = jnp.exp(scores - totals[:, block_index * block_rows : key_reach])
        d_probs = jnp.einsum(
            "qhd,khd->hqk", grad_block, values[:key_reach], preferred_element_type=jnp.float32
        )
        inner_sum = jnp.sum(probability * d_probs, axis=-1, keepdims=True)
        d_scores = (probability * (d_probs - inner_sum)).astype(jnp.bfloat16)
        d_queries.append(
            jnp.einsum(
                "hqk,khd->qhd", d_scores, key_vecs[:key_reach], preferred_element_type=jnp.float32
            )
            * factor_scale
        )
        padding = ((0, length - key_reach), (0, 0), (0, 0))
        d_keys = d_keys + jnp.pad(
            jnp.einsum("hqk,qhd->khd", d_scores, query_block, preferred_element_type=jnp.float32)
            * factor_scale,
            padding,
        )
        d_values = d_values + jnp.pad(
            jnp.einsum(
                "hqk,qhd->khd",
                probability.astype(jnp.bfloat16),
                grad_block,
                preferred_element_type=jnp.float32,
            ),
            padding,
        )
    return (jnp.concatenate(d_queries, axis=0), d_keys, d_values)


def own_slice(values, first_row, own_rows):
    return lax.dynamic_slice_in_dim(values, first_row, own_rows, 0)


def body(
    tokens,
    cotangent,
    domain_ids,
    domain_weight,
    gains,
    gain_mom,
    factor_w,
    factor_mom,
    out_w,
    out_mom,
    gate_up_w,
    gate_up_mom,
    down_w,
    down_mom,
):
    own_rows, model_width = tokens.shape
    seq_rows = own_rows * lax.axis_size("dp")
    first_row = lax.axis_index("dp") * own_rows
    factor_low, out_low, gate_up_low, down_low = (
        lax.all_gather(factor_w.astype(jnp.bfloat16), "dp", axis=0, tiled=True),
        lax.all_gather(out_w.astype(jnp.bfloat16), "dp", axis=0, tiled=True),
        lax.all_gather(gate_up_w.astype(jnp.bfloat16), "dp", axis=1, tiled=True),
        lax.all_gather(down_w.astype(jnp.bfloat16), "dp", axis=1, tiled=True),
    )
    x_float = tokens.astype(jnp.float32)
    first_normed, first_scale = normalize(x_float)
    first_own = (first_normed * gains[0]).astype(jnp.bfloat16)
    first_in = lax.all_gather(first_own, "dp", axis=0, tiled=True)
    factors = product(first_in, factor_low)
    head_q, head_k, head_v, dim_q, dim_k, dim_v = split_blocks(factors)
    seq_shape = (seq_rows, HEADS, HEAD_DIM)
    queries = compose(head_q, dim_q, RANK_Q)
    key_vecs = compose(head_k, dim_k, RANK_KV)
    values = compose(head_v, dim_v, RANK_KV)
    attended, totals = attend_seq(queries, key_vecs, values)
    attended_low = attended.reshape(seq_rows, model_width).astype(jnp.bfloat16)
    attended_own = own_slice(attended_low, first_row, own_rows)
    residual = x_float + product(attended_own, out_low)
    second_normed, second_scale = normalize(residual)
    second_in = lax.all_gather(
        (second_normed * gains[1]).astype(jnp.bfloat16), "mp", axis=0, tiled=True
    )
    gate_value = product(second_in, gate_up_low[0])
    upward = product(second_in, gate_up_low[1])
    sigmoid_gate = jax.nn.sigmoid(gate_value)
    active = gate_value * sigmoid_gate
    hidden = (active * upward).astype(jnp.bfloat16)
    branch = lax.psum_scatter(product(hidden, down_low), "mp", scatter_dimension=0, tiled=True)
    block_out = (residual + branch).astype(jnp.bfloat16)
    domain_range = jnp.arange(domain_weight.shape[0], dtype=jnp.int32)
    seq_weight = jnp.sum(jnp.where(domain_ids[0, 0] == domain_range, domain_weight, 0.0))
    d_output = cotangent.astype(jnp.float32) * seq_weight
    d_output_all = lax.all_gather(d_output.astype(jnp.bfloat16), "mp", axis=0, tiled=True)
    grad_down = product_tn(hidden, d_output_all)
    d_hidden = product_nt(d_output_all, down_low)
    d_gate = (d_hidden * upward * sigmoid_gate * (1.0 + gate_value * (1.0 - sigmoid_gate))).astype(
        jnp.bfloat16
    )
    d_upward = (d_hidden * active).astype(jnp.bfloat16)
    grad_gate = product_tn(second_in, d_gate)
    grad_up = product_tn(second_in, d_upward)
    d_second = lax.psum_scatter(
        product_nt(d_gate, gate_up_low[0]) + product_nt(d_upward, gate_up_low[1]),
        "mp",
        scatter_dimension=0,
        tiled=True,
    )
    d_resid_norm, gain_second = norm_back(d_second, second_normed, second_scale, gains[1])
    d_residual = d_output + d_resid_norm
    d_residual_low = d_residual.astype(jnp.bfloat16)
    d_branch_seq = lax.all_gather(d_residual_low, "dp", axis=0, tiled=True)
    grad_out = product_tn(attended_own, d_residual_low)
    d_attended = product_nt(d_branch_seq, out_low).astype(jnp.bfloat16)
    d_queries, d_keys, d_values = attend_back(
        queries, key_vecs, values, totals, d_attended.reshape(seq_shape)
    )
    dq_heads, dq_dims = compose_back(
        own_slice(d_queries, first_row, own_rows),
        own_slice(head_q, first_row, own_rows),
        own_slice(dim_q, first_row, own_rows),
        RANK_Q,
    )
    dk_heads, dk_dims = compose_back(
        own_slice(d_keys, first_row, own_rows),
        own_slice(head_k, first_row, own_rows),
        own_slice(dim_k, first_row, own_rows),
        RANK_KV,
    )
    dv_heads, dv_dims = compose_back(
        own_slice(d_values, first_row, own_rows),
        own_slice(head_v, first_row, own_rows),
        own_slice(dim_v, first_row, own_rows),
        RANK_KV,
    )
    d_factors = jnp.concatenate(
        [dq_heads, dk_heads, dv_heads, dq_dims, dk_dims, dv_dims], axis=1
    ).astype(jnp.bfloat16)
    grad_factor = product_tn(first_own, d_factors)
    d_first = product_nt(d_factors, factor_low)
    d_input_norm, gain_first = norm_back(d_first, first_normed, first_scale, gains[0])
    input_grad = d_residual + d_input_norm
    grad_ffn = jnp.concatenate([grad_gate, grad_up, grad_down.T], axis=1)
    gain_terms = jnp.stack([gain_first, gain_second])
    red_factor, red_out, red_ffn, red_gain = (
        lax.psum_scatter(grad_factor, "dp", scatter_dimension=0, tiled=True),
        lax.psum_scatter(grad_out, "dp", scatter_dimension=0, tiled=True),
        lax.psum_scatter(grad_ffn, "dp", scatter_dimension=0, tiled=True),
        lax.psum_scatter(gain_terms, "dp", scatter_dimension=1, tiled=True),
    )
    red_factor, red_out, gain_grad = lax.psum((red_factor, red_out, red_gain), "mp")
    feature_count = gain_grad.shape[1]
    own_gains = lax.dynamic_slice_in_dim(
        gains, lax.axis_index("dp") * feature_count, feature_count, 1
    )
    new_gain_mom = MOMENTUM * gain_mom + gain_grad
    new_gains = own_gains - LEARN_VEC * new_gain_mom
    local_width = gate_up_w.shape[2]
    weight_rows = factor_w.shape[0]
    mom_factor = MOMENTUM * factor_mom + red_factor
    mom_out = MOMENTUM * out_mom + red_out
    ffn_old_mom = jnp.stack([gate_up_mom[0], gate_up_mom[1], down_mom.T])
    ffn_grad = red_ffn.reshape(weight_rows, 3, local_width).transpose(1, 0, 2)
    mom_ffn = MOMENTUM * ffn_old_mom + ffn_grad
    feedforward_iterate_matrix = mom_ffn
    factor_iter = mom_factor
    out_iter = mom_out
    for iteration in range(NS_STEPS):
        factor_full, out_full, feedforward_complete = (
            lax.all_gather(factor_iter, "dp", axis=0, tiled=True),
            lax.all_gather(out_iter, "dp", axis=0, tiled=True),
            lax.all_gather(feedforward_iterate_matrix, "dp", axis=1, tiled=True),
        )
        gramian_row_matrix = jnp.einsum(
            "cnb,cqb->cnq",
            feedforward_iterate_matrix,
            feedforward_complete,
            precision=HIGH_PRECISION,
        )
        column_squares = jnp.sum(feedforward_complete * feedforward_complete, axis=(1, 2))
        gramian_row_matrix, ffn_squares = lax.psum((gramian_row_matrix, column_squares), "mp")
        if iteration == 0:
            column_scale = jnp.concatenate(
                [
                    jnp.ones((piece.shape[1],), jnp.float32)
                    / (jnp.sqrt(jnp.sum(piece * piece)) + NS_EPS)
                    for piece in split_blocks(factor_full)
                ]
            )
            factor_full = factor_full * column_scale
            factor_iter = factor_iter * column_scale
            out_norm = jnp.sqrt(jnp.sum(out_full * out_full)) + NS_EPS
            out_full = out_full / out_norm
            out_iter = out_iter / out_norm
            ffn_norm = (jnp.sqrt(ffn_squares) + NS_EPS)[:, None, None]
            feedforward_complete = feedforward_complete / ffn_norm
            feedforward_iterate_matrix = feedforward_iterate_matrix / ffn_norm
            gramian_row_matrix = gramian_row_matrix / (ffn_norm * ffn_norm)
        updated = []
        for full_piece, own_piece in zip(split_blocks(factor_full), split_blocks(factor_iter)):
            gram_block = exact_tn(full_piece, full_piece)
            poly_block = COEF_B * gram_block + COEF_C * exact(gram_block, gram_block)
            updated.append(COEF_A * own_piece + exact(own_piece, poly_block))
        factor_iter = jnp.concatenate(updated, axis=1)
        out_gram = exact_nt(out_iter, out_full)
        out_first = exact(out_gram, out_full)
        out_second = exact(exact_nt(out_first, out_full), out_full)
        out_iter = COEF_A * out_iter + COEF_B * out_first + COEF_C * out_second
        feedforward_first_product = jnp.einsum(
            "sgw,swa->sga", gramian_row_matrix, feedforward_complete, precision=HIGH_PRECISION
        )
        feedforward_first_complete = lax.all_gather(
            feedforward_first_product, "dp", axis=1, tiled=True
        )
        feedforward_second_product = jnp.einsum(
            "sgw,swa->sga", gramian_row_matrix, feedforward_first_complete, precision=HIGH_PRECISION
        )
        feedforward_iterate_matrix = (
            COEF_A * feedforward_iterate_matrix
            + COEF_B * feedforward_first_product
            + COEF_C * feedforward_second_product
        )
    factor_rate = jnp.concatenate(
        [
            jnp.full(
                (piece.shape[1],), LEARN * 0.2 * math.sqrt(max(D, piece.shape[1])), jnp.float32
            )
            for piece in split_blocks(factor_iter)
        ]
    )
    new_factor_w = factor_w - factor_rate * factor_iter
    new_out_w = out_w - LEARN * 0.2 * math.sqrt(D) * out_iter
    ffn_rate = LEARN * 0.2 * math.sqrt(max(D, FF))
    ffn_old = jnp.stack([gate_up_w[0], gate_up_w[1], down_w.T])
    ffn_new = ffn_old - ffn_rate * feedforward_iterate_matrix
    return (
        block_out,
        input_grad,
        gain_grad,
        new_gains,
        new_gain_mom,
        mom_factor,
        new_factor_w,
        mom_out,
        new_out_w,
        mom_ffn[:2],
        ffn_new[:2],
        mom_ffn[2].T,
        ffn_new[2].T,
    )


def solution(mesh):
    return jax.shard_map(
        body,
        mesh=mesh,
        in_specs=(
            P(("mp", "dp"), None),
            P(("mp", "dp"), None),
            P("mp", None),
            P(),
            P(),
            P(None, "dp"),
            P("dp", None),
            P("dp", None),
            P("dp", None),
            P("dp", None),
            P(None, "dp", "mp"),
            P(None, "dp", "mp"),
            P("mp", "dp"),
            P("mp", "dp"),
        ),
        out_specs=(
            P(("mp", "dp"), None),
            P(("mp", "dp"), None),
            P(None, "dp"),
            P(None, "dp"),
            P(None, "dp"),
            P("dp", None),
            P("dp", None),
            P("dp", None),
            P("dp", None),
            P(None, "dp", "mp"),
            P(None, "dp", "mp"),
            P("mp", "dp"),
            P("mp", "dp"),
        ),
        check_vma=False,
    )
```

profile of v0, /device:TPU:0, one launch (start us, length us, event | category | flops | bytes accessed | tf_op | source)
XLA Modules:
  0.0 2478.0 jit_solution(17708584912261223911)
XLA Ops:
  15.4 29.2 %all-gather.30.cloned.1.call-done = bf16[1024,800]{0,1:T(8,128)(2,1)} async-done(((bf16[256,800]{0,1:T(8,128)(2,1)}), bf16[1024,800]{0,1:T(8,128)(2,1)}) %all-gather.30.cloned.1.call-update) | async-done | bytes 1638416 | tf_op jit(solution)/shard_map/all_gather | solution.py:208
  44.5 37.8 %all-gather.28.cloned.1.call-done = bf16[1024,1024]{1,0:T(8,128)(2,1)} async-done(((bf16[256,1024]{1,0:T(8,128)(2,1)}), bf16[1024,1024]{1,0:T(8,128)(2,1)}) %all-gather.28.cloned.1.call-update) | async-done | bytes 2097168 | tf_op jit(solution)/shard_map/all_gather | solution.py:216
  89.6 14.8 multiply_convert_fusion.2
  111.9 15.0 multiply_convert_fusion.4
  146.8 15.7 multiply_convert_fusion.3
  170.3 8.5 fusion.186
  178.9 8.4 fusion.6
  187.3 14.6 fusion.185
  202.0 15.0 fusion
  217.1 13.9 fusion.53
  243.0 18.0 all_gather.89
  261.0 26.7 %all-gather.34.cloned.1.call-done = bf16[2048,1024]{1,0:T(8,128)(2,1)} async-done(((bf16[256,1024]{1,0:T(8,128)(2,1)}), bf16[2048,1024]{1,0:T(8,128)(2,1)}) %all-gather.34.cloned.1.call-update) | async-done | bytes 4194320 | tf_op jit(solution)/shard_map/all_gather | solution.py:228
  296.7 38.9 %all-gather.38.cloned.1.call-done = bf16[2048,1024]{1,0:T(8,128)(2,1)} async-done(((bf16[256,1024]{1,0:T(8,128)(2,1)}), bf16[2048,1024]{1,0:T(8,128)(2,1)}) %all-gather.38.cloned.1.call-update) | async-done | bytes 4194320 | tf_op jit(solution)/shard_map/all_gather | solution.py:241
  363.7 76.8 %reduce-scatter.11.cloned.1.call-done = f32[256,1024]{1,0:T(8,128)} async-done(((f32[2048,1024]{1,0:T(8,128)}), f32[256,1024]{1,0:T(8,128)}) %reduce-scatter.11.cloned.1.call-update) | async-done | bytes 1048592 | tf_op jit(solution)/shard_map/reduce_scatter | solution.py:250
  456.5 39.1 %reduce-scatter.17.cloned.1.call-done = f32[256,1056]{0,1:T(8,128)} async-done(((f32[1024,1056]{0,1:T(8,128)}), f32[256,1056]{0,1:T(8,128)}) %reduce-scatter.17.cloned.1.call-update) | async-done | bytes 1081360 | tf_op jit(solution)/shard_map/reduce_scatter | solution.py:295
  498.1 35.3 %all-gather.40.cloned.1.call-done = bf16[1024,1024]{1,0:T(8,128)(2,1)} async-done(((bf16[256,1024]{1,0:T(8,128)(2,1)}), bf16[1024,1024]{1,0:T(8,128)(2,1)}) %all-gather.40.cloned.1.call-update) | async-done | bytes 2097168 | tf_op jit(solution)/shard_map/all_gather | solution.py:259
  538.7 11.1 fusion.19
  549.9 10.4 multiply_reduce_fusion.1
  560.2 16.1 fusion.16
  576.4 22.3 multiply_reduce_fusion
  598.7 27.9 %multiply_convert_fusion = bf16[16,512,1024]{2,1,0:T(8,128)(2,1)} fusion(f32[16,512,1024]{2,1,0:T(8,128)} %get-tuple-element.54, f32[16,512,1024]{2,1,0:T(8,128)} %get-tuple-element.46, f32[16,512]{1,0:T(8,128)S(1)} %get-tuple-element.53, f32[16,512]{1,0:T(8,128)S(1)} %copy-done.56), kind=kLoop, calls=%fused_computation | loop fusion | flops 33554432 | bytes 83951616 | tf_op jit(solution)/shard_map/convert_element_type | solution.py:159
  626.6 8.8 multiply_bitcast_fusion
  635.4 11.9 multiply_convert_fusion.1
  670.2 12.9 multiply_bitcast_fusion.2
  714.4 8.3 fusion.206
  725.6 14.9 reduce-scatter.19.cloned.1.call-done
  741.4 17.3 all-reduce.2
  758.7 61.1 %all-reduce.10.cloned.1.call-done = f32[3,256,1024]{2,1,0:T(8,128)} async-done(((f32[3,256,1024]{2,1,0:T(8,128)}), f32[3,256,1024]{2,1,0:T(8,128)}) %all-reduce.10.cloned.1.call-update) | async-done | bytes 3145744 | tf_op jit(solution)/shard_map/psum | solution.py:328
  819.8 8.5 fusion.12
  828.6 53.4 %all-gather.64.cloned.1.call-done = f32[3,1024,352]{1,2,0:T(8,128)} async-done(((f32[3,256,352]{1,2,0:T(8,128)}), f32[3,1024,352]{1,2,0:T(8,128)}) %all-gather.64.cloned.1.call-update) | async-done | bytes 4325392 | tf_op jit(solution)/shard_map/all_gather | solution.py:359
  882.0 8.7 fusion.45
  890.8 53.8 %all-gather.66.cloned.1.call-done = f32[3,1024,352]{1,2,0:T(8,128)} async-done(((f32[3,256,352]{1,2,0:T(8,128)}), f32[3,1024,352]{1,2,0:T(8,128)}) %all-gather.66.cloned.1.call-update) | async-done | bytes 4325392 | tf_op jit(solution)/shard_map/all_gather | solution.py:319
  944.6 8.6 fusion.207
  953.2 77.0 %all-reduce.12.cloned.1.call-done = f32[3,256,1024]{2,1,0:T(8,128)} async-done(((f32[3,256,1024]{2,1,0:T(8,128)}), f32[3,256,1024]{2,1,0:T(8,128)}) %all-reduce.12.cloned.1.call-update) | async-done | bytes 3145744 | tf_op jit(solution)/shard_map/psum | solution.py:328
  1038.8 53.4 %all-gather.68.cloned.1.call-done = f32[3,1024,352]{1,2,0:T(8,128)} async-done(((f32[3,256,352]{1,2,0:T(8,128)}), f32[3,1024,352]{1,2,0:T(8,128)}) %all-gather.68.cloned.1.call-update) | async-done | bytes 4325392 | tf_op jit(solution)/shard_map/all_gather | solution.py:359
  1092.2 8.5 fusion.44
  1100.8 53.8 %all-gather.70.cloned.1.call-done = f32[3,1024,352]{1,2,0:T(8,128)} async-done(((f32[3,256,352]{1,2,0:T(8,128)}), f32[3,1024,352]{1,2,0:T(8,128)}) %all-gather.70.cloned.1.call-update) | async-done | bytes 4325392 | tf_op jit(solution)/shard_map/all_gather | solution.py:319
  1154.5 8.6 fusion.209
  1163.2 77.0 %all-reduce.14.cloned.1.call-done = f32[3,256,1024]{2,1,0:T(8,128)} async-done(((f32[3,256,1024]{2,1,0:T(8,128)}), f32[3,256,1024]{2,1,0:T(8,128)}) %all-reduce.14.cloned.1.call-update) | async-done | bytes 3145744 | tf_op jit(solution)/shard_map/psum | solution.py:328
  1248.9 53.2 %all-gather.72.cloned.1.call-done = f32[3,1024,352]{1,2,0:T(8,128)} async-done(((f32[3,256,352]{1,2,0:T(8,128)}), f32[3,1024,352]{1,2,0:T(8,128)}) %all-gather.72.cloned.1.call-update) | async-done | bytes 4325392 | tf_op jit(solution)/shard_map/all_gather | solution.py:359
  1302.1 8.5 fusion.43
  1310.7 53.8 %all-gather.74.cloned.1.call-done = f32[3,1024,352]{1,2,0:T(8,128)} async-done(((f32[3,256,352]{1,2,0:T(8,128)}), f32[3,1024,352]{1,2,0:T(8,128)}) %all-gather.74.cloned.1.call-update) | async-done | bytes 4325392 | tf_op jit(solution)/shard_map/all_gather | solution.py:319
  1364.5 8.6 fusion.211
  1373.1 77.0 %all-reduce.16.cloned.1.call-done = f32[3,256,1024]{2,1,0:T(8,128)} async-done(((f32[3,256,1024]{2,1,0:T(8,128)}), f32[3,256,1024]{2,1,0:T(8,128)}) %all-reduce.16.cloned.1.call-update) | async-done | bytes 3145744 | tf_op jit(solution)/shard_map/psum | solution.py:328
  1458.6 53.4 %all-gather.76.cloned.1.call-done = f32[3,1024,352]{1,2,0:T(8,128)} async-done(((f32[3,256,352]{1,2,0:T(8,128)}), f32[3,1024,352]{1,2,0:T(8,128)}) %all-gather.76.cloned.1.call-update) | async-done | bytes 4325392 | tf_op jit(solution)/shard_map/all_gather | solution.py:359
  1512.0 8.5 fusion.42
  1527.9 46.5 %all-gather.78.cloned.1.call-done = f32[3,1024,352]{1,2,0:T(8,128)} async-done(((f32[3,256,352]{1,2,0:T(8,128)}), f32[3,1024,352]{1,2,0:T(8,128)}) %all-gather.78.cloned.1.call-update) | async-done | bytes 4325392 | tf_op jit(solution)/shard_map/all_gather | solution.py:319
  1574.4 8.2 fusion.213
  1582.7 47.6 %reduce-scatter.15.cloned.1.call-done = f32[256,1024]{1,0:T(8,128)} async-done(((f32[1024,1024]{1,0:T(8,128)}), f32[256,1024]{1,0:T(8,128)}) %reduce-scatter.15.cloned.1.call-update) | async-done | bytes 1048592 | tf_op jit(solution)/shard_map/reduce_scatter | solution.py:294
  1630.3 48.1 %reduce-scatter.13.cloned.1.call-done = f32[256,800]{0,1:T(8,128)} async-done(((f32[1024,800]{0,1:T(8,128)}), f32[256,800]{0,1:T(8,128)}) %reduce-scatter.13.cloned.1.call-update) | async-done | bytes 819216 | tf_op jit(solution)/shard_map/reduce_scatter | solution.py:293
  1678.4 115.6 %all-reduce.18.cloned.1.call-done = (f32[256,800]{0,1:T(8,128)}, f32[256,1024]{1,0:T(8,128)}, f32[3,256,1024]{2,1,0:T(8,128)}) async-done(((f32[256,800]{0,1:T(8,128)}, f32[256,1024]{1,0:T(8,128)}, f32[3,256,1024]{2,1,0:T(8,128)}), (f32[256,800]{0,1:T(8,128)}, f32[256,1024]{1,0:T(8,128)}, f32[3,256,1024]{2,1,0:T(8,128)})) %all-reduce.18.cloned.1.call-update) | async-done | bytes 5013520 | tf_op jit(solution)/shard_map/psum | solution.py:298
  1799.1 42.3 %all-gather.42.cloned.1.call-done = f32[1024,800]{0,1:T(8,128)} async-done(((f32[256,800]{0,1:T(8,128)}), f32[1024,800]{0,1:T(8,128)}) %all-gather.42.cloned.1.call-update) | async-done | bytes 3276816 | tf_op jit(solution)/shard_map/all_gather | solution.py:317
  1868.7 28.0 %all-gather.52.cloned.1.call-done = f32[1024,1024]{1,0:T(8,128)} async-done(((f32[256,1024]{1,0:T(8,128)}), f32[1024,1024]{1,0:T(8,128)}) %all-gather.52.cloned.1.call-update) | async-done | bytes 4194320 | tf_op jit(solution)/shard_map/all_gather | solution.py:318
  1920.3 24.0 all-gather.44.cloned.1.call-done
  1967.7 31.7 %all-gather.54.cloned.1.call-done = f32[1024,1024]{1,0:T(8,128)} async-done(((f32[256,1024]{1,0:T(8,128)}), f32[1024,1024]{1,0:T(8,128)}) %all-gather.54.cloned.1.call-update) | async-done | bytes 4194320 | tf_op jit(solution)/shard_map/all_gather | solution.py:318
  2018.3 28.6 %all-gather.46.cloned.1.call-done = f32[1024,800]{0,1:T(8,128)} async-done(((f32[256,800]{0,1:T(8,128)}), f32[1024,800]{0,1:T(8,128)}) %all-gather.46.cloned.1.call-update) | async-done | bytes 3276816 | tf_op jit(solution)/shard_map/all_gather | solution.py:317
  2068.5 33.7 %all-gather.56.cloned.1.call-done = f32[1024,1024]{1,0:T(8,128)} async-done(((f32[256,1024]{1,0:T(8,128)}), f32[1024,1024]{1,0:T(8,128)}) %all-gather.56.cloned.1.call-update) | async-done | bytes 4194320 | tf_op jit(solution)/shard_map/all_gather | solution.py:318
  2128.3 8.4 fusion.214
  2137.1 12.4 all-gather.48.cloned.1.call-done
  2172.1 32.8 %all-gather.58.cloned.1.call-done = f32[1024,1024]{1,0:T(8,128)} async-done(((f32[256,1024]{1,0:T(8,128)}), f32[1024,1024]{1,0:T(8,128)}) %all-gather.58.cloned.1.call-update) | async-done | bytes 4194320 | tf_op jit(solution)/shard_map/all_gather | solution.py:318
  2224.1 72.8 %reduce-scatter.9.cloned.1.call-done = f32[256,1024]{1,0:T(8,128)} async-done(((f32[2048,1024]{1,0:T(8,128)}), f32[256,1024]{1,0:T(8,128)}) %reduce-scatter.9.cloned.1.call-update) | async-done | bytes 1048592 | tf_op jit(solution)/shard_map/reduce_scatter | solution.py:236
  2302.8 48.0 %all-gather.80.cloned.1.call-done = f32[3,1024,352]{1,2,0:T(8,128)} async-done(((f32[3,256,352]{1,2,0:T(8,128)}), f32[3,1024,352]{1,2,0:T(8,128)}) %all-gather.80.cloned.1.call-update) | async-done | bytes 4325392 | tf_op jit(solution)/shard_map/all_gather | solution.py:359
  2360.4 37.7 %all-gather.50.cloned.1.call-done = f32[1024,800]{0,1:T(8,128)} async-done(((f32[256,800]{0,1:T(8,128)}), f32[1024,800]{0,1:T(8,128)}) %all-gather.50.cloned.1.call-update) | async-done | bytes 3276816 | tf_op jit(solution)/shard_map/all_gather | solution.py:317
  2416.6 36.3 %all-gather.60.cloned.1.call-done = f32[1024,1024]{1,0:T(8,128)} async-done(((f32[256,1024]{1,0:T(8,128)}), f32[1024,1024]{1,0:T(8,128)}) %all-gather.60.cloned.1.call-update) | async-done | bytes 4194320 | tf_op jit(solution)/shard_map/all_gather | solution.py:318
  (536 shorter events, 448.1 us)
Async XLA Ops:
  7.2 37.3 %all-gather.30.cloned.1.call-start = ((), (), s32[]{:S(2)}) async-start(), calls=%async_computation.7 | async-start | bytes 2048000 | tf_op jit(solution)/shard_map/all_gather | solution.py:208
  9.3 73.0 %all-gather.28.cloned.1.call-start = ((), (), s32[]{:S(2)}) async-start(), calls=%async_computation.6 | async-start | bytes 2621440 | tf_op jit(solution)/shard_map/all_gather | solution.py:216
  10.6 75.7 %copy-start.87 = (f32[256]{0:T(256)}, f32[256]{0:T(256)S(1)}, u32[]{:S(2)}) copy-start(f32[256]{0:T(256)S(1)} %add_rsqrt_fusion.1) | copy-start | bytes 3076
  11.4 74.9 %copy-start.85 = (f32[1,1024]{1,0:T(1,128)}, f32[1,1024]{1,0:T(1,128)S(1)}, u32[]{:S(2)}) copy-start(f32[1,1024]{1,0:T(1,128)S(1)} %get-tuple-element.42) | copy-start | bytes 12292
  11.4 430.7 %copy-start.83 = (f32[1,1024]{1,0:T(1,128)}, f32[1,1024]{1,0:T(1,128)S(1)}, u32[]{:S(2)}) copy-start(f32[1,1024]{1,0:T(1,128)S(1)} %get-tuple-element.41) | copy-start | bytes 12292
  13.5 222.7 %all-gather.32.cloned.1.call-start = ((), (), s32[]{:S(2)}) async-start(), calls=%async_computation.8 | async-start | bytes 2621440 | tf_op jit(solution)/shard_map/all_gather | solution.py:209
  14.4 246.5 %all-gather.36.cloned.1.call-start = ((), (), s32[]{:S(2)}) async-start(), calls=%async_computation.10 | async-start | bytes 1802240 | tf_op jit(solution)/shard_map/all_gather | solution.py:210
  15.3 272.4 %all-gather.34.cloned.1.call-start = ((), (), s32[]{:S(2)}) async-start(), calls=%async_computation.9 | async-start | bytes 4718592 | tf_op jit(solution)/shard_map/all_gather | solution.py:228
  87.0 57.1 %copy-start.47 = (f32[1024,96]{0,1:T(8,128)}, f32[1024,96]{0,1:T(8,128)S(1)}, u32[]{:S(2)}) copy-start(f32[1024,96]{0,1:T(8,128)S(1)} %slice.274) | copy-start | bytes 1179652
  178.9 52.1 %copy-start.72 = (f32[16,512]{1,0:T(8,128)}, f32[16,512]{1,0:T(8,128)S(1)}, u32[]{:S(2)}) copy-start(f32[16,512]{1,0:T(8,128)S(1)} %get-tuple-element.47) | copy-start | bytes 98308
  187.3 43.6 %copy-start.74 = (f32[16,512]{1,0:T(8,128)}, f32[16,512]{1,0:T(8,128)S(1)}, u32[]{:S(2)}) copy-start(f32[16,512]{1,0:T(8,128)S(1)} %fusion.6) | copy-start | bytes 98308
  238.9 203.2 %copy-start.5 = (f32[256,1024]{1,0:T(8,128)}, f32[256,1024]{1,0:T(8,128)S(1)}, u32[]{:S(2)}) copy-start(f32[256,1024]{1,0:T(8,128)S(1)} %get-tuple-element.50) | copy-start | bytes 3145732
  238.9 203.2 %copy-start.89 = (f32[256]{0:T(256)}, f32[256]{0:T(256)S(1)}, u32[]{:S(2)}) copy-start(f32[256]{0:T(256)S(1)} %add_rsqrt_fusion) | copy-start | bytes 3076
  240.0 95.5 %all-gather.38.cloned.1.call-start = ((), (), s32[]{:S(2)}) async-start(), calls=%async_computation.12 | async-start | bytes 4718592 | tf_op jit(solution)/shard_map/all_gather | solution.py:241
  242.9 197.6 %reduce-scatter.11.cloned.1.call-start = ((), (), s32[]{:S(2)}) async-start(), calls=%async_computation.13 | async-start | bytes 9437184 | tf_op jit(solution)/shard_map/reduce_scatter | solution.py:250
  352.0 143.6 %reduce-scatter.17.cloned.1.call-start = ((), (), s32[]{:S(2)}) async-start(), calls=%async_computation.27 | async-start | bytes 5406720 | tf_op jit(solution)/shard_map/reduce_scatter | solution.py:295
  363.7 169.7 %all-gather.40.cloned.1.call-start = ((), (), s32[]{:S(2)}) async-start(), calls=%async_computation.14 | async-start | bytes 2621440 | tf_op jit(solution)/shard_map/all_gather | solution.py:259
  445.1 50.5 %copy-start.62 = (f32[2,256,352]{1,2,0:T(8,128)S(1)}, f32[2,256,352]{1,2,0:T(8,128)}, u32[]{:S(2)}) copy-start(f32[2,256,352]{1,2,0:T(8,128)} %param.25) | copy-start | bytes 2162692
  445.1 269.3 %all-gather.62.cloned.1.call-start = ((), (), s32[]{:S(2)}) async-start(), calls=%async_computation.28 | async-start | bytes 5406720 | tf_op jit(solution)/shard_map/all_gather | solution.py:319
  452.7 80.7 %copy-start.46 = (bf16[1024,1024]{1,0:T(8,128)(2,1)S(1)}, bf16[1024,1024]{1,0:T(8,128)(2,1)}, u32[]{:S(2)}) copy-start(bf16[1024,1024]{1,0:T(8,128)(2,1)} %all-gather.32.cloned.1.call-done) | copy-start | bytes 6291460
  498.1 242.4 %reduce-scatter.19.cloned.1.call-start = ((), (), s32[]{:S(2)}) async-start(), calls=%async_computation.42 | async-start | bytes 655360
  714.4 105.5 %all-reduce.10.cloned.1.call-start = ((), (), s32[]{:S(2)}) async-start(), calls=%async_computation.29 | async-start | bytes 6291456 | tf_op jit(solution)/shard_map/psum | solution.py:328
  722.8 159.2 %all-gather.64.cloned.1.call-start = ((), (), s32[]{:S(2)}) async-start(), calls=%async_computation.30 | async-start | bytes 5406720 | tf_op jit(solution)/shard_map/all_gather | solution.py:359
  828.4 116.2 %all-gather.66.cloned.1.call-start = ((), (), s32[]{:S(2)}) async-start(), calls=%async_computation.31 | async-start | bytes 5406720 | tf_op jit(solution)/shard_map/all_gather | solution.py:319
  890.8 139.5 %all-reduce.12.cloned.1.call-start = ((), (), s32[]{:S(2)}) async-start(), calls=%async_computation.32 | async-start | bytes 6291456 | tf_op jit(solution)/shard_map/psum | solution.py:328
  953.2 139.0 %copy-start.20 = (f32[3,256,352]{1,2,0:T(8,128)S(1)}, f32[3,256,352]{1,2,0:T(8,128)}, u32[]{:S(2)}) copy-start(f32[3,256,352]{1,2,0:T(8,128)} %fusion.45) | copy-start | bytes 3244036
  953.2 139.0 %all-gather.68.cloned.1.call-start = ((), (), s32[]{:S(2)}) async-start(), calls=%async_computation.33 | async-start | bytes 5406720 | tf_op jit(solution)/shard_map/all_gather | solution.py:359
  1038.5 116.0 %all-gather.70.cloned.1.call-start = ((), (), s32[]{:S(2)}) async-start(), calls=%async_computation.34 | async-start | bytes 5406720 | tf_op jit(solution)/shard_map/all_gather | solution.py:319
  1100.7 139.5 %all-reduce.14.cloned.1.call-start = ((), (), s32[]{:S(2)}) async-start(), calls=%async_computation.35 | async-start | bytes 6291456 | tf_op jit(solution)/shard_map/psum | solution.py:328
  1163.2 138.9 %copy-start.9 = (f32[3,256,352]{1,2,0:T(8,128)S(1)}, f32[3,256,352]{1,2,0:T(8,128)}, u32[]{:S(2)}) copy-start(f32[3,256,352]{1,2,0:T(8,128)} %fusion.44) | copy-start | bytes 3244036
  1163.2 138.9 %all-gather.72.cloned.1.call-start = ((), (), s32[]{:S(2)}) async-start(), calls=%async_computation.36 | async-start | bytes 5406720 | tf_op jit(solution)/shard_map/all_gather | solution.py:359
  1248.4 116.0 %all-gather.74.cloned.1.call-start = ((), (), s32[]{:S(2)}) async-start(), calls=%async_computation.37 | async-start | bytes 5406720 | tf_op jit(solution)/shard_map/all_gather | solution.py:319
  1310.6 139.5 %all-reduce.16.cloned.1.call-start = ((), (), s32[]{:S(2)}) async-start(), calls=%async_computation.38 | async-start | bytes 6291456 | tf_op jit(solution)/shard_map/psum | solution.py:328
  1373.1 139.0 %copy-start.10 = (f32[3,256,352]{1,2,0:T(8,128)S(1)}, f32[3,256,352]{1,2,0:T(8,128)}, u32[]{:S(2)}) copy-start(f32[3,256,352]{1,2,0:T(8,128)} %fusion.43) | copy-start | bytes 3244036
  1373.1 139.0 %all-gather.76.cloned.1.call-start = ((), (), s32[]{:S(2)}) async-start(), calls=%async_computation.39 | async-start | bytes 5406720 | tf_op jit(solution)/shard_map/all_gather | solution.py:359
  1458.4 62.3 %copy-start.30 = (bf16[256,1024]{1,0:T(8,128)(2,1)S(1)}, bf16[256,1024]{1,0:T(8,128)(2,1)}, u32[]{:S(2)}) copy-start(bf16[256,1024]{1,0:T(8,128)(2,1)} %fusion.177) | copy-start | bytes 1572868
  1458.4 116.0 %all-gather.78.cloned.1.call-start = ((), (), s32[]{:S(2)}) async-start(), calls=%async_computation.40 | async-start | bytes 5406720 | tf_op jit(solution)/shard_map/all_gather | solution.py:319
  1520.6 109.6 %reduce-scatter.15.cloned.1.call-start = ((), (), s32[]{:S(2)}) async-start(), calls=%async_computation.21 | async-start | bytes 5242880 | tf_op jit(solution)/shard_map/reduce_scatter | solution.py:294
  1524.5 49.9 %copy-start.8 = (f32[3,256,352]{1,2,0:T(8,128)S(1)}, f32[3,256,352]{1,2,0:T(8,128)}, u32[]{:S(2)}) copy-start(f32[3,256,352]{1,2,0:T(8,128)} %fusion.42) | copy-start | bytes 3244036
  1524.5 153.8 %reduce-scatter.13.cloned.1.call-start = ((), (), s32[]{:S(2)}) async-start(), calls=%async_computation.15 | async-start | bytes 4096000 | tf_op jit(solution)/shard_map/reduce_scatter | solution.py:293
  1527.9 266.1 %all-reduce.18.cloned.1.call-start = ((), (), s32[]{:S(2)}) async-start(), calls=%async_computation.43 | async-start | bytes 10027008 | tf_op jit(solution)/shard_map/psum | solution.py:298
  1678.3 118.1 %copy-start.57 = (f32[256,1024]{1,0:T(8,128)S(1)}, f32[256,1024]{1,0:T(8,128)}, u32[]{:S(2)}) copy-start(f32[256,1024]{1,0:T(8,128)} %param.23) | copy-start | bytes 3145732
  1678.3 163.0 %all-gather.42.cloned.1.call-start = ((), (), s32[]{:S(2)}) async-start(), calls=%async_computation.16 | async-start | bytes 4096000 | tf_op jit(solution)/shard_map/all_gather | solution.py:317
  1796.4 100.3 %all-gather.52.cloned.1.call-start = ((), (), s32[]{:S(2)}) async-start(), calls=%async_computation.22 | async-start | bytes 5242880 | tf_op jit(solution)/shard_map/all_gather | solution.py:318
  1798.8 145.4 %all-gather.44.cloned.1.call-start = ((), (), s32[]{:S(2)}) async-start(), calls=%async_computation.17 | async-start | bytes 4096000 | tf_op jit(solution)/shard_map/all_gather | solution.py:317
  1868.7 130.7 %all-gather.54.cloned.1.call-start = ((), (), s32[]{:S(2)}) async-start(), calls=%async_computation.23 | async-start | bytes 5242880 | tf_op jit(solution)/shard_map/all_gather | solution.py:318
  1920.0 126.9 %all-gather.46.cloned.1.call-start = ((), (), s32[]{:S(2)}) async-start(), calls=%async_computation.18 | async-start | bytes 4096000 | tf_op jit(solution)/shard_map/all_gather | solution.py:317
  1957.6 41.8 %copy-start.21 = (f32[256,1024]{1,0:T(8,128)S(1)}, f32[256,1024]{1,0:T(8,128)}, u32[]{:S(2)}) copy-start(f32[256,1024]{1,0:T(8,128)} %fusion.50) | copy-start | bytes 3145732
  1967.7 134.5 %all-gather.56.cloned.1.call-start = ((), (), s32[]{:S(2)}) async-start(), calls=%async_computation.24 | async-start | bytes 5242880 | tf_op jit(solution)/shard_map/all_gather | solution.py:318
  2017.8 131.7 %all-gather.48.cloned.1.call-start = ((), (), s32[]{:S(2)}) async-start(), calls=%async_computation.19 | async-start | bytes 4096000 | tf_op jit(solution)/shard_map/all_gather | solution.py:317
  2058.3 43.9 %copy-start.14 = (f32[256,1024]{1,0:T(8,128)S(1)}, f32[256,1024]{1,0:T(8,128)}, u32[]{:S(2)}) copy-start(f32[256,1024]{1,0:T(8,128)} %fusion.49) | copy-start | bytes 3145732
  2068.5 136.4 %all-gather.58.cloned.1.call-start = ((), (), s32[]{:S(2)}) async-start(), calls=%async_computation.25 | async-start | bytes 5242880 | tf_op jit(solution)/shard_map/all_gather | solution.py:318
  2120.6 176.3 %reduce-scatter.9.cloned.1.call-start = ((), (), s32[]{:S(2)}) async-start(), calls=%async_computation.11 | async-start | bytes 9437184 | tf_op jit(solution)/shard_map/reduce_scatter | solution.py:236
  2128.2 222.6 %all-gather.80.cloned.1.call-start = ((), (), s32[]{:S(2)}) async-start(), calls=%async_computation.41 | async-start | bytes 5406720 | tf_op jit(solution)/shard_map/all_gather | solution.py:359
  2136.7 261.5 %all-gather.50.cloned.1.call-start = ((), (), s32[]{:S(2)}) async-start(), calls=%async_computation.20 | async-start | bytes 4096000 | tf_op jit(solution)/shard_map/all_gather | solution.py:317
  2171.1 281.8 %all-gather.60.cloned.1.call-start = ((), (), s32[]{:S(2)}) async-start(), calls=%async_computation.26 | async-start | bytes 5242880 | tf_op jit(solution)/shard_map/all_gather | solution.py:318
  2218.4 78.5 %copy-start.6 = (f32[256,1024]{1,0:T(8,128)S(1)}, f32[256,1024]{1,0:T(8,128)}, u32[]{:S(2)}) copy-start(f32[256,1024]{1,0:T(8,128)} %copy-done.5) | copy-start | bytes 3145732
  2218.4 78.5 %copy-start.84 = (f32[1,1024]{1,0:T(1,128)S(1)}, f32[1,1024]{1,0:T(1,128)}, u32[]{:S(2)}) copy-start(f32[1,1024]{1,0:T(1,128)} %copy-done.83) | copy-start | bytes 12292
  2218.4 78.5 %copy-start.90 = (f32[256]{0:T(256)S(1)}, f32[256]{0:T(256)}, u32[]{:S(2)}) copy-start(f32[256]{0:T(256)} %copy-done.89) | copy-start | bytes 3076
  2218.4 78.5 %copy-start.92 = (f32[256]{0:T(256)S(1)}, f32[256]{0:T(256)}, u32[]{:S(2)}) copy-start(f32[256]{0:T(256)} %copy-done.91) | copy-start | bytes 3076
  2296.9 53.8 %copy-start.19 = (f32[3,256,352]{1,2,0:T(8,128)S(1)}, f32[3,256,352]{1,2,0:T(8,128)}, u32[]{:S(2)}) copy-start(f32[3,256,352]{1,2,0:T(8,128)} %fusion.214) | copy-start | bytes 3244036
  2350.8 51.9 %copy-start.69 = (f32[256,96]{0,1:T(8,128)S(1)}, f32[256,96]{0,1:T(8,128)}, u32[]{:S(2)}) copy-start(f32[256,96]{0,1:T(8,128)} %get-tuple-element.93) | copy-start | bytes 294916
  2358.8 44.2 %copy-start.77 = (f32[256,32]{0,1:T(8,128)S(1)}, f32[256,32]{0,1:T(8,128)}, u32[]{:S(2)}) copy-start(f32[256,32]{0,1:T(8,128)} %get-tuple-element.95) | copy-start | bytes 98308
  2412.5 40.4 %copy-start.11 = (f32[256,1024]{1,0:T(8,128)S(1)}, f32[256,1024]{1,0:T(8,128)}, u32[]{:S(2)}) copy-start(f32[256,1024]{1,0:T(8,128)} %fusion.47) | copy-start | bytes 3145732
  (82 other events, 939.4 us)
Sparse Core Ops, SparseCore 0:
  10.4 34.0 all-gather.29
  47.0 35.3 all-gather.27
  84.7 35.2 all-gather.31
  122.3 29.7 all-gather.35
  240.2 47.4 all-gather.33
  289.7 45.8 all-gather.37
  352.1 88.3 reduce-scatter.10
  443.5 52.1 reduce-scatter.16
  498.1 35.3 all-gather.39
  535.1 53.6 all-gather.61
  714.5 25.9 reduce-scatter.18
  742.8 77.0 all-reduce.9
  828.5 53.4 all-gather.63
  890.9 53.6 all-gather.65
  953.3 76.9 all-reduce.11
  1038.6 53.4 all-gather.67
  1100.8 53.6 all-gather.69
  1163.3 76.9 all-reduce.13
  1248.6 53.4 all-gather.71
  1310.8 53.6 all-gather.73
  1373.2 76.9 all-reduce.15
  1458.5 53.4 all-gather.75
  1520.7 53.6 all-gather.77
  1577.5 52.6 reduce-scatter.14
  1633.3 45.0 reduce-scatter.12
  1680.8 113.1 all-reduce.17
  1796.5 44.8 all-gather.41
  1843.9 52.7 all-gather.51
  1899.3 44.9 all-gather.43
  1946.6 52.6 all-gather.53
  2001.9 44.9 all-gather.45
  2049.5 52.6 all-gather.55
  2104.6 44.9 all-gather.47
  2152.1 52.6 all-gather.57
  2207.3 89.5 reduce-scatter.8
  2298.7 52.0 all-gather.79
  2353.2 44.9 all-gather.49
  2400.1 52.7 all-gather.59
where the time goes:
time: 2490 us; the launch traced here: 2480 us
  waiting for transfers between devices  1650 us (66%)
  matrix products  572 us (23%)
  other arithmetic  120 us (5%)
  local copies, waits for them, and re-layouts  72.5 us (3%)
  blocking collectives  35.2 us (1%)
    psum x4, waiting for transfers between devices, body(): lax.psum((gramian_row_matrix, column_squares), 'mp')  292 us
    all_gather x5, waiting for transfers between devices, body(): lax.all_gather(feedforward_first_product, 'dp', axis=1, tiled=True)  261 us
    all_gather x5, waiting for transfers between devices, body(): lax.all_gather(feedforward_iterate_matrix, 'dp', axis=1, tiled=True)  208 us
    all_gather x5, waiting for transfers between devices, body(): lax.all_gather(out_iter, 'dp', axis=0, tiled=True)  162 us
    all_gather x5, waiting for transfers between devices, body(): lax.all_gather(factor_iter, 'dp', axis=0, tiled=True)  145 us
    psum x1, waiting for transfers between devices, body(): lax.psum((red_factor, red_out, red_gain), 'mp')  116 us
    dot_general x70, matrix products, exact(): return jnp.dot(left_mat, right_mat, precision=HIGH_PRECISION)  82.3 us
    reduce_scatter x1, waiting for transfers between devices, body(): lax.psum_scatter(product_nt(d_gate, gate_up_low[0]) + product_nt(d_upward...  76.8 us
  transfers between devices with their start and end apart: 38, of which 35 were waited for; matrix products, arithmetic and copies ran while one was open for 25% of the time, Pallas kernels for 0%

commit v1 on v0

v1 whole, which is shorter than its diff:
```python
import math
import jax
import jax.numpy as jnp
from jax import lax
from jax.experimental import pallas as pl
from jax.experimental.pallas import tpu as pltpu
BF=jnp.bfloat16; F32=jnp.float32
HEADS=16; HD=64; RQ=6; RK=2; D=1024
COEF_A=3.4445; COEF_B=-4.775; COEF_C=2.0315
NEG=-1e30

def split2(x):
    hi=x.astype(BF); return hi,(x-hi.astype(F32)).astype(BF)
def dot(a,b): return jnp.dot(a,b,preferred_element_type=F32)
def dot_nt(a,b): return lax.dot_general(a,b,(((1,),(1,)),((),())),preferred_element_type=F32)
def dot_tn(a,b): return lax.dot_general(a,b,(((0,),(0,)),((),())),preferred_element_type=F32)

def spread(shape, pair, rank):
    rows=lax.broadcasted_iota(jnp.int32,shape,0); lanes=lax.broadcasted_iota(jnp.int32,shape,1)
    return (rows==rank*HEADS+2*pair+lanes//HD).astype(BF)

def dup(dims,r):
    part=dims[:,r*HD:(r+1)*HD]
    return jnp.concatenate([part,part],axis=1)

def attn_fwd_body(base_ref,head_q,dim_q,head_k,dim_k,head_v,dim_v,o_ref,lse_ref,q_ref,k_ref,v_ref,bias_ref,hq,hk,hv,dq,dk,dv):
    rows,keys=o_ref.shape[0],k_ref.shape[0]
    r_id=lax.broadcasted_iota(jnp.int32,(rows,keys),0)+base_ref[0]*rows
    c_id=lax.broadcasted_iota(jnp.int32,(rows,keys),1)
    bias_ref[...]=jnp.where(c_id<=r_id,0.0,NEG)
    for src,dst in ((head_q,hq),(head_k,hk),(head_v,hv)):
        dst[0],dst[1]=split2(src[...])
    for src,dst,rank in ((dim_q,dq,RQ),(dim_k,dk,RK),(dim_v,dv,RK)):
        for r in range(rank):
            dst[r]=dup(src[...],r)*(1.0/rank)
    def compose(h,d,rank,pair):
        total=None
        for r in range(rank):
            e=spread((rank*HEADS,128),pair,r)
            term=(dot(h[0],e)+dot(h[1],e))*d[r]
            total=term if total is None else total+term
        return total.astype(BF)
    lane=lax.broadcasted_iota(jnp.int32,(1,128),1)
    def step(pair,_):
        cols=pl.ds(pl.multiple_of(pair*128,128),128)
        q=compose(hq,dq,RQ,pair); k=compose(hk,dk,RK,pair); v=compose(hv,dv,RK,pair)
        q_ref[:,cols]=q; k_ref[:,cols]=k; v_ref[:,cols]=v
        qs=q.astype(F32)*(HD**-0.5)
        out=None
        for half in range(2):
            keep=(lane//HD)==half
            qm=jnp.where(keep,qs,0.0).astype(BF)
            s=dot_nt(qm,k)+bias_ref[...]
            m=jnp.max(s,axis=1,keepdims=True)
            e=jnp.exp(s-m)
            l=jnp.sum(e,axis=1,keepdims=True)
            p=(e*(1.0/l)).astype(BF)
            o=dot(p,v)
            out=o if half==0 else jnp.where(keep,o,out)
            lse=m+jnp.log(l)
            col=lax.broadcasted_iota(jnp.int32,(1,HEADS),1)==2*pair+half
            lse_ref[...]=jnp.where(col,lse,lse_ref[...])
        o_ref[:,cols]=out.astype(BF)
        return 0
    lse_ref[...]=jnp.zeros_like(lse_ref)
    lax.fori_loop(0,HEADS//2,step,0)

def attn_fwd(base,head_q,dim_q,head_k,dim_k,head_v,dim_v,interpret=False):
    rows,keys=head_q.shape[0],head_k.shape[0]
    vm=pl.BlockSpec(memory_space=pltpu.VMEM)
    return pl.pallas_call(attn_fwd_body,
        out_shape=(jax.ShapeDtypeStruct((rows,D),BF),jax.ShapeDtypeStruct((rows,HEADS),F32),jax.ShapeDtypeStruct((rows,D),BF),jax.ShapeDtypeStruct((keys,D),BF),jax.ShapeDtypeStruct((keys,D),BF)),
        in_specs=[pl.BlockSpec(memory_space=pltpu.SMEM)]+[vm]*6,
        out_specs=(vm,)*5,
        scratch_shapes=[pltpu.VMEM((rows,keys),F32),pltpu.VMEM((2,rows,RQ*HEADS),BF),pltpu.VMEM((2,keys,RK*HEADS),BF),pltpu.VMEM((2,keys,RK*HEADS),BF),
          pltpu.VMEM((RQ,rows,128),F32),pltpu.VMEM((RK,keys,128),F32),pltpu.VMEM((RK,keys,128),F32)],
        compiler_params=pltpu.CompilerParams(vmem_limit_bytes=48<<20),name="attn_fwd",interpret=interpret,
    )(base,head_q,dim_q,head_k,dim_k,head_v,dim_v)

def attn_bwd_body(base_ref,q_ref,k_ref,v_ref,do_ref,lse_ref,head_q,dim_q,head_k,dim_k,head_v,dim_v,
                  dhq_ref,ddq_ref,dhk_ref,ddk_ref,dhv_ref,ddv_ref,bias_ref,hq,hk,hv,dq,dk,dv,aq,ak,av):
    rows,keys=q_ref.shape[0],k_ref.shape[0]
    r_id=lax.broadcasted_iota(jnp.int32,(rows,keys),0)+base_ref[0]*rows
    c_id=lax.broadcasted_iota(jnp.int32,(rows,keys),1)
    bias_ref[...]=jnp.where(c_id<=r_id,0.0,NEG)
    for src,dst in ((head_q,hq),(head_k,hk),(head_v,hv)):
        dst[0],dst[1]=split2(src[...])
    for src,dst,rank in ((dim_q,dq,RQ),(dim_k,dk,RK),(dim_v,dv,RK)):
        for r in range(rank):
            dst[r]=dup(src[...],r)
    for ref in (aq,ak,av,dhq_ref,dhk_ref,dhv_ref): ref[...]=jnp.zeros_like(ref)
    lane=lax.broadcasted_iota(jnp.int32,(1,128),1)
    def back(grad,h,d,acc,dh_ref,rank,pair):
        total=None
        for r in range(rank):
            e=spread((rank*HEADS,128),pair,r)
            acc[r]+=grad*(dot(h[0],e)+dot(h[1],e))
            hi,lo=split2(grad*d[r])
            t=dot_nt(hi,e)+dot_nt(lo,e)
            total=t if total is None else total+t
        dh_ref[...]+=total
    def step(pair,_):
        cols=pl.ds(pl.multiple_of(pair*128,128),128)
        q=q_ref[:,cols]; k=k_ref[:,cols]; v=v_ref[:,cols]; do=do_ref[:,cols]
        qs=q.astype(F32)*(HD**-0.5); dof=do.astype(F32)
        gq=gk=gv=None
        for half in range(2):
            keep=(lane//HD)==half
            qm=jnp.where(keep,qs,0.0).astype(BF); dom=jnp.where(keep,dof,0.0).astype(BF)
            col=lax.broadcasted_iota(jnp.int32,(1,HEADS),1)==2*pair+half
            lse=jnp.sum(jnp.where(col,lse_ref[...],0.0),axis=1,keepdims=True)
            p=jnp.exp(dot_nt(qm,k)+bias_ref[...]-lse)
            dp=dot_nt(dom,v)
            inner=jnp.sum(p*dp,axis=1,keepdims=True)
            ds=(p*(dp-inner)).astype(BF)
            nq=dot(ds,k); nk=dot_tn(ds,qm); nv=dot_tn(p.astype(BF),dom)
            if half==0: gq,gk,gv=nq,nk,nv
            else:
                gq=jnp.where(keep,nq,gq); gk=gk+nk; gv=gv+nv
        scale=HD**-0.5
        back(gq*(scale/RQ),hq,dq,aq,dhq_ref,RQ,pair)
        back(gk*(1.0/RK),hk,dk,ak,dhk_ref,RK,pair)
        back(gv*(1.0/RK),hv,dv,av,dhv_ref,RK,pair)
        return 0
    lax.fori_loop(0,HEADS//2,step,0)
    for acc,ref,rank in ((aq,ddq_ref,RQ),(ak,ddk_ref,RK),(av,ddv_ref,RK)):
        for r in range(rank):
            ref[:,r*HD:(r+1)*HD]=acc[r][:,:HD]+acc[r][:,HD:]

def attn_bwd(base,q,k,v,do,lse,head_q,dim_q,head_k,dim_k,head_v,dim_v,interpret=False):
    rows,keys=q.shape[0],k.shape[0]
    vm=pl.BlockSpec(memory_space=pltpu.VMEM)
    sd=jax.ShapeDtypeStruct
    return pl.pallas_call(attn_bwd_body,
        out_shape=(sd((rows,RQ*HEADS),F32),sd((rows,RQ*HD),F32),sd((keys,RK*HEADS),F32),sd((keys,RK*HD),F32),sd((keys,RK*HEADS),F32),sd((keys,RK*HD),F32)),
        in_specs=[pl.BlockSpec(memory_space=pltpu.SMEM)]+[vm]*11,
        out_specs=(vm,)*6,
        scratch_shapes=[pltpu.VMEM((rows,keys),F32),pltpu.VMEM((2,rows,RQ*HEADS),BF),pltpu.VMEM((2,keys,RK*HEADS),BF),pltpu.VMEM((2,keys,RK*HEADS),BF),
          pltpu.VMEM((RQ,rows,128),F32),pltpu.VMEM((RK,keys,128),F32),pltpu.VMEM((RK,keys,128),F32),
          pltpu.VMEM((RQ,rows,128),F32),pltpu.VMEM((RK,keys,128),F32),pltpu.VMEM((RK,keys,128),F32)],
        compiler_params=pltpu.CompilerParams(vmem_limit_bytes=56<<20),name="attn_bwd",interpret=interpret,
    )(base,q,k,v,do,lse,head_q,dim_q,head_k,dim_k,head_v,dim_v)

BK=256
def tri_cols(j): return (j*(j+1)//2)*BK

def store_sym(hi,lo,i,j,val):
    h,l=split2(val)
    hi[i*BK:(i+1)*BK,j*BK:(j+1)*BK]=h; lo[i*BK:(i+1)*BK,j*BK:(j+1)*BK]=l
    if i!=j:
        t=val.T
        h,l=split2(t)
        hi[j*BK:(j+1)*BK,i*BK:(i+1)*BK]=h; lo[j*BK:(j+1)*BK,i*BK:(i+1)*BK]=l

def mul_upper(xh,xl,yh,yl,n,emit):
    for j in range(n):
        top=(j+1)*BK; cs=slice(j*BK,(j+1)*BK)
        r=dot(xh[:top,:],yh[:,cs])+dot(xh[:top,:],yl[:,cs])+dot(xl[:top,:],yh[:,cs])
        for i in range(j+1): emit(i,j,r[i*BK:(i+1)*BK])

def ns_body(g_ref,y_ref,o_ref,a_up,ah,al,ph,pw,bh,bl):
    n=o_ref.shape[1]//BK
    eye=(lax.broadcasted_iota(jnp.int32,(BK,BK),0)==lax.broadcasted_iota(jnp.int32,(BK,BK),1)).astype(F32)
    blk=lambda i,j:(slice(i*BK,(i+1)*BK),slice(j*BK,(j+1)*BK))
    trace=None
    for j in range(n):
        off=tri_cols(j)+j*BK
        part=g_ref[:,off:off+BK]*eye
        trace=part if trace is None else trace+part
    trace=jnp.sum(jnp.sum(trace,axis=1,keepdims=True),axis=0,keepdims=True)
    scale=1.0/(jnp.sqrt(trace)+1e-7)
    for j in range(n):
        for i in range(j+1):
            off=tri_cols(j)+i*BK
            val=g_ref[:,off:off+BK]*(scale*scale)
            a_up[blk(i,j)]=val; store_sym(ah,al,i,j,val)
    o_ref[...]=y_ref[...]*scale
    def poly():
        def emit(i,j,c):
            store_sym(ph,pw,i,j,COEF_B*a_up[blk(i,j)]+COEF_C*c)
        mul_upper(ah,al,ah,al,n,emit)
    def apply():
        y=o_ref[...]; yh,yl=split2(y)
        o_ref[...]=COEF_A*y+(dot(yh,ph[...])+dot(yh,pw[...])+dot(yl,ph[...]))
    def step(_,c):
        poly()
        apply()
        def emit_b(i,j,m):
            val=COEF_A*a_up[blk(i,j)]+m
            a_up[blk(i,j)]=val; store_sym(bh,bl,i,j,val)
        mul_upper(ah,al,ph,pw,n,emit_b)
        def emit_a(i,j,m):
            val=COEF_A*a_up[blk(i,j)]+m
            a_up[blk(i,j)]=val; store_sym(ah,al,i,j,val)
        mul_upper(bh,bl,ph,pw,n,emit_a)
        return c
    lax.fori_loop(0,4,step,0)
    poly(); apply()

def ns_big(gram,y,interpret=False):
    w,d=y.shape
    vm=pl.BlockSpec(memory_space=pltpu.VMEM)
    return pl.pallas_call(ns_body,out_shape=jax.ShapeDtypeStruct((w,d),F32),
        in_specs=[vm,vm],out_specs=vm,
        scratch_shapes=[pltpu.VMEM((d,d),F32)]+[pltpu.VMEM((d,d),BF)]*6,
        compiler_params=pltpu.CompilerParams(vmem_limit_bytes=56<<20),name="ns_gram",interpret=interpret)(gram,y)

def gram_body(y_ref,g_ref):
    n=y_ref.shape[1]//BK
    yh,yl=split2(y_ref[...])
    for j in range(n):
        top=(j+1)*BK; cs=slice(j*BK,top)
        r=dot_tn(yh[:,:top],yh[:,cs])+dot_tn(yh[:,:top],yl[:,cs])+dot_tn(yl[:,:top],yh[:,cs])
        for i in range(j+1):
            off=tri_cols(j)+i*BK
            g_ref[:,off:off+BK]=r[i*BK:(i+1)*BK]

def gram_upper(y,interpret=False):
    d=y.shape[1]; n=d//BK
    vm=pl.BlockSpec(memory_space=pltpu.VMEM)
    return pl.pallas_call(gram_body,out_shape=jax.ShapeDtypeStruct((BK,n*(n+1)//2*BK),F32),in_specs=[vm],out_specs=vm,
        compiler_params=pltpu.CompilerParams(vmem_limit_bytes=48<<20),name="gram_upper",interpret=interpret)(y)

def mm3(x,y,f=dot):
    xh,xl=split2(x); yh,yl=split2(y)
    return f(xh,yh)+f(xh,yl)+f(xl,yh)

HEAD_SEGS=(RQ*HEADS,RK*HEADS,RK*HEADS)
def seg_mask(n,widths):
    def ids(axis):
        pos=lax.broadcasted_iota(jnp.int32,(n,n),axis); out=jnp.zeros_like(pos); edge=0
        for w in widths:
            edge+=w; out=out+(pos>=edge).astype(jnp.int32)
        return out
    return (ids(0)==ids(1)).astype(F32)

def ns_factor_body(fh_ref,fd_ref,oh_ref,od_ref,rh_ref,rd_ref):
    nh=fh_ref.shape[1]
    wq=RQ*HD; wk=RK*HD
    groups=((fh_ref,oh_ref,rh_ref,slice(0,nh),HEAD_SEGS),(fd_ref,od_ref,rd_ref,slice(0,wq),(wq,)),(fd_ref,od_ref,rd_ref,slice(wq,wq+2*wk),(wk,wk)))
    for full,own,out,cs,widths in groups:
        n=cs.stop-cs.start
        mask=seg_mask(n,widths)
        eye=(lax.broadcasted_iota(jnp.int32,(n,n),0)==lax.broadcasted_iota(jnp.int32,(n,n),1)).astype(F32)
        a=mm3(full[:,cs],full[:,cs],dot_tn)*mask
        diag=a*eye
        row=jnp.sum(mask*jnp.sum(diag,axis=1,keepdims=True),axis=0,keepdims=True)
        col=jnp.sum(mask*jnp.sum(diag,axis=0,keepdims=True),axis=1,keepdims=True)
        row=1.0/(jnp.sqrt(row)+1e-7); col=1.0/(jnp.sqrt(col)+1e-7)
        a=a*row*col; x=own[:,cs]*row
        def step(_,c):
            a,x=c
            p=COEF_B*a+COEF_C*mm3(a,a)
            x=COEF_A*x+mm3(x,p)
            b=COEF_A*a+mm3(a,p)
            return COEF_A*b+mm3(b,p),x
        a,x=lax.fori_loop(0,4,step,(a,x))
        out[:,cs]=COEF_A*x+mm3(x,COEF_B*a+COEF_C*mm3(a,a))

def ns_factor(fh,fd,oh,od,interpret=False):
    vm=pl.BlockSpec(memory_space=pltpu.VMEM)
    return pl.pallas_call(ns_factor_body,out_shape=(jax.ShapeDtypeStruct(oh.shape,F32),jax.ShapeDtypeStruct(od.shape,F32)),in_specs=[vm]*4,out_specs=(vm,vm),
        compiler_params=pltpu.CompilerParams(vmem_limit_bytes=48<<20),name="ns_factor",interpret=interpret)(fh,fd,oh,od)


EPS = 1e-06
MOMENTUM = 0.5
LEARN = 0.2
LEARN_VEC = 0.002
P = jax.sharding.PartitionSpec
NQ, NK = RQ * HEADS, RK * HEADS
WQ, WK = RQ * HD, RK * HD
FFN = 3


def normalize(values):
    row_scale = lax.rsqrt(jnp.mean(values * values, axis=-1, keepdims=True) + EPS)
    return values * row_scale, row_scale


def norm_back(grad_in, normed, row_scale, gain):
    scaled = grad_in * gain
    inner_sum = jnp.mean(scaled * normed, axis=-1, keepdims=True)
    return row_scale * (scaled - normed * inner_sum), jnp.sum(grad_in * normed, axis=0)


def dp_pairs(shift, keep=lambda target: True):
    return [(j, j ^ shift) for j in range(lax.axis_size("dp")) if keep(j ^ shift)]


def place(parts, axis):
    me = lax.axis_index("dp")
    step = parts[0].shape[axis]
    shape = list(parts[0].shape)
    shape[axis] *= len(parts)
    out = jnp.zeros(shape, parts[0].dtype)
    for shift, part in enumerate(parts):
        out = lax.dynamic_update_slice_in_dim(out, part, (me ^ shift) * step, axis)
    return out


def gather_dp(own, axis=0):
    return place([own] + [lax.ppermute(own, "dp", dp_pairs(s)) for s in range(1, lax.axis_size("dp"))], axis)


def scatter_mp(partial):
    mp = lax.axis_size("mp")
    if mp != 8:
        return lax.psum_scatter(partial, "mp", scatter_dimension=0, tiled=True)
    me = lax.axis_index("mp")
    rows = partial.shape[0] // mp
    blocks = partial.reshape(mp // 2, 2, rows, partial.shape[1])
    core, place_z = me % 2, me // 2
    away = lax.dynamic_index_in_dim(blocks, 1 - core, 1, keepdims=False).astype(BF)
    near = lax.dynamic_index_in_dim(blocks, core, 1, keepdims=False)
    near = near + lax.ppermute(away, "mp", [(j, j ^ 1) for j in range(mp)]).astype(F32)
    total = lax.dynamic_index_in_dim(near, place_z, 0, keepdims=False)
    for shift in range(1, mp // 2):
        block = lax.dynamic_index_in_dim(near, place_z ^ shift, 0, keepdims=False).astype(BF)
        total = total + lax.ppermute(block, "mp", [(j, j ^ (2 * shift)) for j in range(mp)]).astype(F32)
    return total


def body(
    tokens,
    cotangent,
    domain_ids,
    domain_weight,
    gains,
    gain_mom,
    factor_w,
    factor_mom,
    out_w,
    out_mom,
    gate_up_w,
    gate_up_mom,
    down_w,
    down_mom,
):
    n_dp, n_mp = lax.axis_size("dp"), lax.axis_size("mp")
    me, mz = lax.axis_index("dp"), lax.axis_index("mp")
    rows = tokens.shape[0]
    d_own = factor_w.shape[0]
    hidden_own = gate_up_w.shape[2]
    out_own = D // n_mp
    base = me.astype(jnp.int32).reshape(1)
    shifts = range(1, n_dp)
    ffn_slot = jnp.minimum(me, FFN - 1)

    factor_low = gather_dp(factor_w.astype(BF))
    x_float = tokens.astype(F32)
    first_normed, first_scale = normalize(x_float)
    first_own = (first_normed * gains[0]).astype(BF)
    factors = dot(first_own, factor_low)
    heads_q, heads_kv = factors[:, :NQ], factors[:, NQ : NQ + 2 * NK]
    dims_q, dims_kv = factors[:, NQ + 2 * NK : NQ + 2 * NK + WQ], factors[:, NQ + 2 * NK + WQ :]
    kv_all = gather_dp(jnp.concatenate([heads_kv, dims_kv], axis=1))
    parts = (
        heads_q,
        dims_q,
        kv_all[:, :NK],
        kv_all[:, 2 * NK : 2 * NK + WK],
        kv_all[:, NK : 2 * NK],
        kv_all[:, 2 * NK + WK :],
    )
    attended, lse, queries, key_vecs, values = attn_fwd(base, *parts)
    out_low = lax.all_gather(out_w.astype(BF), "dp", axis=0, tiled=True)
    residual = x_float + dot(attended, out_low)
    second_normed, second_scale = normalize(residual)

    ffn_old = jnp.stack([gate_up_w[0], gate_up_w[1], down_w.T])
    ffn_low = lax.all_gather(ffn_old.astype(BF), "dp", axis=1, tiled=True)
    gate_low, up_low, down_low = ffn_low[0], ffn_low[1], ffn_low[2]
    domain_range = jnp.arange(domain_weight.shape[0], dtype=jnp.int32)
    seq_weight = jnp.sum(jnp.where(domain_ids[0, 0] == domain_range, domain_weight, 0.0))
    d_output = cotangent.astype(F32) * seq_weight
    d_output_all = lax.all_gather(d_output.astype(BF), "mp", axis=0, tiled=True)
    second_in = lax.all_gather((second_normed * gains[1]).astype(BF), "mp", axis=0, tiled=True)
    gate_value = dot(second_in, gate_low)
    upward = dot(second_in, up_low)
    sigmoid_gate = jax.nn.sigmoid(gate_value)
    active = gate_value * sigmoid_gate
    hidden = (active * upward).astype(BF)
    d_hidden = dot(d_output_all, down_low)
    d_gate = (d_hidden * upward * sigmoid_gate * (1.0 + gate_value * (1.0 - sigmoid_gate))).astype(BF)
    d_upward = (d_hidden * active).astype(BF)
    d_second = scatter_mp(dot_nt(d_gate, gate_low) + dot_nt(d_upward, up_low))
    grads = jnp.stack([dot_tn(d_gate, second_in), dot_tn(d_upward, second_in), dot_tn(hidden, d_output_all)])
    branch = scatter_mp(dot_nt(hidden, down_low))
    block_out = (residual + branch).astype(BF)

    ffn_mom = jnp.stack([gate_up_mom[0].T, gate_up_mom[1].T, down_mom])
    to_ffn = lambda target: target < FFN
    own_mom = [lax.dynamic_index_in_dim(ffn_mom, ffn_slot, 0, keepdims=False)]
    matrix = lax.dynamic_index_in_dim(grads, ffn_slot, 0, keepdims=False)
    for s in shifts:
        slot = jnp.minimum(me ^ s, FFN - 1)
        own_mom.append(lax.ppermute(lax.dynamic_index_in_dim(ffn_mom, slot, 0, keepdims=False), "dp", dp_pairs(s, to_ffn)))
        matrix = matrix + lax.ppermute(lax.dynamic_index_in_dim(grads, slot, 0, keepdims=False), "dp", dp_pairs(s, to_ffn))
    matrix = matrix + MOMENTUM * place(own_mom, 1)

    d_resid_norm, gain_second = norm_back(d_second, second_normed, second_scale, gains[1])
    d_residual = d_output + d_resid_norm
    d_residual_low = d_residual.astype(BF)
    grad_out = None
    for s in range(n_dp):
        cols = lax.dynamic_slice_in_dim(attended, (me ^ s) * d_own, d_own, 1)
        block = dot_tn(d_residual_low, cols)
        if s:
            block = lax.ppermute(block, "dp", dp_pairs(s))
        grad_out = block if grad_out is None else grad_out + block
    grad_out = lax.psum_scatter(grad_out, "mp", scatter_dimension=0, tiled=True)
    out_tile = MOMENTUM * lax.dynamic_slice_in_dim(out_mom, mz * out_own, out_own, 1).T + grad_out
    new_out_mom = lax.all_gather(out_tile, "mp", axis=0, tiled=True).T
    out_rows = place([out_tile] + [lax.ppermute(out_tile, "dp", [(j ^ s, j) for j in range(FFN, n_dp)]) for s in shifts], 1)
    out_rows = jnp.pad(out_rows, ((0, hidden_own - out_own), (0, 0)))
    matrix = jnp.where(me < FFN, matrix, out_rows)
    gram = lax.psum(gram_upper(matrix), "mp")
    ortho = ns_big(gram, matrix)

    def give_back(whole):
        pieces = [lax.dynamic_slice_in_dim(whole, (me ^ s) * d_own, d_own, 1) for s in range(n_dp)]
        return place([pieces[0][None]] + [lax.ppermute(pieces[s], "dp", dp_pairs(s))[None] for s in shifts], 0)

    mom_back = give_back(matrix)
    ortho_back = give_back(ortho)
    turn = lambda stack: jnp.stack([stack[0].T, stack[1].T])
    ffn_rate = LEARN * 0.2 * math.sqrt(max(D, hidden_own * n_mp))
    new_gate_up_mom, new_down_mom = turn(mom_back), mom_back[2]
    new_gate_up_w = gate_up_w - ffn_rate * turn(ortho_back)
    new_down_w = down_w - ffn_rate * ortho_back[2]
    out_ortho = lax.all_gather(ortho_back[FFN, :out_own], "mp", axis=0, tiled=True).T
    new_out_w = out_w - LEARN * 0.2 * math.sqrt(D) * out_ortho

    d_attended = dot_nt(d_residual_low, out_low).astype(BF)
    dq_heads, dq_dims, dk_heads, dk_dims, dv_heads, dv_dims = attn_bwd(
        base, queries, key_vecs, values, d_attended, lse, *parts
    )
    d_kv_all = jnp.concatenate([dk_heads, dv_heads, dk_dims, dv_dims], axis=1)
    d_kv = None
    for s in range(n_dp):
        block = lax.dynamic_slice_in_dim(d_kv_all, (me ^ s) * rows, rows, 0)
        if s:
            block = lax.ppermute(block, "dp", dp_pairs(s))
        d_kv = block if d_kv is None else d_kv + block
    d_factors = jnp.concatenate([dq_heads, d_kv[:, : 2 * NK], dq_dims, d_kv[:, 2 * NK :]], axis=1).astype(BF)
    d_first = dot_nt(d_factors, factor_low)
    d_input_norm, gain_first = norm_back(d_first, first_normed, first_scale, gains[0])
    input_grad = d_residual + d_input_norm

    grad_factor = None
    for s in range(n_dp):
        cols = lax.dynamic_slice_in_dim(first_own, (me ^ s) * d_own, d_own, 1)
        block = dot_tn(cols, d_factors)
        if s:
            block = lax.ppermute(block, "dp", dp_pairs(s))
        grad_factor = block if grad_factor is None else grad_factor + block
    grad_factor = lax.psum(grad_factor, "mp")
    new_factor_mom = MOMENTUM * factor_mom + grad_factor
    head_cols = NQ + 2 * NK
    mom_heads = jnp.pad(new_factor_mom[:, :head_cols], ((0, 0), (0, 256 - head_cols)))
    mom_dims = new_factor_mom[:, head_cols:]
    factor_all = gather_dp(new_factor_mom)
    ortho_heads, ortho_dims = ns_factor(
        jnp.pad(factor_all[:, :head_cols], ((0, 0), (0, 256 - head_cols))), factor_all[:, head_cols:], mom_heads, mom_dims
    )
    widths = [NQ, NK, NK, WQ, WK, WK]
    factor_rate = jnp.concatenate([jnp.full((w,), LEARN * 0.2 * math.sqrt(max(D, w)), F32) for w in widths])
    new_factor_w = factor_w - factor_rate * jnp.concatenate([ortho_heads[:, :head_cols], ortho_dims], axis=1)

    gain_all = lax.psum(jnp.stack([gain_first, gain_second]), ("dp", "mp"))
    feature_count = gain_mom.shape[1]
    gain_grad = lax.dynamic_slice_in_dim(gain_all, me * feature_count, feature_count, 1)
    new_gain_mom = MOMENTUM * gain_mom + gain_grad
    new_gains = lax.dynamic_slice_in_dim(gains, me * feature_count, feature_count, 1) - LEARN_VEC * new_gain_mom
    return (
        block_out,
        input_grad,
        gain_grad,
        new_gains,
        new_gain_mom,
        new_factor_mom,
        new_factor_w,
        new_out_mom,
        new_out_w,
        new_gate_up_mom,
        new_gate_up_w,
        new_down_mom,
        new_down_w,
    )


def solution(mesh):
    token = P(("mp", "dp"), None)
    row = P("dp", None)
    ffn = P(None, "dp", "mp")
    down = P("mp", "dp")
    vec = P(None, "dp")
    return jax.shard_map(
        body,
        mesh=mesh,
        in_specs=(token, token, P("mp", None), P(), P(), vec, row, row, row, row, ffn, ffn, down, down),
        out_specs=(token, token, vec, vec, vec, row, row, row, row, ffn, ffn, down, down),
        check_vma=False,
    )
```

time: 2490 us -> 868 us (0.35)
  waiting for transfers between devices: 1650 us -> 361 us
  matrix products: 572 us -> 53.1 us
  Pallas kernels: 0 us -> 168 us
  starting transfers between devices: 4.16 us -> 94.8 us
  other arithmetic: 120 us -> 40.6 us
    all_gather x27 -> x6, waiting for transfers between devices: 944 us -> 96.2 us  [the longest x1 49.4 us: body(): lax.all_gather((second_normed * gains[1]).astype(BF), 'mp', axis=0, tiled...]
    dot_general x161 -> x21, matrix products: 572 us -> 53.1 us  [the longest x5 21.6 us: dot(): return jnp.dot(a, b, preferred_element_type=F32)]
    psum x5 -> x1, waiting for transfers between devices: 408 us -> 0.01 us  [body(): grad_factor = lax.psum(grad_factor, 'mp')]
    reduce_scatter x5 -> x1, waiting for transfers between devices: 284 us -> 0.01 us  [body(): grad_out = lax.psum_scatter(grad_out, 'mp', scatter_dimension=0, tiled=True)]
    ppermute x0 -> x41, waiting for transfers between devices: none -> 264 us  [the longest x9 87.4 us: body(): block = lax.ppermute(block, 'dp', dp_pairs(s))]
    pallas_call x0 -> x5, Pallas kernels: none -> 168 us  [the longest x1 86.5 us: ns_big(): pl.pallas_call(ns_body, out_shape=jax.ShapeDtypeStruct((w, d), F32), in_s...]
    ppermute x0 -> x41, starting transfers between devices: none -> 93.8 us  [the longest x3 26.8 us: body(): lax.ppermute(out_tile, 'dp', [(j ^ s, j) for j in range(FFN, n_dp)])]
    convert_element_type x10 -> x5, other arithmetic: 51.1 us -> 6.03 us  [the longest x1 2.17 us: body(): out_low = lax.all_gather(out_w.astype(BF), 'dp', axis=0, tiled=True)]
  transfers between devices with their start and end apart: 38 -> 49, of which waited for: 35 -> 22; matrix products, arithmetic and copies ran while one was open for 25% -> 15% of each run, Pallas kernels for 0% -> 9%
where the time goes in v1:
time: 868 us; the launch traced here: 860 us
  waiting for transfers between devices  361 us (42%)
  Pallas kernels  168 us (19%)
  starting transfers between devices  94.8 us (11%)
  local copies, waits for them, and re-layouts  73.2 us (8%)
  blocking collectives  53.9 us (6%)
  matrix products  53.1 us (6%)
  other arithmetic  40.6 us (5%)
  between operations  16.7 us (2%)
    ppermute x9, waiting for transfers between devices, body(): block = lax.ppermute(block, 'dp', dp_pairs(s))  87.4 us
    pallas_call x1, Pallas kernels, ns_big(): pl.pallas_call(ns_body, out_shape=jax.ShapeDtypeStruct((w, d), F32), in_s...  86.5 us
    ppermute x6, waiting for transfers between devices, scatter_mp(): lax.ppermute(block, 'mp', [(j, j ^ 2 * shift) for j in range(mp)])  64.8 us
    ppermute x6, waiting for transfers between devices, give_back(): lax.ppermute(pieces[s], 'dp', dp_pairs(s))[None]  58.2 us
    psum x1, blocking collectives, body(): gain_all = lax.psum(jnp.stack([gain_first, gain_second]), ('dp', 'mp'))  53.9 us
    all_gather x1, waiting for transfers between devices, body(): lax.all_gather((second_normed * gains[1]).astype(BF), 'mp', axis=0, tiled...  49.4 us
    ppermute x9, waiting for transfers between devices, gather_dp(): lax.ppermute(own, 'dp', dp_pairs(s))  46.3 us
    all_gather x1, waiting for transfers between devices, body(): d_output_all = lax.all_gather(d_output.astype(BF), 'mp', axis=0, tiled=True)  37.7 us
  transfers between devices with their start and end apart: 49, of which 22 were waited for; matrix products, arithmetic and copies ran while one was open for 15% of the time, Pallas kernels for 9%

profile of v1, /device:TPU:0, one launch (start us, length us, event | category | flops | bytes accessed | tf_op | source)
XLA Modules:
  0.0 860.5 jit_solution(14854698148372288553)
XLA Ops:
  11.5 2.9 collective-permute-start
  17.4 10.4 %collective-permute-done = bf16[256,800]{0,1:T(8,128)(2,1)} collective-permute-done((bf16[256,800]{0,1:T(8,128)(2,1)}, bf16[256,800]{0,1:T(8,128)(2,1)}, u32[]{:S(2)}, u32[]{:S(2)}) %collective-permute-start) | collective-permute-done | bytes 409632 | tf_op jit(solution)/shard_map/ppermute | solution.py:303
  28.8 4.9 collective-permute-done.1
  34.7 5.1 collective-permute-done.2
  46.2 15.1 %collective-permute-done.3 = f32[256,320]{1,0:T(8,128)S(1)} collective-permute-done((f32[256,320]{1,0:T(8,128)S(1)}, f32[256,320]{1,0:T(8,128)S(1)}, u32[]{:S(2)}, u32[]{:S(2)}) %collective-permute-start.3) | collective-permute-done | bytes 327712 | tf_op jit(solution)/shard_map/ppermute | solution.py:303
  61.4 6.0 collective-permute-done.4
  67.4 4.9 collective-permute-done.5
  72.9 18.5 %attn_fwd.1 = (bf16[256,1024]{1,0:T(8,128)(2,1)S(1)}, f32[256,16]{1,0:T(8,128)S(1)}, bf16[256,1024]{1,0:T(8,128)(2,1)S(1)}, bf16[1024,1024]{1,0:T(8,128)(2,1)S(1)}, bf16[1024,1024]{1,0:T(8,128)(2,1)}) custom-call(s32[1]{0:T(128)} %bitcast.base_ref, f32[256,96]{1,0:T(8,128)S(1)} %slice.125.head_q, f32[256,384]{1,0:T(8,128)S(1)} %slice.126.dim_q, ...), custom_call_target="tpu_custom_call" | custom-call | tf_op jit(solution)/shard_map/attn_fwd/pallas_call | solution.py:71
  95.0 2.6 multiply_reduce_fusion.2
  102.1 9.1 %all-gather.12.cloned.1.call-done = bf16[3,1024,352]{1,2,0:T(8,128)(2,1)} async-done(((bf16[3,256,352]{1,2,0:T(8,128)(2,1)}), bf16[3,1024,352]{1,2,0:T(8,128)(2,1)}) %all-gather.12.cloned.1.call-update) | async-done | bytes 2162704 | tf_op jit(solution)/shard_map/all_gather | solution.py:372
  111.2 49.4 %all-gather.10.cloned.1.call-done = bf16[2048,1024]{1,0:T(8,128)(2,1)} async-done(((bf16[256,1024]{1,0:T(8,128)(2,1)}), bf16[2048,1024]{1,0:T(8,128)(2,1)}) %all-gather.10.cloned.1.call-update) | async-done | bytes 4194320 | tf_op jit(solution)/shard_map/all_gather | solution.py:378
  160.6 5.8 fusion.35
  166.4 4.4 fusion.36
  170.7 37.7 %all-gather.14.cloned.1.call-done = bf16[2048,1024]{1,0:T(8,128)(2,1)} async-done(((bf16[256,1024]{1,0:T(8,128)(2,1)}), bf16[2048,1024]{1,0:T(8,128)(2,1)}) %all-gather.14.cloned.1.call-update) | async-done | bytes 4194320 | tf_op jit(solution)/shard_map/all_gather | solution.py:377
  208.5 8.0 multiply_convert_fusion
  216.5 2.4 fusion.34
  218.9 2.4 convolution_add_fusion
  221.3 3.3 copy-done.15
  228.7 3.3 collective-permute-start.29
  235.4 2.5 copy.108
  237.9 2.4 copy.106
  241.1 2.4 copy.96
  244.7 7.6 collective-permute-done.30
  255.5 3.9 dot_general.69
  259.5 3.5 bitcast_add_fusion
  265.0 2.7 collective-permute-start.13
  267.7 3.5 fusion.11
  273.1 13.5 %collective-permute-done.11 = bf16[256,1024]{1,0:T(8,128)(2,1)S(1)} collective-permute-done((bf16[256,1024]{1,0:T(8,128)(2,1)S(1)}, bf16[256,1024]{1,0:T(8,128)(2,1)S(1)}, u32[]{:S(2)}, u32[]{:S(2)}) %collective-permute-start.11) | collective-permute-done | bytes 524320 | tf_op jit(solution)/shard_map/ppermute | solution.py:320
  286.6 15.1 %collective-permute-done.12 = bf16[256,1024]{1,0:T(8,128)(2,1)S(1)} collective-permute-done((bf16[256,1024]{1,0:T(8,128)(2,1)S(1)}, bf16[256,1024]{1,0:T(8,128)(2,1)S(1)}, u32[]{:S(2)}, u32[]{:S(2)}) %collective-permute-start.12) | collective-permute-done | bytes 524320 | tf_op jit(solution)/shard_map/ppermute | solution.py:320
  305.3 2.9 collective-permute-start.25
  310.0 2.8 convolution_bitcast_fusion.2
  312.8 2.8 convolution_bitcast_fusion
  315.6 15.3 %collective-permute-done.23 = f32[1024,256]{1,0:T(8,128)S(1)} collective-permute-done((f32[1024,256]{1,0:T(8,128)S(1)}, f32[1024,256]{1,0:T(8,128)S(1)}, u32[]{:S(2)}, u32[]{:S(2)}) %collective-permute-start.23) | collective-permute-done | bytes 1048608 | tf_op jit(solution)/shard_map/ppermute | solution.py:410
  330.9 17.7 %collective-permute-done.25 = f32[1024,256]{1,0:T(8,128)S(1)} collective-permute-done((f32[1024,256]{1,0:T(8,128)S(1)}, f32[1024,256]{1,0:T(8,128)S(1)}, u32[]{:S(2)}, u32[]{:S(2)}) %collective-permute-start.25) | collective-permute-done | bytes 1048608 | tf_op jit(solution)/shard_map/ppermute | solution.py:410
  350.1 3.1 convolution_convert_fusion.do_ref
  353.3 35.7 %attn_bwd.1 = (f32[256,96]{1,0:T(8,128)}, f32[256,384]{1,0:T(8,128)}, f32[1024,32]{1,0:T(8,128)}, f32[1024,128]{1,0:T(8,128)}, f32[1024,32]{1,0:T(8,128)}, /*index=5*/f32[1024,128]{1,0:T(8,128)}) custom-call(s32[1]{0:T(128)} %bitcast.base_ref, bf16[256,1024]{1,0:T(8,128)(2,1)} %copy-done.13, bf16[1024,1024]{1,0:T(8,128)(2,1)} %copy-done.11, ...), custom_call_target="tpu_custom_call" | custom-call | tf_op jit(solution)/shard_map/attn_bwd/pallas_call | solution.py:134
  388.9 2.5 pad_maximum_fusion.1
  397.7 3.7 collective-permute-start.26
  403.7 3.0 collective-permute-start.27
  406.7 5.9 collective-permute-done.16
  415.3 2.6 bitcast_add_fusion.1
  426.8 46.3 %collective-permute-done.18 = f32[256,800]{0,1:T(8,128)} collective-permute-done((f32[256,800]{0,1:T(8,128)}, f32[256,800]{0,1:T(8,128)}, u32[]{:S(2)}, u32[]{:S(2)}) %collective-permute-start.18) | collective-permute-done | bytes 819232 | tf_op jit(solution)/shard_map/ppermute | solution.py:456
  475.0 4.1 fusion.20
  485.4 2.4 copy.99
  488.5 24.7 %collective-permute-start.34 = (f32[128,256]{1,0:T(8,128)}, f32[128,256]{1,0:T(8,128)S(1)}, u32[]{:S(2)}, u32[]{:S(2)}) collective-permute-start(f32[128,256]{1,0:T(8,128)} %get-tuple-element.100), channel_id=1, source_target_pairs={{0,24},{1,25},{2,26},{3,27},{4,28},{5,29},{6,30},{7,31}} | collective-permute-start | bytes 393224 | tf_op jit(solution)/shard_map/ppermute | solution.py:415
  513.3 2.2 add_add_fusion
  516.5 15.3 %collective-permute-start.7 = (bf16[256,1024]{1,0:T(8,128)(2,1)}, bf16[256,1024]{1,0:T(8,128)(2,1)}, u32[]{:S(2)}, u32[]{:S(2)}) collective-permute-start(bf16[256,1024]{1,0:T(8,128)(2,1)} %get-tuple-element.116), channel_id=1, source_target_pairs={{0,2},{1,3},{2,0},{3,1},{4,6},{5,7},{6,4},{7,5},{8,10},{9,11},{10,... | collective-permute-start | bytes 1572872 | tf_op jit(solution)/shard_map/ppermute | solution.py:320
  531.9 2.3 collective-permute-start.9
  535.1 3.7 fusion.10.y_ref
  538.8 2.2 gram_upper.1
  542.6 11.9 %collective-permute-done.7 = bf16[256,1024]{1,0:T(8,128)(2,1)} collective-permute-done((bf16[256,1024]{1,0:T(8,128)(2,1)}, bf16[256,1024]{1,0:T(8,128)(2,1)}, u32[]{:S(2)}, u32[]{:S(2)}) %collective-permute-start.7) | collective-permute-done | bytes 524320 | tf_op jit(solution)/shard_map/ppermute | solution.py:320
  554.5 17.5 %collective-permute-done.8 = bf16[256,1024]{1,0:T(8,128)(2,1)} collective-permute-done((bf16[256,1024]{1,0:T(8,128)(2,1)}, bf16[256,1024]{1,0:T(8,128)(2,1)}, u32[]{:S(2)}, u32[]{:S(2)}) %collective-permute-start.8) | collective-permute-done | bytes 524320 | tf_op jit(solution)/shard_map/ppermute | solution.py:320
  572.0 6.9 collective-permute-done.9
  578.9 4.9 fusion.19
  584.5 53.9 %psum.21 = f32[2,1024]{1,0:T(2,128)S(1)} all-reduce(f32[2,1024]{1,0:T(2,128)S(1)} %pad_maximum_fusion.7), channel_id=1, replica_groups=mesh['dp'=4,'mp'=8] {'dp','mp'}, use_global_device_ids=true, to_apply=%region_7.8 | all-reduce | flops 2048 | bytes 16384 | tf_op jit(solution)/shard_map/psum | solution.py:471
  639.7 2.3 collective-permute-start.39
  643.6 13.9 %collective-permute-done.39 = f32[352,256]{1,0:T(8,128)S(1)} collective-permute-done((f32[352,256]{1,0:T(8,128)S(1)}, f32[352,256]{1,0:T(8,128)S(1)}, u32[]{:S(2)}, u32[]{:S(2)}) %collective-permute-start.39) | collective-permute-done | bytes 360480 | tf_op jit(solution)/shard_map/ppermute | solution.py:423
  659.3 2.5 copy.111
  661.9 86.5 %ns_gram.1 = f32[352,1024]{1,0:T(8,128)} custom-call(f32[256,2560]{1,0:T(8,128)} %get-tuple-element.96.g_ref, f32[352,1024]{1,0:T(8,128)} %copy-done.2), custom_call_target="tpu_custom_call" | custom-call | tf_op jit(solution)/shard_map/ns_gram/pallas_call | solution.py:203
  748.4 2.2 constant_dynamic-slice_fusion.2
  764.3 44.3 %collective-permute-done.36 = f32[352,256]{1,0:T(8,128)S(1)} collective-permute-done((f32[352,256]{1,0:T(8,128)}, f32[352,256]{1,0:T(8,128)S(1)}, u32[]{:S(2)}, u32[]{:S(2)}) %collective-permute-start.36) | collective-permute-done | bytes 360480 | tf_op jit(solution)/shard_map/ppermute | solution.py:423
  815.0 2.4 copy.105
  820.4 2.7 slice.139.fd_ref
  824.4 24.6 %ns_factor.1 = (f32[256,256]{1,0:T(8,128)S(1)}, f32[256,640]{1,0:T(8,128)S(1)}) custom-call(f32[1024,256]{1,0:T(8,128)S(1)} %slice_select_fusion.fh_ref, f32[1024,640]{1,0:T(8,128)S(1)} %slice.139.fd_ref, f32[256,256]{1,0:T(8,128)S(1)} %slice_select_fusion.1.oh_ref, f32[256,640]{1,0:T(8,128)S(1)} %slice.141.od_ref), custom_call_target="tpu_custom_call" | custom-call | tf_op jit(solution)/shard_map/ns_factor/pallas_call | solution.py:262
  (328 shorter events, 112.6 us)
Async XLA Ops:
  7.2 233.1 %copy-start = (f32[256,1024]{1,0:T(8,128)S(1)}, f32[256,1024]{1,0:T(8,128)}, u32[]{:S(2)}) copy-start(f32[256,1024]{1,0:T(8,128)} %param.23) | copy-start | bytes 3145732
  7.2 87.8 %all-gather.8.cloned.1.call-start = ((), (), s32[]{:S(2)}) async-start(), calls=%async_computation.1 | async-start | bytes 2621440 | tf_op jit(solution)/shard_map/all_gather | solution.py:367
  9.4 101.8 %all-gather.12.cloned.1.call-start = ((), (), s32[]{:S(2)}) async-start(), calls=%async_computation.3 | async-start | bytes 2703360 | tf_op jit(solution)/shard_map/all_gather | solution.py:372
  11.5 16.3 %collective-permute-start = (bf16[256,800]{0,1:T(8,128)(2,1)}, bf16[256,800]{0,1:T(8,128)(2,1)}, u32[]{:S(2)}, u32[]{:S(2)}) collective-permute-start(bf16[256,800]{0,1:T(8,128)(2,1)} %get-tuple-element.106), channel_id=1, source_target_pairs={{0,8},{8,0},{16,24},{24,16},{1,9},{9,1},{17,25},{25,17},{2,10},{10... | collective-permute-start | bytes 1228808 | tf_op jit(solution)/shard_map/ppermute | solution.py:303
  14.4 19.2 %collective-permute-start.1 = (bf16[256,800]{0,1:T(8,128)(2,1)}, bf16[256,800]{0,1:T(8,128)(2,1)}, u32[]{:S(2)}, u32[]{:S(2)}) collective-permute-start(bf16[256,800]{0,1:T(8,128)(2,1)} %get-tuple-element.106), channel_id=1, source_target_pairs={{0,16},{8,24},{16,0},{24,8},{1,17},{9,25},{17,1},{25,9},{2,18},{10... | collective-permute-start | bytes 1228808 | tf_op jit(solution)/shard_map/ppermute | solution.py:303
  15.9 23.9 %collective-permute-start.2 = (bf16[256,800]{0,1:T(8,128)(2,1)}, bf16[256,800]{0,1:T(8,128)(2,1)}, u32[]{:S(2)}, u32[]{:S(2)}) collective-permute-start(bf16[256,800]{0,1:T(8,128)(2,1)} %get-tuple-element.106), channel_id=1, source_target_pairs={{0,24},{8,16},{16,8},{24,0},{1,25},{9,17},{17,9},{25,1},{2,26},{10... | collective-permute-start | bytes 1228808 | tf_op jit(solution)/shard_map/ppermute | solution.py:303
  16.9 143.7 %all-gather.10.cloned.1.call-start = ((), (), s32[]{:S(2)}) async-start(), calls=%async_computation.2 | async-start | bytes 4718592 | tf_op jit(solution)/shard_map/all_gather | solution.py:378
  17.4 24.3 %copy-start.37 = (bf16[256,1024]{1,0:T(8,128)(2,1)}, bf16[256,1024]{1,0:T(8,128)(2,1)S(1)}, u32[]{:S(2)}) copy-start(bf16[256,1024]{1,0:T(8,128)(2,1)S(1)} %fusion.15) | copy-start | bytes 1572868
  42.5 18.9 %collective-permute-start.3 = (f32[256,320]{1,0:T(8,128)S(1)}, f32[256,320]{1,0:T(8,128)S(1)}, u32[]{:S(2)}, u32[]{:S(2)}) collective-permute-start(f32[256,320]{1,0:T(8,128)S(1)} %get-tuple-element.144), channel_id=1, source_target_pairs={{0,8},{8,0},{16,24},{24,16},{1,9},{9,1},{17,25},{25,17},{2,10},{10... | collective-permute-start | bytes 983048 | tf_op jit(solution)/shard_map/ppermute | solution.py:303
  44.0 23.3 %collective-permute-start.4 = (f32[256,320]{1,0:T(8,128)S(1)}, f32[256,320]{1,0:T(8,128)S(1)}, u32[]{:S(2)}, u32[]{:S(2)}) collective-permute-start(f32[256,320]{1,0:T(8,128)S(1)} %get-tuple-element.144), channel_id=1, source_target_pairs={{0,16},{8,24},{16,0},{24,8},{1,17},{9,25},{17,1},{25,9},{2,18},{10... | collective-permute-start | bytes 983048 | tf_op jit(solution)/shard_map/ppermute | solution.py:303
  44.5 27.7 %collective-permute-start.5 = (f32[256,320]{1,0:T(8,128)S(1)}, f32[256,320]{1,0:T(8,128)S(1)}, u32[]{:S(2)}, u32[]{:S(2)}) collective-permute-start(f32[256,320]{1,0:T(8,128)S(1)} %get-tuple-element.144), channel_id=1, source_target_pairs={{0,24},{8,16},{16,8},{24,0},{1,25},{9,17},{17,9},{25,1},{2,26},{10... | collective-permute-start | bytes 983048 | tf_op jit(solution)/shard_map/ppermute | solution.py:303
  46.2 26.7 %copy-start.8 = (f32[256,384]{1,0:T(8,128)}, f32[256,384]{1,0:T(8,128)S(1)}, u32[]{:S(2)}) copy-start(f32[256,384]{1,0:T(8,128)S(1)} %slice.126.dim_q) | copy-start | bytes 1179652
  46.2 26.6 %copy-start.12 = (f32[256,96]{1,0:T(8,128)}, f32[256,96]{1,0:T(8,128)S(1)}, u32[]{:S(2)}) copy-start(f32[256,96]{1,0:T(8,128)S(1)} %slice.125.head_q) | copy-start | bytes 294916
  72.8 24.8 %copy-start.6 = (f32[1024,32]{1,0:T(8,128)}, f32[1024,32]{1,0:T(8,128)S(1)}, u32[]{:S(2)}) copy-start(f32[1024,32]{1,0:T(8,128)S(1)} %get-tuple-element.124.head_v) | copy-start | bytes 393220
  72.8 24.8 %copy-start.7 = (f32[1024,32]{1,0:T(8,128)}, f32[1024,32]{1,0:T(8,128)S(1)}, u32[]{:S(2)}) copy-start(f32[1024,32]{1,0:T(8,128)S(1)} %get-tuple-element.125.head_k) | copy-start | bytes 393220
  98.7 109.8 %all-gather.14.cloned.1.call-start = ((), (), s32[]{:S(2)}) async-start(), calls=%async_computation.4 | async-start | bytes 4718592 | tf_op jit(solution)/shard_map/all_gather | solution.py:377
  101.6 323.4 %reduce-scatter.2.cloned.1.call-start = ((), (), s32[]{:S(2)}) async-start(), calls=%async_computation.5 | async-start | bytes 1179648 | tf_op jit(solution)/shard_map/reduce_scatter | solution.py:412
  226.4 33.1 %collective-permute-start.10 = (bf16[4,256,1024]{2,1,0:T(8,128)(2,1)}, bf16[4,256,1024]{2,1,0:T(8,128)(2,1)}, u32[]{:S(2)}, u32[]{:S(2)}) collective-permute-start(bf16[4,256,1024]{2,1,0:T(8,128)(2,1)} %fusion.2), channel_id=1, source_target_pairs={{0,1},{1,0},{2,3},{3,2},{4,5},{5,4},{6,7},{7,6},{8,9},{9,8},{10,11... | collective-permute-start | bytes 6291464 | tf_op jit(solution)/shard_map/ppermute | solution.py:316
  228.7 14.9 %collective-permute-start.29 = (f32[352,256]{1,0:T(8,128)}, f32[352,256]{1,0:T(8,128)}, u32[]{:S(2)}, u32[]{:S(2)}) collective-permute-start(f32[352,256]{1,0:T(8,128)} %get-tuple-element.139), channel_id=1, source_target_pairs={{0,8},{8,0},{24,16},{1,9},{9,1},{25,17},{2,10},{10,2},{26,18},{3,1... | collective-permute-start | bytes 1081352 | tf_op jit(solution)/shard_map/ppermute | solution.py:398
  232.1 20.3 %collective-permute-start.30 = (f32[352,256]{1,0:T(8,128)}, f32[352,256]{1,0:T(8,128)}, u32[]{:S(2)}, u32[]{:S(2)}) collective-permute-start(f32[352,256]{1,0:T(8,128)} %get-tuple-element.138), channel_id=1, source_target_pairs={{0,16},{16,0},{24,8},{1,17},{17,1},{25,9},{2,18},{18,2},{26,10},{3... | collective-permute-start | bytes 1081352 | tf_op jit(solution)/shard_map/ppermute | solution.py:398
  234.0 19.4 %collective-permute-start.31 = (f32[352,256]{1,0:T(8,128)}, f32[352,256]{1,0:T(8,128)}, u32[]{:S(2)}, u32[]{:S(2)}) collective-permute-start(f32[352,256]{1,0:T(8,128)} %get-tuple-element.137), channel_id=1, source_target_pairs={{8,16},{16,8},{24,0},{9,17},{17,9},{25,1},{10,18},{18,10},{26,2},{... | collective-permute-start | bytes 1081352 | tf_op jit(solution)/shard_map/ppermute | solution.py:398
  263.2 23.3 %collective-permute-start.11 = (bf16[256,1024]{1,0:T(8,128)(2,1)S(1)}, bf16[256,1024]{1,0:T(8,128)(2,1)S(1)}, u32[]{:S(2)}, u32[]{:S(2)}) collective-permute-start(bf16[256,1024]{1,0:T(8,128)(2,1)S(1)} %get-tuple-element.113), channel_id=1, source_target_pairs={{0,2},{1,3},{2,0},{3,1},{4,6},{5,7},{6,4},{7,5},{8,10},{9,11},{10,... | collective-permute-start | bytes 1572872 | tf_op jit(solution)/shard_map/ppermute | solution.py:320
  263.3 38.3 %collective-permute-start.12 = (bf16[256,1024]{1,0:T(8,128)(2,1)S(1)}, bf16[256,1024]{1,0:T(8,128)(2,1)S(1)}, u32[]{:S(2)}, u32[]{:S(2)}) collective-permute-start(bf16[256,1024]{1,0:T(8,128)(2,1)S(1)} %get-tuple-element.115), channel_id=1, source_target_pairs={{0,4},{1,5},{2,6},{3,7},{4,0},{5,1},{6,2},{7,3},{8,12},{9,13},{10,... | collective-permute-start | bytes 1572872 | tf_op jit(solution)/shard_map/ppermute | solution.py:320
  265.0 36.6 %collective-permute-start.13 = (bf16[256,1024]{1,0:T(8,128)(2,1)S(1)}, bf16[256,1024]{1,0:T(8,128)(2,1)S(1)}, u32[]{:S(2)}, u32[]{:S(2)}) collective-permute-start(bf16[256,1024]{1,0:T(8,128)(2,1)S(1)} %get-tuple-element.114), channel_id=1, source_target_pairs={{0,6},{1,7},{2,4},{3,5},{4,2},{5,3},{6,0},{7,1},{8,14},{9,15},{10,... | collective-permute-start | bytes 1572872 | tf_op jit(solution)/shard_map/ppermute | solution.py:320
  271.2 32.2 %copy-start.16 = (f32[4,2,256,1024]{3,2,1,0:T(8,128)}, f32[4,2,256,1024]{3,2,1,0:T(8,128)S(1)}, u32[]{:S(2)}) copy-start(f32[4,2,256,1024]{3,2,1,0:T(8,128)S(1)} %fusion.11) | copy-start | bytes 25165828
  273.1 29.1 %copy-start.27 = (bf16[256,1024]{1,0:T(8,128)(2,1)S(1)}, bf16[256,1024]{1,0:T(8,128)(2,1)}, u32[]{:S(2)}) copy-start(bf16[256,1024]{1,0:T(8,128)(2,1)} %param.15) | copy-start | bytes 1572868
  273.1 142.2 %collective-permute-start.6 = (bf16[4,256,1024]{2,1,0:T(8,128)(2,1)}, bf16[4,256,1024]{2,1,0:T(8,128)(2,1)}, u32[]{:S(2)}, u32[]{:S(2)}) collective-permute-start(bf16[4,256,1024]{2,1,0:T(8,128)(2,1)} %fusion.1), channel_id=1, source_target_pairs={{0,1},{1,0},{2,3},{3,2},{4,5},{5,4},{6,7},{7,6},{8,9},{9,8},{10,11... | collective-permute-start | bytes 6291464 | tf_op jit(solution)/shard_map/ppermute | solution.py:316
  304.7 26.2 %collective-permute-start.23 = (f32[1024,256]{1,0:T(8,128)S(1)}, f32[1024,256]{1,0:T(8,128)S(1)}, u32[]{:S(2)}, u32[]{:S(2)}) collective-permute-start(f32[1024,256]{1,0:T(8,128)S(1)} %fusion.51), channel_id=1, source_target_pairs={{0,8},{8,0},{16,24},{24,16},{1,9},{9,1},{17,25},{25,17},{2,10},{10... | collective-permute-start | bytes 3145736 | tf_op jit(solution)/shard_map/ppermute | solution.py:410
  305.3 25.5 %collective-permute-start.24 = (f32[1024,256]{1,0:T(8,128)S(1)}, f32[1024,256]{1,0:T(8,128)S(1)}, u32[]{:S(2)}, u32[]{:S(2)}) collective-permute-start(f32[1024,256]{1,0:T(8,128)S(1)} %fusion.49), channel_id=1, source_target_pairs={{0,16},{8,24},{16,0},{24,8},{1,17},{9,25},{17,1},{25,9},{2,18},{10... | collective-permute-start | bytes 3145736 | tf_op jit(solution)/shard_map/ppermute | solution.py:410
  305.3 43.2 %collective-permute-start.25 = (f32[1024,256]{1,0:T(8,128)S(1)}, f32[1024,256]{1,0:T(8,128)S(1)}, u32[]{:S(2)}, u32[]{:S(2)}) collective-permute-start(f32[1024,256]{1,0:T(8,128)S(1)} %fusion.47), channel_id=1, source_target_pairs={{0,24},{8,16},{16,8},{24,0},{1,25},{9,17},{17,9},{25,1},{2,26},{10... | collective-permute-start | bytes 3145736 | tf_op jit(solution)/shard_map/ppermute | solution.py:410
  349.9 309.5 %all-gather.16.cloned.1.call-start = ((), (), s32[]{:S(2)}) async-start(), calls=%async_computation.6 | async-start | bytes 1179648 | tf_op jit(solution)/shard_map/all_gather | solution.py:414
  391.5 12.1 %collective-permute-start.14 = (f32[256,320]{1,0:T(8,128)S(1)}, f32[256,320]{1,0:T(8,128)S(1)}, u32[]{:S(2)}, u32[]{:S(2)}) collective-permute-start(f32[256,320]{1,0:T(8,128)S(1)} %get-tuple-element.119), channel_id=1, source_target_pairs={{0,8},{8,0},{16,24},{24,16},{1,9},{9,1},{17,25},{25,17},{2,10},{10... | collective-permute-start | bytes 983048 | tf_op jit(solution)/shard_map/ppermute | solution.py:444
  393.0 13.7 %collective-permute-start.15 = (f32[256,320]{1,0:T(8,128)S(1)}, f32[256,320]{1,0:T(8,128)S(1)}, u32[]{:S(2)}, u32[]{:S(2)}) collective-permute-start(f32[256,320]{1,0:T(8,128)S(1)} %get-tuple-element.121), channel_id=1, source_target_pairs={{0,16},{8,24},{16,0},{24,8},{1,17},{9,25},{17,1},{25,9},{2,18},{10... | collective-permute-start | bytes 983048 | tf_op jit(solution)/shard_map/ppermute | solution.py:444
  393.9 18.7 %collective-permute-start.16 = (f32[256,320]{1,0:T(8,128)S(1)}, f32[256,320]{1,0:T(8,128)S(1)}, u32[]{:S(2)}, u32[]{:S(2)}) collective-permute-start(f32[256,320]{1,0:T(8,128)S(1)} %get-tuple-element.120), channel_id=1, source_target_pairs={{0,24},{8,16},{16,8},{24,0},{1,25},{9,17},{17,9},{25,1},{2,26},{10... | collective-permute-start | bytes 983048 | tf_op jit(solution)/shard_map/ppermute | solution.py:444
  397.7 118.7 %collective-permute-start.26 = (f32[352,1024]{1,0:T(8,128)}, f32[352,1024]{1,0:T(8,128)}, u32[]{:S(2)}, u32[]{:S(2)}) collective-permute-start(f32[352,1024]{1,0:T(8,128)} %get-tuple-element.110), channel_id=1, source_target_pairs={{0,8},{8,0},{24,16},{1,9},{9,1},{25,17},{2,10},{10,2},{26,18},{3,1... | collective-permute-start | bytes 4325384 | tf_op jit(solution)/shard_map/ppermute | solution.py:399
  403.7 130.6 %collective-permute-start.27 = (f32[352,1024]{1,0:T(8,128)}, f32[352,1024]{1,0:T(8,128)}, u32[]{:S(2)}, u32[]{:S(2)}) collective-permute-start(f32[352,1024]{1,0:T(8,128)} %get-tuple-element.112), channel_id=1, source_target_pairs={{0,16},{16,0},{24,8},{1,17},{17,1},{25,9},{2,18},{18,2},{26,10},{3... | collective-permute-start | bytes 4325384 | tf_op jit(solution)/shard_map/ppermute | solution.py:399
  414.4 58.7 %collective-permute-start.18 = (f32[256,800]{0,1:T(8,128)}, f32[256,800]{0,1:T(8,128)}, u32[]{:S(2)}, u32[]{:S(2)}) collective-permute-start(f32[256,800]{0,1:T(8,128)} %fusion.56), channel_id=1, source_target_pairs={{0,16},{8,24},{16,0},{24,8},{1,17},{9,25},{17,1},{25,9},{2,18},{10... | collective-permute-start | bytes 2457608 | tf_op jit(solution)/shard_map/ppermute | solution.py:456
  420.9 54.0 %copy-start.22 = (bf16[256,1024]{1,0:T(8,128)(2,1)S(1)}, bf16[256,1024]{1,0:T(8,128)(2,1)}, u32[]{:S(2)}) copy-start(bf16[256,1024]{1,0:T(8,128)(2,1)} %param.14) | copy-start | bytes 1572868
  420.9 58.7 %collective-permute-start.17 = (f32[256,800]{0,1:T(8,128)}, f32[256,800]{0,1:T(8,128)S(1)}, u32[]{:S(2)}, u32[]{:S(2)}) collective-permute-start(f32[256,800]{0,1:T(8,128)} %fusion.58), channel_id=1, source_target_pairs={{0,8},{8,0},{16,24},{24,16},{1,9},{9,1},{17,25},{25,17},{2,10},{10... | collective-permute-start | bytes 2457608 | tf_op jit(solution)/shard_map/ppermute | solution.py:456
  423.9 61.5 %collective-permute-start.19 = (f32[256,800]{0,1:T(8,128)}, f32[256,800]{0,1:T(8,128)}, u32[]{:S(2)}, u32[]{:S(2)}) collective-permute-start(f32[256,800]{0,1:T(8,128)} %fusion.54), channel_id=1, source_target_pairs={{0,24},{8,16},{16,8},{24,0},{1,25},{9,17},{17,9},{25,1},{2,26},{10... | collective-permute-start | bytes 2457608 | tf_op jit(solution)/shard_map/ppermute | solution.py:456
  426.8 235.1 %all-reduce.4.cloned.1.call-start = ((), (), s32[]{:S(2)}) async-start(), calls=%async_computation.8 | async-start | bytes 7077888 | tf_op jit(solution)/shard_map/psum | solution.py:458
  473.1 62.0 %collective-permute-start.28 = (f32[352,1024]{1,0:T(8,128)}, f32[352,1024]{1,0:T(8,128)}, u32[]{:S(2)}, u32[]{:S(2)}) collective-permute-start(f32[352,1024]{1,0:T(8,128)} %get-tuple-element.111), channel_id=1, source_target_pairs={{8,16},{16,8},{24,0},{9,17},{17,9},{25,1},{10,18},{18,10},{26,2},{... | collective-permute-start | bytes 4325384 | tf_op jit(solution)/shard_map/ppermute | solution.py:399
  480.5 8.0 collective-permute-start.32
  487.7 47.3 %copy-start.25 = (f32[352,1024]{1,0:T(8,128)S(1)}, f32[352,1024]{1,0:T(8,128)}, u32[]{:S(2)}) copy-start(f32[352,1024]{1,0:T(8,128)} %copy-done.24) | copy-start | bytes 4325380
  487.7 44.1 %collective-permute-start.33 = (f32[128,256]{1,0:T(8,128)}, f32[128,256]{1,0:T(8,128)S(1)}, u32[]{:S(2)}, u32[]{:S(2)}) collective-permute-start(f32[128,256]{1,0:T(8,128)} %get-tuple-element.100), channel_id=1, source_target_pairs={{8,24},{9,25},{10,26},{11,27},{12,28},{13,29},{14,30},{15,31}} | collective-permute-start | bytes 393224 | tf_op jit(solution)/shard_map/ppermute | solution.py:415
  488.5 43.4 %collective-permute-start.34 = (f32[128,256]{1,0:T(8,128)}, f32[128,256]{1,0:T(8,128)S(1)}, u32[]{:S(2)}, u32[]{:S(2)}) collective-permute-start(f32[128,256]{1,0:T(8,128)} %get-tuple-element.100), channel_id=1, source_target_pairs={{0,24},{1,25},{2,26},{3,27},{4,28},{5,29},{6,30},{7,31}} | collective-permute-start | bytes 393224 | tf_op jit(solution)/shard_map/ppermute | solution.py:415
  516.5 38.1 %collective-permute-start.7 = (bf16[256,1024]{1,0:T(8,128)(2,1)}, bf16[256,1024]{1,0:T(8,128)(2,1)}, u32[]{:S(2)}, u32[]{:S(2)}) collective-permute-start(bf16[256,1024]{1,0:T(8,128)(2,1)} %get-tuple-element.116), channel_id=1, source_target_pairs={{0,2},{1,3},{2,0},{3,1},{4,6},{5,7},{6,4},{7,5},{8,10},{9,11},{10,... | collective-permute-start | bytes 1572872 | tf_op jit(solution)/shard_map/ppermute | solution.py:320
  531.8 40.2 %collective-permute-start.8 = (bf16[256,1024]{1,0:T(8,128)(2,1)}, bf16[256,1024]{1,0:T(8,128)(2,1)}, u32[]{:S(2)}, u32[]{:S(2)}) collective-permute-start(bf16[256,1024]{1,0:T(8,128)(2,1)} %get-tuple-element.118), channel_id=1, source_target_pairs={{0,4},{1,5},{2,6},{3,7},{4,0},{5,1},{6,2},{7,3},{8,12},{9,13},{10,... | collective-permute-start | bytes 1572872 | tf_op jit(solution)/shard_map/ppermute | solution.py:320
  531.9 47.0 %collective-permute-start.9 = (bf16[256,1024]{1,0:T(8,128)(2,1)}, bf16[256,1024]{1,0:T(8,128)(2,1)}, u32[]{:S(2)}, u32[]{:S(2)}) collective-permute-start(bf16[256,1024]{1,0:T(8,128)(2,1)} %get-tuple-element.117), channel_id=1, source_target_pairs={{0,6},{1,7},{2,4},{3,5},{4,2},{5,3},{6,0},{7,1},{8,14},{9,15},{10,... | collective-permute-start | bytes 1572872 | tf_op jit(solution)/shard_map/ppermute | solution.py:320
  538.8 104.7 %copy-start.2 = (f32[352,1024]{1,0:T(8,128)}, f32[352,1024]{1,0:T(8,128)S(1)}, u32[]{:S(2)}) copy-start(f32[352,1024]{1,0:T(8,128)S(1)} %fusion.10.y_ref) | copy-start | bytes 4325380
  542.6 36.3 %copy-start.20 = (f32[256,1024]{1,0:T(8,128)S(1)}, f32[256,1024]{1,0:T(8,128)}, u32[]{:S(2)}) copy-start(f32[256,1024]{1,0:T(8,128)} %copy-done.19) | copy-start | bytes 3145732
  542.6 307.9 %all-gather.18.cloned.1.call-start = ((), (), s32[]{:S(2)}) async-start(), calls=%async_computation.7 | async-start | bytes 1179648 | tf_op jit(solution)/shard_map/all_gather | solution.py:432
  583.8 54.6 %copy-start.67 = (f32[2,256]{1,0:T(2,128)S(1)}, f32[2,256]{1,0:T(2,128)}, u32[]{:S(2)}) copy-start(f32[2,256]{1,0:T(2,128)} %param.19) | copy-start | bytes 6148
  583.9 59.7 %collective-permute-start.38 = (f32[352,256]{1,0:T(8,128)S(1)}, f32[352,256]{1,0:T(8,128)S(1)}, u32[]{:S(2)}, u32[]{:S(2)}) collective-permute-start(f32[352,256]{1,0:T(8,128)S(1)} %get-tuple-element.133), channel_id=1, source_target_pairs={{0,8},{8,0},{16,24},{24,16},{1,9},{9,1},{17,25},{25,17},{2,10},{10... | collective-permute-start | bytes 1081352 | tf_op jit(solution)/shard_map/ppermute | solution.py:423
  639.7 17.9 %collective-permute-start.39 = (f32[352,256]{1,0:T(8,128)S(1)}, f32[352,256]{1,0:T(8,128)S(1)}, u32[]{:S(2)}, u32[]{:S(2)}) collective-permute-start(f32[352,256]{1,0:T(8,128)S(1)} %get-tuple-element.132), channel_id=1, source_target_pairs={{0,16},{8,24},{16,0},{24,8},{1,17},{9,25},{17,1},{25,9},{2,18},{10... | collective-permute-start | bytes 1081352 | tf_op jit(solution)/shard_map/ppermute | solution.py:423
  642.0 15.6 %collective-permute-start.40 = (f32[352,256]{1,0:T(8,128)S(1)}, f32[352,256]{1,0:T(8,128)S(1)}, u32[]{:S(2)}, u32[]{:S(2)}) collective-permute-start(f32[352,256]{1,0:T(8,128)S(1)} %get-tuple-element.131), channel_id=1, source_target_pairs={{0,24},{8,16},{16,8},{24,0},{1,25},{9,17},{17,9},{25,1},{2,26},{10... | collective-permute-start | bytes 1081352 | tf_op jit(solution)/shard_map/ppermute | solution.py:423
  750.6 11.1 %collective-permute-start.35 = (f32[352,256]{1,0:T(8,128)}, f32[352,256]{1,0:T(8,128)}, u32[]{:S(2)}, u32[]{:S(2)}) collective-permute-start(f32[352,256]{1,0:T(8,128)} %get-tuple-element.136), channel_id=1, source_target_pairs={{0,8},{8,0},{16,24},{24,16},{1,9},{9,1},{17,25},{25,17},{2,10},{10... | collective-permute-start | bytes 1081352 | tf_op jit(solution)/shard_map/ppermute | solution.py:423
  756.6 55.5 %collective-permute-start.20 = (f32[256,800]{0,1:T(8,128)}, f32[256,800]{0,1:T(8,128)}, u32[]{:S(2)}, u32[]{:S(2)}) collective-permute-start(f32[256,800]{0,1:T(8,128)} %copy.109), channel_id=1, source_target_pairs={{0,8},{8,0},{16,24},{24,16},{1,9},{9,1},{17,25},{25,17},{2,10},{10... | collective-permute-start | bytes 2457608 | tf_op jit(solution)/shard_map/ppermute | solution.py:303
  757.1 56.5 %collective-permute-start.21 = (f32[256,800]{0,1:T(8,128)}, f32[256,800]{0,1:T(8,128)}, u32[]{:S(2)}, u32[]{:S(2)}) collective-permute-start(f32[256,800]{0,1:T(8,128)} %copy.109), channel_id=1, source_target_pairs={{0,16},{8,24},{16,0},{24,8},{1,17},{9,25},{17,1},{25,9},{2,18},{10... | collective-permute-start | bytes 2457608 | tf_op jit(solution)/shard_map/ppermute | solution.py:303
  758.6 56.4 %collective-permute-start.22 = (f32[256,800]{0,1:T(8,128)}, f32[256,800]{0,1:T(8,128)}, u32[]{:S(2)}, u32[]{:S(2)}) collective-permute-start(f32[256,800]{0,1:T(8,128)} %copy.109), channel_id=1, source_target_pairs={{0,24},{8,16},{16,8},{24,0},{1,25},{9,17},{17,9},{25,1},{2,26},{10... | collective-permute-start | bytes 2457608 | tf_op jit(solution)/shard_map/ppermute | solution.py:303
  760.1 48.5 %collective-permute-start.36 = (f32[352,256]{1,0:T(8,128)}, f32[352,256]{1,0:T(8,128)S(1)}, u32[]{:S(2)}, u32[]{:S(2)}) collective-permute-start(f32[352,256]{1,0:T(8,128)} %get-tuple-element.135), channel_id=1, source_target_pairs={{0,16},{8,24},{16,0},{24,8},{1,17},{9,25},{17,1},{25,9},{2,18},{10... | collective-permute-start | bytes 1081352 | tf_op jit(solution)/shard_map/ppermute | solution.py:423
  760.7 48.7 %copy-start.66 = (pred[256]{0:T(512)(128)(4,1)S(1)}, pred[256]{0:T(512)(128)(4,1)}, u32[]{:S(2)}) copy-start(pred[256]{0:T(512)(128)(4,1)} %constant.129.clone.1) | copy-start | bytes 772
  761.7 46.9 %collective-permute-start.37 = (f32[352,256]{1,0:T(8,128)S(1)}, f32[352,256]{1,0:T(8,128)S(1)}, u32[]{:S(2)}, u32[]{:S(2)}) collective-permute-start(f32[352,256]{1,0:T(8,128)S(1)} %copy-done.56), channel_id=1, source_target_pairs={{0,24},{8,16},{16,8},{24,0},{1,25},{9,17},{17,9},{25,1},{2,26},{10... | collective-permute-start | bytes 1081352 | tf_op jit(solution)/shard_map/ppermute | solution.py:423
  824.3 24.6 %copy-start.32 = (f32[256,800]{1,0:T(8,128)S(1)}, f32[256,800]{1,0:T(8,128)}, u32[]{:S(2)}) copy-start(f32[256,800]{1,0:T(8,128)} %copy.106) | copy-start | bytes 2457604
  (59 other events, 361.1 us)
Sparse Core Ops, SparseCore 0:
  10.4 63.1 all-gather.7
  76.1 35.0 all-gather.11
  113.4 47.1 all-gather.9
  162.6 45.8 all-gather.13
  350.0 42.0 reduce-scatter.1
  426.9 31.9 all-gather.15
  542.7 108.3 all-reduce.3
  809.4 20.5 all-gather.17

commit v2 on v1

v2 whole, which is shorter than its diff:
```python
import math
import jax
import jax.numpy as jnp
from jax import lax
from jax.experimental import pallas as pl
from jax.experimental.pallas import tpu as pltpu
BF=jnp.bfloat16; F32=jnp.float32
HEADS=16; HD=64; RQ=6; RK=2; D=1024
COEF_A=3.4445; COEF_B=-4.775; COEF_C=2.0315
NEG=-1e30
NS_STEPS=5

def split2(x):
    hi=x.astype(BF); return hi,(x-hi.astype(F32)).astype(BF)
def dot(a,b): return jnp.dot(a,b,preferred_element_type=F32)
def dot_nt(a,b): return lax.dot_general(a,b,(((1,),(1,)),((),())),preferred_element_type=F32)
def dot_tn(a,b): return lax.dot_general(a,b,(((0,),(0,)),((),())),preferred_element_type=F32)

def one_hot(rows, first, pair):
    row=lax.broadcasted_iota(jnp.int32,(rows,128),0); lane=lax.broadcasted_iota(jnp.int32,(rows,128),1)
    return (row==first+2*pair+(lane>=HD).astype(jnp.int32)).astype(BF)

def twice(dims,r,scale):
    part=dims[:,r*HD:(r+1)*HD]*scale
    return jnp.concatenate([part,part],axis=1)

WQ,WK=RQ*HD,RK*HD
NQ,NK=RQ*HEADS,RK*HEADS
SIDES=((0,RQ,0),(0,RK,0),(RK,RK,NK))

def attn_setup(base_ref,fq_ref,fk_ref,bias_ref,hq,hk,dq,dk,scaled):
    rows,keys=bias_ref.shape
    r_id=lax.broadcasted_iota(jnp.int32,(rows,keys),0)+base_ref[0]*rows
    c_id=lax.broadcasted_iota(jnp.int32,(rows,keys),1)
    bias_ref[...]=jnp.where(c_id<=r_id,0.0,NEG)
    hq[0],hq[1]=split2(fq_ref[:,WQ:]); hk[0],hk[1]=split2(fk_ref[:,2*WK:])
    for r in range(RQ): dq[r]=twice(fq_ref,r,1.0/RQ if scaled else 1.0)
    for r in range(2*RK): dk[r]=twice(fk_ref,r,1.0/RK if scaled else 1.0)

def attn_scratch(rows,keys):
    return [pltpu.VMEM((rows,keys),F32),pltpu.VMEM((2,rows,NQ),BF),pltpu.VMEM((2,keys,2*NK),BF),pltpu.VMEM((RQ,rows,128),F32),pltpu.VMEM((2*RK,keys,128),F32)]

def attn_fwd_body(base_ref,fq_ref,fk_ref,o_ref,lse_ref,q_ref,k_ref,v_ref,bias_ref,hq,hk,dq,dk):
    attn_setup(base_ref,fq_ref,fk_ref,bias_ref,hq,hk,dq,dk,True)
    def compose(h,d,side,pair):
        first,rank,head=side
        total=None
        for r in range(rank):
            e=one_hot(h.shape[2],head+r*HEADS,pair)
            term=(dot(h[0],e)+dot(h[1],e))*d[first+r]
            total=term if total is None else total+term
        return total.astype(BF)
    lane=lax.broadcasted_iota(jnp.int32,(1,128),1)
    head_id=lax.broadcasted_iota(jnp.int32,(1,HEADS),1)
    lse_ref[...]=jnp.zeros_like(lse_ref)
    def step(pair,_):
        cols=pl.ds(pl.multiple_of(pair*128,128),128)
        q=compose(hq,dq,SIDES[0],pair); k=compose(hk,dk,SIDES[1],pair); v=compose(hk,dk,SIDES[2],pair)
        q_ref[:,cols]=q; k_ref[:,cols]=k; v_ref[:,cols]=v
        qs=q.astype(F32)*(HD**-0.5)
        out=None
        for half in range(2):
            keep=(lane>=HD) if half else (lane<HD)
            qm=jnp.where(keep,qs,0.0).astype(BF)
            s=dot_nt(qm,k)+bias_ref[...]
            m=jnp.max(s,axis=1,keepdims=True)
            e=jnp.exp(s-m)
            l=jnp.sum(e,axis=1,keepdims=True)
            p=(e*(1.0/l)).astype(BF)
            o=dot(p,v)
            out=jnp.where(keep,o,out) if half else o
            lse_ref[...]=jnp.where(head_id==2*pair+half,m+jnp.log(l),lse_ref[...])
        o_ref[:,cols]=out.astype(BF)
        return 0
    lax.fori_loop(0,HEADS//2,step,0)

VM=pl.BlockSpec(memory_space=pltpu.VMEM)
SM=pl.BlockSpec(memory_space=pltpu.SMEM)
def shape(dims,dtype=F32): return jax.ShapeDtypeStruct(dims,dtype)
def cost(us): return pl.CostEstimate(flops=int(us*1.15e9),transcendentals=0,bytes_accessed=1<<20)
def limit(mib): return pltpu.CompilerParams(vmem_limit_bytes=mib<<20)

def attn_fwd(base,fq,fk,interpret=False):
    rows,keys=fq.shape[0],fk.shape[0]
    return pl.pallas_call(attn_fwd_body,
        out_shape=(shape((rows,D),BF),shape((rows,HEADS)),shape((rows,D),BF),shape((keys,D),BF),shape((keys,D),BF)),
        in_specs=[SM,VM,VM],out_specs=(VM,)*5,scratch_shapes=attn_scratch(rows,keys),
        compiler_params=limit(48),cost_estimate=cost(18),name="attn_fwd",interpret=interpret)(base,fq,fk)

def attn_bwd_body(base_ref,q_ref,k_ref,v_ref,do_ref,lse_ref,fq_ref,fk_ref,gq_ref,gk_ref,bias_ref,hq,hk,dq,dk,aq,ak,tq,tk):
    attn_setup(base_ref,fq_ref,fk_ref,bias_ref,hq,hk,dq,dk,False)
    for ref in (aq,ak,tq,tk): ref[...]=jnp.zeros_like(ref)
    lane=lax.broadcasted_iota(jnp.int32,(1,128),1)
    head_id=lax.broadcasted_iota(jnp.int32,(1,HEADS),1)
    def back(grad,h,d,acc,tot,side,pair):
        first,rank,head=side
        total=None
        for r in range(rank):
            e=one_hot(h.shape[2],head+r*HEADS,pair)
            acc[first+r]+=grad*(dot(h[0],e)+dot(h[1],e))
            hi,lo=split2(grad*d[first+r])
            t=dot_nt(hi,e)+dot_nt(lo,e)
            total=t if total is None else total+t
        tot[...]+=total
    def step(pair,_):
        cols=pl.ds(pl.multiple_of(pair*128,128),128)
        q=q_ref[:,cols]; k=k_ref[:,cols]; v=v_ref[:,cols]; do=do_ref[:,cols]
        qs=q.astype(F32)*(HD**-0.5); dof=do.astype(F32)
        gq=gk=gv=None
        for half in range(2):
            keep=(lane>=HD) if half else (lane<HD)
            qm=jnp.where(keep,qs,0.0).astype(BF); dom=jnp.where(keep,dof,0.0).astype(BF)
            lse=jnp.sum(jnp.where(head_id==2*pair+half,lse_ref[...],0.0),axis=1,keepdims=True)
            p=jnp.exp(dot_nt(qm,k)+bias_ref[...]-lse)
            dp=dot_nt(dom,v)
            inner=jnp.sum(p*dp,axis=1,keepdims=True)
            ds=(p*(dp-inner)).astype(BF)
            nq=dot(ds,k); nk=dot_tn(ds,qm); nv=dot_tn(p.astype(BF),dom)
            if half==0: gq,gk,gv=nq,nk,nv
            else:
                gq=jnp.where(keep,nq,gq); gk=gk+nk; gv=gv+nv
        back(gq*(HD**-0.5/RQ),hq,dq,aq,tq,SIDES[0],pair)
        back(gk*(1.0/RK),hk,dk,ak,tk,SIDES[1],pair)
        back(gv*(1.0/RK),hk,dk,ak,tk,SIDES[2],pair)
        return 0
    lax.fori_loop(0,HEADS//2,step,0)
    for acc,tot,ref in ((aq,tq,gq_ref),(ak,tk,gk_ref)):
        count=acc.shape[0]
        for r in range(0,count,2):
            even=acc[r]; odd=acc[r+1]
            ref[:,r*HD:(r+2)*HD]=jnp.concatenate([even[:,:HD]+even[:,HD:],odd[:,:HD]+odd[:,HD:]],axis=1)
        ref[:,count*HD:]=tot[...]

def attn_bwd(base,q,k,v,do,lse,fq,fk,interpret=False):
    rows,keys=q.shape[0],k.shape[0]
    return pl.pallas_call(attn_bwd_body,out_shape=(shape(fq.shape),shape(fk.shape)),
        in_specs=[SM]+[VM]*7,out_specs=(VM,)*2,
        scratch_shapes=attn_scratch(rows,keys)+[pltpu.VMEM((RQ,rows,128),F32),pltpu.VMEM((2*RK,keys,128),F32),pltpu.VMEM((rows,NQ),F32),pltpu.VMEM((keys,2*NK),F32)],
        compiler_params=limit(56),cost_estimate=cost(36),name="attn_bwd",interpret=interpret)(base,q,k,v,do,lse,fq,fk)

BK=256
def tri_cols(j): return (j*(j+1)//2)*BK

def store_sym(hi,lo,i,j,val):
    h,l=split2(val)
    hi[i*BK:(i+1)*BK,j*BK:(j+1)*BK]=h; lo[i*BK:(i+1)*BK,j*BK:(j+1)*BK]=l
    if i!=j:
        t=val.T
        h,l=split2(t)
        hi[j*BK:(j+1)*BK,i*BK:(i+1)*BK]=h; lo[j*BK:(j+1)*BK,i*BK:(i+1)*BK]=l

def mul_upper(xh,xl,yh,yl,n,emit):
    for j in range(n):
        top=(j+1)*BK; cs=slice(j*BK,(j+1)*BK)
        r=dot(xh[:top,:],yh[:,cs])+dot(xh[:top,:],yl[:,cs])+dot(xl[:top,:],yh[:,cs])
        for i in range(j+1): emit(i,j,r[i*BK:(i+1)*BK])

def ns_body(g_ref,y_ref,o_ref,a_up,ah,al,ph,pw,bh,bl):
    n=o_ref.shape[1]//BK
    eye=(lax.broadcasted_iota(jnp.int32,(BK,BK),0)==lax.broadcasted_iota(jnp.int32,(BK,BK),1)).astype(F32)
    blk=lambda i,j:(slice(i*BK,(i+1)*BK),slice(j*BK,(j+1)*BK))
    trace=None
    for j in range(n):
        off=tri_cols(j)+j*BK
        part=g_ref[:,off:off+BK]*eye
        trace=part if trace is None else trace+part
    trace=jnp.sum(jnp.sum(trace,axis=1,keepdims=True),axis=0,keepdims=True)
    scale=1.0/(jnp.sqrt(trace)+1e-7)
    for j in range(n):
        for i in range(j+1):
            off=tri_cols(j)+i*BK
            val=g_ref[:,off:off+BK]*(scale*scale)
            a_up[blk(i,j)]=val; store_sym(ah,al,i,j,val)
    o_ref[...]=y_ref[...]*scale
    def poly():
        def emit(i,j,c):
            store_sym(ph,pw,i,j,COEF_B*a_up[blk(i,j)]+COEF_C*c)
        mul_upper(ah,al,ah,al,n,emit)
    def apply():
        y=o_ref[...]; yh,yl=split2(y)
        o_ref[...]=COEF_A*y+(dot(yh,ph[...])+dot(yh,pw[...])+dot(yl,ph[...]))
    def step(k,c):
        poly()
        apply()
        def emit_b(i,j,m):
            val=COEF_A*a_up[blk(i,j)]+m
            a_up[blk(i,j)]=val; store_sym(bh,bl,i,j,val)
        mul_upper(ah,al,ph,pw,n,emit_b)
        def emit_a(i,j,m):
            val=COEF_A*a_up[blk(i,j)]+m
            a_up[blk(i,j)]=val; store_sym(ah,al,i,j,val)
        mul_upper(bh,bl,ph,pw,n,emit_a)
        return c
    lax.fori_loop(0,NS_STEPS-1,step,0)
    poly(); apply()

def ns_big(gram,y,interpret=False):
    w,d=y.shape
    vm=pl.BlockSpec(memory_space=pltpu.VMEM)
    return pl.pallas_call(ns_body,out_shape=jax.ShapeDtypeStruct((w,d),F32),
        in_specs=[vm,vm],out_specs=vm,
        scratch_shapes=[pltpu.VMEM((d,d),F32)]+[pltpu.VMEM((d,d),BF)]*6,
        compiler_params=pltpu.CompilerParams(vmem_limit_bytes=56<<20),cost_estimate=cost(86),name="ns_gram",interpret=interpret)(gram,y)

def gram_body(y_ref,g_ref):
    n=y_ref.shape[1]//BK
    yh,yl=split2(y_ref[...])
    for j in range(n):
        top=(j+1)*BK; cs=slice(j*BK,top)
        r=dot_tn(yh[:,:top],yh[:,cs])+dot_tn(yh[:,:top],yl[:,cs])+dot_tn(yl[:,:top],yh[:,cs])
        for i in range(j+1):
            off=tri_cols(j)+i*BK
            g_ref[:,off:off+BK]=r[i*BK:(i+1)*BK]

def gram_upper(y,interpret=False):
    d=y.shape[1]; n=d//BK
    vm=pl.BlockSpec(memory_space=pltpu.VMEM)
    return pl.pallas_call(gram_body,out_shape=jax.ShapeDtypeStruct((BK,n*(n+1)//2*BK),F32),in_specs=[vm],out_specs=vm,
        compiler_params=pltpu.CompilerParams(vmem_limit_bytes=48<<20),cost_estimate=cost(3),name="gram_upper",interpret=interpret)(y)


def mm3(x,y,f=dot):
    xh,xl=split2(x); yh,yl=split2(y)
    return f(xh,yh)+f(xh,yl)+f(xl,yh)

def seg_mask(n,widths):
    def ids(axis):
        pos=lax.broadcasted_iota(jnp.int32,(n,n),axis); out=jnp.zeros_like(pos); edge=0
        for w in widths:
            edge+=w; out=out+(pos>=edge).astype(jnp.int32)
        return out
    return (ids(0)==ids(1)).astype(F32)

GROUPS=((0,(NQ,NK,NK)),(NQ+2*NK,(WQ,)),(NQ+2*NK+WQ,(WK,WK)))

def ns_factor_body(all_ref,own_ref,out_ref):
    out_ref[sum(GROUPS[-1][1])+GROUPS[-1][0]:,:]=jnp.zeros((out_ref.shape[0]-sum(GROUPS[-1][1])-GROUPS[-1][0],out_ref.shape[1]),F32)
    for start,widths in GROUPS:
        n=sum(widths); rs=slice(start,start+n)
        mask=seg_mask(n,widths)
        eye=(lax.broadcasted_iota(jnp.int32,(n,n),0)==lax.broadcasted_iota(jnp.int32,(n,n),1)).astype(F32)
        a=mask*sum(mm3(all_ref[d,rs,:],all_ref[d,rs,:],dot_nt) for d in range(all_ref.shape[0]))
        diag=a*eye
        row=jnp.sum(mask*jnp.sum(diag,axis=1,keepdims=True),axis=0,keepdims=True)
        col=jnp.sum(mask*jnp.sum(diag,axis=0,keepdims=True),axis=1,keepdims=True)
        row=1.0/(jnp.sqrt(row)+1e-7); col=1.0/(jnp.sqrt(col)+1e-7)
        a=a*row*col; x=own_ref[rs,:]*col
        def step(_,c):
            a,x=c
            p=COEF_B*a+COEF_C*mm3(a,a)
            x=COEF_A*x+mm3(p,x)
            b=COEF_A*a+mm3(a,p)
            return COEF_A*b+mm3(b,p),x
        a,x=lax.fori_loop(0,NS_STEPS-1,step,(a,x))
        out_ref[rs,:]=COEF_A*x+mm3(COEF_B*a+COEF_C*mm3(a,a),x)

def ns_factor(tiles,own,interpret=False):
    return pl.pallas_call(ns_factor_body,out_shape=shape(own.shape),in_specs=[VM]*2,out_specs=VM,
        compiler_params=limit(48),cost_estimate=cost(22),name="ns_factor",interpret=interpret)(tiles,own)

def ffn_chunk_body(ids_ref,x_ref,g_ref,w_ref,hin,gin,uin,keep_ref,away_ref,hid_ref,dg_ref,du_ref):
    del ids_ref,hin,gin,uin
    x=x_ref[...]
    gate=dot_nt(x,w_ref[0]); up=dot_nt(x,w_ref[1]); dh=dot_nt(g_ref[...],w_ref[2])
    sig=1.0/(1.0+jnp.exp(-gate))
    act=gate*sig
    hid_ref[...]=(act*up).astype(BF)
    dg=(dh*up*sig*(1.0+gate*(1.0-sig))).astype(BF)
    du=(dh*act).astype(BF)
    dg_ref[...]=dg; du_ref[...]=du
    total=dot(dg,w_ref[0])+dot(du,w_ref[1])
    @pl.when(pl.program_id(0)==0)
    def _(): keep_ref[...]=total
    @pl.when(pl.program_id(0)==1)
    def _(): away_ref[...]=total.astype(BF)

def ffn_chunk(ids,x_all,g_all,w,saved,rows,interpret=False):
    hid=w.shape[1]
    block=pl.BlockSpec((rows,D),lambda i,ids:(ids[i],0))
    part=pl.BlockSpec((rows,hid),lambda i,ids:(ids[i],0))
    whole=pl.BlockSpec((rows,D),lambda i,ids:(0,0))
    stay=pl.BlockSpec(memory_space=pl.ANY)
    return pl.pallas_call(ffn_chunk_body,
        out_shape=(shape((rows,D)),shape((rows,D),BF))+tuple(shape(v.shape,BF) for v in saved),
        grid_spec=pltpu.PrefetchScalarGridSpec(num_scalar_prefetch=1,grid=(2,),
            in_specs=[block,block,pl.BlockSpec(w.shape,lambda i,ids:(0,0,0)),stay,stay,stay],
            out_specs=(whole,whole,part,part,part)),
        input_output_aliases={4:2,5:3,6:4},
        compiler_params=limit(40),cost_estimate=cost(6),name="ffn_chunk",interpret=interpret)(ids,x_all,g_all,w,*saved)


EPS = 1e-06
MOMENTUM = 0.5
LEARN = 0.2
LEARN_VEC = 0.002
P = jax.sharding.PartitionSpec
FFN = 3


def normalize(values):
    row_scale = lax.rsqrt(jnp.mean(values * values, axis=-1, keepdims=True) + EPS)
    return values * row_scale, row_scale


def norm_back(grad_in, normed, row_scale, gain):
    scaled = grad_in * gain
    inner_sum = jnp.mean(scaled * normed, axis=-1, keepdims=True)
    return row_scale * (scaled - normed * inner_sum), jnp.sum(grad_in * normed, axis=0)


def dp_pairs(shift, keep=lambda target: True):
    return [(j, j ^ shift) for j in range(lax.axis_size("dp")) if keep(j ^ shift)]


def place(parts, axis, me=None):
    me = lax.axis_index("dp") if me is None else me
    step = parts[0].shape[axis]
    shape = list(parts[0].shape)
    shape[axis] *= len(parts)
    out = jnp.zeros(shape, parts[0].dtype)
    for shift, part in enumerate(parts):
        out = lax.dynamic_update_slice_in_dim(out, part, (me ^ shift) * step, axis)
    return out


def gather_dp(own, axis=0):
    return place([own] + [lax.ppermute(own, "dp", dp_pairs(s)) for s in range(1, lax.axis_size("dp"))], axis)


def sum_dp(block_for, during=None, alongside=None, gate=None):
    me = lax.axis_index("dp")
    sent = [block_for(me ^ s).astype(BF) for s in range(1, lax.axis_size("dp"))]
    if gate is not None:
        sent = [after(block, gate) for block in sent]
    total = block_for(me)
    aside = None
    if during is not None:
        aside = during(*sent)
        total = after(total, *aside, alongside)
    for s, block in enumerate(sent, 1):
        total = total + lax.ppermute(block, "dp", dp_pairs(s)).astype(F32)
    return total if during is None else (total, aside)


def after(value, *others):
    return lax.optimization_barrier((value, *others))[0]


def pass_core(x):
    return lax.ppermute(x, "mp", [(j, j ^ 1) for j in range(lax.axis_size("mp"))])


def pass_chip(x, shift):
    return lax.ppermute(x, "mp", [(j, j ^ (2 * shift)) for j in range(lax.axis_size("mp"))])


def pick(x, index):
    return lax.dynamic_index_in_dim(x, index, 0, keepdims=False)


CHIPS = 4


def collect(near):
    total = near[0]
    for s in (2, 3, 1):
        total = total + pass_chip(near[s].astype(BF), s).astype(F32)
    return total


def scatter_mp(partial):
    mp = lax.axis_size("mp")
    if mp != 2 * CHIPS:
        return (lax.psum_scatter(partial, "mp", scatter_dimension=0, tiled=True),) * 2
    me = lax.axis_index("mp")
    blocks = partial.reshape(CHIPS, 2, partial.shape[0] // mp, partial.shape[1])
    away = lax.dynamic_index_in_dim(blocks, 1 - me % 2, 1, keepdims=False).astype(BF)
    near = lax.dynamic_index_in_dim(blocks, me % 2, 1, keepdims=False) + pass_core(away).astype(F32)
    near = [pick(near, (me // 2) ^ s) for s in range(CHIPS)]
    return collect(near), near[0]


def ffn_pieces(second_own, d_output_all, low, early):
    second_in = lax.all_gather(second_own, "mp", axis=0, tiled=True)
    if lax.axis_size("mp") != 2 * CHIPS:
        gate_value, upward, d_hidden = dot_nt(second_in, low[0]), dot_nt(second_in, low[1]), dot_nt(d_output_all, low[2])
        sigmoid_gate = jax.nn.sigmoid(gate_value)
        active = gate_value * sigmoid_gate
        hidden = (active * upward).astype(BF)
        d_gate = (d_hidden * upward * sigmoid_gate * (1.0 + gate_value * (1.0 - sigmoid_gate))).astype(BF)
        d_upward = (d_hidden * active).astype(BF)
        d_second, _ = scatter_mp(dot(d_gate, low[0]) + dot(d_upward, low[1]))
        return d_second, *ffn_products(hidden, d_gate, d_upward, second_in, d_output_all, low)
    me = lax.axis_index("mp").astype(jnp.int32)
    rows = second_own.shape[0]
    saved = tuple(jnp.zeros((second_in.shape[0], low.shape[1]), BF) for _ in range(3))
    near = [None] * CHIPS
    order = (2, 3, 1, 0)
    for turn, s in enumerate(order):
        ids = jnp.stack([me ^ (2 * s), me ^ (2 * s + 1)])
        ids = after(ids, near[order[turn - 2]] if turn > 1 else early)
        keep, away, *saved = ffn_chunk(ids, second_in, d_output_all, low, saved, rows)
        near[s] = keep + pass_core(away).astype(F32)
        near[s] = near[s].astype(BF) if s else near[s]
    grads, branch = ffn_products(*saved, second_in, d_output_all, low)
    near[0] = after(near[0], grads, branch)
    return collect(near), grads, branch


def ffn_products(hidden, d_gate, d_upward, second_in, d_output_all, low):
    grads = [dot_tn(d_gate, second_in), dot_tn(d_upward, second_in), dot_tn(hidden, d_output_all)]
    spare = jnp.zeros((low.shape[1] * (lax.axis_size("dp") - FFN), D), BF)
    return jnp.concatenate([g.astype(BF) for g in grads] + [spare]), dot(hidden, low[2]).astype(BF)


def body(
    tokens,
    cotangent,
    domain_ids,
    domain_weight,
    gains,
    gain_mom,
    factor_w,
    factor_mom,
    out_w,
    out_mom,
    gate_up_w,
    gate_up_mom,
    down_w,
    down_mom,
):
    n_dp, n_mp = lax.axis_size("dp"), lax.axis_size("mp")
    me, mz = lax.axis_index("dp"), lax.axis_index("mp")
    rows = tokens.shape[0]
    d_own = factor_w.shape[0]
    hidden_own = gate_up_w.shape[2]
    out_own = d_own // n_mp
    base = me.astype(jnp.int32).reshape(1)
    shifts = range(1, n_dp)

    edge = NQ + 2 * NK

    def q_rows(m):
        return jnp.concatenate([m[edge : edge + WQ], m[:NQ]])

    def kv_rows(m):
        return jnp.concatenate([m[edge + WQ :], m[NQ:edge]])

    factor_own = factor_w.T.astype(BF)
    kv_low = gather_dp(kv_rows(factor_own), 1)
    x_float = tokens.astype(F32)
    first_normed, first_scale = normalize(x_float)
    first_own = (first_normed * gains[0]).astype(BF)
    domain_range = jnp.arange(domain_weight.shape[0], dtype=jnp.int32)
    seq_weight = jnp.sum(jnp.where(domain_ids[0, 0] == domain_range, domain_weight, 0.0))
    d_output = cotangent.astype(F32) * seq_weight
    d_output_all = lax.all_gather(d_output.astype(BF), "mp", axis=0, tiled=True)
    kv_all = gather_dp(dot_nt(first_own, kv_low))
    q_low = gather_dp(after(q_rows(factor_own), kv_low), 1)
    q_own = dot_nt(first_own, q_low)
    attended, lse, queries, key_vecs, values = attn_fwd(base, q_own, kv_all)
    out_low = gather_dp(after(out_w.astype(BF), kv_all))
    residual = x_float + dot(attended, out_low)
    second_normed, second_scale = normalize(residual)

    ffn_own = jnp.stack([gate_up_w[0].T, gate_up_w[1].T, down_w])
    ffn_low = gather_dp(after(ffn_own.astype(BF), out_low), 2)
    second_own = (second_normed * gains[1]).astype(BF)
    to_ffn = lambda target: target < FFN
    ffn_slot = jnp.minimum(me, FFN - 1)
    ffn_mom = after(jnp.stack([gate_up_mom[0].T, gate_up_mom[1].T, down_mom]), ffn_low)
    own_mom = [pick(ffn_mom, ffn_slot)]
    for s in shifts:
        own_mom.append(lax.ppermute(pick(ffn_mom, jnp.minimum(me ^ s, FFN - 1)), "dp", dp_pairs(s, to_ffn)))
    own_mom = MOMENTUM * place(own_mom, 1)
    d_second, grads, branch = ffn_pieces(second_own, d_output_all, ffn_low, own_mom)
    matrix = lax.psum_scatter(grads, "dp", scatter_dimension=0, tiled=True)

    d_resid_norm, gain_second = norm_back(d_second, second_normed, second_scale, gains[1])
    d_residual = d_output + d_resid_norm
    d_residual_low = d_residual.astype(BF)
    out_block = lambda t: dot_tn(lax.dynamic_slice_in_dim(attended, t * d_own, d_own, 1), d_residual_low)
    d_attended = dot_nt(d_residual_low, out_low).astype(BF)
    backward = lambda *sent: attn_bwd(after(base, *sent), queries, key_vecs, values, d_attended, lse, q_own, kv_all)
    grad_out, (d_q, d_kv) = sum_dp(out_block, during=backward, alongside=matrix)
    grad_out, grad_out_chip = scatter_mp(grad_out)
    out_tile = MOMENTUM * lax.dynamic_slice_in_dim(out_mom, mz * out_own, out_own, 0) + grad_out
    out_rows = place([out_tile] + [lax.ppermute(out_tile, "dp", [(j ^ s, j) for j in range(FFN, n_dp)]) for s in shifts], 0)
    out_rows = jnp.pad(out_rows, ((0, hidden_own - out_rows.shape[0]), (0, 0)))
    matrix = jnp.where(me < FFN, own_mom + matrix.astype(F32), out_rows)
    gram_part = gram_upper(matrix)
    gram = lax.psum(gram_part, "mp")

    d_kv = after(d_kv, grad_out_chip)
    d_kv = sum_dp(lambda t: lax.dynamic_slice_in_dim(d_kv, t * rows, rows, 0))
    d_q, d_kv = d_q.astype(BF), d_kv.astype(BF)
    d_first = dot(d_q, q_low) + dot(d_kv, kv_low)
    d_input_norm, gain_first = norm_back(d_first, first_normed, first_scale, gains[0])
    input_grad = d_residual + d_input_norm

    gain_rows = jnp.stack([gain_first, gain_second])
    filler = -(factor_w.shape[1] + 2) % (8 * n_mp)

    def factor_block(t):
        cols = lax.dynamic_slice_in_dim(first_own, t * d_own, d_own, 1)
        q, kv = dot_tn(d_q, cols), dot_tn(d_kv, cols)
        tail = jnp.pad(lax.dynamic_slice_in_dim(gain_rows, t * d_own, d_own, 1), ((0, filler), (0, 0)))
        return jnp.concatenate([q[WQ:], kv[2 * WK :], q[:WQ], kv[: 2 * WK], tail])

    d_q, d_kv = after((d_q, d_kv), grad_out)
    grad_factor = sum_dp(factor_block, gate=gram_part)
    grad_factor, _ = scatter_mp(grad_factor)
    height = grad_factor.shape[0]
    factor_piece = jnp.pad(MOMENTUM * factor_mom.T, ((0, filler + 2), (0, 0)))
    factor_piece = lax.dynamic_slice_in_dim(factor_piece, mz * height, height, 0) + grad_factor
    factor_all = lax.all_gather(factor_piece, ("dp", "mp"), axis=0, tiled=True).reshape(n_dp, n_mp * height, d_own)
    factor_tile = pick(factor_all, me)
    gain_grad = factor_tile[factor_w.shape[1] : factor_w.shape[1] + 2]
    branch = lax.psum_scatter(after(branch, factor_piece), "mp", scatter_dimension=0, tiled=True)
    block_out = (residual + branch.astype(F32)).astype(BF)

    def give_back(whole):
        pieces = [lax.dynamic_slice_in_dim(whole, (me ^ s) * d_own, d_own, 1) for s in range(n_dp)]
        came = [lax.ppermute(pieces[s], "dp", dp_pairs(s, lambda t: t ^ s < FFN))[None] for s in shifts]
        return place([pieces[0][None]] + came, 0), pieces[1:]

    ortho = ns_big(gram, after(matrix, factor_piece))
    out_ortho = lax.dynamic_slice_in_dim(ortho, me * out_own, out_own, 0)
    for s in shifts:
        piece = lax.dynamic_slice_in_dim(ortho, (me ^ s) * out_own, out_own, 0)
        piece = lax.ppermute(piece, "dp", [(j, j ^ s) for j in range(FFN, n_dp)])
        out_ortho = jnp.where(me ^ s == FFN, piece, out_ortho)
    out_both = after(jnp.stack([out_tile, out_ortho]), factor_all, branch)
    out_both = lax.all_gather(out_both, "mp", axis=1, tiled=True)
    new_out_mom = out_both[0]
    new_out_w = out_w - LEARN * 0.2 * math.sqrt(D) * out_both[1]
    mom_back, _ = give_back(after(matrix, ortho))
    ortho_back, sent = give_back(ortho)
    turn = lambda stack: jnp.stack([stack[0].T, stack[1].T])
    ffn_rate = LEARN * 0.2 * math.sqrt(max(D, hidden_own * n_mp))
    new_gate_up_mom, new_down_mom = turn(mom_back), mom_back[2]
    new_gate_up_w = gate_up_w - ffn_rate * turn(ortho_back)
    new_down_w = down_w - ffn_rate * ortho_back[2]

    factor_ortho = ns_factor(factor_all, after(factor_tile, *sent))
    widths = [NQ, NK, NK, WQ, WK, WK]
    factor_rate = jnp.concatenate([jnp.full((w, 1), LEARN * 0.2 * math.sqrt(max(D, w)), F32) for w in widths])
    new_factor_mom = factor_tile[: factor_w.shape[1]].T
    new_factor_w = factor_w - (factor_rate * factor_ortho[: factor_w.shape[1]]).T

    new_gain_mom = MOMENTUM * gain_mom + gain_grad
    new_gains = lax.dynamic_slice_in_dim(gains, me * d_own, d_own, 1) - LEARN_VEC * new_gain_mom
    return (
        block_out,
        input_grad,
        gain_grad,
        new_gains,
        new_gain_mom,
        new_factor_mom,
        new_factor_w,
        new_out_mom,
        new_out_w,
        new_gate_up_mom,
        new_gate_up_w,
        new_down_mom,
        new_down_w,
    )


def solution(mesh):
    token = P(("mp", "dp"), None)
    row = P("dp", None)
    ffn = P(None, "dp", "mp")
    down = P("mp", "dp")
    vec = P(None, "dp")
    return jax.shard_map(
        body,
        mesh=mesh,
        in_specs=(token, token, P("mp", None), P(), P(), vec, row, row, row, row, ffn, ffn, down, down),
        out_specs=(token, token, vec, vec, vec, row, row, row, row, ffn, ffn, down, down),
        check_vma=False,
    )
```

time: 868 us -> 546 us (0.63)
  waiting for transfers between devices: 361 us -> 159 us
  blocking collectives: 53.9 us -> 0 us
  matrix products: 53.1 us -> 19.6 us
  local copies, waits for them, and re-layouts: 73.2 us -> 44.5 us
  Pallas kernels: 168 us -> 187 us
  starting transfers between devices: 94.8 us -> 76.6 us
    ppermute x29 -> x36, waiting for transfers between devices: 218 us -> 69 us  [the longest x9 29.9 us: pass_chip(): lax.ppermute(x, 'mp', [(j, j ^ 2 * shift) for j in range(lax.axis_size('m...]
    all_gather x5 -> x3, waiting for transfers between devices: 58.4 us -> 0.01 us  [the longest x1 0.01 us: ffn_pieces(): second_in = lax.all_gather(second_own, 'mp', axis=0, tiled=True)]
    psum x1 -> x0, blocking collectives: 53.9 us -> none  [body(): gain_all = lax.psum(jnp.stack([gain_first, gain_second]), ('dp', 'mp'))]
    psum x1, waiting for transfers between devices: 0.01 us -> 43.6 us  [body(): gram = lax.psum(gram_part, 'mp')]
    all_gather x1, waiting for transfers between devices: 37.7 us -> 0.01 us  [body(): d_output_all = lax.all_gather(d_output.astype(BF), 'mp', axis=0, tiled=True)]
    ppermute x3, starting transfers between devices: 26.8 us -> 6.76 us  [body(): lax.ppermute(out_tile, 'dp', [(j ^ s, j) for j in range(FFN, n_dp)])]
    pallas_call x3 -> x7, Pallas kernels: 78.8 us -> 96.8 us  [the longest x1 35.7 us: attn_bwd(): pl.pallas_call(attn_bwd_body, out_shape=(shape(fq.shape), shape(fk.shape)...]
    unnamed x156 -> x132, local copies, waits for them, and re-layouts: 28.3 us -> 12.7 us
  transfers between devices with their start and end apart: 49 -> 61, of which waited for: 22 -> 29; matrix products, arithmetic and copies ran while one was open for 15% -> 13% of each run, Pallas kernels for 9% -> 34%
where the time goes in v2:
time: 546 us; the launch traced here: 538 us
  Pallas kernels  187 us (34%)
  waiting for transfers between devices  159 us (29%)
  starting transfers between devices  76.6 us (14%)
  local copies, waits for them, and re-layouts  44.5 us (8%)
  other arithmetic  34.5 us (6%)
  matrix products  19.6 us (4%)
  between operations  17.1 us (3%)
    pallas_call x1, Pallas kernels, ns_big(): pl.pallas_call(ns_body, out_shape=jax.ShapeDtypeStruct((w, d), F32), in_s...  86.7 us
    ppermute x15, waiting for transfers between devices, gather_dp(): lax.ppermute(own, 'dp', dp_pairs(s))  45.4 us
    psum x1, waiting for transfers between devices, body(): gram = lax.psum(gram_part, 'mp')  43.6 us
    pallas_call x1, Pallas kernels, attn_bwd(): pl.pallas_call(attn_bwd_body, out_shape=(shape(fq.shape), shape(fk.shape)...  35.7 us
    ppermute x9, waiting for transfers between devices, pass_chip(): lax.ppermute(x, 'mp', [(j, j ^ 2 * shift) for j in range(lax.axis_size('m...  29.9 us
    pallas_call x1, Pallas kernels, ns_factor(): pl.pallas_call(ns_factor_body, out_shape=shape(own.shape), in_specs=[VM]...  21.9 us
    pallas_call x4, Pallas kernels, ffn_chunk(): pl.pallas_call(ffn_chunk_body, out_shape=(shape((rows, D)), shape((rows,...  20.8 us
    ppermute x15, starting transfers between devices, gather_dp(): lax.ppermute(own, 'dp', dp_pairs(s))  18.9 us
  transfers between devices with their start and end apart: 61, of which 29 were waited for; matrix products, arithmetic and copies ran while one was open for 13% of the time, Pallas kernels for 34%

profile of v2, /device:TPU:0, one launch (start us, length us, event | category | flops | bytes accessed | tf_op | source)
XLA Modules:
  0.0 538.1 jit_solution(5313981473171520470)
XLA Ops:
  9.3 2.6 fusion.13
  12.1 3.0 collective-permute-start
  17.3 3.0 collective-permute-done
  21.2 3.2 collective-permute-done.1
  25.6 1.9 collective-permute-start.4
  29.8 1.9 collective-permute-start.7
  31.8 2.5 collective-permute-done.3
  35.9 2.3 collective-permute-done.4
  38.2 2.4 collective-permute-done.5
  41.1 6.9 %collective-permute-done.6 = f32[256,320]{1,0:T(8,128)S(1)} collective-permute-done((f32[256,320]{1,0:T(8,128)S(1)}, f32[256,320]{1,0:T(8,128)S(1)}, u32[]{:S(2)}, u32[]{:S(2)}) %collective-permute-start.6) | collective-permute-done | bytes 327712 | tf_op jit(solution)/shard_map/ppermute | solution.py:327
  48.1 5.3 collective-permute-done.7
  53.4 2.3 collective-permute-done.8
  56.0 1.7 collective-permute-start.10
  59.3 18.3 %attn_fwd.1 = (bf16[256,1024]{1,0:T(8,128)(2,1)S(1)}, f32[256,16]{1,0:T(8,128)S(1)}, bf16[256,1024]{1,0:T(8,128)(2,1)S(1)}, bf16[1024,1024]{1,0:T(8,128)(2,1)S(1)}, bf16[1024,1024]{1,0:T(8,128)(2,1)}) custom-call(s32[1]{0:T(128)} %bitcast.base_ref, f32[256,480]{1,0:T(8,128)S(1)} %fusion.70.fq_ref, f32[1024,320]{1,0:T(8,128)S(1)} %constant_dynamic-update-slice_fusion.22.fk_ref), custom_call_target="tpu_custom_call" | custom-call | flops 20700000256 | bytes 1048576 | tf_op jit(solution)/shard_map/attn_fwd/pallas_call | solution.py:85
  87.3 11.3 %collective-permute-done.12 = bf16[3,352,256]{2,1,0:T(8,128)(2,1)} collective-permute-done((bf16[3,352,256]{2,1,0:T(8,128)(2,1)S(1)}, bf16[3,352,256]{2,1,0:T(8,128)(2,1)}, u32[]{:S(2)}, u32[]{:S(2)}) %collective-permute-start.12) | collective-permute-done | bytes 540704 | tf_op jit(solution)/shard_map/ppermute | solution.py:327
  99.8 6.2 %collective-permute-done.13 = bf16[3,352,256]{2,1,0:T(8,128)(2,1)} collective-permute-done((bf16[3,352,256]{2,1,0:T(8,128)(2,1)S(1)}, bf16[3,352,256]{2,1,0:T(8,128)(2,1)}, u32[]{:S(2)}, u32[]{:S(2)}) %collective-permute-start.13) | collective-permute-done | bytes 540704 | tf_op jit(solution)/shard_map/ppermute | solution.py:327
  109.0 3.6 collective-permute-start.15
  112.7 1.9 collective-permute-start.16
  117.6 1.8 bitcast_dynamic-update-slice_fusion.8
  119.4 1.7 collective-permute-done.15
  121.1 1.8 constant_dynamic-update-slice_fusion.13
  122.8 4.4 collective-permute-done.16
  127.2 1.8 constant_dynamic-update-slice_fusion.12
  130.3 1.8 copy-done.9
  132.1 4.9 ffn_chunk.4
  137.1 4.9 ffn_chunk.5
  144.6 4.9 ffn_chunk.6
  152.1 6.0 %ffn_chunk.7 = (f32[256,1024]{1,0:T(8,128)S(1)}, bf16[256,1024]{1,0:T(8,128)(2,1)}, bf16[2048,352]{1,0:T(8,128)(2,1)S(1)}, bf16[2048,352]{1,0:T(8,128)(2,1)S(1)}, bf16[2048,352]{1,0:T(8,128)(2,1)S(1)}) custom-call(s32[2]{0:T(128)S(1)} %pad_add_fusion.ids_ref, ...), custom_call_target="tpu_custom_call", output_to_operand_aliasing={{2}: (4, {}), {3}: (5, {}), {4}: (6, {})} | custom-call | flops 6899999744 | bytes 1048576 | tf_op jit(solution)/shard_map/ffn_chunk/pallas_call | solution.py:283
  159.8 1.7 convolution_convert_fusion.2
  163.2 3.2 maximum_maximum_fusion
  166.7 2.4 add_convert_fusion.1
  170.2 4.4 convolution_convert_fusion
  176.3 4.5 collective-permute-done.21
  180.9 11.0 %collective-permute-done.24 = bf16[256,1024]{1,0:T(8,128)(2,1)S(1)} collective-permute-done((bf16[256,1024]{1,0:T(8,128)(2,1)}, bf16[256,1024]{1,0:T(8,128)(2,1)S(1)}, u32[]{:S(2)}, u32[]{:S(2)}) %collective-permute-start.24) | collective-permute-done | bytes 524320 | tf_op jit(solution)/shard_map/ppermute | solution.py:354
  191.9 1.7 multiply_reduce_fusion
  195.0 1.8 collective-permute-start.27
  202.3 35.7 %attn_bwd.1 = (f32[256,480]{1,0:T(8,128)}, f32[1024,320]{1,0:T(8,128)}) custom-call(s32[1]{0:T(128)} %bitcast.base_ref, bf16[256,1024]{1,0:T(8,128)(2,1)} %copy-done.11, bf16[1024,1024]{1,0:T(8,128)(2,1)} %copy-done.10, bf16[1024,1024]{1,0:T(8,128)(2,1)} %get-tuple-element.95.v_ref, bf16[256,1024]{1,0:T(8,128)(2,1)} %convolution_convert_fusion.7.do_ref, ...), custom_call_target="tpu_custom_call" | custom-call | flops 41400000512 | bytes 1048576 | tf_op jit(solution)/shard_map/attn_bwd/pallas_call | solution.py:136
  242.4 2.3 collective-permute-start.33
  245.9 3.2 collective-permute-done.33
  249.1 2.5 collective-permute-done.32
  254.1 5.3 collective-permute-start.37
  259.4 2.1 dynamic-slice_convert_fusion.2
  262.9 2.1 collective-permute-start.29
  266.7 3.7 gram_upper.1
  280.8 3.4 collective-permute-start.40
  289.0 6.2 %collective-permute-done.40 = bf16[832,256]{1,0:T(8,128)(2,1)S(1)} collective-permute-done((bf16[832,256]{1,0:T(8,128)(2,1)}, bf16[832,256]{1,0:T(8,128)(2,1)S(1)}, u32[]{:S(2)}, u32[]{:S(2)}) %collective-permute-start.40) | collective-permute-done | bytes 426016 | tf_op jit(solution)/shard_map/ppermute | solution.py:341
  295.2 6.6 %collective-permute-done.39 = bf16[832,256]{1,0:T(8,128)(2,1)S(1)} collective-permute-done((bf16[832,256]{1,0:T(8,128)(2,1)}, bf16[832,256]{1,0:T(8,128)(2,1)S(1)}, u32[]{:S(2)}, u32[]{:S(2)}) %collective-permute-start.39) | collective-permute-done | bytes 426016 | tf_op jit(solution)/shard_map/ppermute | solution.py:341
  303.7 1.9 collective-permute-start.43
  307.3 2.1 collective-permute-done.44
  309.4 2.3 collective-permute-done.43
  311.7 3.5 collective-permute-done.42
  316.6 43.6 %all-reduce.8.cloned.1.call-done.g_ref = f32[256,2560]{1,0:T(8,128)} async-done(((f32[256,2560]{1,0:T(8,128)}), f32[256,2560]{1,0:T(8,128)}) %all-reduce.8.cloned.1.call-update) | async-done | bytes 2621456 | tf_op jit(solution)/shard_map/psum | solution.py:492
  360.2 86.7 %ns_gram.1 = f32[352,1024]{1,0:T(8,128)} custom-call(f32[256,2560]{1,0:T(8,128)} %all-reduce.8.cloned.1.call-done.g_ref, f32[352,1024]{1,0:T(8,128)} %copy-done), custom_call_target="tpu_custom_call" | custom-call | flops 98900000768 | bytes 1048576 | tf_op jit(solution)/shard_map/ns_gram/pallas_call | solution.py:200
  451.7 3.4 collective-permute-start.48
  455.0 6.6 %collective-permute-start.49 = (f32[352,256]{1,0:T(8,128)}, f32[352,256]{1,0:T(8,128)}, u32[]{:S(2)}, u32[]{:S(2)}) collective-permute-start(f32[352,256]{1,0:T(8,128)} %get-tuple-element.132), channel_id=1, source_target_pairs={{0,16},{8,24},{16,0},{1,17},{9,25},{17,1},{2,18},{10,26},{18,2},{3... | collective-permute-start | bytes 1081352 | tf_op jit(solution)/shard_map/ppermute | solution.py:524
  462.9 2.0 collective-permute-start.50
  465.0 3.3 collective-permute-start.51
  468.3 1.9 collective-permute-start.52
  473.3 10.4 %collective-permute-done.51 = f32[352,256]{1,0:T(8,128)} collective-permute-done((f32[352,256]{1,0:T(8,128)}, f32[352,256]{1,0:T(8,128)}, u32[]{:S(2)}, u32[]{:S(2)}) %collective-permute-start.51) | collective-permute-done | bytes 360480 | tf_op jit(solution)/shard_map/ppermute | solution.py:524
  485.7 5.3 collective-permute-done.52
  499.9 21.9 %ns_factor.1 = f32[832,256]{1,0:T(8,128)S(1)} custom-call(f32[4,832,256]{2,1,0:T(8,128)S(1)} %bitcast.201, f32[832,256]{1,0:T(8,128)S(1)} %dynamic-slice_bitcast_fusion.own_ref), custom_call_target="tpu_custom_call" | custom-call | flops 25300000768 | bytes 1048576 | tf_op jit(solution)/shard_map/ns_factor/pallas_call | solution.py:258
  523.7 2.3 fusion.9
  526.0 2.4 slice_bitcast_fusion
  528.4 2.4 fusion.12
  (348 shorter events, 100.8 us)
Async XLA Ops:
  7.2 122.7 %all-gather.7.cloned.1.call-start = ((), (), s32[]{:S(2)}) async-start(), calls=%async_computation.3 | async-start | bytes 4718592 | tf_op jit(solution)/shard_map/all_gather | solution.py:457
  11.8 118.0 %all-gather.5.cloned.1.call-start = ((), (), s32[]{:S(2)}) async-start(), calls=%async_computation.2 | async-start | bytes 4718592 | tf_op jit(solution)/shard_map/all_gather | solution.py:384
  12.1 8.1 %collective-permute-start = (bf16[320,256]{1,0:T(8,128)(2,1)S(1)}, bf16[320,256]{1,0:T(8,128)(2,1)}, u32[]{:S(2)}, u32[]{:S(2)}) collective-permute-start(bf16[320,256]{1,0:T(8,128)(2,1)S(1)} %get-tuple-element.155), channel_id=1, source_target_pairs={{0,8},{8,0},{16,24},{24,16},{1,9},{9,1},{17,25},{25,17},{2,10},{10... | collective-permute-start | bytes 491528 | tf_op jit(solution)/shard_map/ppermute | solution.py:327
  15.1 9.3 %collective-permute-start.1 = (bf16[320,256]{1,0:T(8,128)(2,1)S(1)}, bf16[320,256]{1,0:T(8,128)(2,1)}, u32[]{:S(2)}, u32[]{:S(2)}) collective-permute-start(bf16[320,256]{1,0:T(8,128)(2,1)S(1)} %get-tuple-element.155), channel_id=1, source_target_pairs={{0,16},{8,24},{16,0},{24,8},{1,17},{9,25},{17,1},{25,9},{2,18},{10... | collective-permute-start | bytes 491528 | tf_op jit(solution)/shard_map/ppermute | solution.py:327
  16.7 8.7 %collective-permute-start.2 = (bf16[320,256]{1,0:T(8,128)(2,1)S(1)}, bf16[320,256]{1,0:T(8,128)(2,1)S(1)}, u32[]{:S(2)}, u32[]{:S(2)}) collective-permute-start(bf16[320,256]{1,0:T(8,128)(2,1)S(1)} %get-tuple-element.155), channel_id=1, source_target_pairs={{0,24},{8,16},{16,8},{24,0},{1,25},{9,17},{17,9},{25,1},{2,26},{10... | collective-permute-start | bytes 491528 | tf_op jit(solution)/shard_map/ppermute | solution.py:327
  16.9 176.7 %copy-start.48 = (f32[1,1024]{1,0:T(1,128)}, f32[1,1024]{1,0:T(1,128)S(1)}, u32[]{:S(2)}) copy-start(f32[1,1024]{1,0:T(1,128)S(1)} %get-tuple-element.160) | copy-start | bytes 12292
  25.4 9.0 %collective-permute-start.3 = (bf16[480,256]{1,0:T(8,128)(2,1)S(1)}, bf16[480,256]{1,0:T(8,128)(2,1)S(1)}, u32[]{:S(2)}, u32[]{:S(2)}) collective-permute-start(bf16[480,256]{1,0:T(8,128)(2,1)S(1)} %pad_maximum_fusion.4), channel_id=1, source_target_pairs={{0,8},{8,0},{16,24},{24,16},{1,9},{9,1},{17,25},{25,17},{2,10},{10... | collective-permute-start | bytes 737288 | tf_op jit(solution)/shard_map/ppermute | solution.py:327
  25.6 12.5 %collective-permute-start.4 = (bf16[480,256]{1,0:T(8,128)(2,1)S(1)}, bf16[480,256]{1,0:T(8,128)(2,1)S(1)}, u32[]{:S(2)}, u32[]{:S(2)}) collective-permute-start(bf16[480,256]{1,0:T(8,128)(2,1)S(1)} %pad_maximum_fusion.4), channel_id=1, source_target_pairs={{0,16},{8,24},{16,0},{24,8},{1,17},{9,25},{17,1},{25,9},{2,18},{10... | collective-permute-start | bytes 737288 | tf_op jit(solution)/shard_map/ppermute | solution.py:327
  27.5 13.0 %collective-permute-start.5 = (bf16[480,256]{1,0:T(8,128)(2,1)S(1)}, bf16[480,256]{1,0:T(8,128)(2,1)S(1)}, u32[]{:S(2)}, u32[]{:S(2)}) collective-permute-start(bf16[480,256]{1,0:T(8,128)(2,1)S(1)} %pad_maximum_fusion.4), channel_id=1, source_target_pairs={{0,24},{8,16},{16,8},{24,0},{1,25},{9,17},{17,9},{25,1},{2,26},{10... | collective-permute-start | bytes 737288 | tf_op jit(solution)/shard_map/ppermute | solution.py:327
  29.5 18.5 %collective-permute-start.6 = (f32[256,320]{1,0:T(8,128)S(1)}, f32[256,320]{1,0:T(8,128)S(1)}, u32[]{:S(2)}, u32[]{:S(2)}) collective-permute-start(f32[256,320]{1,0:T(8,128)S(1)} %get-tuple-element.163), channel_id=1, source_target_pairs={{0,8},{8,0},{16,24},{24,16},{1,9},{9,1},{17,25},{25,17},{2,10},{10... | collective-permute-start | bytes 983048 | tf_op jit(solution)/shard_map/ppermute | solution.py:327
  29.8 23.6 %collective-permute-start.7 = (f32[256,320]{1,0:T(8,128)S(1)}, f32[256,320]{1,0:T(8,128)S(1)}, u32[]{:S(2)}, u32[]{:S(2)}) collective-permute-start(f32[256,320]{1,0:T(8,128)S(1)} %get-tuple-element.163), channel_id=1, source_target_pairs={{0,16},{8,24},{16,0},{24,8},{1,17},{9,25},{17,1},{25,9},{2,18},{10... | collective-permute-start | bytes 983048 | tf_op jit(solution)/shard_map/ppermute | solution.py:327
  34.4 21.4 %collective-permute-start.8 = (f32[256,320]{1,0:T(8,128)S(1)}, f32[256,320]{1,0:T(8,128)S(1)}, u32[]{:S(2)}, u32[]{:S(2)}) collective-permute-start(f32[256,320]{1,0:T(8,128)S(1)} %get-tuple-element.163), channel_id=1, source_target_pairs={{0,24},{8,16},{16,8},{24,0},{1,25},{9,17},{17,9},{25,1},{2,26},{10... | collective-permute-start | bytes 983048 | tf_op jit(solution)/shard_map/ppermute | solution.py:327
  55.8 23.4 %collective-permute-start.9 = (bf16[256,1024]{1,0:T(8,128)(2,1)S(1)}, bf16[256,1024]{1,0:T(8,128)(2,1)S(1)}, u32[]{:S(2)}, u32[]{:S(2)}) collective-permute-start(bf16[256,1024]{1,0:T(8,128)(2,1)S(1)} %convert_element_type.221), channel_id=1, source_target_pairs={{0,8},{8,0},{16,24},{24,16},{1,9},{9,1},{17,25},{25,17},{2,10},{10... | collective-permute-start | bytes 1572872 | tf_op jit(solution)/shard_map/ppermute | solution.py:327
  56.0 23.2 %collective-permute-start.10 = (bf16[256,1024]{1,0:T(8,128)(2,1)S(1)}, bf16[256,1024]{1,0:T(8,128)(2,1)S(1)}, u32[]{:S(2)}, u32[]{:S(2)}) collective-permute-start(bf16[256,1024]{1,0:T(8,128)(2,1)S(1)} %convert_element_type.221), channel_id=1, source_target_pairs={{0,16},{8,24},{16,0},{24,8},{1,17},{9,25},{17,1},{25,9},{2,18},{10... | collective-permute-start | bytes 1572872 | tf_op jit(solution)/shard_map/ppermute | solution.py:327
  57.7 21.6 %collective-permute-start.11 = (bf16[256,1024]{1,0:T(8,128)(2,1)S(1)}, bf16[256,1024]{1,0:T(8,128)(2,1)S(1)}, u32[]{:S(2)}, u32[]{:S(2)}) collective-permute-start(bf16[256,1024]{1,0:T(8,128)(2,1)S(1)} %convert_element_type.221), channel_id=1, source_target_pairs={{0,24},{8,16},{16,8},{24,0},{1,25},{9,17},{17,9},{25,1},{2,26},{10... | collective-permute-start | bytes 1572872 | tf_op jit(solution)/shard_map/ppermute | solution.py:327
  81.1 112.6 %copy-start.50 = (f32[256]{0:T(256)}, f32[256]{0:T(256)S(1)}, u32[]{:S(2)}) copy-start(f32[256]{0:T(256)S(1)} %add_rsqrt_fusion) | copy-start | bytes 3076
  83.0 155.4 %reduce-scatter.3.cloned.1.call-start = ((), (), s32[]{:S(2)}) async-start(), calls=%async_computation.4 | async-start | bytes 3604480 | tf_op jit(solution)/shard_map/reduce_scatter | solution.py:477
  83.2 15.4 %collective-permute-start.12 = (bf16[3,352,256]{2,1,0:T(8,128)(2,1)S(1)}, bf16[3,352,256]{2,1,0:T(8,128)(2,1)}, u32[]{:S(2)}, u32[]{:S(2)}) collective-permute-start(bf16[3,352,256]{2,1,0:T(8,128)(2,1)S(1)} %pad_maximum_fusion.2), channel_id=1, source_target_pairs={{0,8},{8,0},{16,24},{24,16},{1,9},{9,1},{17,25},{25,17},{2,10},{10... | collective-permute-start | bytes 1622024 | tf_op jit(solution)/shard_map/ppermute | solution.py:327
  83.9 22.1 %collective-permute-start.13 = (bf16[3,352,256]{2,1,0:T(8,128)(2,1)S(1)}, bf16[3,352,256]{2,1,0:T(8,128)(2,1)}, u32[]{:S(2)}, u32[]{:S(2)}) collective-permute-start(bf16[3,352,256]{2,1,0:T(8,128)(2,1)S(1)} %pad_maximum_fusion.2), channel_id=1, source_target_pairs={{0,16},{8,24},{16,0},{24,8},{1,17},{9,25},{17,1},{25,9},{2,18},{10... | collective-permute-start | bytes 1622024 | tf_op jit(solution)/shard_map/ppermute | solution.py:327
  85.2 21.9 %collective-permute-start.14 = (bf16[3,352,256]{2,1,0:T(8,128)(2,1)S(1)}, bf16[3,352,256]{2,1,0:T(8,128)(2,1)}, u32[]{:S(2)}, u32[]{:S(2)}) collective-permute-start(bf16[3,352,256]{2,1,0:T(8,128)(2,1)S(1)} %pad_maximum_fusion.2), channel_id=1, source_target_pairs={{0,24},{8,16},{16,8},{24,0},{1,25},{9,17},{17,9},{25,1},{2,26},{10... | collective-permute-start | bytes 1622024 | tf_op jit(solution)/shard_map/ppermute | solution.py:327
  109.0 12.0 %collective-permute-start.15 = (f32[352,256]{1,0:T(8,128)}, f32[352,256]{1,0:T(8,128)}, u32[]{:S(2)}, u32[]{:S(2)}) collective-permute-start(f32[352,256]{1,0:T(8,128)} %get-tuple-element.142), channel_id=1, source_target_pairs={{0,8},{8,0},{24,16},{1,9},{9,1},{25,17},{2,10},{10,2},{26,18},{3,1... | collective-permute-start | bytes 1081352 | tf_op jit(solution)/shard_map/ppermute | solution.py:474
  112.7 14.5 %collective-permute-start.16 = (f32[352,256]{1,0:T(8,128)S(1)}, f32[352,256]{1,0:T(8,128)}, u32[]{:S(2)}, u32[]{:S(2)}) collective-permute-start(f32[352,256]{1,0:T(8,128)S(1)} %get-tuple-element.141), channel_id=1, source_target_pairs={{0,16},{16,0},{24,8},{1,17},{17,1},{25,9},{2,18},{18,2},{26,10},{3... | collective-permute-start | bytes 1081352 | tf_op jit(solution)/shard_map/ppermute | solution.py:474
  114.8 14.2 %collective-permute-start.17 = (f32[352,256]{1,0:T(8,128)S(1)}, f32[352,256]{1,0:T(8,128)S(1)}, u32[]{:S(2)}, u32[]{:S(2)}) collective-permute-start(f32[352,256]{1,0:T(8,128)S(1)} %get-tuple-element.140), channel_id=1, source_target_pairs={{8,16},{16,8},{24,0},{9,17},{17,9},{25,1},{10,18},{18,10},{26,2},{... | collective-permute-start | bytes 1081352 | tf_op jit(solution)/shard_map/ppermute | solution.py:474
  137.0 5.6 %collective-permute-start.19 = (bf16[256,1024]{1,0:T(8,128)(2,1)S(1)}, bf16[256,1024]{1,0:T(8,128)(2,1)S(1)}, u32[]{:S(2)}, u32[]{:S(2)}) collective-permute-start(bf16[256,1024]{1,0:T(8,128)(2,1)S(1)} %get-tuple-element.76), channel_id=1, source_target_pairs={{0,1},{1,0},{2,3},{3,2},{4,5},{5,4},{6,7},{7,6},{8,9},{9,8},{10,11... | collective-permute-start | bytes 1572872 | tf_op jit(solution)/shard_map/ppermute | solution.py:350
  142.0 7.6 %collective-permute-start.18 = (bf16[256,1024]{1,0:T(8,128)(2,1)S(1)}, bf16[256,1024]{1,0:T(8,128)(2,1)S(1)}, u32[]{:S(2)}, u32[]{:S(2)}) collective-permute-start(bf16[256,1024]{1,0:T(8,128)(2,1)S(1)} %get-tuple-element.73), channel_id=1, source_target_pairs={{0,1},{1,0},{2,3},{3,2},{4,5},{5,4},{6,7},{7,6},{8,9},{9,8},{10,11... | collective-permute-start | bytes 1572872 | tf_op jit(solution)/shard_map/ppermute | solution.py:350
  143.5 37.3 %collective-permute-start.21 = (bf16[256,1024]{1,0:T(8,128)(2,1)}, bf16[256,1024]{1,0:T(8,128)(2,1)}, u32[]{:S(2)}, u32[]{:S(2)}) collective-permute-start(bf16[256,1024]{1,0:T(8,128)(2,1)} %add_convert_fusion.2), channel_id=1, source_target_pairs={{0,4},{1,5},{2,6},{3,7},{4,0},{5,1},{6,2},{7,3},{8,12},{9,13},{10,... | collective-permute-start | bytes 1572872 | tf_op jit(solution)/shard_map/ppermute | solution.py:354
  149.6 17.1 %collective-permute-start.23 = (bf16[256,1024]{1,0:T(8,128)(2,1)S(1)}, bf16[256,1024]{1,0:T(8,128)(2,1)}, u32[]{:S(2)}, u32[]{:S(2)}) collective-permute-start(bf16[256,1024]{1,0:T(8,128)(2,1)S(1)} %get-tuple-element.91), channel_id=1, source_target_pairs={{0,1},{1,0},{2,3},{3,2},{4,5},{5,4},{6,7},{7,6},{8,9},{9,8},{10,11... | collective-permute-start | bytes 1572872 | tf_op jit(solution)/shard_map/ppermute | solution.py:350
  150.7 25.6 %collective-permute-start.22 = (bf16[256,1024]{1,0:T(8,128)(2,1)}, bf16[256,1024]{1,0:T(8,128)(2,1)}, u32[]{:S(2)}, u32[]{:S(2)}) collective-permute-start(bf16[256,1024]{1,0:T(8,128)(2,1)} %add_convert_fusion.3), channel_id=1, source_target_pairs={{0,6},{1,7},{2,4},{3,5},{4,2},{5,3},{6,0},{7,1},{8,14},{9,15},{10,... | collective-permute-start | bytes 1572872 | tf_op jit(solution)/shard_map/ppermute | solution.py:354
  158.1 16.6 %collective-permute-start.20 = (bf16[256,1024]{1,0:T(8,128)(2,1)}, bf16[256,1024]{1,0:T(8,128)(2,1)}, u32[]{:S(2)}, u32[]{:S(2)}) collective-permute-start(bf16[256,1024]{1,0:T(8,128)(2,1)} %get-tuple-element.86), channel_id=1, source_target_pairs={{0,1},{1,0},{2,3},{3,2},{4,5},{5,4},{6,7},{7,6},{8,9},{9,8},{10,11... | collective-permute-start | bytes 1572872 | tf_op jit(solution)/shard_map/ppermute | solution.py:350
  166.4 193.7 %all-reduce.8.cloned.1.call-start = ((), (), s32[]{:S(2)}) async-start(), calls=%async_computation.7 | async-start | bytes 5242880 | tf_op jit(solution)/shard_map/psum | solution.py:492
  169.1 22.7 %collective-permute-start.24 = (bf16[256,1024]{1,0:T(8,128)(2,1)}, bf16[256,1024]{1,0:T(8,128)(2,1)S(1)}, u32[]{:S(2)}, u32[]{:S(2)}) collective-permute-start(bf16[256,1024]{1,0:T(8,128)(2,1)} %add_convert_fusion.1), channel_id=1, source_target_pairs={{0,2},{1,3},{2,0},{3,1},{4,6},{5,7},{6,4},{7,5},{8,10},{9,11},{10,... | collective-permute-start | bytes 1572872 | tf_op jit(solution)/shard_map/ppermute | solution.py:354
  195.0 43.5 %collective-permute-start.27 = (bf16[256,1024]{1,0:T(8,128)(2,1)S(1)}, bf16[256,1024]{1,0:T(8,128)(2,1)S(1)}, u32[]{:S(2)}, u32[]{:S(2)}) collective-permute-start(bf16[256,1024]{1,0:T(8,128)(2,1)S(1)} %convolution_convert_fusion.4), channel_id=1, source_target_pairs={{0,24},{8,16},{16,8},{24,0},{1,25},{9,17},{17,9},{25,1},{2,26},{10... | collective-permute-start | bytes 1572872 | tf_op jit(solution)/shard_map/ppermute | solution.py:341
  197.9 40.5 %collective-permute-start.26 = (bf16[256,1024]{1,0:T(8,128)(2,1)}, bf16[256,1024]{1,0:T(8,128)(2,1)S(1)}, u32[]{:S(2)}, u32[]{:S(2)}) collective-permute-start(bf16[256,1024]{1,0:T(8,128)(2,1)} %convolution_convert_fusion.5), channel_id=1, source_target_pairs={{0,16},{8,24},{16,0},{24,8},{1,17},{9,25},{17,1},{25,9},{2,18},{10... | collective-permute-start | bytes 1572872 | tf_op jit(solution)/shard_map/ppermute | solution.py:341
  199.6 38.8 %collective-permute-start.25 = (bf16[256,1024]{1,0:T(8,128)(2,1)}, bf16[256,1024]{1,0:T(8,128)(2,1)}, u32[]{:S(2)}, u32[]{:S(2)}) collective-permute-start(bf16[256,1024]{1,0:T(8,128)(2,1)} %convolution_convert_fusion.6), channel_id=1, source_target_pairs={{0,8},{8,0},{16,24},{24,16},{1,9},{9,1},{17,25},{25,17},{2,10},{10... | collective-permute-start | bytes 1572872 | tf_op jit(solution)/shard_map/ppermute | solution.py:341
  239.9 1.6 collective-permute-start.28
  241.6 4.3 collective-permute-start.34
  242.4 6.7 %collective-permute-start.33 = (bf16[32,1024]{1,0:T(8,128)(2,1)S(1)}, bf16[32,1024]{1,0:T(8,128)(2,1)S(1)}, u32[]{:S(2)}, u32[]{:S(2)}) collective-permute-start(bf16[32,1024]{1,0:T(8,128)(2,1)S(1)} %get-tuple-element.149), channel_id=1, source_target_pairs={{0,6},{1,7},{2,4},{3,5},{4,2},{5,3},{6,0},{7,1},{8,14},{9,15},{10,... | collective-permute-start | bytes 196616 | tf_op jit(solution)/shard_map/ppermute | solution.py:354
  244.7 6.8 %collective-permute-start.32 = (bf16[32,1024]{1,0:T(8,128)(2,1)S(1)}, bf16[32,1024]{1,0:T(8,128)(2,1)S(1)}, u32[]{:S(2)}, u32[]{:S(2)}) collective-permute-start(bf16[32,1024]{1,0:T(8,128)(2,1)S(1)} %get-tuple-element.147), channel_id=1, source_target_pairs={{0,4},{1,5},{2,6},{3,7},{4,0},{5,1},{6,2},{7,3},{8,12},{9,13},{10,... | collective-permute-start | bytes 196616 | tf_op jit(solution)/shard_map/ppermute | solution.py:354
  252.6 10.3 %collective-permute-start.35 = (f32[32,1024]{1,0:T(8,128)S(1)}, f32[32,1024]{1,0:T(8,128)S(1)}, u32[]{:S(2)}, u32[]{:S(2)}) collective-permute-start(f32[32,1024]{1,0:T(8,128)S(1)} %get-tuple-element.119), channel_id=1, source_target_pairs={{16,24},{17,25},{18,26},{19,27},{20,28},{21,29},{22,30},{23,31}} | collective-permute-start | bytes 393224 | tf_op jit(solution)/shard_map/ppermute | solution.py:488
  253.5 11.6 %collective-permute-start.36 = (f32[32,1024]{1,0:T(8,128)S(1)}, f32[32,1024]{1,0:T(8,128)S(1)}, u32[]{:S(2)}, u32[]{:S(2)}) collective-permute-start(f32[32,1024]{1,0:T(8,128)S(1)} %get-tuple-element.119), channel_id=1, source_target_pairs={{8,24},{9,25},{10,26},{11,27},{12,28},{13,29},{14,30},{15,31}} | collective-permute-start | bytes 393224 | tf_op jit(solution)/shard_map/ppermute | solution.py:488
  254.1 10.9 %collective-permute-start.37 = (f32[32,1024]{1,0:T(8,128)S(1)}, f32[32,1024]{1,0:T(8,128)S(1)}, u32[]{:S(2)}, u32[]{:S(2)}) collective-permute-start(f32[32,1024]{1,0:T(8,128)S(1)} %get-tuple-element.119), channel_id=1, source_target_pairs={{0,24},{1,25},{2,26},{3,27},{4,28},{5,29},{6,30},{7,31}} | collective-permute-start | bytes 393224 | tf_op jit(solution)/shard_map/ppermute | solution.py:488
  261.5 9.1 %collective-permute-start.31 = (bf16[256,320]{1,0:T(8,128)(2,1)}, bf16[256,320]{1,0:T(8,128)(2,1)}, u32[]{:S(2)}, u32[]{:S(2)}) collective-permute-start(bf16[256,320]{1,0:T(8,128)(2,1)} %get-tuple-element.124), channel_id=1, source_target_pairs={{0,24},{8,16},{16,8},{24,0},{1,25},{9,17},{17,9},{25,1},{2,26},{10... | collective-permute-start | bytes 491528 | tf_op jit(solution)/shard_map/ppermute | solution.py:341
  261.5 10.5 %collective-permute-start.30 = (bf16[256,320]{1,0:T(8,128)(2,1)}, bf16[256,320]{1,0:T(8,128)(2,1)}, u32[]{:S(2)}, u32[]{:S(2)}) collective-permute-start(bf16[256,320]{1,0:T(8,128)(2,1)} %get-tuple-element.125), channel_id=1, source_target_pairs={{0,16},{8,24},{16,0},{24,8},{1,17},{9,25},{17,1},{25,9},{2,18},{10... | collective-permute-start | bytes 491528 | tf_op jit(solution)/shard_map/ppermute | solution.py:341
  262.9 9.1 %collective-permute-start.29 = (bf16[256,320]{1,0:T(8,128)(2,1)}, bf16[256,320]{1,0:T(8,128)(2,1)}, u32[]{:S(2)}, u32[]{:S(2)}) collective-permute-start(bf16[256,320]{1,0:T(8,128)(2,1)} %get-tuple-element.123), channel_id=1, source_target_pairs={{0,8},{8,0},{16,24},{24,16},{1,9},{9,1},{17,25},{25,17},{2,10},{10... | collective-permute-start | bytes 491528 | tf_op jit(solution)/shard_map/ppermute | solution.py:341
  280.8 14.4 %collective-permute-start.40 = (bf16[832,256]{1,0:T(8,128)(2,1)}, bf16[832,256]{1,0:T(8,128)(2,1)S(1)}, u32[]{:S(2)}, u32[]{:S(2)}) collective-permute-start(bf16[832,256]{1,0:T(8,128)(2,1)} %constant_dynamic-update-slice_fusion.5), channel_id=1, source_target_pairs={{0,24},{8,16},{16,8},{24,0},{1,25},{9,17},{17,9},{25,1},{2,26},{10... | collective-permute-start | bytes 1277960 | tf_op jit(solution)/shard_map/ppermute | solution.py:341
  287.4 14.4 %collective-permute-start.39 = (bf16[832,256]{1,0:T(8,128)(2,1)}, bf16[832,256]{1,0:T(8,128)(2,1)S(1)}, u32[]{:S(2)}, u32[]{:S(2)}) collective-permute-start(bf16[832,256]{1,0:T(8,128)(2,1)} %constant_dynamic-update-slice_fusion.3), channel_id=1, source_target_pairs={{0,16},{8,24},{16,0},{24,8},{1,17},{9,25},{17,1},{25,9},{2,18},{10... | collective-permute-start | bytes 1277960 | tf_op jit(solution)/shard_map/ppermute | solution.py:341
  288.3 206.9 %all-gather.9.cloned.1.call-start = ((), (), s32[]{:S(2)}) async-start(), calls=%async_computation.6 | async-start | bytes 3514368 | tf_op jit(solution)/shard_map/all_gather | solution.py:516
  288.4 13.5 %collective-permute-start.38 = (bf16[832,256]{1,0:T(8,128)(2,1)}, bf16[832,256]{1,0:T(8,128)(2,1)S(1)}, u32[]{:S(2)}, u32[]{:S(2)}) collective-permute-start(bf16[832,256]{1,0:T(8,128)(2,1)} %copy-done.55), channel_id=1, source_target_pairs={{0,8},{8,0},{16,24},{24,16},{1,9},{9,1},{17,25},{25,17},{2,10},{10... | collective-permute-start | bytes 1277960 | tf_op jit(solution)/shard_map/ppermute | solution.py:341
  302.0 1.5 collective-permute-start.41
  303.7 5.7 %collective-permute-start.44 = (bf16[104,256]{1,0:T(8,128)(2,1)S(1)}, bf16[104,256]{1,0:T(8,128)(2,1)S(1)}, u32[]{:S(2)}, u32[]{:S(2)}) collective-permute-start(bf16[104,256]{1,0:T(8,128)(2,1)S(1)} %get-tuple-element.151), channel_id=1, source_target_pairs={{0,2},{1,3},{2,0},{3,1},{4,6},{5,7},{6,4},{7,5},{8,10},{9,11},{10,... | collective-permute-start | bytes 159752 | tf_op jit(solution)/shard_map/ppermute | solution.py:354
  303.7 8.0 %collective-permute-start.43 = (bf16[104,256]{1,0:T(8,128)(2,1)S(1)}, bf16[104,256]{1,0:T(8,128)(2,1)S(1)}, u32[]{:S(2)}, u32[]{:S(2)}) collective-permute-start(bf16[104,256]{1,0:T(8,128)(2,1)S(1)} %get-tuple-element.152), channel_id=1, source_target_pairs={{0,6},{1,7},{2,4},{3,5},{4,2},{5,3},{6,0},{7,1},{8,14},{9,15},{10,... | collective-permute-start | bytes 159752 | tf_op jit(solution)/shard_map/ppermute | solution.py:354
  305.7 9.6 %collective-permute-start.42 = (bf16[104,256]{1,0:T(8,128)(2,1)S(1)}, bf16[104,256]{1,0:T(8,128)(2,1)S(1)}, u32[]{:S(2)}, u32[]{:S(2)}) collective-permute-start(bf16[104,256]{1,0:T(8,128)(2,1)S(1)} %get-tuple-element.150), channel_id=1, source_target_pairs={{0,4},{1,5},{2,6},{3,7},{4,0},{5,1},{6,2},{7,3},{8,12},{9,13},{10,... | collective-permute-start | bytes 159752 | tf_op jit(solution)/shard_map/ppermute | solution.py:354
  315.9 179.3 %reduce-scatter.5.cloned.1.call-start = ((), (), s32[]{:S(2)}) async-start(), calls=%async_computation.5 | async-start | bytes 4718592 | tf_op jit(solution)/shard_map/reduce_scatter | solution.py:519
  316.5 134.1 %copy-start.1 = (f32[352,1024]{1,0:T(8,128)S(1)}, f32[352,1024]{1,0:T(8,128)}, u32[]{:S(2)}) copy-start(f32[352,1024]{1,0:T(8,128)} %copy-done) | copy-start | bytes 4325380
  316.5 209.5 %all-gather.11.cloned.1.call-start = ((), (), s32[]{:S(2)}) async-start(), calls=%async_computation.8 | async-start | bytes 2359296 | tf_op jit(solution)/shard_map/all_gather | solution.py:534
  448.0 14.9 %collective-permute-start.45 = (f32[32,1024]{1,0:T(8,128)S(1)}, f32[32,1024]{1,0:T(8,128)S(1)}, u32[]{:S(2)}, u32[]{:S(2)}) collective-permute-start(f32[32,1024]{1,0:T(8,128)S(1)} %get-tuple-element.136), channel_id=1, source_target_pairs={{24,0},{25,1},{26,2},{27,3},{28,4},{29,5},{30,6},{31,7}} | collective-permute-start | bytes 393224 | tf_op jit(solution)/shard_map/ppermute | solution.py:531
  449.3 15.7 %collective-permute-start.46 = (f32[32,1024]{1,0:T(8,128)S(1)}, f32[32,1024]{1,0:T(8,128)S(1)}, u32[]{:S(2)}, u32[]{:S(2)}) collective-permute-start(f32[32,1024]{1,0:T(8,128)S(1)} %get-tuple-element.135), channel_id=1, source_target_pairs={{24,8},{25,9},{26,10},{27,11},{28,12},{29,13},{30,14},{31,15}} | collective-permute-start | bytes 393224 | tf_op jit(solution)/shard_map/ppermute | solution.py:531
  450.0 18.3 %collective-permute-start.47 = (f32[32,1024]{1,0:T(8,128)S(1)}, f32[32,1024]{1,0:T(8,128)S(1)}, u32[]{:S(2)}, u32[]{:S(2)}) collective-permute-start(f32[32,1024]{1,0:T(8,128)S(1)} %get-tuple-element.134), channel_id=1, source_target_pairs={{24,16},{25,17},{26,18},{27,19},{28,20},{29,21},{30,22},{31,23}} | collective-permute-start | bytes 393224 | tf_op jit(solution)/shard_map/ppermute | solution.py:531
  451.7 19.3 %collective-permute-start.48 = (f32[352,256]{1,0:T(8,128)}, f32[352,256]{1,0:T(8,128)}, u32[]{:S(2)}, u32[]{:S(2)}) collective-permute-start(f32[352,256]{1,0:T(8,128)} %get-tuple-element.133), channel_id=1, source_target_pairs={{0,8},{8,0},{16,24},{1,9},{9,1},{17,25},{2,10},{10,2},{18,26},{3,1... | collective-permute-start | bytes 1081352 | tf_op jit(solution)/shard_map/ppermute | solution.py:524
  455.0 29.7 %collective-permute-start.49 = (f32[352,256]{1,0:T(8,128)}, f32[352,256]{1,0:T(8,128)}, u32[]{:S(2)}, u32[]{:S(2)}) collective-permute-start(f32[352,256]{1,0:T(8,128)} %get-tuple-element.132), channel_id=1, source_target_pairs={{0,16},{8,24},{16,0},{1,17},{9,25},{17,1},{2,18},{10,26},{18,2},{3... | collective-permute-start | bytes 1081352 | tf_op jit(solution)/shard_map/ppermute | solution.py:524
  462.9 29.1 %collective-permute-start.50 = (f32[352,256]{1,0:T(8,128)}, f32[352,256]{1,0:T(8,128)}, u32[]{:S(2)}, u32[]{:S(2)}) collective-permute-start(f32[352,256]{1,0:T(8,128)} %get-tuple-element.131), channel_id=1, source_target_pairs={{0,24},{8,16},{16,8},{1,25},{9,17},{17,9},{2,26},{10,18},{18,10},{... | collective-permute-start | bytes 1081352 | tf_op jit(solution)/shard_map/ppermute | solution.py:524
  465.0 18.7 %collective-permute-start.51 = (f32[352,256]{1,0:T(8,128)}, f32[352,256]{1,0:T(8,128)}, u32[]{:S(2)}, u32[]{:S(2)}) collective-permute-start(f32[352,256]{1,0:T(8,128)} %get-tuple-element.139), channel_id=1, source_target_pairs={{0,8},{8,0},{16,24},{1,9},{9,1},{17,25},{2,10},{10,2},{18,26},{3,1... | collective-permute-start | bytes 1081352 | tf_op jit(solution)/shard_map/ppermute | solution.py:524
  468.3 22.7 %collective-permute-start.52 = (f32[352,256]{1,0:T(8,128)}, f32[352,256]{1,0:T(8,128)}, u32[]{:S(2)}, u32[]{:S(2)}) collective-permute-start(f32[352,256]{1,0:T(8,128)} %get-tuple-element.138), channel_id=1, source_target_pairs={{0,16},{8,24},{16,0},{1,17},{9,25},{17,1},{2,18},{10,26},{18,2},{3... | collective-permute-start | bytes 1081352 | tf_op jit(solution)/shard_map/ppermute | solution.py:524
  471.0 22.1 %collective-permute-start.53 = (f32[352,256]{1,0:T(8,128)}, f32[352,256]{1,0:T(8,128)S(1)}, u32[]{:S(2)}, u32[]{:S(2)}) collective-permute-start(f32[352,256]{1,0:T(8,128)} %get-tuple-element.137), channel_id=1, source_target_pairs={{0,24},{8,16},{16,8},{1,25},{9,17},{17,9},{2,26},{10,18},{18,10},{... | collective-permute-start | bytes 1081352 | tf_op jit(solution)/shard_map/ppermute | solution.py:524
  (55 other events, 386.6 us)
Sparse Core Ops, SparseCore 0:
  12.0 49.8 all-gather.6
  83.1 46.1 all-gather.4
  166.6 59.4 reduce-scatter.2
  287.7 72.3 all-reduce.7
  363.4 58.8 all-gather.8
  424.4 48.7 reduce-scatter.4
  495.4 29.2 all-gather.10

commit v3 on v2

v3 whole, which is shorter than its diff:
```python
import functools
import math
import jax
import jax.numpy as jnp
from jax import lax
from jax.experimental import pallas as pl
from jax.experimental.pallas import tpu as pltpu
BF=jnp.bfloat16; F32=jnp.float32
HEADS=16; HD=64; RQ=6; RK=2; D=1024
COEF_A=3.4445; COEF_B=-4.775; COEF_C=2.0315
NEG=-1e30
NS_STEPS=5

def split2(x):
    hi=x.astype(BF); return hi,(x-hi.astype(F32)).astype(BF)
def dot(a,b): return jnp.dot(a,b,preferred_element_type=F32)
def dot_nt(a,b): return lax.dot_general(a,b,(((1,),(1,)),((),())),preferred_element_type=F32)
def dot_tn(a,b): return lax.dot_general(a,b,(((0,),(0,)),((),())),preferred_element_type=F32)

def index_map(ref, heads):
    row=lax.broadcasted_iota(jnp.int32,ref.shape,0); col=lax.broadcasted_iota(jnp.int32,ref.shape,1)
    row=jnp.where(row>=heads,row-heads,row)
    ref[...]=row-HEADS*lax.shift_right_logical(col,7)-(lax.bitwise_and(col,127)>=HD).astype(jnp.int32)

def one_hot(ref, pair): return jnp.where(ref[...]==2*pair,1.0,0.0).astype(BF)

def twice(dims,r,scale):
    part=dims[:,r*HD:(r+1)*HD]*scale
    return jnp.concatenate([part,part],axis=1)

WQ,WK=RQ*HD,RK*HD
NQ,NK=RQ*HEADS,RK*HEADS

def attn_setup(base_ref,fq_ref,fk_ref,bias_ref,hq,hk,dq,dk,iq,ik,scaled):
    rows,keys=bias_ref.shape
    r_id=lax.broadcasted_iota(jnp.int32,(rows,keys),0)+base_ref[0]*rows
    c_id=lax.broadcasted_iota(jnp.int32,(rows,keys),1)
    bias_ref[...]=jnp.where(c_id<=r_id,0.0,NEG)
    hq[...]=jnp.concatenate(split2(fq_ref[:,WQ:]),axis=1); hk[...]=jnp.concatenate(split2(fk_ref[:,2*WK:]),axis=1)
    for r in range(RQ): dq[r]=twice(fq_ref,r,1.0/RQ if scaled else 1.0)
    for r in range(2*RK): dk[r]=twice(fk_ref,r,1.0/RK if scaled else 1.0)
    index_map(iq,NQ); index_map(ik,2*NK)

def attn_scratch(rows,keys):
    return [pltpu.VMEM((rows,keys),F32),pltpu.VMEM((rows,2*NQ),BF),pltpu.VMEM((keys,4*NK),BF),pltpu.VMEM((RQ,rows,128),F32),pltpu.VMEM((2*RK,keys,128),F32),
        pltpu.VMEM((2*NQ,RQ*128),jnp.int32),pltpu.VMEM((4*NK,2*RK*128),jnp.int32)]

def lanes(x,r): return x[:,r*128:(r+1)*128]

def attn_fwd_body(base_ref,fq_ref,fk_ref,o_ref,lse_ref,q_ref,k_ref,v_ref,bias_ref,hq,hk,dq,dk,iq,ik):
    attn_setup(base_ref,fq_ref,fk_ref,bias_ref,hq,hk,dq,dk,iq,ik,True)
    lane=lax.broadcasted_iota(jnp.int32,(1,128),1)
    head_id=lax.broadcasted_iota(jnp.int32,(1,HEADS),1)
    lse_ref[...]=jnp.zeros_like(lse_ref)
    def step(pair,_):
        cols=pl.ds(pl.multiple_of(pair*128,128),128)
        wide_q=dot(hq[...],one_hot(iq,pair)); wide_k=dot(hk[...],one_hot(ik,pair))
        q=sum(lanes(wide_q,r)*dq[r] for r in range(RQ)).astype(BF)
        k=sum(lanes(wide_k,r)*dk[r] for r in range(RK)).astype(BF)
        v=sum(lanes(wide_k,r)*dk[r] for r in range(RK,2*RK)).astype(BF)
        q_ref[:,cols]=q; k_ref[:,cols]=k; v_ref[:,cols]=v
        qs=q.astype(F32)*(HD**-0.5)
        out=None
        for half in range(2):
            keep=(lane>=HD) if half else (lane<HD)
            qm=jnp.where(keep,qs,0.0).astype(BF)
            s=dot_nt(qm,k)+bias_ref[...]
            m=jnp.max(s,axis=1,keepdims=True)
            e=jnp.exp(s-m)
            l=jnp.sum(e,axis=1,keepdims=True)
            p=(e*(1.0/l)).astype(BF)
            o=dot(p,v)
            out=jnp.where(keep,o,out) if half else o
            lse_ref[...]=jnp.where(head_id==2*pair+half,m+jnp.log(l),lse_ref[...])
        o_ref[:,cols]=out.astype(BF)
        return 0
    lax.fori_loop(0,HEADS//2,step,0)

VM=pl.BlockSpec(memory_space=pltpu.VMEM)
SM=pl.BlockSpec(memory_space=pltpu.SMEM)
def shape(dims,dtype=F32): return jax.ShapeDtypeStruct(dims,dtype)
def cost(us): return pl.CostEstimate(flops=int(us*1.15e9),transcendentals=0,bytes_accessed=1<<20)
def limit(mib): return pltpu.CompilerParams(vmem_limit_bytes=mib<<20)

def attn_fwd(base,fq,fk,interpret=False):
    rows,keys=fq.shape[0],fk.shape[0]
    return pl.pallas_call(attn_fwd_body,
        out_shape=(shape((rows,D),BF),shape((rows,HEADS)),shape((rows,D),BF),shape((keys,D),BF),shape((keys,D),BF)),
        in_specs=[SM,VM,VM],out_specs=(VM,)*5,scratch_shapes=attn_scratch(rows,keys),
        compiler_params=limit(28),cost_estimate=cost(16),name="attn_fwd",interpret=interpret)(base,fq,fk)

def attn_bwd_body(first,last,base_ref,q_ref,k_ref,v_ref,do_ref,lse_ref,fq_ref,fk_ref,gq_ref,gk_ref,bias_ref,hq,hk,dq,dk,iq,ik,aq,ak,tq,tk):
    attn_setup(base_ref,fq_ref,fk_ref,bias_ref,hq,hk,dq,dk,iq,ik,False)
    for ref in (aq,ak,tq,tk): ref[...]=jnp.zeros_like(ref)
    lane=lax.broadcasted_iota(jnp.int32,(1,128),1)
    head_id=lax.broadcasted_iota(jnp.int32,(1,HEADS),1)
    def back(grads,h,d,index,acc,tot,pair):
        e=one_hot(index,pair)
        wide=dot(h[...],e)
        for r,grad in enumerate(grads): acc[r]+=grad*lanes(wide,r)
        terms=jnp.concatenate([(grad*d[r]).astype(BF) for r,grad in enumerate(grads)],axis=1)
        tot[...]+=dot_nt(terms,e[:tot.shape[1]])
    def step(pair,_):
        cols=pl.ds(pl.multiple_of(pair*128,128),128)
        q=q_ref[:,cols]; k=k_ref[:,cols]; v=v_ref[:,cols]; do=do_ref[:,cols]
        qs=q.astype(F32)*(HD**-0.5); dof=do.astype(F32)
        gq=gk=gv=None
        for half in range(2):
            keep=(lane>=HD) if half else (lane<HD)
            qm=jnp.where(keep,qs,0.0).astype(BF); dom=jnp.where(keep,dof,0.0).astype(BF)
            lse=jnp.sum(jnp.where(head_id==2*pair+half,lse_ref[...],0.0),axis=1,keepdims=True)
            p=jnp.exp(dot_nt(qm,k)+bias_ref[...]-lse)
            dp=dot_nt(dom,v)
            inner=jnp.sum(p*dp,axis=1,keepdims=True)
            ds=(p*(dp-inner)).astype(BF)
            nq=dot(ds,k); nk=dot_tn(ds,qm); nv=dot_tn(p.astype(BF),dom)
            if half==0: gq,gk,gv=nq,nk,nv
            else:
                gq=jnp.where(keep,nq,gq); gk=gk+nk; gv=gv+nv
        gq=gq*(HD**-0.5/RQ); gk=gk*(1.0/RK); gv=gv*(1.0/RK)
        back([gq]*RQ,hq,dq,iq,aq,tq,pair)
        back([gk]*RK+[gv]*RK,hk,dk,ik,ak,tk,pair)
        return 0
    lax.fori_loop(first,last,step,0)
    for acc,tot,ref in ((aq,tq,gq_ref),(ak,tk,gk_ref)):
        count=acc.shape[0]
        for r in range(0,count,2):
            even=acc[r]; odd=acc[r+1]
            ref[:,r*HD:(r+2)*HD]=jnp.concatenate([even[:,:HD]+even[:,HD:],odd[:,:HD]+odd[:,HD:]],axis=1)
        ref[:,count*HD:]=tot[...]

def attn_bwd(pairs,base,q,k,v,do,lse,fq,fk,us,interpret=False):
    rows,keys=q.shape[0],k.shape[0]
    return pl.pallas_call(functools.partial(attn_bwd_body,*pairs),out_shape=(shape(fq.shape),shape(fk.shape)),
        in_specs=[SM]+[VM]*7,out_specs=(VM,)*2,
        scratch_shapes=attn_scratch(rows,keys)+[pltpu.VMEM((RQ,rows,128),F32),pltpu.VMEM((2*RK,keys,128),F32),pltpu.VMEM((rows,NQ),F32),pltpu.VMEM((keys,2*NK),F32)],
        compiler_params=limit(36),cost_estimate=cost(us),name="attn_bwd",interpret=interpret)(base,q,k,v,do,lse,fq,fk)

BK=256
def tri_cols(j): return (j*(j+1)//2)*BK

def store_sym(hi,lo,i,j,val):
    h,l=split2(val)
    hi[i*BK:(i+1)*BK,j*BK:(j+1)*BK]=h; lo[i*BK:(i+1)*BK,j*BK:(j+1)*BK]=l
    if i!=j:
        t=val.T
        h,l=split2(t)
        hi[j*BK:(j+1)*BK,i*BK:(i+1)*BK]=h; lo[j*BK:(j+1)*BK,i*BK:(i+1)*BK]=l

def mul_upper(xh,xl,yh,yl,n,emit):
    for j in reversed(range(n)):
        top=(j+1)*BK; cs=slice(j*BK,(j+1)*BK)
        r=dot(xh[:top,:],yh[:,cs])+dot(xh[:top,:],yl[:,cs])+dot(xl[:top,:],yh[:,cs])
        for i in range(j+1): emit(i,j,r[i*BK:(i+1)*BK])

def ns_body(g_ref,y_ref,o_ref,a_up,ah,al,ph,pw,bh,bl):
    n=o_ref.shape[1]//BK
    eye=(lax.broadcasted_iota(jnp.int32,(BK,BK),0)==lax.broadcasted_iota(jnp.int32,(BK,BK),1)).astype(F32)
    blk=lambda i,j:(slice(i*BK,(i+1)*BK),slice(j*BK,(j+1)*BK))
    trace=None
    for j in range(n):
        off=tri_cols(j)+j*BK
        part=g_ref[:,off:off+BK]*eye
        trace=part if trace is None else trace+part
    trace=jnp.sum(jnp.sum(trace,axis=1,keepdims=True),axis=0,keepdims=True)
    scale=1.0/(jnp.sqrt(trace)+1e-7)
    for j in range(n):
        for i in range(j+1):
            off=tri_cols(j)+i*BK
            val=g_ref[:,off:off+BK]*(scale*scale)
            a_up[blk(i,j)]=val; store_sym(ah,al,i,j,val)
    o_ref[...]=y_ref[...]*scale
    def poly():
        def emit(i,j,c):
            store_sym(ph,pw,i,j,COEF_B*a_up[blk(i,j)]+COEF_C*c)
        mul_upper(ah,al,ah,al,n,emit)
    def apply():
        y=o_ref[...]; yh,yl=split2(y)
        o_ref[...]=COEF_A*y+(dot(yh,ph[...])+dot(yh,pw[...])+dot(yl,ph[...]))
    def step(k,c):
        poly()
        def emit_b(i,j,m):
            val=COEF_A*a_up[blk(i,j)]+m
            a_up[blk(i,j)]=val; store_sym(bh,bl,i,j,val)
        mul_upper(ah,al,ph,pw,n,emit_b)
        apply()
        def emit_a(i,j,m):
            val=COEF_A*a_up[blk(i,j)]+m
            a_up[blk(i,j)]=val; store_sym(ah,al,i,j,val)
        mul_upper(bh,bl,ph,pw,n,emit_a)
        return c
    lax.fori_loop(0,NS_STEPS-1,step,0)
    poly(); apply()

def ns_big(gram,y,interpret=False):
    w,d=y.shape
    vm=pl.BlockSpec(memory_space=pltpu.VMEM)
    return pl.pallas_call(ns_body,out_shape=jax.ShapeDtypeStruct((w,d),F32),
        in_specs=[vm,vm],out_specs=vm,
        scratch_shapes=[pltpu.VMEM((d,d),F32)]+[pltpu.VMEM((d,d),BF)]*6,
        compiler_params=pltpu.CompilerParams(vmem_limit_bytes=40<<20),cost_estimate=cost(71),name="ns_gram",interpret=interpret)(gram,y)

def gram_body(y_ref,g_ref):
    n=y_ref.shape[1]//BK
    yh,yl=split2(y_ref[...])
    for j in range(n):
        top=(j+1)*BK; cs=slice(j*BK,top)
        r=dot_tn(yh[:,:top],yh[:,cs])+dot_tn(yh[:,:top],yl[:,cs])+dot_tn(yl[:,:top],yh[:,cs])
        for i in range(j+1):
            off=tri_cols(j)+i*BK
            g_ref[:,off:off+BK]=r[i*BK:(i+1)*BK]

def gram_upper(y,interpret=False):
    d=y.shape[1]; n=d//BK
    vm=pl.BlockSpec(memory_space=pltpu.VMEM)
    return pl.pallas_call(gram_body,out_shape=jax.ShapeDtypeStruct((BK,n*(n+1)//2*BK),F32),in_specs=[vm],out_specs=vm,
        compiler_params=pltpu.CompilerParams(vmem_limit_bytes=16<<20),cost_estimate=cost(3),name="gram_upper",interpret=interpret)(y)


def mm3(x,y,f=dot):
    xh,xl=split2(x); yh,yl=split2(y)
    return f(xh,yh)+f(xh,yl)+f(xl,yh)

def seg_mask(n,widths):
    def ids(axis):
        pos=lax.broadcasted_iota(jnp.int32,(n,n),axis); out=jnp.zeros_like(pos); edge=0
        for w in widths:
            edge+=w; out=out+(pos>=edge).astype(jnp.int32)
        return out
    return (ids(0)==ids(1)).astype(F32)

GROUPS=((0,(NQ,NK,NK)),(NQ+2*NK,(WQ,)),(NQ+2*NK+WQ,(WK,WK)))

def ns_factor_body(all_ref,own_ref,out_ref):
    out_ref[sum(GROUPS[-1][1])+GROUPS[-1][0]:,:]=jnp.zeros((out_ref.shape[0]-sum(GROUPS[-1][1])-GROUPS[-1][0],out_ref.shape[1]),F32)
    state=[]
    for start,widths in GROUPS:
        n=sum(widths); rs=slice(start,start+n)
        mask=seg_mask(n,widths)
        eye=(lax.broadcasted_iota(jnp.int32,(n,n),0)==lax.broadcasted_iota(jnp.int32,(n,n),1)).astype(F32)
        a=mask*sum(mm3(all_ref[d,rs,:],all_ref[d,rs,:],dot_nt) for d in range(all_ref.shape[0]))
        diag=a*eye
        row=jnp.sum(mask*jnp.sum(diag,axis=1,keepdims=True),axis=0,keepdims=True)
        col=jnp.sum(mask*jnp.sum(diag,axis=0,keepdims=True),axis=1,keepdims=True)
        row=1.0/(jnp.sqrt(row)+1e-7); col=1.0/(jnp.sqrt(col)+1e-7)
        state+=[a*row*col,own_ref[rs,:]*col]
    def step(_,c):
        out=[]
        for a,x in zip(c[::2],c[1::2]):
            p=COEF_B*a+COEF_C*mm3(a,a)
            x=COEF_A*x+mm3(p,x)
            b=COEF_A*a+mm3(a,p)
            out+=[COEF_A*b+mm3(b,p),x]
        return tuple(out)
    state=lax.fori_loop(0,NS_STEPS-1,step,tuple(state))
    for (start,widths),a,x in zip(GROUPS,state[::2],state[1::2]):
        out_ref[start:start+sum(widths),:]=COEF_A*x+mm3(COEF_B*a+COEF_C*mm3(a,a),x)

def ns_factor(tiles,own,interpret=False):
    return pl.pallas_call(ns_factor_body,out_shape=shape(own.shape),in_specs=[VM]*2,out_specs=VM,
        compiler_params=limit(28),cost_estimate=cost(22),name="ns_factor",interpret=interpret)(tiles,own)

def ffn_body(x_ref,g_ref,w_ref,second_ref,branch_ref,hid_ref,dg_ref,du_ref):
    x=x_ref[...]
    gate=dot_nt(x,w_ref[0]); up=dot_nt(x,w_ref[1]); dh=dot_nt(g_ref[...],w_ref[2])
    sig=1.0/(1.0+jnp.exp(-gate))
    act=gate*sig
    hid=(act*up).astype(BF)
    dg=(dh*up*sig*(1.0+gate*(1.0-sig))).astype(BF)
    du=(dh*act).astype(BF)
    hid_ref[...]=hid; dg_ref[...]=dg; du_ref[...]=du
    second_ref[...]=(dot(dg,w_ref[0])+dot(du,w_ref[1])).astype(BF)
    branch_ref[...]=dot(hid,w_ref[2]).astype(BF)

def in_hbm(x): return pltpu.with_memory_space_constraint(x,pltpu.HBM)

def ffn_tokens(x_all,g_all,w,interpret=False):
    tokens=x_all.shape[0]; rows=256; hid=w.shape[1]
    block=pl.BlockSpec((rows,D),lambda i:(i,0)); part=pl.BlockSpec((rows,hid),lambda i:(i,0))
    return pl.pallas_call(ffn_body,out_shape=(pltpu.HBM((tokens,D),BF),shape((tokens,D),BF))+(shape((tokens,hid),BF),)*3,
        grid=(tokens//rows,),in_specs=[block,block,pl.BlockSpec(w.shape,lambda i:(0,0,0),pipeline_mode=pl.Buffered(1))],
        out_specs=(block,block,part,part,part),
        compiler_params=limit(20),cost_estimate=cost(20),name="ffn_tokens",interpret=interpret)(in_hbm(x_all),in_hbm(g_all),w)

def ffn_grads_body(steps,hid_ref,dg_ref,du_ref,x_ref,g_ref,grad_ref,*total):
    width=hid_ref.shape[1]
    for c,(left,right) in enumerate(((dg_ref,x_ref),(du_ref,x_ref),(hid_ref,g_ref))):
        here=slice(c*width,(c+1)*width)
        part=dot_tn(left[...],right[...])
        if steps>1:
            part=jnp.where(pl.program_id(0)==0,part,part+total[0][c])
            total[0][c]=part
        grad_ref[here,:]=part.astype(BF)
    grad_ref[3*width:,:]=jnp.zeros((grad_ref.shape[0]-3*width,D),BF)

def ffn_grads(saved,x_all,g_all,n_dp,interpret=False):
    tokens,hid=saved[0].shape; rows=min(tokens,2048); steps=tokens//rows
    block=pl.BlockSpec((rows,D),lambda i:(i,0)); part=pl.BlockSpec((rows,hid),lambda i:(i,0))
    out=(n_dp*hid,D)
    return pl.pallas_call(functools.partial(ffn_grads_body,steps),out_shape=shape(out,BF),grid=(steps,),
        in_specs=[part]*3+[block]*2,out_specs=pl.BlockSpec(out,lambda i:(0,0)),
        scratch_shapes=[] if steps==1 else [pltpu.VMEM((3,hid,D),F32)],
        compiler_params=limit(40),cost_estimate=cost(10),name="ffn_grads",interpret=interpret)(*saved,x_all,g_all)


EPS = 1e-06
MOMENTUM = 0.5
LEARN = 0.2
LEARN_VEC = 0.002
P = jax.sharding.PartitionSpec
FFN = 3


def normalize(values):
    row_scale = lax.rsqrt(jnp.mean(values * values, axis=-1, keepdims=True) + EPS)
    return values * row_scale, row_scale


def norm_back(grad_in, normed, row_scale, gain):
    scaled = grad_in * gain
    inner_sum = jnp.mean(scaled * normed, axis=-1, keepdims=True)
    return row_scale * (scaled - normed * inner_sum), jnp.sum(grad_in * normed, axis=0)


def dp_pairs(shift, keep=lambda target: True):
    return [(j, j ^ shift) for j in range(lax.axis_size("dp")) if keep(j ^ shift)]


def place(parts, axis, me=None):
    me = lax.axis_index("dp") if me is None else me
    step = parts[0].shape[axis]
    shape = list(parts[0].shape)
    shape[axis] *= len(parts)
    out = jnp.zeros(shape, parts[0].dtype)
    for shift, part in enumerate(parts):
        out = lax.dynamic_update_slice_in_dim(out, part, (me ^ shift) * step, axis)
    return out


def gather_dp(own, axis=0):
    return place([own] + [lax.ppermute(own, "dp", dp_pairs(s)) for s in range(1, lax.axis_size("dp"))], axis)


def sum_dp(block_for, during=None, alongside=(), gate=None):
    me = lax.axis_index("dp")
    sent = [block_for(me ^ s).astype(BF) for s in range(1, lax.axis_size("dp"))]
    if gate is not None:
        sent = [after(block, gate) for block in sent]
    total = block_for(me)
    aside = None
    if during is not None:
        aside = during(*sent)
        total = after(total, *aside, *alongside)
    for s, block in enumerate(sent, 1):
        total = total + lax.ppermute(block, "dp", dp_pairs(s)).astype(F32)
    return total if during is None else (total, aside)


def after(value, *others):
    return lax.optimization_barrier((value, *others))[0]


def pass_core(x):
    return lax.ppermute(x, "mp", [(j, j ^ 1) for j in range(lax.axis_size("mp"))])


def pass_chip(x, shift):
    return lax.ppermute(x, "mp", [(j, j ^ (2 * shift)) for j in range(lax.axis_size("mp"))])


def pick(x, index):
    return lax.dynamic_index_in_dim(x, index, 0, keepdims=False)


CHIPS = 4


def cross_chips(near):
    if len(near) == 1:
        return [lax.psum_scatter(near[0], "mp", scatter_dimension=0, tiled=True)]
    return [near[0]] + [pass_chip(near[s].astype(BF), s) for s in range(1, len(near))]


def collect(near):
    return sum(part.astype(F32) for part in cross_chips(near))


def core_half(partial, axis):
    core = lax.axis_index("mp") % 2
    away = lax.dynamic_index_in_dim(partial, 1 - core, axis, keepdims=False).astype(BF)
    return lax.dynamic_index_in_dim(partial, core, axis, keepdims=False) + pass_core(away).astype(F32)


def chip_sums(partial):
    if lax.axis_size("mp") != 2 * CHIPS:
        return [partial]
    near = core_half(partial.reshape(CHIPS, 2, -1, partial.shape[1]), 1)
    near = [pick(near, (lax.axis_index("mp") // 2) ^ s) for s in range(CHIPS)]
    return [near[0]] + [part.astype(BF) for part in near[1:]]


def body(
    tokens,
    cotangent,
    domain_ids,
    domain_weight,
    gains,
    gain_mom,
    factor_w,
    factor_mom,
    out_w,
    out_mom,
    gate_up_w,
    gate_up_mom,
    down_w,
    down_mom,
):
    n_dp, n_mp = lax.axis_size("dp"), lax.axis_size("mp")
    me, mz = lax.axis_index("dp"), lax.axis_index("mp")
    rows = tokens.shape[0]
    d_own = factor_w.shape[0]
    hidden_own = gate_up_w.shape[2]
    out_own = d_own // n_mp
    base = me.astype(jnp.int32).reshape(1)
    shifts = range(1, n_dp)

    edge = NQ + 2 * NK

    def q_rows(m):
        return jnp.concatenate([m[edge : edge + WQ], m[:NQ]])

    def kv_rows(m):
        return jnp.concatenate([m[edge + WQ :], m[NQ:edge]])

    factor_own = factor_w.T.astype(BF)
    kv_low = gather_dp(kv_rows(factor_own), 1)
    x_float = tokens.astype(F32)
    first_normed, first_scale = normalize(x_float)
    first_own = (first_normed * gains[0]).astype(BF)
    domain_range = jnp.arange(domain_weight.shape[0], dtype=jnp.int32)
    seq_weight = jnp.sum(jnp.where(domain_ids[0, 0] == domain_range, domain_weight, 0.0))
    d_output = cotangent.astype(F32) * seq_weight
    d_output_all = lax.all_gather(d_output.astype(BF), "mp", axis=0, tiled=True)
    kv_all = gather_dp(dot_nt(first_own, kv_low))
    q_low = gather_dp(after(q_rows(factor_own), kv_low), 1)
    q_own = dot_nt(first_own, q_low)
    attended, lse, queries, key_vecs, values = attn_fwd(base, q_own, kv_all)
    out_low = gather_dp(after(out_w.astype(BF), kv_all))
    residual = x_float + dot(attended, out_low)
    second_normed, second_scale = normalize(residual)

    ffn_own = jnp.stack([gate_up_w[0].T, gate_up_w[1].T, down_w])
    ffn_low = gather_dp(after(ffn_own.astype(BF), out_low), 2)
    second_own = (second_normed * gains[1]).astype(BF)
    to_ffn = lambda target: target < FFN
    ffn_slot = jnp.minimum(me, FFN - 1)
    ffn_mom = after(jnp.stack([gate_up_mom[0].T, gate_up_mom[1].T, down_mom]), ffn_low)
    own_mom = [pick(ffn_mom, ffn_slot)]
    for s in shifts:
        own_mom.append(lax.ppermute(pick(ffn_mom, jnp.minimum(me ^ s, FFN - 1)), "dp", dp_pairs(s, to_ffn)))
    second_in = lax.all_gather(second_own, "mp", axis=0, tiled=True)
    d_second, branch, *saved = ffn_tokens(second_in, d_output_all, after(ffn_low, *own_mom[1:]))
    d_second = lax.psum_scatter(d_second, "mp", scatter_dimension=0, tiled=True).astype(F32)
    grads = ffn_grads(saved, second_in, d_output_all, n_dp)
    branch = chip_sums(branch)
    d_second = after(d_second, grads, *branch)
    own_mom = MOMENTUM * place(own_mom, 1)
    matrix = lax.psum_scatter(grads, "dp", scatter_dimension=0, tiled=True)

    d_resid_norm, gain_second = norm_back(d_second, second_normed, second_scale, gains[1])
    d_residual = d_output + d_resid_norm
    d_residual_low = d_residual.astype(BF)
    d_attended = dot_nt(d_residual_low, out_low).astype(BF)

    def backward(pairs, us, *gates):
        return attn_bwd(pairs, after(base, *gates), queries, key_vecs, values, d_attended, lse, q_own, kv_all, us)

    grad_out = dot_tn(attended, d_residual_low)
    if n_mp == 2 * CHIPS:
        grad_out = core_half(grad_out.reshape(n_dp, CHIPS, 2, out_own, D), 2)
    grad_out = grad_out.reshape(n_dp, -1, D)
    last, branch = branch[3:], cross_chips([after(part, d_second) for part in branch[:3]])
    grad_out, (d_q, d_kv) = sum_dp(
        lambda t: pick(grad_out, t), during=functools.partial(backward, (0, HEADS // 2), 26), alongside=(matrix, *branch[1:])
    )
    d_q, d_kv = after((d_q, d_kv), grad_out)
    if n_mp == 2 * CHIPS:
        grad_out = grad_out.reshape(CHIPS, out_own, D)
        near = [pick(grad_out, (mz // 2) ^ s) for s in range(CHIPS)]
        near = near[:1] + [part.astype(BF) for part in near[1:]]
        grad_out = collect(near)
    else:
        grad_out = lax.psum_scatter(grad_out, "mp", scatter_dimension=0, tiled=True)
    out_tile = MOMENTUM * lax.dynamic_slice_in_dim(out_mom, mz * out_own, out_own, 0) + grad_out
    out_rows = place([out_tile] + [lax.ppermute(out_tile, "dp", [(j ^ s, j) for j in range(FFN, n_dp)]) for s in shifts], 0)
    out_rows = jnp.pad(out_rows, ((0, hidden_own - out_rows.shape[0]), (0, 0)))
    matrix = jnp.where(me < FFN, own_mom + matrix.astype(F32), out_rows)
    gram_part = gram_upper(matrix)
    gram = lax.psum(gram_part, "mp")

    d_kv = sum_dp(lambda t: lax.dynamic_slice_in_dim(d_kv, t * rows, rows, 0))
    d_q, d_kv = d_q.astype(BF), d_kv.astype(BF)
    d_first = dot(d_q, q_low) + dot(d_kv, kv_low)
    d_input_norm, gain_first = norm_back(d_first, first_normed, first_scale, gains[0])
    input_grad = d_residual + d_input_norm

    gain_rows = jnp.stack([gain_first, gain_second])
    filler = -(factor_w.shape[1] + 2) % (8 * n_mp)

    d_all = jnp.concatenate([d_q[:, WQ:], d_kv[:, 2 * WK :], d_q[:, :WQ], d_kv[:, : 2 * WK]], axis=1)
    grad_factor = jnp.concatenate([dot_tn(d_all, first_own), jnp.pad(gain_rows, ((0, filler), (0, 0)))])
    height = grad_factor.shape[0] // n_mp
    if n_mp == 2 * CHIPS:
        grad_factor = core_half(grad_factor.reshape(CHIPS, 2, height, D), 1).reshape(CHIPS * height, D)
    grad_factor = sum_dp(lambda t: lax.dynamic_slice_in_dim(grad_factor, t * d_own, d_own, 1))
    dp_summed = grad_factor
    if n_mp == 2 * CHIPS:
        grad_factor = grad_factor.reshape(CHIPS, height, d_own)
        grad_factor = collect([pick(grad_factor, (mz // 2) ^ s) for s in range(CHIPS)])
    else:
        grad_factor = lax.psum_scatter(grad_factor, "mp", scatter_dimension=0, tiled=True)
    factor_piece = jnp.pad(MOMENTUM * factor_mom.T, ((0, filler + 2), (0, 0)))
    factor_piece = lax.dynamic_slice_in_dim(factor_piece, mz * height, height, 0) + grad_factor
    factor_all = lax.all_gather(factor_piece, ("dp", "mp"), axis=0, tiled=True).reshape(n_dp, n_mp * height, d_own)
    factor_tile = pick(factor_all, me)
    gain_grad = factor_tile[factor_w.shape[1] : factor_w.shape[1] + 2]

    def give_back(whole):
        pieces = [lax.dynamic_slice_in_dim(whole, (me ^ s) * d_own, d_own, 1) for s in range(n_dp)]
        came = [lax.ppermute(pieces[s], "dp", dp_pairs(s, lambda t: t ^ s < FFN))[None] for s in shifts]
        return place([pieces[0][None]] + came, 0), pieces[1:]

    mom_back, _ = give_back(after(matrix, dp_summed))
    ortho = ns_big(gram, after(matrix, factor_piece, mom_back))
    ortho = after(ortho, factor_all)
    branch += [pass_chip(after(part, ortho), 3) for part in last]
    block_out = (residual + sum(part.astype(F32) for part in branch)).astype(BF)
    out_ortho = lax.dynamic_slice_in_dim(ortho, me * out_own, out_own, 0)
    for s in shifts:
        piece = lax.dynamic_slice_in_dim(ortho, (me ^ s) * out_own, out_own, 0)
        piece = lax.ppermute(piece, "dp", [(j, j ^ s) for j in range(FFN, n_dp)])
        out_ortho = jnp.where(me ^ s == FFN, piece, out_ortho)
    out_pair = after(jnp.stack([out_tile, out_ortho]), factor_all)
    out_both = lax.all_gather(out_pair, "mp", axis=1, tiled=True)
    new_out_mom = out_both[0]
    new_out_w = out_w - LEARN * 0.2 * math.sqrt(D) * out_both[1]
    ortho_back, sent = give_back(after(ortho, out_ortho))
    factor_ortho = ns_factor(factor_all, after(factor_tile, out_pair, *sent))
    ortho_back = after(ortho_back, factor_ortho)
    turn = lambda stack: jnp.stack([stack[0].T, stack[1].T])
    ffn_rate = LEARN * 0.2 * math.sqrt(max(D, hidden_own * n_mp))
    new_gate_up_mom, new_down_mom = turn(mom_back), mom_back[2]
    new_gate_up_w = gate_up_w - ffn_rate * turn(ortho_back)
    new_down_w = down_w - ffn_rate * ortho_back[2]
    widths = [NQ, NK, NK, WQ, WK, WK]
    factor_rate = jnp.concatenate([jnp.full((w, 1), LEARN * 0.2 * math.sqrt(max(D, w)), F32) for w in widths])
    new_factor_mom = factor_tile[: factor_w.shape[1]].T
    new_factor_w = factor_w - (factor_rate * factor_ortho[: factor_w.shape[1]]).T

    new_gain_mom = MOMENTUM * gain_mom + gain_grad
    new_gains = lax.dynamic_slice_in_dim(gains, me * d_own, d_own, 1) - LEARN_VEC * new_gain_mom
    return (
        block_out,
        input_grad,
        gain_grad,
        new_gains,
        new_gain_mom,
        new_factor_mom,
        new_factor_w,
        new_out_mom,
        new_out_w,
        new_gate_up_mom,
        new_gate_up_w,
        new_down_mom,
        new_down_w,
    )


def solution(mesh):
    token = P(("mp", "dp"), None)
    row = P("dp", None)
    ffn = P(None, "dp", "mp")
    down = P("mp", "dp")
    vec = P(None, "dp")
    return jax.shard_map(
        body,
        mesh=mesh,
        in_specs=(token, token, P("mp", None), P(), P(), vec, row, row, row, row, ffn, ffn, down, down),
        out_specs=(token, token, vec, vec, vec, row, row, row, row, ffn, ffn, down, down),
        check_vma=False,
    )
```

time: 546 us -> 496 us (0.908)
  Pallas kernels: 187 us -> 156 us
  waiting for transfers between devices: 159 us -> 137 us
  matrix products: 19.6 us -> 5.27 us
  starting transfers between devices: 76.6 us -> 86.3 us
  local copies, waits for them, and re-layouts: 44.5 us -> 53.3 us
    ppermute x9, waiting for transfers between devices: 29.9 us -> 3.2 us  [pass_chip(): lax.ppermute(x, 'mp', [(j, j ^ 2 * shift) for j in range(lax.axis_size('m...]
    pallas_call x1, Pallas kernels: 86.7 us -> 68.1 us  [ns_big(): pl.pallas_call(ns_body, out_shape=jax.ShapeDtypeStruct((w, d), F32), in_s...]
    reduce_scatter x1, waiting for transfers between devices: 0.01 us -> 15.4 us  [body(): lax.psum_scatter(d_second, 'mp', scatter_dimension=0, tiled=True)]
    reduce_scatter x1, waiting for transfers between devices: 0.02 us -> 12.7 us  [body(): matrix = lax.psum_scatter(grads, 'dp', scatter_dimension=0, tiled=True)]
    psum x1, waiting for transfers between devices: 43.6 us -> 31.8 us  [body(): gram = lax.psum(gram_part, 'mp')]
    reduce_scatter x1, starting transfers between devices: 0.04 us -> 10.8 us  [body(): matrix = lax.psum_scatter(grads, 'dp', scatter_dimension=0, tiled=True)]
    unnamed x132 -> x122, local copies, waits for them, and re-layouts: 12.7 us -> 23.1 us
    ppermute x9, waiting for transfers between devices: 14.4 us -> 5.67 us  [sum_dp(): total = total + lax.ppermute(block, 'dp', dp_pairs(s)).astype(F32)]
  transfers between devices with their start and end apart: 61 -> 58, of which waited for: 29 -> 21; matrix products, arithmetic and copies ran while one was open for 13% -> 12% of each run, Pallas kernels for 34% -> 29%
where the time goes in v3:
time: 496 us; the launch traced here: 488 us
  Pallas kernels  156 us (31%)
  waiting for transfers between devices  137 us (28%)
  starting transfers between devices  86.3 us (17%)
  local copies, waits for them, and re-layouts  53.3 us (11%)
  other arithmetic  32.2 us (6%)
  between operations  16.7 us (3%)
  matrix products  5.27 us (1%)
    pallas_call x1, Pallas kernels, ns_big(): pl.pallas_call(ns_body, out_shape=jax.ShapeDtypeStruct((w, d), F32), in_s...  68.1 us
    ppermute x15, waiting for transfers between devices, gather_dp(): lax.ppermute(own, 'dp', dp_pairs(s))  46.1 us
    psum x1, waiting for transfers between devices, body(): gram = lax.psum(gram_part, 'mp')  31.8 us
    pallas_call x1, Pallas kernels, attn_bwd(): pl.pallas_call(functools.partial(attn_bwd_body, *pairs), out_shape=(shape...  25.9 us
    unnamed x122, local copies, waits for them, and re-layouts  23.1 us
    ppermute x6, starting transfers between devices, give_back(): lax.ppermute(pieces[s], 'dp', dp_pairs(s, lambda t: t ^ s < FFN))[None]  19.4 us
    ppermute x15, starting transfers between devices, gather_dp(): lax.ppermute(own, 'dp', dp_pairs(s))  18.7 us
    pallas_call x1, Pallas kernels, ns_factor(): pl.pallas_call(ns_factor_body, out_shape=shape(own.shape), in_specs=[VM]...  18.7 us
  transfers between devices with their start and end apart: 58, of which 21 were waited for; matrix products, arithmetic and copies ran while one was open for 12% of the time, Pallas kernels for 29%

profile of v3, /device:TPU:0, one launch (start us, length us, event | category | flops | bytes accessed | tf_op | source)
XLA Modules:
  0.0 487.5 jit_solution(2279321017276121833)
XLA Ops:
  9.2 2.6 fusion.14
  12.1 3.0 collective-permute-start
  15.1 1.5 collective-permute-start.1
  17.8 2.3 collective-permute-done
  20.2 4.1 collective-permute-done.1
  27.1 1.6 collective-permute-start.6
  29.1 1.5 collective-permute-start.5
  30.8 2.5 collective-permute-done.3
  33.3 1.5 collective-permute-start.8
  34.9 13.2 %collective-permute-done.5 = bf16[480,256]{1,0:T(8,128)(2,1)S(1)} collective-permute-done((bf16[480,256]{1,0:T(8,128)(2,1)S(1)}, bf16[480,256]{1,0:T(8,128)(2,1)S(1)}, u32[]{:S(2)}, u32[]{:S(2)}) %collective-permute-start.5) | collective-permute-done | bytes 245792 | tf_op jit(solution)/shard_map/ppermute | solution.py:341
  48.7 5.6 %collective-permute-done.7 = f32[256,320]{1,0:T(8,128)S(1)} collective-permute-done((f32[256,320]{1,0:T(8,128)S(1)}, f32[256,320]{1,0:T(8,128)S(1)}, u32[]{:S(2)}, u32[]{:S(2)}) %collective-permute-start.7) | collective-permute-done | bytes 327712 | tf_op jit(solution)/shard_map/ppermute | solution.py:341
  55.1 1.5 collective-permute-start.10
  56.6 1.3 collective-permute-start.11
  57.9 15.9 %attn_fwd.1 = (bf16[256,1024]{1,0:T(8,128)(2,1)S(1)}, f32[256,16]{1,0:T(8,128)S(1)}, bf16[256,1024]{1,0:T(8,128)(2,1)S(1)}, bf16[1024,1024]{1,0:T(8,128)(2,1)S(1)}, bf16[1024,1024]{1,0:T(8,128)(2,1)S(1)}) custom-call(s32[1]{0:T(128)} %bitcast.base_ref, f32[256,480]{1,0:T(8,128)S(1)} %fusion.55.fq_ref, f32[1024,320]{1,0:T(8,128)S(1)} %constant_dynamic-update-slice_fusion.15.fk_ref), custom_call_target="tpu_custom_call" | custom-call | flops 18400000000 | bytes 1048576 | tf_op jit(solution)/shard_map/attn_fwd/pallas_call | solution.py:87
  81.5 1.7 collective-permute-start.12
  86.7 10.4 %collective-permute-done.12 = bf16[3,352,256]{2,1,0:T(8,128)(2,1)} collective-permute-done((bf16[3,352,256]{2,1,0:T(8,128)(2,1)}, bf16[3,352,256]{2,1,0:T(8,128)(2,1)}, u32[]{:S(2)}, u32[]{:S(2)}) %collective-permute-start.12) | collective-permute-done | bytes 540704 | tf_op jit(solution)/shard_map/ppermute | solution.py:341
  98.2 7.4 %collective-permute-done.13 = bf16[3,352,256]{2,1,0:T(8,128)(2,1)} collective-permute-done((bf16[3,352,256]{2,1,0:T(8,128)(2,1)}, bf16[3,352,256]{2,1,0:T(8,128)(2,1)}, u32[]{:S(2)}, u32[]{:S(2)}) %collective-permute-start.13) | collective-permute-done | bytes 540704 | tf_op jit(solution)/shard_map/ppermute | solution.py:341
  107.9 2.4 collective-permute-start.15
  110.3 1.9 collective-permute-start.16
  113.5 5.9 %collective-permute-done.15 = f32[352,256]{1,0:T(8,128)S(1)} collective-permute-done((f32[352,256]{1,0:T(8,128)S(1)}, f32[352,256]{1,0:T(8,128)S(1)}, u32[]{:S(2)}, u32[]{:S(2)}) %collective-permute-start.15) | collective-permute-done | bytes 360480 | tf_op jit(solution)/shard_map/ppermute | solution.py:460
  119.4 5.4 %collective-permute-done.16 = f32[352,256]{1,0:T(8,128)S(1)} collective-permute-done((f32[352,256]{1,0:T(8,128)S(1)}, f32[352,256]{1,0:T(8,128)S(1)}, u32[]{:S(2)}, u32[]{:S(2)}) %collective-permute-start.16) | collective-permute-done | bytes 360480 | tf_op jit(solution)/shard_map/ppermute | solution.py:460
  125.5 2.1 all-gather.5.cloned.1.call-done.x_ref
  127.6 17.0 %ffn_tokens.1 = (bf16[2048,1024]{1,0:T(8,128)(2,1)}, bf16[2048,1024]{1,0:T(8,128)(2,1)S(1)}, bf16[2048,352]{1,0:T(8,128)(2,1)S(1)}, bf16[2048,352]{1,0:T(8,128)(2,1)S(1)}, bf16[2048,352]{1,0:T(8,128)(2,1)S(1)}) custom-call(bf16[2048,1024]{1,0:T(8,128)(2,1)} %all-gather.5.cloned.1.call-done.x_ref, bf16[2048,1024]{1,0:T(8,128)(2,1)} %all-gather.7.cloned.1.call-done.g_ref, ...), custom_call_target="tpu_custom_call" | custom-call | flops 23000000512 | bytes 1048576 | tf_op jit(solution)/shard_map/ffn_tokens/pallas_call | solution.py:280
  144.6 2.0 copy-done
  150.1 10.8 %reduce-scatter.5.cloned.1.call-start = ((), (), s32[]{:S(2)}) async-start(), calls=%async_computation.5 | async-start | bytes 3604480 | tf_op jit(solution)/shard_map/reduce_scatter | solution.py:468
  161.0 3.2 dynamic-slice_bitcast_fusion
  164.4 2.2 copy-done.5
  166.7 1.4 copy-done.10
  168.1 1.4 copy-done.12
  169.5 8.5 %ffn_grads.1 = bf16[1408,1024]{1,0:T(8,128)(2,1)} custom-call(bf16[2048,352]{1,0:T(8,128)(2,1)S(1)} %copy-done.8, bf16[2048,352]{1,0:T(8,128)(2,1)S(1)} %copy-done.10, bf16[2048,352]{1,0:T(8,128)(2,1)S(1)} %copy-done.12, bf16[2048,1024]{1,0:T(8,128)(2,1)S(1)} %copy-done.5, bf16[2048,1024]{1,0:T(8,128)(2,1)} %all-gather.7.cloned.1.call-done.g_ref), custom_call_target="tpu_custom_call" | custom-call | flops 11500000256 | bytes 1048576 | tf_op jit(solution)/shard_map/ffn_grads/pallas_call | solution.py:300
  178.1 3.2 convert_add_fusion
  183.6 15.4 %reduce-scatter.3.cloned.1.call-done = bf16[256,1024]{1,0:T(8,128)(2,1)} async-done(((bf16[2048,1024]{1,0:T(8,128)(2,1)}), bf16[256,1024]{1,0:T(8,128)(2,1)}) %reduce-scatter.3.cloned.1.call-update) | async-done | bytes 524304 | tf_op jit(solution)/shard_map/reduce_scatter | solution.py:463
  211.3 1.5 collective-permute-start.23
  214.1 25.9 %attn_bwd.1 = (f32[256,480]{1,0:T(8,128)S(1)}, f32[1024,320]{1,0:T(8,128)S(1)}) custom-call(s32[1]{0:T(128)} %bitcast.base_ref, bf16[256,1024]{1,0:T(8,128)(2,1)S(1)} %copy-done.18, bf16[1024,1024]{1,0:T(8,128)(2,1)S(1)} %copy-done.14, bf16[1024,1024]{1,0:T(8,128)(2,1)S(1)} %copy-done.16, bf16[256,1024]{1,0:T(8,128)(2,1)S(1)} %convolution_convert_fusion.do_ref, ...), custom_call_target="tpu_custom_call" | custom-call | flops 29899999232 | bytes 1048576 | tf_op jit(solution)/shard_map/attn_bwd/pallas_call | solution.py:134
  240.0 12.7 %reduce-scatter.5.cloned.1.call-done = bf16[352,1024]{1,0:T(8,128)(2,1)} async-done(((bf16[1408,1024]{1,0:T(8,128)(2,1)}), bf16[352,1024]{1,0:T(8,128)(2,1)}) %reduce-scatter.5.cloned.1.call-update) | async-done | bytes 720912 | tf_op jit(solution)/shard_map/reduce_scatter | solution.py:468
  254.2 1.6 collective-permute-start.25
  255.8 2.4 collective-permute-start.26
  258.7 1.5 collective-permute-start.31
  260.8 1.5 collective-permute-start.33
  266.9 4.8 collective-permute-start.30
  277.8 2.2 gram_upper.1
  280.0 1.5 copy-done.1
  281.7 2.0 bitcast_add_fusion.1
  284.3 3.0 collective-permute-start.37
  288.6 3.3 collective-permute-done.35
  291.9 2.4 collective-permute-done.36
  295.3 3.7 collective-permute-start.41
  299.8 2.8 collective-permute-start.39
  303.7 3.0 collective-permute-start.42
  306.7 2.0 collective-permute-start.43
  311.7 7.5 %collective-permute-done.42 = f32[352,256]{1,0:T(8,128)} collective-permute-done((f32[352,256]{1,0:T(8,128)}, f32[352,256]{1,0:T(8,128)}, u32[]{:S(2)}, u32[]{:S(2)}) %collective-permute-start.42) | collective-permute-done | bytes 360480 | tf_op jit(solution)/shard_map/ppermute | solution.py:530
  323.0 31.8 %all-reduce.5.cloned.1.call-done.g_ref = f32[256,2560]{1,0:T(8,128)} async-done(((f32[256,2560]{1,0:T(8,128)}), f32[256,2560]{1,0:T(8,128)}) %all-reduce.5.cloned.1.call-update) | async-done | bytes 2621456 | tf_op jit(solution)/shard_map/psum | solution.py:499
  354.8 1.7 copy-done.6
  356.5 68.1 %ns_gram.1 = f32[352,1024]{1,0:T(8,128)S(1)} custom-call(f32[256,2560]{1,0:T(8,128)S(1)} %copy-done.6, f32[352,1024]{1,0:T(8,128)S(1)} %pad_select_fusion.y_ref), custom_call_target="tpu_custom_call" | custom-call | flops 81649999872 | bytes 1048576 | tf_op jit(solution)/shard_map/ns_gram/pallas_call | solution.py:198
  428.7 1.5 collective-permute-start.44
  431.4 2.1 dynamic-slice_bitcast_fusion.3
  433.5 1.4 collective-permute-done.45
  435.9 2.6 collective-permute-start.48
  438.5 5.9 %collective-permute-start.49 = (f32[352,256]{1,0:T(8,128)}, f32[352,256]{1,0:T(8,128)}, u32[]{:S(2)}, u32[]{:S(2)}) collective-permute-start(f32[352,256]{1,0:T(8,128)} %get-tuple-element.106), channel_id=1, source_target_pairs={{0,16},{8,24},{16,0},{1,17},{9,25},{17,1},{2,18},{10,26},{18,2},{3... | collective-permute-start | bytes 1081352 | tf_op jit(solution)/shard_map/ppermute | solution.py:530
  444.5 2.1 collective-permute-start.50
  447.3 2.0 copy-done.4
  449.3 18.7 %ns_factor.1 = f32[832,256]{1,0:T(8,128)S(1)} custom-call(f32[4,832,256]{2,1,0:T(8,128)S(1)} %bitcast.194, f32[832,256]{1,0:T(8,128)S(1)} %dynamic-slice_bitcast_fusion.2.own_ref), custom_call_target="tpu_custom_call" | custom-call | flops 25300000768 | bytes 1048576 | tf_op jit(solution)/shard_map/ns_factor/pallas_call | solution.py:260
  474.2 2.7 add_convert_fusion
  476.9 2.5 fusion.13
  (311 shorter events, 81.9 us)
Async XLA Ops:
  7.2 118.3 %all-gather.7.cloned.1.call-start = ((), (), s32[]{:S(2)}) async-start(), calls=%async_computation.3 | async-start | bytes 4718592 | tf_op jit(solution)/shard_map/all_gather | solution.py:443
  11.8 115.8 %all-gather.5.cloned.1.call-start = ((), (), s32[]{:S(2)}) async-start(), calls=%async_computation.2 | async-start | bytes 4718592 | tf_op jit(solution)/shard_map/all_gather | solution.py:461
  12.1 8.0 %collective-permute-start = (bf16[320,256]{1,0:T(8,128)(2,1)S(1)}, bf16[320,256]{1,0:T(8,128)(2,1)S(1)}, u32[]{:S(2)}, u32[]{:S(2)}) collective-permute-start(bf16[320,256]{1,0:T(8,128)(2,1)S(1)} %get-tuple-element.127), channel_id=1, source_target_pairs={{0,8},{8,0},{16,24},{24,16},{1,9},{9,1},{17,25},{25,17},{2,10},{10... | collective-permute-start | bytes 491528 | tf_op jit(solution)/shard_map/ppermute | solution.py:341
  15.1 9.2 %collective-permute-start.1 = (bf16[320,256]{1,0:T(8,128)(2,1)S(1)}, bf16[320,256]{1,0:T(8,128)(2,1)S(1)}, u32[]{:S(2)}, u32[]{:S(2)}) collective-permute-start(bf16[320,256]{1,0:T(8,128)(2,1)S(1)} %get-tuple-element.127), channel_id=1, source_target_pairs={{0,16},{8,24},{16,0},{24,8},{1,17},{9,25},{17,1},{25,9},{2,18},{10... | collective-permute-start | bytes 491528 | tf_op jit(solution)/shard_map/ppermute | solution.py:341
  16.6 7.7 %collective-permute-start.2 = (bf16[320,256]{1,0:T(8,128)(2,1)S(1)}, bf16[320,256]{1,0:T(8,128)(2,1)S(1)}, u32[]{:S(2)}, u32[]{:S(2)}) collective-permute-start(bf16[320,256]{1,0:T(8,128)(2,1)S(1)} %get-tuple-element.127), channel_id=1, source_target_pairs={{0,24},{8,16},{16,8},{24,0},{1,25},{9,17},{17,9},{25,1},{2,26},{10... | collective-permute-start | bytes 491528 | tf_op jit(solution)/shard_map/ppermute | solution.py:341
  24.4 9.0 %collective-permute-start.3 = (bf16[480,256]{1,0:T(8,128)(2,1)S(1)}, bf16[480,256]{1,0:T(8,128)(2,1)S(1)}, u32[]{:S(2)}, u32[]{:S(2)}) collective-permute-start(bf16[480,256]{1,0:T(8,128)(2,1)S(1)} %pad_maximum_fusion.5), channel_id=1, source_target_pairs={{0,8},{8,0},{16,24},{24,16},{1,9},{9,1},{17,25},{25,17},{2,10},{10... | collective-permute-start | bytes 737288 | tf_op jit(solution)/shard_map/ppermute | solution.py:341
  25.6 9.2 %collective-permute-start.4 = (bf16[480,256]{1,0:T(8,128)(2,1)S(1)}, bf16[480,256]{1,0:T(8,128)(2,1)S(1)}, u32[]{:S(2)}, u32[]{:S(2)}) collective-permute-start(bf16[480,256]{1,0:T(8,128)(2,1)S(1)} %pad_maximum_fusion.5), channel_id=1, source_target_pairs={{0,16},{8,24},{16,0},{24,8},{1,17},{9,25},{17,1},{25,9},{2,18},{10... | collective-permute-start | bytes 737288 | tf_op jit(solution)/shard_map/ppermute | solution.py:341
  27.1 21.5 %collective-permute-start.6 = (f32[256,320]{1,0:T(8,128)S(1)}, f32[256,320]{1,0:T(8,128)S(1)}, u32[]{:S(2)}, u32[]{:S(2)}) collective-permute-start(f32[256,320]{1,0:T(8,128)S(1)} %get-tuple-element.132), channel_id=1, source_target_pairs={{0,8},{8,0},{16,24},{24,16},{1,9},{9,1},{17,25},{25,17},{2,10},{10... | collective-permute-start | bytes 983048 | tf_op jit(solution)/shard_map/ppermute | solution.py:341
  28.6 25.6 %collective-permute-start.7 = (f32[256,320]{1,0:T(8,128)S(1)}, f32[256,320]{1,0:T(8,128)S(1)}, u32[]{:S(2)}, u32[]{:S(2)}) collective-permute-start(f32[256,320]{1,0:T(8,128)S(1)} %get-tuple-element.132), channel_id=1, source_target_pairs={{0,16},{8,24},{16,0},{24,8},{1,17},{9,25},{17,1},{25,9},{2,18},{10... | collective-permute-start | bytes 983048 | tf_op jit(solution)/shard_map/ppermute | solution.py:341
  29.1 18.9 %collective-permute-start.5 = (bf16[480,256]{1,0:T(8,128)(2,1)S(1)}, bf16[480,256]{1,0:T(8,128)(2,1)S(1)}, u32[]{:S(2)}, u32[]{:S(2)}) collective-permute-start(bf16[480,256]{1,0:T(8,128)(2,1)S(1)} %pad_maximum_fusion.5), channel_id=1, source_target_pairs={{0,24},{8,16},{16,8},{24,0},{1,25},{9,17},{17,9},{25,1},{2,26},{10... | collective-permute-start | bytes 737288 | tf_op jit(solution)/shard_map/ppermute | solution.py:341
  33.3 21.0 %collective-permute-start.8 = (f32[256,320]{1,0:T(8,128)S(1)}, f32[256,320]{1,0:T(8,128)S(1)}, u32[]{:S(2)}, u32[]{:S(2)}) collective-permute-start(f32[256,320]{1,0:T(8,128)S(1)} %get-tuple-element.132), channel_id=1, source_target_pairs={{0,24},{8,16},{16,8},{24,0},{1,25},{9,17},{17,9},{25,1},{2,26},{10... | collective-permute-start | bytes 983048 | tf_op jit(solution)/shard_map/ppermute | solution.py:341
  54.4 19.5 %copy-start.2 = (f32[1024,320]{1,0:T(8,128)}, f32[1024,320]{1,0:T(8,128)S(1)}, u32[]{:S(2)}) copy-start(f32[1024,320]{1,0:T(8,128)S(1)} %constant_dynamic-update-slice_fusion.15.fk_ref) | copy-start | bytes 3932164
  54.4 20.7 %collective-permute-start.9 = (bf16[256,1024]{1,0:T(8,128)(2,1)S(1)}, bf16[256,1024]{1,0:T(8,128)(2,1)S(1)}, u32[]{:S(2)}, u32[]{:S(2)}) collective-permute-start(bf16[256,1024]{1,0:T(8,128)(2,1)S(1)} %copy-done.46), channel_id=1, source_target_pairs={{0,8},{8,0},{16,24},{24,16},{1,9},{9,1},{17,25},{25,17},{2,10},{10... | collective-permute-start | bytes 1572872 | tf_op jit(solution)/shard_map/ppermute | solution.py:341
  55.1 22.3 %collective-permute-start.10 = (bf16[256,1024]{1,0:T(8,128)(2,1)S(1)}, bf16[256,1024]{1,0:T(8,128)(2,1)S(1)}, u32[]{:S(2)}, u32[]{:S(2)}) collective-permute-start(bf16[256,1024]{1,0:T(8,128)(2,1)S(1)} %copy-done.46), channel_id=1, source_target_pairs={{0,16},{8,24},{16,0},{24,8},{1,17},{9,25},{17,1},{25,9},{2,18},{10... | collective-permute-start | bytes 1572872 | tf_op jit(solution)/shard_map/ppermute | solution.py:341
  56.6 20.8 %collective-permute-start.11 = (bf16[256,1024]{1,0:T(8,128)(2,1)S(1)}, bf16[256,1024]{1,0:T(8,128)(2,1)S(1)}, u32[]{:S(2)}, u32[]{:S(2)}) collective-permute-start(bf16[256,1024]{1,0:T(8,128)(2,1)S(1)} %copy-done.46), channel_id=1, source_target_pairs={{0,24},{8,16},{16,8},{24,0},{1,25},{9,17},{17,9},{25,1},{2,26},{10... | collective-permute-start | bytes 1572872 | tf_op jit(solution)/shard_map/ppermute | solution.py:341
  79.8 119.2 %reduce-scatter.3.cloned.1.call-start = ((), (), s32[]{:S(2)}) async-start(), calls=%async_computation.4 | async-start | bytes 4718592 | tf_op jit(solution)/shard_map/reduce_scatter | solution.py:463
  81.5 15.5 %collective-permute-start.12 = (bf16[3,352,256]{2,1,0:T(8,128)(2,1)}, bf16[3,352,256]{2,1,0:T(8,128)(2,1)}, u32[]{:S(2)}, u32[]{:S(2)}) collective-permute-start(bf16[3,352,256]{2,1,0:T(8,128)(2,1)} %pad_maximum_fusion.3), channel_id=1, source_target_pairs={{0,8},{8,0},{16,24},{24,16},{1,9},{9,1},{17,25},{25,17},{2,10},{10... | collective-permute-start | bytes 1622024 | tf_op jit(solution)/shard_map/ppermute | solution.py:341
  83.2 22.4 %collective-permute-start.13 = (bf16[3,352,256]{2,1,0:T(8,128)(2,1)}, bf16[3,352,256]{2,1,0:T(8,128)(2,1)}, u32[]{:S(2)}, u32[]{:S(2)}) collective-permute-start(bf16[3,352,256]{2,1,0:T(8,128)(2,1)} %pad_maximum_fusion.3), channel_id=1, source_target_pairs={{0,16},{8,24},{16,0},{24,8},{1,17},{9,25},{17,1},{25,9},{2,18},{10... | collective-permute-start | bytes 1622024 | tf_op jit(solution)/shard_map/ppermute | solution.py:341
  83.7 22.9 %collective-permute-start.14 = (bf16[3,352,256]{2,1,0:T(8,128)(2,1)}, bf16[3,352,256]{2,1,0:T(8,128)(2,1)}, u32[]{:S(2)}, u32[]{:S(2)}) collective-permute-start(bf16[3,352,256]{2,1,0:T(8,128)(2,1)} %pad_maximum_fusion.3), channel_id=1, source_target_pairs={{0,24},{8,16},{16,8},{24,0},{1,25},{9,17},{17,9},{25,1},{2,26},{10... | collective-permute-start | bytes 1622024 | tf_op jit(solution)/shard_map/ppermute | solution.py:341
  85.2 22.6 %copy-start.32 = (f32[3,352,256]{2,1,0:T(8,128)}, f32[3,352,256]{2,1,0:T(8,128)S(1)}, u32[]{:S(2)}) copy-start(f32[3,352,256]{2,1,0:T(8,128)S(1)} %pad_maximum_fusion.1) | copy-start | bytes 3244036
  107.9 11.5 %collective-permute-start.15 = (f32[352,256]{1,0:T(8,128)S(1)}, f32[352,256]{1,0:T(8,128)S(1)}, u32[]{:S(2)}, u32[]{:S(2)}) collective-permute-start(f32[352,256]{1,0:T(8,128)S(1)} %get-tuple-element.116), channel_id=1, source_target_pairs={{0,8},{8,0},{24,16},{1,9},{9,1},{25,17},{2,10},{10,2},{26,18},{3,1... | collective-permute-start | bytes 1081352 | tf_op jit(solution)/shard_map/ppermute | solution.py:460
  110.3 14.5 %collective-permute-start.16 = (f32[352,256]{1,0:T(8,128)S(1)}, f32[352,256]{1,0:T(8,128)S(1)}, u32[]{:S(2)}, u32[]{:S(2)}) collective-permute-start(f32[352,256]{1,0:T(8,128)S(1)} %get-tuple-element.115), channel_id=1, source_target_pairs={{0,16},{16,0},{24,8},{1,17},{17,1},{25,9},{2,18},{18,2},{26,10},{3... | collective-permute-start | bytes 1081352 | tf_op jit(solution)/shard_map/ppermute | solution.py:460
  112.2 13.3 %collective-permute-start.17 = (f32[352,256]{1,0:T(8,128)S(1)}, f32[352,256]{1,0:T(8,128)}, u32[]{:S(2)}, u32[]{:S(2)}) collective-permute-start(f32[352,256]{1,0:T(8,128)S(1)} %get-tuple-element.114), channel_id=1, source_target_pairs={{8,16},{16,8},{24,0},{9,17},{17,9},{25,1},{10,18},{18,10},{26,2},{... | collective-permute-start | bytes 1081352 | tf_op jit(solution)/shard_map/ppermute | solution.py:460
  150.1 102.7 %reduce-scatter.5.cloned.1.call-start = ((), (), s32[]{:S(2)}) async-start(), calls=%async_computation.5 | async-start | bytes 3604480 | tf_op jit(solution)/shard_map/reduce_scatter | solution.py:468
  164.2 13.9 %collective-permute-start.18 = (bf16[4,256,1024]{2,1,0:T(8,128)(2,1)}, bf16[4,256,1024]{2,1,0:T(8,128)(2,1)}, u32[]{:S(2)}, u32[]{:S(2)}) collective-permute-start(bf16[4,256,1024]{2,1,0:T(8,128)(2,1)} %dynamic-slice_bitcast_fusion), channel_id=1, source_target_pairs={{0,1},{1,0},{2,3},{3,2},{4,5},{5,4},{6,7},{7,6},{8,9},{9,8},{10,11... | collective-permute-start | bytes 6291464 | tf_op jit(solution)/shard_map/ppermute | solution.py:364
  178.0 176.7 %all-reduce.5.cloned.1.call-start = ((), (), s32[]{:S(2)}) async-start(), calls=%async_computation.6 | async-start | bytes 5242880 | tf_op jit(solution)/shard_map/psum | solution.py:499
  182.5 17.7 %copy-start.20 = (f32[256,1024]{1,0:T(8,128)S(1)}, f32[256,1024]{1,0:T(8,128)}, u32[]{:S(2)}) copy-start(f32[256,1024]{1,0:T(8,128)} %copy-done.19) | copy-start | bytes 3145732
  202.6 6.6 %collective-permute-start.21 = (bf16[4,4,32,1024]{3,2,1,0:T(8,128)(2,1)S(1)}, bf16[4,4,32,1024]{3,2,1,0:T(8,128)(2,1)S(1)}, u32[]{:S(2)}, u32[]{:S(2)}) collective-permute-start(bf16[4,4,32,1024]{3,2,1,0:T(8,128)(2,1)S(1)} %fusion.11), channel_id=1, source_target_pairs={{0,1},{1,0},{2,3},{3,2},{4,5},{5,4},{6,7},{7,6},{8,9},{9,8},{10,11... | collective-permute-start | bytes 3145736 | tf_op jit(solution)/shard_map/ppermute | solution.py:364
  207.1 45.7 %collective-permute-start.20 = (bf16[256,1024]{1,0:T(8,128)(2,1)}, bf16[256,1024]{1,0:T(8,128)(2,1)}, u32[]{:S(2)}, u32[]{:S(2)}) collective-permute-start(bf16[256,1024]{1,0:T(8,128)(2,1)} %get-tuple-element.60), channel_id=1, source_target_pairs={{0,4},{1,5},{2,6},{3,7},{4,0},{5,1},{6,2},{7,3},{8,12},{9,13},{10,... | collective-permute-start | bytes 1572872 | tf_op jit(solution)/shard_map/ppermute | solution.py:368
  207.2 45.6 %collective-permute-start.19 = (bf16[256,1024]{1,0:T(8,128)(2,1)}, bf16[256,1024]{1,0:T(8,128)(2,1)}, u32[]{:S(2)}, u32[]{:S(2)}) collective-permute-start(bf16[256,1024]{1,0:T(8,128)(2,1)} %get-tuple-element.59), channel_id=1, source_target_pairs={{0,2},{1,3},{2,0},{3,1},{4,6},{5,7},{6,4},{7,5},{8,10},{9,11},{10,... | collective-permute-start | bytes 1572872 | tf_op jit(solution)/shard_map/ppermute | solution.py:368
  210.6 42.2 %collective-permute-start.22 = (bf16[128,1024]{1,0:T(8,128)(2,1)}, bf16[128,1024]{1,0:T(8,128)(2,1)}, u32[]{:S(2)}, u32[]{:S(2)}) collective-permute-start(bf16[128,1024]{1,0:T(8,128)(2,1)} %get-tuple-element.91), channel_id=1, source_target_pairs={{0,8},{8,0},{16,24},{24,16},{1,9},{9,1},{17,25},{25,17},{2,10},{10... | collective-permute-start | bytes 786440 | tf_op jit(solution)/shard_map/ppermute | solution.py:355
  211.3 41.5 %collective-permute-start.23 = (bf16[128,1024]{1,0:T(8,128)(2,1)}, bf16[128,1024]{1,0:T(8,128)(2,1)}, u32[]{:S(2)}, u32[]{:S(2)}) collective-permute-start(bf16[128,1024]{1,0:T(8,128)(2,1)} %get-tuple-element.93), channel_id=1, source_target_pairs={{0,16},{8,24},{16,0},{24,8},{1,17},{9,25},{17,1},{25,9},{2,18},{10... | collective-permute-start | bytes 786440 | tf_op jit(solution)/shard_map/ppermute | solution.py:355
  212.7 40.1 %collective-permute-start.24 = (bf16[128,1024]{1,0:T(8,128)(2,1)}, bf16[128,1024]{1,0:T(8,128)(2,1)}, u32[]{:S(2)}, u32[]{:S(2)}) collective-permute-start(bf16[128,1024]{1,0:T(8,128)(2,1)} %get-tuple-element.92), channel_id=1, source_target_pairs={{0,24},{8,16},{16,8},{24,0},{1,25},{9,17},{17,9},{25,1},{2,26},{10... | collective-permute-start | bytes 786440 | tf_op jit(solution)/shard_map/ppermute | solution.py:355
  254.2 6.6 %collective-permute-start.25 = (bf16[32,1024]{1,0:T(8,128)(2,1)S(1)}, bf16[32,1024]{1,0:T(8,128)(2,1)S(1)}, u32[]{:S(2)}, u32[]{:S(2)}) collective-permute-start(bf16[32,1024]{1,0:T(8,128)(2,1)S(1)} %get-tuple-element.119), channel_id=1, source_target_pairs={{0,2},{1,3},{2,0},{3,1},{4,6},{5,7},{6,4},{7,5},{8,10},{9,11},{10,... | collective-permute-start | bytes 196616 | tf_op jit(solution)/shard_map/ppermute | solution.py:368
  255.8 7.3 %collective-permute-start.26 = (bf16[32,1024]{1,0:T(8,128)(2,1)S(1)}, bf16[32,1024]{1,0:T(8,128)(2,1)S(1)}, u32[]{:S(2)}, u32[]{:S(2)}) collective-permute-start(bf16[32,1024]{1,0:T(8,128)(2,1)S(1)} %get-tuple-element.121), channel_id=1, source_target_pairs={{0,4},{1,5},{2,6},{3,7},{4,0},{5,1},{6,2},{7,3},{8,12},{9,13},{10,... | collective-permute-start | bytes 196616 | tf_op jit(solution)/shard_map/ppermute | solution.py:368
  258.2 6.2 %collective-permute-start.27 = (bf16[32,1024]{1,0:T(8,128)(2,1)S(1)}, bf16[32,1024]{1,0:T(8,128)(2,1)S(1)}, u32[]{:S(2)}, u32[]{:S(2)}) collective-permute-start(bf16[32,1024]{1,0:T(8,128)(2,1)S(1)} %get-tuple-element.120), channel_id=1, source_target_pairs={{0,6},{1,7},{2,4},{3,5},{4,2},{5,3},{6,0},{7,1},{8,14},{9,15},{10,... | collective-permute-start | bytes 196616 | tf_op jit(solution)/shard_map/ppermute | solution.py:368
  258.7 13.2 %copy-start.31 = (bf16[320,1024]{1,0:T(8,128)(2,1)S(1)}, bf16[320,1024]{1,0:T(8,128)(2,1)}, u32[]{:S(2)}) copy-start(bf16[320,1024]{1,0:T(8,128)(2,1)} %copy-done.30) | copy-start | bytes 1966084
  258.7 8.1 %collective-permute-start.31 = (bf16[256,320]{1,0:T(8,128)(2,1)S(1)}, bf16[256,320]{1,0:T(8,128)(2,1)S(1)}, u32[]{:S(2)}, u32[]{:S(2)}) collective-permute-start(bf16[256,320]{1,0:T(8,128)(2,1)S(1)} %get-tuple-element.97), channel_id=1, source_target_pairs={{0,8},{8,0},{16,24},{24,16},{1,9},{9,1},{17,25},{25,17},{2,10},{10... | collective-permute-start | bytes 491528 | tf_op jit(solution)/shard_map/ppermute | solution.py:355
  260.2 11.5 %collective-permute-start.32 = (bf16[256,320]{1,0:T(8,128)(2,1)S(1)}, bf16[256,320]{1,0:T(8,128)(2,1)S(1)}, u32[]{:S(2)}, u32[]{:S(2)}) collective-permute-start(bf16[256,320]{1,0:T(8,128)(2,1)S(1)} %get-tuple-element.99), channel_id=1, source_target_pairs={{0,16},{8,24},{16,0},{24,8},{1,17},{9,25},{17,1},{25,9},{2,18},{10... | collective-permute-start | bytes 491528 | tf_op jit(solution)/shard_map/ppermute | solution.py:355
  260.8 10.9 %collective-permute-start.33 = (bf16[256,320]{1,0:T(8,128)(2,1)S(1)}, bf16[256,320]{1,0:T(8,128)(2,1)S(1)}, u32[]{:S(2)}, u32[]{:S(2)}) collective-permute-start(bf16[256,320]{1,0:T(8,128)(2,1)S(1)} %get-tuple-element.98), channel_id=1, source_target_pairs={{0,24},{8,16},{16,8},{24,0},{1,25},{9,17},{17,9},{25,1},{2,26},{10... | collective-permute-start | bytes 491528 | tf_op jit(solution)/shard_map/ppermute | solution.py:355
  265.4 10.1 %collective-permute-start.28 = (f32[32,1024]{1,0:T(8,128)S(1)}, f32[32,1024]{1,0:T(8,128)S(1)}, u32[]{:S(2)}, u32[]{:S(2)}) collective-permute-start(f32[32,1024]{1,0:T(8,128)S(1)} %get-tuple-element.87), channel_id=1, source_target_pairs={{16,24},{17,25},{18,26},{19,27},{20,28},{21,29},{22,30},{23,31}} | collective-permute-start | bytes 393224 | tf_op jit(solution)/shard_map/ppermute | solution.py:495
  266.2 9.3 %collective-permute-start.29 = (f32[32,1024]{1,0:T(8,128)S(1)}, f32[32,1024]{1,0:T(8,128)S(1)}, u32[]{:S(2)}, u32[]{:S(2)}) collective-permute-start(f32[32,1024]{1,0:T(8,128)S(1)} %get-tuple-element.87), channel_id=1, source_target_pairs={{8,24},{9,25},{10,26},{11,27},{12,28},{13,29},{14,30},{15,31}} | collective-permute-start | bytes 393224 | tf_op jit(solution)/shard_map/ppermute | solution.py:495
  266.9 8.6 %collective-permute-start.30 = (f32[32,1024]{1,0:T(8,128)S(1)}, f32[32,1024]{1,0:T(8,128)S(1)}, u32[]{:S(2)}, u32[]{:S(2)}) collective-permute-start(f32[32,1024]{1,0:T(8,128)S(1)} %get-tuple-element.87), channel_id=1, source_target_pairs={{0,24},{1,25},{2,26},{3,27},{4,28},{5,29},{6,30},{7,31}} | collective-permute-start | bytes 393224 | tf_op jit(solution)/shard_map/ppermute | solution.py:495
  275.4 6.2 %collective-permute-start.34 = (bf16[4,104,1024]{2,1,0:T(8,128)(2,1)}, bf16[4,104,1024]{2,1,0:T(8,128)(2,1)}, u32[]{:S(2)}, u32[]{:S(2)}) collective-permute-start(bf16[4,104,1024]{2,1,0:T(8,128)(2,1)} %fusion.15), channel_id=1, source_target_pairs={{0,1},{1,0},{2,3},{3,2},{4,5},{5,4},{6,7},{7,6},{8,9},{9,8},{10,11... | collective-permute-start | bytes 2555912 | tf_op jit(solution)/shard_map/ppermute | solution.py:364
  281.6 143.1 %all-gather.9.cloned.1.call-start = ((), (), s32[]{:S(2)}) async-start(), calls=%async_computation.7 | async-start | bytes 3514368 | tf_op jit(solution)/shard_map/all_gather | solution.py:524
  283.7 8.1 %collective-permute-start.35 = (bf16[416,256]{1,0:T(8,128)(2,1)S(1)}, bf16[416,256]{1,0:T(8,128)(2,1)S(1)}, u32[]{:S(2)}, u32[]{:S(2)}) collective-permute-start(bf16[416,256]{1,0:T(8,128)(2,1)S(1)} %get-tuple-element.94), channel_id=1, source_target_pairs={{0,8},{8,0},{16,24},{24,16},{1,9},{9,1},{17,25},{25,17},{2,10},{10... | collective-permute-start | bytes 638984 | tf_op jit(solution)/shard_map/ppermute | solution.py:355
  283.8 10.4 %collective-permute-start.36 = (bf16[416,256]{1,0:T(8,128)(2,1)S(1)}, bf16[416,256]{1,0:T(8,128)(2,1)S(1)}, u32[]{:S(2)}, u32[]{:S(2)}) collective-permute-start(bf16[416,256]{1,0:T(8,128)(2,1)S(1)} %get-tuple-element.96), channel_id=1, source_target_pairs={{0,16},{8,24},{16,0},{24,8},{1,17},{9,25},{17,1},{25,9},{2,18},{10... | collective-permute-start | bytes 638984 | tf_op jit(solution)/shard_map/ppermute | solution.py:355
  284.3 9.9 %collective-permute-start.37 = (bf16[416,256]{1,0:T(8,128)(2,1)S(1)}, bf16[416,256]{1,0:T(8,128)(2,1)S(1)}, u32[]{:S(2)}, u32[]{:S(2)}) collective-permute-start(bf16[416,256]{1,0:T(8,128)(2,1)S(1)} %get-tuple-element.95), channel_id=1, source_target_pairs={{0,24},{8,16},{16,8},{24,0},{1,25},{9,17},{17,9},{25,1},{2,26},{10... | collective-permute-start | bytes 638984 | tf_op jit(solution)/shard_map/ppermute | solution.py:355
  295.3 14.6 %copy-start.42 = (f32[800,256]{1,0:T(8,128)S(1)}, f32[800,256]{1,0:T(8,128)}, u32[]{:S(2)}) copy-start(f32[800,256]{1,0:T(8,128)} %multiply_bitcast_fusion) | copy-start | bytes 2457604
  295.3 15.3 %collective-permute-start.41 = (f32[352,256]{1,0:T(8,128)}, f32[352,256]{1,0:T(8,128)}, u32[]{:S(2)}, u32[]{:S(2)}) collective-permute-start(f32[352,256]{1,0:T(8,128)} %get-tuple-element.113), channel_id=1, source_target_pairs={{0,8},{8,0},{16,24},{1,9},{9,1},{17,25},{2,10},{10,2},{18,26},{3,1... | collective-permute-start | bytes 1081352 | tf_op jit(solution)/shard_map/ppermute | solution.py:530
  299.1 7.6 %collective-permute-start.38 = (bf16[104,256]{1,0:T(8,128)(2,1)S(1)}, bf16[104,256]{1,0:T(8,128)(2,1)S(1)}, u32[]{:S(2)}, u32[]{:S(2)}) collective-permute-start(bf16[104,256]{1,0:T(8,128)(2,1)S(1)} %get-tuple-element.122), channel_id=1, source_target_pairs={{0,2},{1,3},{2,0},{3,1},{4,6},{5,7},{6,4},{7,5},{8,10},{9,11},{10,... | collective-permute-start | bytes 159752 | tf_op jit(solution)/shard_map/ppermute | solution.py:368
  299.8 8.9 %collective-permute-start.39 = (bf16[104,256]{1,0:T(8,128)(2,1)S(1)}, bf16[104,256]{1,0:T(8,128)(2,1)S(1)}, u32[]{:S(2)}, u32[]{:S(2)}) collective-permute-start(bf16[104,256]{1,0:T(8,128)(2,1)S(1)} %get-tuple-element.124), channel_id=1, source_target_pairs={{0,4},{1,5},{2,6},{3,7},{4,0},{5,1},{6,2},{7,3},{8,12},{9,13},{10,... | collective-permute-start | bytes 159752 | tf_op jit(solution)/shard_map/ppermute | solution.py:368
  302.6 7.2 %collective-permute-start.40 = (bf16[104,256]{1,0:T(8,128)(2,1)S(1)}, bf16[104,256]{1,0:T(8,128)(2,1)S(1)}, u32[]{:S(2)}, u32[]{:S(2)}) collective-permute-start(bf16[104,256]{1,0:T(8,128)(2,1)S(1)} %get-tuple-element.123), channel_id=1, source_target_pairs={{0,6},{1,7},{2,4},{3,5},{4,2},{5,3},{6,0},{7,1},{8,14},{9,15},{10,... | collective-permute-start | bytes 159752 | tf_op jit(solution)/shard_map/ppermute | solution.py:368
  303.7 15.5 %collective-permute-start.42 = (f32[352,256]{1,0:T(8,128)}, f32[352,256]{1,0:T(8,128)}, u32[]{:S(2)}, u32[]{:S(2)}) collective-permute-start(f32[352,256]{1,0:T(8,128)} %get-tuple-element.112), channel_id=1, source_target_pairs={{0,16},{8,24},{16,0},{1,17},{9,25},{17,1},{2,18},{10,26},{18,2},{3... | collective-permute-start | bytes 1081352 | tf_op jit(solution)/shard_map/ppermute | solution.py:530
  306.7 13.5 %collective-permute-start.43 = (f32[352,256]{1,0:T(8,128)S(1)}, f32[352,256]{1,0:T(8,128)}, u32[]{:S(2)}, u32[]{:S(2)}) collective-permute-start(f32[352,256]{1,0:T(8,128)S(1)} %get-tuple-element.111), channel_id=1, source_target_pairs={{0,24},{8,16},{16,8},{1,25},{9,17},{17,9},{2,26},{10,18},{18,10},{... | collective-permute-start | bytes 1081352 | tf_op jit(solution)/shard_map/ppermute | solution.py:530
  310.6 166.3 %all-gather.11.cloned.1.call-start = ((), (), s32[]{:S(2)}) async-start(), calls=%async_computation.8 | async-start | bytes 2359296 | tf_op jit(solution)/shard_map/all_gather | solution.py:544
  426.0 8.9 %collective-permute-start.45 = (f32[32,1024]{1,0:T(8,128)S(1)}, f32[32,1024]{1,0:T(8,128)S(1)}, u32[]{:S(2)}, u32[]{:S(2)}) collective-permute-start(f32[32,1024]{1,0:T(8,128)S(1)} %get-tuple-element.110), channel_id=1, source_target_pairs={{24,0},{25,1},{26,2},{27,3},{28,4},{29,5},{30,6},{31,7}} | collective-permute-start | bytes 393224 | tf_op jit(solution)/shard_map/ppermute | solution.py:541
  427.3 7.6 %collective-permute-start.46 = (f32[32,1024]{1,0:T(8,128)S(1)}, f32[32,1024]{1,0:T(8,128)S(1)}, u32[]{:S(2)}, u32[]{:S(2)}) collective-permute-start(f32[32,1024]{1,0:T(8,128)S(1)} %get-tuple-element.109), channel_id=1, source_target_pairs={{24,8},{25,9},{26,10},{27,11},{28,12},{29,13},{30,14},{31,15}} | collective-permute-start | bytes 393224 | tf_op jit(solution)/shard_map/ppermute | solution.py:541
  428.0 6.9 %collective-permute-start.47 = (f32[32,1024]{1,0:T(8,128)S(1)}, f32[32,1024]{1,0:T(8,128)S(1)}, u32[]{:S(2)}, u32[]{:S(2)}) collective-permute-start(f32[32,1024]{1,0:T(8,128)S(1)} %get-tuple-element.108), channel_id=1, source_target_pairs={{24,16},{25,17},{26,18},{27,19},{28,20},{29,21},{30,22},{31,23}} | collective-permute-start | bytes 393224 | tf_op jit(solution)/shard_map/ppermute | solution.py:541
  428.7 45.6 %collective-permute-start.44 = (bf16[256,1024]{1,0:T(8,128)(2,1)S(1)}, bf16[256,1024]{1,0:T(8,128)(2,1)}, u32[]{:S(2)}, u32[]{:S(2)}) collective-permute-start(bf16[256,1024]{1,0:T(8,128)(2,1)S(1)} %copy-done.53), channel_id=1, source_target_pairs={{0,6},{1,7},{2,4},{3,5},{4,2},{5,3},{6,0},{7,1},{8,14},{9,15},{10,... | collective-permute-start | bytes 1572872 | tf_op jit(solution)/shard_map/ppermute | solution.py:368
  435.9 33.3 %collective-permute-start.48 = (f32[352,256]{1,0:T(8,128)}, f32[352,256]{1,0:T(8,128)}, u32[]{:S(2)}, u32[]{:S(2)}) collective-permute-start(f32[352,256]{1,0:T(8,128)} %get-tuple-element.107), channel_id=1, source_target_pairs={{0,8},{8,0},{16,24},{1,9},{9,1},{17,25},{2,10},{10,2},{18,26},{3,1... | collective-permute-start | bytes 1081352 | tf_op jit(solution)/shard_map/ppermute | solution.py:530
  438.5 31.7 %collective-permute-start.49 = (f32[352,256]{1,0:T(8,128)}, f32[352,256]{1,0:T(8,128)}, u32[]{:S(2)}, u32[]{:S(2)}) collective-permute-start(f32[352,256]{1,0:T(8,128)} %get-tuple-element.106), channel_id=1, source_target_pairs={{0,16},{8,24},{16,0},{1,17},{9,25},{17,1},{2,18},{10,26},{18,2},{3... | collective-permute-start | bytes 1081352 | tf_op jit(solution)/shard_map/ppermute | solution.py:530
  444.5 26.8 %collective-permute-start.50 = (f32[352,256]{1,0:T(8,128)S(1)}, f32[352,256]{1,0:T(8,128)}, u32[]{:S(2)}, u32[]{:S(2)}) collective-permute-start(f32[352,256]{1,0:T(8,128)S(1)} %get-tuple-element.105), channel_id=1, source_target_pairs={{0,24},{8,16},{16,8},{1,25},{9,17},{17,9},{2,26},{10,18},{18,10},{... | collective-permute-start | bytes 1081352 | tf_op jit(solution)/shard_map/ppermute | solution.py:530
  449.3 18.7 %copy-start.41 = (f32[256,800]{0,1:T(8,128)S(1)}, f32[256,800]{0,1:T(8,128)}, u32[]{:S(2)}) copy-start(f32[256,800]{0,1:T(8,128)} %param.20) | copy-start | bytes 2457604
  (55 other events, 170.1 us)
Sparse Core Ops, SparseCore 0:
  11.9 49.8 all-gather.6
  80.0 47.6 all-gather.4
  150.2 48.7 reduce-scatter.2
  201.9 50.8 reduce-scatter.4
  281.7 73.0 all-reduce.4
  358.1 58.8 all-gather.8
  447.5 28.0 all-gather.10

commit v4 on v3

--- a/solution.py
+++ b/solution.py
@@ -277,7 +277,7 @@
 def ffn_tokens(x_all,g_all,w,interpret=False):
     tokens=x_all.shape[0]; rows=256; hid=w.shape[1]
     block=pl.BlockSpec((rows,D),lambda i:(i,0)); part=pl.BlockSpec((rows,hid),lambda i:(i,0))
-    return pl.pallas_call(ffn_body,out_shape=(pltpu.HBM((tokens,D),BF),shape((tokens,D),BF))+(shape((tokens,hid),BF),)*3,
+    return pl.pallas_call(ffn_body,out_shape=(pltpu.HBM((tokens,D),BF),)*2+(pltpu.HBM((tokens,hid),BF),)*3,
         grid=(tokens//rows,),in_specs=[block,block,pl.BlockSpec(w.shape,lambda i:(0,0,0),pipeline_mode=pl.Buffered(1))],
         out_specs=(block,block,part,part,part),
         compiler_params=limit(20),cost_estimate=cost(20),name="ffn_tokens",interpret=interpret)(in_hbm(x_all),in_hbm(g_all),w)
@@ -481,7 +481,7 @@
     grad_out = grad_out.reshape(n_dp, -1, D)
     last, branch = branch[3:], cross_chips([after(part, d_second) for part in branch[:3]])
     grad_out, (d_q, d_kv) = sum_dp(
-        lambda t: pick(grad_out, t), during=functools.partial(backward, (0, HEADS // 2), 26), alongside=(matrix, *branch[1:])
+        lambda t: pick(grad_out, t), during=functools.partial(backward, (0, HEADS // 2), 26), alongside=branch[1:]
     )
     d_q, d_kv = after((d_q, d_kv), grad_out)
     if n_mp == 2 * CHIPS:
@@ -492,6 +492,7 @@
     else:
         grad_out = lax.psum_scatter(grad_out, "mp", scatter_dimension=0, tiled=True)
     out_tile = MOMENTUM * lax.dynamic_slice_in_dim(out_mom, mz * out_own, out_own, 0) + grad_out
+    out_tile = after(out_tile, matrix)
     out_rows = place([out_tile] + [lax.ppermute(out_tile, "dp", [(j ^ s, j) for j in range(FFN, n_dp)]) for s in shifts], 0)
     out_rows = jnp.pad(out_rows, ((0, hidden_own - out_rows.shape[0]), (0, 0)))
     matrix = jnp.where(me < FFN, own_mom + matrix.astype(F32), out_rows)
@@ -533,7 +534,8 @@
     mom_back, _ = give_back(after(matrix, dp_summed))
     ortho = ns_big(gram, after(matrix, factor_piece, mom_back))
     ortho = after(ortho, factor_all)
-    branch += [pass_chip(after(part, ortho), 3) for part in last]
+    branch += [pass_chip(after(part, gram), 3) for part in last]
+    ortho = after(ortho, *branch[3:])
     block_out = (residual + sum(part.astype(F32) for part in branch)).astype(BF)
     out_ortho = lax.dynamic_slice_in_dim(ortho, me * out_own, out_own, 0)
     for s in shifts:

time: 496 us -> 493 us (level)
    psum x1, waiting for transfers between devices: 31.8 us -> 42.4 us  [body(): gram = lax.psum(gram_part, 'mp')]
    ppermute x6, waiting for transfers between devices: 7.56 us -> 0.02 us  [give_back(): lax.ppermute(pieces[s], 'dp', dp_pairs(s, lambda t: t ^ s < FFN))[None]]
    reduce_scatter x1, waiting for transfers between devices: 12.7 us -> 6.71 us  [body(): matrix = lax.psum_scatter(grads, 'dp', scatter_dimension=0, tiled=True)]
    dynamic_update_slice x33 -> x34, local copies, waits for them, and re-layouts: 13.7 us -> 18.5 us  [place(): out = lax.dynamic_update_slice_in_dim(out, part, (me ^ shift) * step, axis)]
    unnamed x122 -> x126, local copies, waits for them, and re-layouts: 23.1 us -> 19 us
  transfers between devices with their start and end apart: 58 -> 58, of which waited for: 21 -> 22; matrix products, arithmetic and copies ran while one was open for 12% -> 13% of each run, Pallas kernels for 29% -> 29%
where the time goes in v4:
time: 493 us; the launch traced here: 484 us
  Pallas kernels  157 us (32%)
  waiting for transfers between devices  134 us (27%)
  starting transfers between devices  85.3 us (17%)
  local copies, waits for them, and re-layouts  56.2 us (11%)
  other arithmetic  29.6 us (6%)
  between operations  16.7 us (3%)
  matrix products  5.32 us (1%)
    pallas_call x1, Pallas kernels, ns_big(): pl.pallas_call(ns_body, out_shape=jax.ShapeDtypeStruct((w, d), F32), in_s...  68.1 us
    ppermute x15, waiting for transfers between devices, gather_dp(): lax.ppermute(own, 'dp', dp_pairs(s))  44.6 us
    psum x1, waiting for transfers between devices, body(): gram = lax.psum(gram_part, 'mp')  42.4 us
    pallas_call x1, Pallas kernels, attn_bwd(): pl.pallas_call(functools.partial(attn_bwd_body, *pairs), out_shape=(shape...  25.9 us
    unnamed x126, local copies, waits for them, and re-layouts  19 us
    ppermute x15, starting transfers between devices, gather_dp(): lax.ppermute(own, 'dp', dp_pairs(s))  18.9 us
    pallas_call x1, Pallas kernels, ns_factor(): pl.pallas_call(ns_factor_body, out_shape=shape(own.shape), in_specs=[VM]...  18.7 us
    dynamic_update_slice x34, local copies, waits for them, and re-layouts, place(): out = lax.dynamic_update_slice_in_dim(out, part, (me ^ shift) * step, axis)  18.5 us
  transfers between devices with their start and end apart: 58, of which 22 were waited for; matrix products, arithmetic and copies ran while one was open for 13% of the time, Pallas kernels for 29%

profile of v4, /device:TPU:0, one launch (start us, length us, event | category | flops | bytes accessed | tf_op | source)
XLA Modules:
  0.0 484.2 jit_solution(3653424848392997179)
XLA Ops:
  9.2 2.6 fusion.14
  12.1 3.0 collective-permute-start
  15.1 1.5 collective-permute-start.1
  17.1 3.2 collective-permute-done
  21.2 3.2 collective-permute-done.1
  26.6 1.8 collective-permute-start.4
  29.0 1.5 collective-permute-start.6
  31.1 1.5 collective-permute-start.5
  32.7 2.4 collective-permute-done.3
  35.2 1.6 collective-permute-start.8
  36.8 13.1 %collective-permute-done.5 = bf16[480,256]{1,0:T(8,128)(2,1)S(1)} collective-permute-done((bf16[480,256]{1,0:T(8,128)(2,1)S(1)}, bf16[480,256]{1,0:T(8,128)(2,1)S(1)}, u32[]{:S(2)}, u32[]{:S(2)}) %collective-permute-start.5) | collective-permute-done | bytes 245792 | tf_op jit(solution)/shard_map/ppermute | solution.py:341
  50.5 3.8 collective-permute-done.7
  54.3 2.1 collective-permute-done.8
  56.9 1.7 collective-permute-start.10
  60.0 15.9 %attn_fwd.1 = (bf16[256,1024]{1,0:T(8,128)(2,1)S(1)}, f32[256,16]{1,0:T(8,128)S(1)}, bf16[256,1024]{1,0:T(8,128)(2,1)S(1)}, bf16[1024,1024]{1,0:T(8,128)(2,1)S(1)}, bf16[1024,1024]{1,0:T(8,128)(2,1)S(1)}) custom-call(s32[1]{0:T(128)} %bitcast.base_ref, f32[256,480]{1,0:T(8,128)S(1)} %fusion.55.fq_ref, f32[1024,320]{1,0:T(8,128)S(1)} %constant_dynamic-update-slice_fusion.15.fk_ref), custom_call_target="tpu_custom_call" | custom-call | flops 18400000000 | bytes 1048576 | tf_op jit(solution)/shard_map/attn_fwd/pallas_call | solution.py:87
  83.5 1.7 collective-permute-start.12
  85.5 1.5 collective-permute-start.14
  88.8 10.3 %collective-permute-done.12 = bf16[3,352,256]{2,1,0:T(8,128)(2,1)} collective-permute-done((bf16[3,352,256]{2,1,0:T(8,128)(2,1)}, bf16[3,352,256]{2,1,0:T(8,128)(2,1)}, u32[]{:S(2)}, u32[]{:S(2)}) %collective-permute-start.12) | collective-permute-done | bytes 540704 | tf_op jit(solution)/shard_map/ppermute | solution.py:341
  100.2 5.1 %collective-permute-done.13 = bf16[3,352,256]{2,1,0:T(8,128)(2,1)} collective-permute-done((bf16[3,352,256]{2,1,0:T(8,128)(2,1)}, bf16[3,352,256]{2,1,0:T(8,128)(2,1)}, u32[]{:S(2)}, u32[]{:S(2)}) %collective-permute-start.13) | collective-permute-done | bytes 540704 | tf_op jit(solution)/shard_map/ppermute | solution.py:341
  108.4 3.6 collective-permute-start.15
  112.1 1.9 collective-permute-start.16
  115.3 6.3 %collective-permute-done.15 = f32[352,256]{1,0:T(8,128)S(1)} collective-permute-done((f32[352,256]{1,0:T(8,128)S(1)}, f32[352,256]{1,0:T(8,128)S(1)}, u32[]{:S(2)}, u32[]{:S(2)}) %collective-permute-start.15) | collective-permute-done | bytes 360480 | tf_op jit(solution)/shard_map/ppermute | solution.py:460
  121.6 4.9 %collective-permute-done.16 = f32[352,256]{1,0:T(8,128)S(1)} collective-permute-done((f32[352,256]{1,0:T(8,128)S(1)}, f32[352,256]{1,0:T(8,128)S(1)}, u32[]{:S(2)}, u32[]{:S(2)}) %collective-permute-start.16) | collective-permute-done | bytes 360480 | tf_op jit(solution)/shard_map/ppermute | solution.py:460
  127.2 1.5 all-gather.5.cloned.1.call-done.x_ref
  128.7 17.4 %ffn_tokens.1 = (bf16[2048,1024]{1,0:T(8,128)(2,1)}, bf16[2048,1024]{1,0:T(8,128)(2,1)}, bf16[2048,352]{1,0:T(8,128)(2,1)}, bf16[2048,352]{1,0:T(8,128)(2,1)}, bf16[2048,352]{1,0:T(8,128)(2,1)}) custom-call(bf16[2048,1024]{1,0:T(8,128)(2,1)} %all-gather.5.cloned.1.call-done.x_ref, bf16[2048,1024]{1,0:T(8,128)(2,1)} %all-gather.7.cloned.1.call-done.g_ref, ...), custom_call_target="tpu_custom_call" | custom-call | flops 23000000512 | bytes 1048576 | tf_op jit(solution)/shard_map/ffn_tokens/pallas_call | solution.py:280
  146.1 10.8 %reduce-scatter.5.cloned.1.call-start = ((), (), s32[]{:S(2)}) async-start(), calls=%async_computation.5 | async-start | bytes 3604480 | tf_op jit(solution)/shard_map/reduce_scatter | solution.py:468
  157.0 3.2 dynamic-slice_bitcast_fusion
  160.5 2.2 copy-done.4
  165.5 8.5 %ffn_grads.1 = bf16[1408,1024]{1,0:T(8,128)(2,1)} custom-call(bf16[2048,352]{1,0:T(8,128)(2,1)S(1)} %copy-done.6, bf16[2048,352]{1,0:T(8,128)(2,1)S(1)} %copy-done.7, bf16[2048,352]{1,0:T(8,128)(2,1)S(1)} %copy-done.8, bf16[2048,1024]{1,0:T(8,128)(2,1)S(1)} %copy-done.4, bf16[2048,1024]{1,0:T(8,128)(2,1)} %all-gather.7.cloned.1.call-done.g_ref), custom_call_target="tpu_custom_call" | custom-call | flops 11500000256 | bytes 1048576 | tf_op jit(solution)/shard_map/ffn_grads/pallas_call | solution.py:300
  174.2 3.2 convert_add_fusion
  179.6 15.4 %reduce-scatter.3.cloned.1.call-done = bf16[256,1024]{1,0:T(8,128)(2,1)} async-done(((bf16[2048,1024]{1,0:T(8,128)(2,1)}), bf16[256,1024]{1,0:T(8,128)(2,1)}) %reduce-scatter.3.cloned.1.call-update) | async-done | bytes 524304 | tf_op jit(solution)/shard_map/reduce_scatter | solution.py:463
  207.0 1.5 collective-permute-start.23
  209.2 25.9 %attn_bwd.1 = (f32[256,480]{1,0:T(8,128)S(1)}, f32[1024,320]{1,0:T(8,128)S(1)}) custom-call(s32[1]{0:T(128)} %bitcast.base_ref, bf16[256,1024]{1,0:T(8,128)(2,1)S(1)} %copy-done.14, bf16[1024,1024]{1,0:T(8,128)(2,1)S(1)} %copy-done.10, bf16[1024,1024]{1,0:T(8,128)(2,1)S(1)} %copy-done.12, bf16[256,1024]{1,0:T(8,128)(2,1)S(1)} %convolution_convert_fusion.do_ref, ...), custom_call_target="tpu_custom_call" | custom-call | flops 29899999232 | bytes 1048576 | tf_op jit(solution)/shard_map/attn_bwd/pallas_call | solution.py:134
  236.2 2.0 collective-permute-start.25
  238.2 1.8 collective-permute-start.26
  242.9 1.4 collective-permute-start.33
  247.1 6.7 %reduce-scatter.5.cloned.1.call-done = bf16[352,1024]{1,0:T(8,128)(2,1)} async-done(((bf16[1408,1024]{1,0:T(8,128)(2,1)}), bf16[352,1024]{1,0:T(8,128)(2,1)}) %reduce-scatter.5.cloned.1.call-update) | async-done | bytes 720912 | tf_op jit(solution)/shard_map/reduce_scatter | solution.py:468
  255.2 4.1 collective-permute-start.30
  266.7 2.2 gram_upper.1
  269.0 1.6 copy-done
  270.6 2.0 bitcast_add_fusion.1
  272.9 3.4 collective-permute-start.38
  277.5 3.4 collective-permute-done.36
  281.0 2.7 collective-permute-done.37
  283.9 3.7 collective-permute-start.42
  287.7 2.2 collective-permute-start.39
  289.9 2.3 collective-permute-start.40
  295.5 2.2 collective-permute-start.43
  297.7 2.1 collective-permute-start.44
  299.8 1.4 collective-permute-done.41
  301.9 42.4 %all-reduce.5.cloned.1.call-done.g_ref = f32[256,2560]{1,0:T(8,128)} async-done(((f32[256,2560]{1,0:T(8,128)}), f32[256,2560]{1,0:T(8,128)}) %all-reduce.5.cloned.1.call-update) | async-done | bytes 2621456 | tf_op jit(solution)/shard_map/psum | solution.py:500
  346.5 1.7 bitcast_dynamic-update-slice_fusion.5
  348.3 1.7 bitcast_dynamic-update-slice_fusion.4
  350.0 1.7 copy-done.5
  351.7 68.1 %ns_gram.1 = f32[352,1024]{1,0:T(8,128)S(1)} custom-call(f32[256,2560]{1,0:T(8,128)S(1)} %copy-done.5, f32[352,1024]{1,0:T(8,128)S(1)} %pad_select_fusion.y_ref), custom_call_target="tpu_custom_call" | custom-call | flops 81649999872 | bytes 1048576 | tf_op jit(solution)/shard_map/ns_gram/pallas_call | solution.py:198
  419.9 2.2 slice_bitcast_fusion.1
  429.4 2.1 dynamic-slice_bitcast_fusion.3
  431.5 2.2 collective-permute-done.45
  434.7 3.3 collective-permute-start.48
  438.0 4.4 collective-permute-start.49
  442.5 2.1 collective-permute-start.50
  445.3 2.0 copy-done.3
  447.2 18.7 %ns_factor.1 = f32[832,256]{1,0:T(8,128)S(1)} custom-call(f32[4,832,256]{2,1,0:T(8,128)S(1)} %bitcast.191, f32[832,256]{1,0:T(8,128)S(1)} %dynamic-slice_bitcast_fusion.2.own_ref), custom_call_target="tpu_custom_call" | custom-call | flops 25300000768 | bytes 1048576 | tf_op jit(solution)/shard_map/ns_factor/pallas_call | solution.py:260
  473.5 2.5 fusion.13
  (316 shorter events, 83.1 us)
Async XLA Ops:
  7.2 120.0 %all-gather.7.cloned.1.call-start = ((), (), s32[]{:S(2)}) async-start(), calls=%async_computation.3 | async-start | bytes 4718592 | tf_op jit(solution)/shard_map/all_gather | solution.py:443
  11.8 116.8 %all-gather.5.cloned.1.call-start = ((), (), s32[]{:S(2)}) async-start(), calls=%async_computation.2 | async-start | bytes 4718592 | tf_op jit(solution)/shard_map/all_gather | solution.py:461
  12.1 8.1 %collective-permute-start = (bf16[320,256]{1,0:T(8,128)(2,1)S(1)}, bf16[320,256]{1,0:T(8,128)(2,1)}, u32[]{:S(2)}, u32[]{:S(2)}) collective-permute-start(bf16[320,256]{1,0:T(8,128)(2,1)S(1)} %get-tuple-element.129), channel_id=1, source_target_pairs={{0,8},{8,0},{16,24},{24,16},{1,9},{9,1},{17,25},{25,17},{2,10},{10... | collective-permute-start | bytes 491528 | tf_op jit(solution)/shard_map/ppermute | solution.py:341
  15.1 9.3 %collective-permute-start.1 = (bf16[320,256]{1,0:T(8,128)(2,1)S(1)}, bf16[320,256]{1,0:T(8,128)(2,1)}, u32[]{:S(2)}, u32[]{:S(2)}) collective-permute-start(bf16[320,256]{1,0:T(8,128)(2,1)S(1)} %get-tuple-element.129), channel_id=1, source_target_pairs={{0,16},{8,24},{16,0},{24,8},{1,17},{9,25},{17,1},{25,9},{2,18},{10... | collective-permute-start | bytes 491528 | tf_op jit(solution)/shard_map/ppermute | solution.py:341
  16.6 8.7 %collective-permute-start.2 = (bf16[320,256]{1,0:T(8,128)(2,1)S(1)}, bf16[320,256]{1,0:T(8,128)(2,1)}, u32[]{:S(2)}, u32[]{:S(2)}) collective-permute-start(bf16[320,256]{1,0:T(8,128)(2,1)S(1)} %get-tuple-element.129), channel_id=1, source_target_pairs={{0,24},{8,16},{16,8},{24,0},{1,25},{9,17},{17,9},{25,1},{2,26},{10... | collective-permute-start | bytes 491528 | tf_op jit(solution)/shard_map/ppermute | solution.py:341
  26.3 8.9 %collective-permute-start.3 = (bf16[480,256]{1,0:T(8,128)(2,1)S(1)}, bf16[480,256]{1,0:T(8,128)(2,1)S(1)}, u32[]{:S(2)}, u32[]{:S(2)}) collective-permute-start(bf16[480,256]{1,0:T(8,128)(2,1)S(1)} %pad_maximum_fusion.5), channel_id=1, source_target_pairs={{0,8},{8,0},{16,24},{24,16},{1,9},{9,1},{17,25},{25,17},{2,10},{10... | collective-permute-start | bytes 737288 | tf_op jit(solution)/shard_map/ppermute | solution.py:341
  26.6 10.1 %collective-permute-start.4 = (bf16[480,256]{1,0:T(8,128)(2,1)S(1)}, bf16[480,256]{1,0:T(8,128)(2,1)S(1)}, u32[]{:S(2)}, u32[]{:S(2)}) collective-permute-start(bf16[480,256]{1,0:T(8,128)(2,1)S(1)} %pad_maximum_fusion.5), channel_id=1, source_target_pairs={{0,16},{8,24},{16,0},{24,8},{1,17},{9,25},{17,1},{25,9},{2,18},{10... | collective-permute-start | bytes 737288 | tf_op jit(solution)/shard_map/ppermute | solution.py:341
  29.0 21.4 %collective-permute-start.6 = (f32[256,320]{1,0:T(8,128)S(1)}, f32[256,320]{1,0:T(8,128)S(1)}, u32[]{:S(2)}, u32[]{:S(2)}) collective-permute-start(f32[256,320]{1,0:T(8,128)S(1)} %get-tuple-element.134), channel_id=1, source_target_pairs={{0,8},{8,0},{16,24},{24,16},{1,9},{9,1},{17,25},{25,17},{2,10},{10... | collective-permute-start | bytes 983048 | tf_op jit(solution)/shard_map/ppermute | solution.py:341
  30.6 23.7 %collective-permute-start.7 = (f32[256,320]{1,0:T(8,128)S(1)}, f32[256,320]{1,0:T(8,128)S(1)}, u32[]{:S(2)}, u32[]{:S(2)}) collective-permute-start(f32[256,320]{1,0:T(8,128)S(1)} %get-tuple-element.134), channel_id=1, source_target_pairs={{0,16},{8,24},{16,0},{24,8},{1,17},{9,25},{17,1},{25,9},{2,18},{10... | collective-permute-start | bytes 983048 | tf_op jit(solution)/shard_map/ppermute | solution.py:341
  31.1 18.8 %collective-permute-start.5 = (bf16[480,256]{1,0:T(8,128)(2,1)S(1)}, bf16[480,256]{1,0:T(8,128)(2,1)S(1)}, u32[]{:S(2)}, u32[]{:S(2)}) collective-permute-start(bf16[480,256]{1,0:T(8,128)(2,1)S(1)} %pad_maximum_fusion.5), channel_id=1, source_target_pairs={{0,24},{8,16},{16,8},{24,0},{1,25},{9,17},{17,9},{25,1},{2,26},{10... | collective-permute-start | bytes 737288 | tf_op jit(solution)/shard_map/ppermute | solution.py:341
  35.2 21.2 %collective-permute-start.8 = (f32[256,320]{1,0:T(8,128)S(1)}, f32[256,320]{1,0:T(8,128)S(1)}, u32[]{:S(2)}, u32[]{:S(2)}) collective-permute-start(f32[256,320]{1,0:T(8,128)S(1)} %get-tuple-element.134), channel_id=1, source_target_pairs={{0,24},{8,16},{16,8},{24,0},{1,25},{9,17},{17,9},{25,1},{2,26},{10... | collective-permute-start | bytes 983048 | tf_op jit(solution)/shard_map/ppermute | solution.py:341
  56.4 19.5 %copy-start.1 = (f32[1024,320]{1,0:T(8,128)}, f32[1024,320]{1,0:T(8,128)S(1)}, u32[]{:S(2)}) copy-start(f32[1024,320]{1,0:T(8,128)S(1)} %constant_dynamic-update-slice_fusion.15.fk_ref) | copy-start | bytes 3932164
  56.5 20.6 %collective-permute-start.9 = (bf16[256,1024]{1,0:T(8,128)(2,1)S(1)}, bf16[256,1024]{1,0:T(8,128)(2,1)S(1)}, u32[]{:S(2)}, u32[]{:S(2)}) collective-permute-start(bf16[256,1024]{1,0:T(8,128)(2,1)S(1)} %convert_element_type.227), channel_id=1, source_target_pairs={{0,8},{8,0},{16,24},{24,16},{1,9},{9,1},{17,25},{25,17},{2,10},{10... | collective-permute-start | bytes 1572872 | tf_op jit(solution)/shard_map/ppermute | solution.py:341
  56.9 22.5 %collective-permute-start.10 = (bf16[256,1024]{1,0:T(8,128)(2,1)S(1)}, bf16[256,1024]{1,0:T(8,128)(2,1)S(1)}, u32[]{:S(2)}, u32[]{:S(2)}) collective-permute-start(bf16[256,1024]{1,0:T(8,128)(2,1)S(1)} %convert_element_type.227), channel_id=1, source_target_pairs={{0,16},{8,24},{16,0},{24,8},{1,17},{9,25},{17,1},{25,9},{2,18},{10... | collective-permute-start | bytes 1572872 | tf_op jit(solution)/shard_map/ppermute | solution.py:341
  58.6 20.9 %collective-permute-start.11 = (bf16[256,1024]{1,0:T(8,128)(2,1)S(1)}, bf16[256,1024]{1,0:T(8,128)(2,1)S(1)}, u32[]{:S(2)}, u32[]{:S(2)}) collective-permute-start(bf16[256,1024]{1,0:T(8,128)(2,1)S(1)} %convert_element_type.227), channel_id=1, source_target_pairs={{0,24},{8,16},{16,8},{24,0},{1,25},{9,17},{17,9},{25,1},{2,26},{10... | collective-permute-start | bytes 1572872 | tf_op jit(solution)/shard_map/ppermute | solution.py:341
  81.9 113.2 %reduce-scatter.3.cloned.1.call-start = ((), (), s32[]{:S(2)}) async-start(), calls=%async_computation.4 | async-start | bytes 4718592 | tf_op jit(solution)/shard_map/reduce_scatter | solution.py:463
  83.5 15.5 %collective-permute-start.12 = (bf16[3,352,256]{2,1,0:T(8,128)(2,1)}, bf16[3,352,256]{2,1,0:T(8,128)(2,1)}, u32[]{:S(2)}, u32[]{:S(2)}) collective-permute-start(bf16[3,352,256]{2,1,0:T(8,128)(2,1)} %pad_maximum_fusion.3), channel_id=1, source_target_pairs={{0,8},{8,0},{16,24},{24,16},{1,9},{9,1},{17,25},{25,17},{2,10},{10... | collective-permute-start | bytes 1622024 | tf_op jit(solution)/shard_map/ppermute | solution.py:341
  85.2 20.1 %collective-permute-start.13 = (bf16[3,352,256]{2,1,0:T(8,128)(2,1)}, bf16[3,352,256]{2,1,0:T(8,128)(2,1)}, u32[]{:S(2)}, u32[]{:S(2)}) collective-permute-start(bf16[3,352,256]{2,1,0:T(8,128)(2,1)} %pad_maximum_fusion.3), channel_id=1, source_target_pairs={{0,16},{8,24},{16,0},{24,8},{1,17},{9,25},{17,1},{25,9},{2,18},{10... | collective-permute-start | bytes 1622024 | tf_op jit(solution)/shard_map/ppermute | solution.py:341
  85.5 21.7 %collective-permute-start.14 = (bf16[3,352,256]{2,1,0:T(8,128)(2,1)}, bf16[3,352,256]{2,1,0:T(8,128)(2,1)}, u32[]{:S(2)}, u32[]{:S(2)}) collective-permute-start(bf16[3,352,256]{2,1,0:T(8,128)(2,1)} %pad_maximum_fusion.3), channel_id=1, source_target_pairs={{0,24},{8,16},{16,8},{24,0},{1,25},{9,17},{17,9},{25,1},{2,26},{10... | collective-permute-start | bytes 1622024 | tf_op jit(solution)/shard_map/ppermute | solution.py:341
  87.2 21.1 %copy-start.28 = (f32[3,352,256]{2,1,0:T(8,128)}, f32[3,352,256]{2,1,0:T(8,128)S(1)}, u32[]{:S(2)}) copy-start(f32[3,352,256]{2,1,0:T(8,128)S(1)} %pad_maximum_fusion.1) | copy-start | bytes 3244036
  108.4 13.1 %collective-permute-start.15 = (f32[352,256]{1,0:T(8,128)S(1)}, f32[352,256]{1,0:T(8,128)S(1)}, u32[]{:S(2)}, u32[]{:S(2)}) collective-permute-start(f32[352,256]{1,0:T(8,128)S(1)} %get-tuple-element.118), channel_id=1, source_target_pairs={{0,8},{8,0},{24,16},{1,9},{9,1},{25,17},{2,10},{10,2},{26,18},{3,1... | collective-permute-start | bytes 1081352 | tf_op jit(solution)/shard_map/ppermute | solution.py:460
  112.1 14.4 %collective-permute-start.16 = (f32[352,256]{1,0:T(8,128)S(1)}, f32[352,256]{1,0:T(8,128)S(1)}, u32[]{:S(2)}, u32[]{:S(2)}) collective-permute-start(f32[352,256]{1,0:T(8,128)S(1)} %get-tuple-element.117), channel_id=1, source_target_pairs={{0,16},{16,0},{24,8},{1,17},{17,1},{25,9},{2,18},{18,2},{26,10},{3... | collective-permute-start | bytes 1081352 | tf_op jit(solution)/shard_map/ppermute | solution.py:460
  114.0 13.2 %collective-permute-start.17 = (f32[352,256]{1,0:T(8,128)S(1)}, f32[352,256]{1,0:T(8,128)}, u32[]{:S(2)}, u32[]{:S(2)}) collective-permute-start(f32[352,256]{1,0:T(8,128)S(1)} %get-tuple-element.116), channel_id=1, source_target_pairs={{8,16},{16,8},{24,0},{9,17},{17,9},{25,1},{10,18},{18,10},{26,2},{... | collective-permute-start | bytes 1081352 | tf_op jit(solution)/shard_map/ppermute | solution.py:460
  146.1 107.6 %reduce-scatter.5.cloned.1.call-start = ((), (), s32[]{:S(2)}) async-start(), calls=%async_computation.5 | async-start | bytes 3604480 | tf_op jit(solution)/shard_map/reduce_scatter | solution.py:468
  160.2 13.9 %collective-permute-start.18 = (bf16[4,256,1024]{2,1,0:T(8,128)(2,1)}, bf16[4,256,1024]{2,1,0:T(8,128)(2,1)}, u32[]{:S(2)}, u32[]{:S(2)}) collective-permute-start(bf16[4,256,1024]{2,1,0:T(8,128)(2,1)} %dynamic-slice_bitcast_fusion), channel_id=1, source_target_pairs={{0,1},{1,0},{2,3},{3,2},{4,5},{5,4},{6,7},{7,6},{8,9},{9,8},{10,11... | collective-permute-start | bytes 6291464 | tf_op jit(solution)/shard_map/ppermute | solution.py:364
  174.1 170.2 %all-reduce.5.cloned.1.call-start = ((), (), s32[]{:S(2)}) async-start(), calls=%async_computation.6 | async-start | bytes 5242880 | tf_op jit(solution)/shard_map/psum | solution.py:500
  178.4 17.8 %copy-start.16 = (f32[256,1024]{1,0:T(8,128)S(1)}, f32[256,1024]{1,0:T(8,128)}, u32[]{:S(2)}) copy-start(f32[256,1024]{1,0:T(8,128)} %copy-done.15) | copy-start | bytes 3145732
  198.6 6.6 %collective-permute-start.21 = (bf16[4,4,32,1024]{3,2,1,0:T(8,128)(2,1)S(1)}, bf16[4,4,32,1024]{3,2,1,0:T(8,128)(2,1)S(1)}, u32[]{:S(2)}, u32[]{:S(2)}) collective-permute-start(bf16[4,4,32,1024]{3,2,1,0:T(8,128)(2,1)S(1)} %fusion.11), channel_id=1, source_target_pairs={{0,1},{1,0},{2,3},{3,2},{4,5},{5,4},{6,7},{7,6},{8,9},{9,8},{10,11... | collective-permute-start | bytes 3145736 | tf_op jit(solution)/shard_map/ppermute | solution.py:364
  203.1 32.1 %collective-permute-start.20 = (bf16[256,1024]{1,0:T(8,128)(2,1)}, bf16[256,1024]{1,0:T(8,128)(2,1)S(1)}, u32[]{:S(2)}, u32[]{:S(2)}) collective-permute-start(bf16[256,1024]{1,0:T(8,128)(2,1)} %get-tuple-element.62), channel_id=1, source_target_pairs={{0,4},{1,5},{2,6},{3,7},{4,0},{5,1},{6,2},{7,3},{8,12},{9,13},{10,... | collective-permute-start | bytes 1572872 | tf_op jit(solution)/shard_map/ppermute | solution.py:368
  204.3 30.9 %collective-permute-start.19 = (bf16[256,1024]{1,0:T(8,128)(2,1)}, bf16[256,1024]{1,0:T(8,128)(2,1)S(1)}, u32[]{:S(2)}, u32[]{:S(2)}) collective-permute-start(bf16[256,1024]{1,0:T(8,128)(2,1)} %get-tuple-element.61), channel_id=1, source_target_pairs={{0,2},{1,3},{2,0},{3,1},{4,6},{5,7},{6,4},{7,5},{8,10},{9,11},{10,... | collective-permute-start | bytes 1572872 | tf_op jit(solution)/shard_map/ppermute | solution.py:368
  205.6 29.6 %collective-permute-start.22 = (bf16[128,1024]{1,0:T(8,128)(2,1)S(1)}, bf16[128,1024]{1,0:T(8,128)(2,1)S(1)}, u32[]{:S(2)}, u32[]{:S(2)}) collective-permute-start(bf16[128,1024]{1,0:T(8,128)(2,1)S(1)} %get-tuple-element.93), channel_id=1, source_target_pairs={{0,8},{8,0},{16,24},{24,16},{1,9},{9,1},{17,25},{25,17},{2,10},{10... | collective-permute-start | bytes 786440 | tf_op jit(solution)/shard_map/ppermute | solution.py:355
  207.0 28.2 %collective-permute-start.23 = (bf16[128,1024]{1,0:T(8,128)(2,1)S(1)}, bf16[128,1024]{1,0:T(8,128)(2,1)S(1)}, u32[]{:S(2)}, u32[]{:S(2)}) collective-permute-start(bf16[128,1024]{1,0:T(8,128)(2,1)S(1)} %get-tuple-element.95), channel_id=1, source_target_pairs={{0,16},{8,24},{16,0},{24,8},{1,17},{9,25},{17,1},{25,9},{2,18},{10... | collective-permute-start | bytes 786440 | tf_op jit(solution)/shard_map/ppermute | solution.py:355
  208.5 26.7 %collective-permute-start.24 = (bf16[128,1024]{1,0:T(8,128)(2,1)S(1)}, bf16[128,1024]{1,0:T(8,128)(2,1)S(1)}, u32[]{:S(2)}, u32[]{:S(2)}) collective-permute-start(bf16[128,1024]{1,0:T(8,128)(2,1)S(1)} %get-tuple-element.94), channel_id=1, source_target_pairs={{0,24},{8,16},{16,8},{24,0},{1,25},{9,17},{17,9},{25,1},{2,26},{10... | collective-permute-start | bytes 786440 | tf_op jit(solution)/shard_map/ppermute | solution.py:355
  236.2 8.1 %collective-permute-start.25 = (bf16[32,1024]{1,0:T(8,128)(2,1)S(1)}, bf16[32,1024]{1,0:T(8,128)(2,1)S(1)}, u32[]{:S(2)}, u32[]{:S(2)}) collective-permute-start(bf16[32,1024]{1,0:T(8,128)(2,1)S(1)} %get-tuple-element.121), channel_id=1, source_target_pairs={{0,2},{1,3},{2,0},{3,1},{4,6},{5,7},{6,4},{7,5},{8,10},{9,11},{10,... | collective-permute-start | bytes 196616 | tf_op jit(solution)/shard_map/ppermute | solution.py:368
  238.2 6.7 %collective-permute-start.26 = (bf16[32,1024]{1,0:T(8,128)(2,1)S(1)}, bf16[32,1024]{1,0:T(8,128)(2,1)S(1)}, u32[]{:S(2)}, u32[]{:S(2)}) collective-permute-start(bf16[32,1024]{1,0:T(8,128)(2,1)S(1)} %get-tuple-element.123), channel_id=1, source_target_pairs={{0,4},{1,5},{2,6},{3,7},{4,0},{5,1},{6,2},{7,3},{8,12},{9,13},{10,... | collective-permute-start | bytes 196616 | tf_op jit(solution)/shard_map/ppermute | solution.py:368
  240.0 6.1 %collective-permute-start.27 = (bf16[32,1024]{1,0:T(8,128)(2,1)S(1)}, bf16[32,1024]{1,0:T(8,128)(2,1)S(1)}, u32[]{:S(2)}, u32[]{:S(2)}) collective-permute-start(bf16[32,1024]{1,0:T(8,128)(2,1)S(1)} %get-tuple-element.122), channel_id=1, source_target_pairs={{0,6},{1,7},{2,4},{3,5},{4,2},{5,3},{6,0},{7,1},{8,14},{9,15},{10,... | collective-permute-start | bytes 196616 | tf_op jit(solution)/shard_map/ppermute | solution.py:368
  241.5 19.1 %copy-start.27 = (bf16[320,1024]{1,0:T(8,128)(2,1)S(1)}, bf16[320,1024]{1,0:T(8,128)(2,1)}, u32[]{:S(2)}) copy-start(bf16[320,1024]{1,0:T(8,128)(2,1)} %copy-done.26) | copy-start | bytes 1966084
  241.5 13.7 %collective-permute-start.32 = (bf16[256,320]{1,0:T(8,128)(2,1)}, bf16[256,320]{1,0:T(8,128)(2,1)}, u32[]{:S(2)}, u32[]{:S(2)}) collective-permute-start(bf16[256,320]{1,0:T(8,128)(2,1)} %get-tuple-element.99), channel_id=1, source_target_pairs={{0,8},{8,0},{16,24},{24,16},{1,9},{9,1},{17,25},{25,17},{2,10},{10... | collective-permute-start | bytes 491528 | tf_op jit(solution)/shard_map/ppermute | solution.py:355
  242.9 16.4 %collective-permute-start.33 = (bf16[256,320]{1,0:T(8,128)(2,1)}, bf16[256,320]{1,0:T(8,128)(2,1)}, u32[]{:S(2)}, u32[]{:S(2)}) collective-permute-start(bf16[256,320]{1,0:T(8,128)(2,1)} %get-tuple-element.101), channel_id=1, source_target_pairs={{0,16},{8,24},{16,0},{24,8},{1,17},{9,25},{17,1},{25,9},{2,18},{10... | collective-permute-start | bytes 491528 | tf_op jit(solution)/shard_map/ppermute | solution.py:355
  244.3 15.0 %collective-permute-start.34 = (bf16[256,320]{1,0:T(8,128)(2,1)S(1)}, bf16[256,320]{1,0:T(8,128)(2,1)}, u32[]{:S(2)}, u32[]{:S(2)}) collective-permute-start(bf16[256,320]{1,0:T(8,128)(2,1)S(1)} %get-tuple-element.100), channel_id=1, source_target_pairs={{0,24},{8,16},{16,8},{24,0},{1,25},{9,17},{17,9},{25,1},{2,26},{10... | collective-permute-start | bytes 491528 | tf_op jit(solution)/shard_map/ppermute | solution.py:355
  253.8 10.6 %collective-permute-start.28 = (f32[32,1024]{1,0:T(8,128)S(1)}, f32[32,1024]{1,0:T(8,128)S(1)}, u32[]{:S(2)}, u32[]{:S(2)}) collective-permute-start(f32[32,1024]{1,0:T(8,128)S(1)} %fusion.38), channel_id=1, source_target_pairs={{16,24},{17,25},{18,26},{19,27},{20,28},{21,29},{22,30},{23,31}} | collective-permute-start | bytes 393224 | tf_op jit(solution)/shard_map/ppermute | solution.py:496
  254.4 10.0 %collective-permute-start.29 = (f32[32,1024]{1,0:T(8,128)S(1)}, f32[32,1024]{1,0:T(8,128)S(1)}, u32[]{:S(2)}, u32[]{:S(2)}) collective-permute-start(f32[32,1024]{1,0:T(8,128)S(1)} %fusion.38), channel_id=1, source_target_pairs={{8,24},{9,25},{10,26},{11,27},{12,28},{13,29},{14,30},{15,31}} | collective-permute-start | bytes 393224 | tf_op jit(solution)/shard_map/ppermute | solution.py:496
  255.2 9.2 %collective-permute-start.30 = (f32[32,1024]{1,0:T(8,128)S(1)}, f32[32,1024]{1,0:T(8,128)S(1)}, u32[]{:S(2)}, u32[]{:S(2)}) collective-permute-start(f32[32,1024]{1,0:T(8,128)S(1)} %fusion.38), channel_id=1, source_target_pairs={{0,24},{1,25},{2,26},{3,27},{4,28},{5,29},{6,30},{7,31}} | collective-permute-start | bytes 393224 | tf_op jit(solution)/shard_map/ppermute | solution.py:496
  264.4 6.2 %collective-permute-start.35 = (bf16[4,104,1024]{2,1,0:T(8,128)(2,1)}, bf16[4,104,1024]{2,1,0:T(8,128)(2,1)}, u32[]{:S(2)}, u32[]{:S(2)}) collective-permute-start(bf16[4,104,1024]{2,1,0:T(8,128)(2,1)} %fusion.15), channel_id=1, source_target_pairs={{0,1},{1,0},{2,3},{3,2},{4,5},{5,4},{6,7},{7,6},{8,9},{9,8},{10,11... | collective-permute-start | bytes 2555912 | tf_op jit(solution)/shard_map/ppermute | solution.py:364
  270.5 153.6 %all-gather.9.cloned.1.call-start = ((), (), s32[]{:S(2)}) async-start(), calls=%async_computation.7 | async-start | bytes 3514368 | tf_op jit(solution)/shard_map/all_gather | solution.py:525
  272.7 8.3 %collective-permute-start.36 = (bf16[416,256]{1,0:T(8,128)(2,1)S(1)}, bf16[416,256]{1,0:T(8,128)(2,1)S(1)}, u32[]{:S(2)}, u32[]{:S(2)}) collective-permute-start(bf16[416,256]{1,0:T(8,128)(2,1)S(1)} %get-tuple-element.96), channel_id=1, source_target_pairs={{0,8},{8,0},{16,24},{24,16},{1,9},{9,1},{17,25},{25,17},{2,10},{10... | collective-permute-start | bytes 638984 | tf_op jit(solution)/shard_map/ppermute | solution.py:355
  272.8 10.9 %collective-permute-start.37 = (bf16[416,256]{1,0:T(8,128)(2,1)S(1)}, bf16[416,256]{1,0:T(8,128)(2,1)S(1)}, u32[]{:S(2)}, u32[]{:S(2)}) collective-permute-start(bf16[416,256]{1,0:T(8,128)(2,1)S(1)} %get-tuple-element.98), channel_id=1, source_target_pairs={{0,16},{8,24},{16,0},{24,8},{1,17},{9,25},{17,1},{25,9},{2,18},{10... | collective-permute-start | bytes 638984 | tf_op jit(solution)/shard_map/ppermute | solution.py:355
  272.9 10.8 %collective-permute-start.38 = (bf16[416,256]{1,0:T(8,128)(2,1)S(1)}, bf16[416,256]{1,0:T(8,128)(2,1)S(1)}, u32[]{:S(2)}, u32[]{:S(2)}) collective-permute-start(bf16[416,256]{1,0:T(8,128)(2,1)S(1)} %get-tuple-element.97), channel_id=1, source_target_pairs={{0,24},{8,16},{16,8},{24,0},{1,25},{9,17},{17,9},{25,1},{2,26},{10... | collective-permute-start | bytes 638984 | tf_op jit(solution)/shard_map/ppermute | solution.py:355
  283.9 61.8 %collective-permute-start.42 = (f32[352,256]{1,0:T(8,128)S(1)}, f32[352,256]{1,0:T(8,128)S(1)}, u32[]{:S(2)}, u32[]{:S(2)}) collective-permute-start(f32[352,256]{1,0:T(8,128)S(1)} %get-tuple-element.115), channel_id=1, source_target_pairs={{0,8},{8,0},{16,24},{1,9},{9,1},{17,25},{2,10},{10,2},{18,26},{3,1... | collective-permute-start | bytes 1081352 | tf_op jit(solution)/shard_map/ppermute | solution.py:531
  287.7 10.0 %collective-permute-start.39 = (bf16[104,256]{1,0:T(8,128)(2,1)S(1)}, bf16[104,256]{1,0:T(8,128)(2,1)S(1)}, u32[]{:S(2)}, u32[]{:S(2)}) collective-permute-start(bf16[104,256]{1,0:T(8,128)(2,1)S(1)} %get-tuple-element.124), channel_id=1, source_target_pairs={{0,2},{1,3},{2,0},{3,1},{4,6},{5,7},{6,4},{7,5},{8,10},{9,11},{10,... | collective-permute-start | bytes 159752 | tf_op jit(solution)/shard_map/ppermute | solution.py:368
  289.9 9.9 %collective-permute-start.40 = (bf16[104,256]{1,0:T(8,128)(2,1)S(1)}, bf16[104,256]{1,0:T(8,128)(2,1)S(1)}, u32[]{:S(2)}, u32[]{:S(2)}) collective-permute-start(bf16[104,256]{1,0:T(8,128)(2,1)S(1)} %get-tuple-element.126), channel_id=1, source_target_pairs={{0,4},{1,5},{2,6},{3,7},{4,0},{5,1},{6,2},{7,3},{8,12},{9,13},{10,... | collective-permute-start | bytes 159752 | tf_op jit(solution)/shard_map/ppermute | solution.py:368
  292.2 52.1 %copy-start.50 = (bf16[256,1024]{1,0:T(8,128)(2,1)S(1)}, bf16[256,1024]{1,0:T(8,128)(2,1)}, u32[]{:S(2)}) copy-start(bf16[256,1024]{1,0:T(8,128)(2,1)} %get-tuple-element.72) | copy-start | bytes 1572868
  292.2 9.0 %collective-permute-start.41 = (bf16[104,256]{1,0:T(8,128)(2,1)S(1)}, bf16[104,256]{1,0:T(8,128)(2,1)S(1)}, u32[]{:S(2)}, u32[]{:S(2)}) collective-permute-start(bf16[104,256]{1,0:T(8,128)(2,1)S(1)} %get-tuple-element.125), channel_id=1, source_target_pairs={{0,6},{1,7},{2,4},{3,5},{4,2},{5,3},{6,0},{7,1},{8,14},{9,15},{10,... | collective-permute-start | bytes 159752 | tf_op jit(solution)/shard_map/ppermute | solution.py:368
  295.5 51.0 %collective-permute-start.43 = (f32[352,256]{1,0:T(8,128)S(1)}, f32[352,256]{1,0:T(8,128)}, u32[]{:S(2)}, u32[]{:S(2)}) collective-permute-start(f32[352,256]{1,0:T(8,128)S(1)} %get-tuple-element.114), channel_id=1, source_target_pairs={{0,16},{8,24},{16,0},{1,17},{9,25},{17,1},{2,18},{10,26},{18,2},{3... | collective-permute-start | bytes 1081352 | tf_op jit(solution)/shard_map/ppermute | solution.py:531
  297.7 50.6 %collective-permute-start.44 = (f32[352,256]{1,0:T(8,128)S(1)}, f32[352,256]{1,0:T(8,128)}, u32[]{:S(2)}, u32[]{:S(2)}) collective-permute-start(f32[352,256]{1,0:T(8,128)S(1)} %get-tuple-element.113), channel_id=1, source_target_pairs={{0,24},{8,16},{16,8},{1,25},{9,17},{17,9},{2,26},{10,18},{18,10},{... | collective-permute-start | bytes 1081352 | tf_op jit(solution)/shard_map/ppermute | solution.py:531
  301.9 171.6 %all-gather.11.cloned.1.call-start = ((), (), s32[]{:S(2)}) async-start(), calls=%async_computation.8 | async-start | bytes 2359296 | tf_op jit(solution)/shard_map/all_gather | solution.py:546
  344.3 78.6 %collective-permute-start.31 = (bf16[256,1024]{1,0:T(8,128)(2,1)S(1)}, bf16[256,1024]{1,0:T(8,128)(2,1)S(1)}, u32[]{:S(2)}, u32[]{:S(2)}) collective-permute-start(bf16[256,1024]{1,0:T(8,128)(2,1)S(1)} %copy-done.50), channel_id=1, source_target_pairs={{0,6},{1,7},{2,4},{3,5},{4,2},{5,3},{6,0},{7,1},{8,14},{9,15},{10,... | collective-permute-start | bytes 1572872 | tf_op jit(solution)/shard_map/ppermute | solution.py:368
  425.5 8.3 %collective-permute-start.45 = (f32[32,1024]{1,0:T(8,128)S(1)}, f32[32,1024]{1,0:T(8,128)S(1)}, u32[]{:S(2)}, u32[]{:S(2)}) collective-permute-start(f32[32,1024]{1,0:T(8,128)S(1)} %get-tuple-element.112), channel_id=1, source_target_pairs={{24,0},{25,1},{26,2},{27,3},{28,4},{29,5},{30,6},{31,7}} | collective-permute-start | bytes 393224 | tf_op jit(solution)/shard_map/ppermute | solution.py:543
  426.8 7.0 %collective-permute-start.46 = (f32[32,1024]{1,0:T(8,128)S(1)}, f32[32,1024]{1,0:T(8,128)S(1)}, u32[]{:S(2)}, u32[]{:S(2)}) collective-permute-start(f32[32,1024]{1,0:T(8,128)S(1)} %get-tuple-element.111), channel_id=1, source_target_pairs={{24,8},{25,9},{26,10},{27,11},{28,12},{29,13},{30,14},{31,15}} | collective-permute-start | bytes 393224 | tf_op jit(solution)/shard_map/ppermute | solution.py:543
  427.4 6.3 %collective-permute-start.47 = (f32[32,1024]{1,0:T(8,128)S(1)}, f32[32,1024]{1,0:T(8,128)S(1)}, u32[]{:S(2)}, u32[]{:S(2)}) collective-permute-start(f32[32,1024]{1,0:T(8,128)S(1)} %get-tuple-element.110), channel_id=1, source_target_pairs={{24,16},{25,17},{26,18},{27,19},{28,20},{29,21},{30,22},{31,23}} | collective-permute-start | bytes 393224 | tf_op jit(solution)/shard_map/ppermute | solution.py:543
  434.7 32.4 %collective-permute-start.48 = (f32[352,256]{1,0:T(8,128)}, f32[352,256]{1,0:T(8,128)}, u32[]{:S(2)}, u32[]{:S(2)}) collective-permute-start(f32[352,256]{1,0:T(8,128)} %get-tuple-element.109), channel_id=1, source_target_pairs={{0,8},{8,0},{16,24},{1,9},{9,1},{17,25},{2,10},{10,2},{18,26},{3,1... | collective-permute-start | bytes 1081352 | tf_op jit(solution)/shard_map/ppermute | solution.py:531
  438.0 30.2 %collective-permute-start.49 = (f32[352,256]{1,0:T(8,128)}, f32[352,256]{1,0:T(8,128)}, u32[]{:S(2)}, u32[]{:S(2)}) collective-permute-start(f32[352,256]{1,0:T(8,128)} %get-tuple-element.108), channel_id=1, source_target_pairs={{0,16},{8,24},{16,0},{1,17},{9,25},{17,1},{2,18},{10,26},{18,2},{3... | collective-permute-start | bytes 1081352 | tf_op jit(solution)/shard_map/ppermute | solution.py:531
  442.5 26.8 %collective-permute-start.50 = (f32[352,256]{1,0:T(8,128)S(1)}, f32[352,256]{1,0:T(8,128)}, u32[]{:S(2)}, u32[]{:S(2)}) collective-permute-start(f32[352,256]{1,0:T(8,128)S(1)} %get-tuple-element.107), channel_id=1, source_target_pairs={{0,24},{8,16},{16,8},{1,25},{9,17},{17,9},{2,26},{10,18},{18,10},{... | collective-permute-start | bytes 1081352 | tf_op jit(solution)/shard_map/ppermute | solution.py:531
  447.2 18.7 %copy-start.37 = (f32[256,800]{0,1:T(8,128)S(1)}, f32[256,800]{0,1:T(8,128)}, u32[]{:S(2)}) copy-start(f32[256,800]{0,1:T(8,128)} %param.20) | copy-start | bytes 2457604
  (57 other events, 217.5 us)
Sparse Core Ops, SparseCore 0:
  11.9 49.8 all-gather.6
  82.0 46.6 all-gather.4
  146.3 48.7 reduce-scatter.2
  197.9 55.7 reduce-scatter.4
  270.7 73.6 all-reduce.4
  347.6 59.4 all-gather.8
  445.4 28.0 all-gather.10

commit v5 on v4

--- a/solution.py
+++ b/solution.py
@@ -442,7 +442,7 @@
     d_output = cotangent.astype(F32) * seq_weight
     d_output_all = lax.all_gather(d_output.astype(BF), "mp", axis=0, tiled=True)
     kv_all = gather_dp(dot_nt(first_own, kv_low))
-    q_low = gather_dp(after(q_rows(factor_own), kv_low), 1)
+    q_low = gather_dp(q_rows(factor_own), 1)
     q_own = dot_nt(first_own, q_low)
     attended, lse, queries, key_vecs, values = attn_fwd(base, q_own, kv_all)
     out_low = gather_dp(after(out_w.astype(BF), kv_all))
@@ -492,8 +492,8 @@
     else:
         grad_out = lax.psum_scatter(grad_out, "mp", scatter_dimension=0, tiled=True)
     out_tile = MOMENTUM * lax.dynamic_slice_in_dim(out_mom, mz * out_own, out_own, 0) + grad_out
-    out_tile = after(out_tile, matrix)
     out_rows = place([out_tile] + [lax.ppermute(out_tile, "dp", [(j ^ s, j) for j in range(FFN, n_dp)]) for s in shifts], 0)
+    out_rows = after(out_rows, matrix)
     out_rows = jnp.pad(out_rows, ((0, hidden_own - out_rows.shape[0]), (0, 0)))
     matrix = jnp.where(me < FFN, own_mom + matrix.astype(F32), out_rows)
     gram_part = gram_upper(matrix)
@@ -529,10 +529,10 @@
     def give_back(whole):
         pieces = [lax.dynamic_slice_in_dim(whole, (me ^ s) * d_own, d_own, 1) for s in range(n_dp)]
         came = [lax.ppermute(pieces[s], "dp", dp_pairs(s, lambda t: t ^ s < FFN))[None] for s in shifts]
-        return place([pieces[0][None]] + came, 0), pieces[1:]
-
-    mom_back, _ = give_back(after(matrix, dp_summed))
-    ortho = ns_big(gram, after(matrix, factor_piece, mom_back))
+        return place([pieces[0][None]] + came, 0), pieces[1:], came
+
+    mom_back, _, came = give_back(after(matrix, dp_summed))
+    ortho = ns_big(gram, after(matrix, factor_piece, *came))
     ortho = after(ortho, factor_all)
     branch += [pass_chip(after(part, gram), 3) for part in last]
     ortho = after(ortho, *branch[3:])
@@ -546,7 +546,7 @@
     out_both = lax.all_gather(out_pair, "mp", axis=1, tiled=True)
     new_out_mom = out_both[0]
     new_out_w = out_w - LEARN * 0.2 * math.sqrt(D) * out_both[1]
-    ortho_back, sent = give_back(after(ortho, out_ortho))
+    ortho_back, sent, _ = give_back(after(ortho, out_ortho))
     factor_ortho = ns_factor(factor_all, after(factor_tile, out_pair, *sent))
     ortho_back = after(ortho_back, factor_ortho)
     turn = lambda stack: jnp.stack([stack[0].T, stack[1].T])

time: 493 us -> 502 us (1.018)
  starting transfers between devices: 85.3 us -> 76.9 us
  local copies, waits for them, and re-layouts: 56.2 us -> 63.2 us
    reduce_scatter x1, waiting for transfers between devices: 15.4 us -> 26.9 us  [body(): lax.psum_scatter(d_second, 'mp', scatter_dimension=0, tiled=True)]
    reduce_scatter x1, starting transfers between devices: 10.8 us -> 0.57 us  [body(): matrix = lax.psum_scatter(grads, 'dp', scatter_dimension=0, tiled=True)]
    ppermute x9, waiting for transfers between devices: 6.17 us -> 15 us  [sum_dp(): total = total + lax.ppermute(block, 'dp', dp_pairs(s)).astype(F32)]
    ppermute x15, waiting for transfers between devices: 44.6 us -> 36 us  [gather_dp(): lax.ppermute(own, 'dp', dp_pairs(s))]
    reduce_scatter x1, waiting for transfers between devices: 6.71 us -> 0.02 us  [body(): matrix = lax.psum_scatter(grads, 'dp', scatter_dimension=0, tiled=True)]
    dynamic_update_slice x34 -> x31, local copies, waits for them, and re-layouts: 18.5 us -> 23.6 us  [place(): out = lax.dynamic_update_slice_in_dim(out, part, (me ^ shift) * step, axis)]
    unnamed x126 -> x116, local copies, waits for them, and re-layouts: 19 us -> 18.4 us
  transfers between devices with their start and end apart: 58 -> 58, of which waited for: 22 -> 17; matrix products, arithmetic and copies ran while one was open for 13% -> 15% of each run, Pallas kernels for 29% -> 28%
where the time goes in v5:
time: 502 us; the launch traced here: 493 us
  Pallas kernels  157 us (31%)
  waiting for transfers between devices  137 us (27%)
  starting transfers between devices  76.9 us (15%)
  local copies, waits for them, and re-layouts  63.2 us (13%)
  other arithmetic  34.1 us (7%)
  between operations  16.4 us (3%)
  matrix products  8.91 us (2%)
    pallas_call x1, Pallas kernels, ns_big(): pl.pallas_call(ns_body, out_shape=jax.ShapeDtypeStruct((w, d), F32), in_s...  68.2 us
    psum x1, waiting for transfers between devices, body(): gram = lax.psum(gram_part, 'mp')  42.1 us
    ppermute x15, waiting for transfers between devices, gather_dp(): lax.ppermute(own, 'dp', dp_pairs(s))  36 us
    reduce_scatter x1, waiting for transfers between devices, body(): lax.psum_scatter(d_second, 'mp', scatter_dimension=0, tiled=True)  26.9 us
    pallas_call x1, Pallas kernels, attn_bwd(): pl.pallas_call(functools.partial(attn_bwd_body, *pairs), out_shape=(shape...  25.9 us
    dynamic_update_slice x31, local copies, waits for them, and re-layouts, place(): out = lax.dynamic_update_slice_in_dim(out, part, (me ^ shift) * step, axis)  23.6 us
    ppermute x15, starting transfers between devices, gather_dp(): lax.ppermute(own, 'dp', dp_pairs(s))  20.6 us
    pallas_call x1, Pallas kernels, ns_factor(): pl.pallas_call(ns_factor_body, out_shape=shape(own.shape), in_specs=[VM]...  18.6 us
  transfers between devices with their start and end apart: 58, of which 17 were waited for; matrix products, arithmetic and copies ran while one was open for 15% of the time, Pallas kernels for 28%

profile of v5, /device:TPU:0, one launch (start us, length us, event | category | flops | bytes accessed | tf_op | source)
XLA Modules:
  0.0 493.0 jit_solution(11472685916547103017)
XLA Ops:
  9.2 2.6 fusion.14
  12.8 2.9 collective-permute-start.3
  15.7 1.5 collective-permute-start.4
  19.1 2.0 collective-permute-start
  21.1 1.5 collective-permute-start.1
  30.8 2.0 collective-permute-start.8
  33.5 2.5 collective-permute-done.1
  37.5 1.7 fusion.55.fq_ref
  39.2 4.4 collective-permute-done.6
  43.6 8.9 %collective-permute-done.7 = f32[256,320]{1,0:T(8,128)S(1)} collective-permute-done((f32[256,320]{1,0:T(8,128)S(1)}, f32[256,320]{1,0:T(8,128)S(1)}, u32[]{:S(2)}, u32[]{:S(2)}) %collective-permute-start.7) | collective-permute-done | bytes 327712 | tf_op jit(solution)/shard_map/ppermute | solution.py:341
  56.1 15.9 %attn_fwd.1 = (bf16[256,1024]{1,0:T(8,128)(2,1)S(1)}, f32[256,16]{1,0:T(8,128)S(1)}, bf16[256,1024]{1,0:T(8,128)(2,1)S(1)}, bf16[1024,1024]{1,0:T(8,128)(2,1)S(1)}, bf16[1024,1024]{1,0:T(8,128)(2,1)S(1)}) custom-call(s32[1]{0:T(128)} %bitcast.base_ref, f32[256,480]{1,0:T(8,128)S(1)} %fusion.55.fq_ref, f32[1024,320]{1,0:T(8,128)S(1)} %constant_dynamic-update-slice_fusion.18.fk_ref), custom_call_target="tpu_custom_call" | custom-call | flops 18400000000 | bytes 1048576 | tf_op jit(solution)/shard_map/attn_fwd/pallas_call | solution.py:87
  74.9 2.9 collective-permute-done.10
  83.6 1.8 collective-permute-start.14
  87.1 10.3 %collective-permute-done.12 = bf16[3,352,256]{2,1,0:T(8,128)(2,1)} collective-permute-done((bf16[3,352,256]{2,1,0:T(8,128)(2,1)}, bf16[3,352,256]{2,1,0:T(8,128)(2,1)}, u32[]{:S(2)}, u32[]{:S(2)}) %collective-permute-start.12) | collective-permute-done | bytes 540704 | tf_op jit(solution)/shard_map/ppermute | solution.py:341
  98.5 6.5 %collective-permute-done.13 = bf16[3,352,256]{2,1,0:T(8,128)(2,1)} collective-permute-done((bf16[3,352,256]{2,1,0:T(8,128)(2,1)}, bf16[3,352,256]{2,1,0:T(8,128)(2,1)}, u32[]{:S(2)}, u32[]{:S(2)}) %collective-permute-start.13) | collective-permute-done | bytes 540704 | tf_op jit(solution)/shard_map/ppermute | solution.py:341
  107.4 3.0 collective-permute-start.15
  110.4 2.7 collective-permute-start.16
  114.4 4.1 collective-permute-done.15
  118.5 8.8 %collective-permute-done.16 = f32[352,256]{1,0:T(8,128)S(1)} collective-permute-done((f32[352,256]{1,0:T(8,128)S(1)}, f32[352,256]{1,0:T(8,128)S(1)}, u32[]{:S(2)}, u32[]{:S(2)}) %collective-permute-start.16) | collective-permute-done | bytes 360480 | tf_op jit(solution)/shard_map/ppermute | solution.py:460
  128.0 17.5 %ffn_tokens.1 = (bf16[2048,1024]{1,0:T(8,128)(2,1)}, bf16[2048,1024]{1,0:T(8,128)(2,1)}, bf16[2048,352]{1,0:T(8,128)(2,1)}, bf16[2048,352]{1,0:T(8,128)(2,1)}, bf16[2048,352]{1,0:T(8,128)(2,1)}) custom-call(bf16[2048,1024]{1,0:T(8,128)(2,1)} %all-gather.5.cloned.1.call-done.x_ref, bf16[2048,1024]{1,0:T(8,128)(2,1)} %all-gather.7.cloned.1.call-done.g_ref, ...), custom_call_target="tpu_custom_call" | custom-call | flops 23000000512 | bytes 1048576 | tf_op jit(solution)/shard_map/ffn_tokens/pallas_call | solution.py:280
  146.1 3.2 dynamic-slice_bitcast_fusion
  149.3 2.4 copy-done.4
  154.5 8.5 %ffn_grads.1 = bf16[1408,1024]{1,0:T(8,128)(2,1)} custom-call(bf16[2048,352]{1,0:T(8,128)(2,1)S(1)} %copy-done.6, bf16[2048,352]{1,0:T(8,128)(2,1)S(1)} %copy-done.7, bf16[2048,352]{1,0:T(8,128)(2,1)S(1)} %copy-done.8, bf16[2048,1024]{1,0:T(8,128)(2,1)S(1)} %copy-done.4, bf16[2048,1024]{1,0:T(8,128)(2,1)} %all-gather.7.cloned.1.call-done.g_ref), custom_call_target="tpu_custom_call" | custom-call | flops 11500000256 | bytes 1048576 | tf_op jit(solution)/shard_map/ffn_grads/pallas_call | solution.py:300
  163.0 3.2 convert_add_fusion
  168.4 26.9 %reduce-scatter.3.cloned.1.call-done = bf16[256,1024]{1,0:T(8,128)(2,1)} async-done(((bf16[2048,1024]{1,0:T(8,128)(2,1)}), bf16[256,1024]{1,0:T(8,128)(2,1)}) %reduce-scatter.3.cloned.1.call-update) | async-done | bytes 524304 | tf_op jit(solution)/shard_map/reduce_scatter | solution.py:463
  202.9 1.8 bitcast_dynamic-update-slice_fusion.5
  206.2 1.9 constant_dynamic-update-slice_fusion.7
  209.7 2.0 convolution_convert_fusion.do_ref
  211.7 2.9 bitcast_add_fusion
  215.2 1.5 collective-permute-start.23
  216.7 1.7 collective-permute-start.24
  218.3 25.9 %attn_bwd.1 = (f32[256,480]{1,0:T(8,128)S(1)}, f32[1024,320]{1,0:T(8,128)S(1)}) custom-call(s32[1]{0:T(128)} %bitcast.base_ref, bf16[256,1024]{1,0:T(8,128)(2,1)S(1)} %copy-done.14, bf16[1024,1024]{1,0:T(8,128)(2,1)S(1)} %copy-done.10, bf16[1024,1024]{1,0:T(8,128)(2,1)S(1)} %copy-done.12, bf16[256,1024]{1,0:T(8,128)(2,1)S(1)} %convolution_convert_fusion.do_ref, ...), custom_call_target="tpu_custom_call" | custom-call | flops 29899999232 | bytes 1048576 | tf_op jit(solution)/shard_map/attn_bwd/pallas_call | solution.py:134
  245.7 3.0 collective-permute-start.26
  251.8 1.5 collective-permute-start.34
  257.3 4.5 collective-permute-done.32
  261.8 3.5 collective-permute-start.30
  267.3 1.8 fusion.9
  270.5 1.8 copy-done.26
  273.4 1.8 pad_select_fusion.y_ref
  275.3 2.2 gram_upper.1
  277.5 1.6 copy-done
  279.2 2.0 bitcast_add_fusion.1
  281.3 2.4 collective-permute-start.36
  286.4 3.3 collective-permute-done.36
  289.7 5.8 %collective-permute-done.37 = bf16[416,256]{1,0:T(8,128)(2,1)S(1)} collective-permute-done((bf16[416,256]{1,0:T(8,128)(2,1)S(1)}, bf16[416,256]{1,0:T(8,128)(2,1)S(1)}, u32[]{:S(2)}, u32[]{:S(2)}) %collective-permute-start.37) | collective-permute-done | bytes 213024 | tf_op jit(solution)/shard_map/ppermute | solution.py:355
  296.7 2.4 collective-permute-start.42
  300.3 3.6 collective-permute-start.40
  305.9 3.7 collective-permute-start.43
  309.6 2.0 collective-permute-start.44
  312.4 42.1 %all-reduce.5.cloned.1.call-done.g_ref = f32[256,2560]{1,0:T(8,128)} async-done(((f32[256,2560]{1,0:T(8,128)}), f32[256,2560]{1,0:T(8,128)}) %all-reduce.5.cloned.1.call-update) | async-done | bytes 2621456 | tf_op jit(solution)/shard_map/psum | solution.py:500
  355.9 1.7 copy-done.5
  357.7 68.2 %ns_gram.1 = f32[352,1024]{1,0:T(8,128)S(1)} custom-call(f32[256,2560]{1,0:T(8,128)S(1)} %copy-done.5, f32[352,1024]{1,0:T(8,128)S(1)} %pad_select_fusion.y_ref), custom_call_target="tpu_custom_call" | custom-call | flops 81649999872 | bytes 1048576 | tf_op jit(solution)/shard_map/ns_gram/pallas_call | solution.py:198
  425.9 1.9 constant_dynamic-update-slice_fusion.2
  427.8 1.7 constant_dynamic-update-slice_fusion.1
  436.0 2.1 dynamic-slice_bitcast_fusion.3
  438.1 2.2 collective-permute-done.45
  441.3 3.2 collective-permute-start.48
  444.6 4.5 collective-permute-start.49
  449.0 2.0 collective-permute-start.50
  451.8 2.0 copy-done.3
  453.8 18.6 %ns_factor.1 = f32[832,256]{1,0:T(8,128)S(1)} custom-call(f32[4,832,256]{2,1,0:T(8,128)S(1)} %bitcast.192, f32[832,256]{1,0:T(8,128)S(1)} %dynamic-slice_bitcast_fusion.2.own_ref), custom_call_target="tpu_custom_call" | custom-call | flops 25300000768 | bytes 1048576 | tf_op jit(solution)/shard_map/ns_factor/pallas_call | solution.py:260
  475.7 1.9 bitcast_dynamic-update-slice_fusion
  477.6 2.0 slice_bitcast_fusion.1
  482.4 2.5 fusion.13
  (303 shorter events, 88.0 us)
Async XLA Ops:
  7.2 120.8 %all-gather.7.cloned.1.call-start = ((), (), s32[]{:S(2)}) async-start(), calls=%async_computation.3 | async-start | bytes 4718592 | tf_op jit(solution)/shard_map/all_gather | solution.py:443
  11.8 116.2 %all-gather.5.cloned.1.call-start = ((), (), s32[]{:S(2)}) async-start(), calls=%async_computation.2 | async-start | bytes 4718592 | tf_op jit(solution)/shard_map/all_gather | solution.py:461
  12.8 10.2 %collective-permute-start.3 = (bf16[320,256]{1,0:T(8,128)(2,1)}, bf16[320,256]{1,0:T(8,128)(2,1)}, u32[]{:S(2)}, u32[]{:S(2)}) collective-permute-start(bf16[320,256]{1,0:T(8,128)(2,1)} %get-tuple-element.131), channel_id=1, source_target_pairs={{0,8},{8,0},{16,24},{24,16},{1,9},{9,1},{17,25},{25,17},{2,10},{10... | collective-permute-start | bytes 491528 | tf_op jit(solution)/shard_map/ppermute | solution.py:341
  15.7 9.9 %collective-permute-start.4 = (bf16[320,256]{1,0:T(8,128)(2,1)}, bf16[320,256]{1,0:T(8,128)(2,1)}, u32[]{:S(2)}, u32[]{:S(2)}) collective-permute-start(bf16[320,256]{1,0:T(8,128)(2,1)} %get-tuple-element.131), channel_id=1, source_target_pairs={{0,16},{8,24},{16,0},{24,8},{1,17},{9,25},{17,1},{25,9},{2,18},{10... | collective-permute-start | bytes 491528 | tf_op jit(solution)/shard_map/ppermute | solution.py:341
  17.2 9.3 %collective-permute-start.5 = (bf16[320,256]{1,0:T(8,128)(2,1)}, bf16[320,256]{1,0:T(8,128)(2,1)}, u32[]{:S(2)}, u32[]{:S(2)}) collective-permute-start(bf16[320,256]{1,0:T(8,128)(2,1)} %get-tuple-element.131), channel_id=1, source_target_pairs={{0,24},{8,16},{16,8},{24,0},{1,25},{9,17},{17,9},{25,1},{2,26},{10... | collective-permute-start | bytes 491528 | tf_op jit(solution)/shard_map/ppermute | solution.py:341
  19.1 11.7 %collective-permute-start = (bf16[480,256]{1,0:T(8,128)(2,1)S(1)}, bf16[480,256]{1,0:T(8,128)(2,1)S(1)}, u32[]{:S(2)}, u32[]{:S(2)}) collective-permute-start(bf16[480,256]{1,0:T(8,128)(2,1)S(1)} %get-tuple-element.129), channel_id=1, source_target_pairs={{0,8},{8,0},{16,24},{24,16},{1,9},{9,1},{17,25},{25,17},{2,10},{10... | collective-permute-start | bytes 737288 | tf_op jit(solution)/shard_map/ppermute | solution.py:341
  21.1 14.9 %collective-permute-start.1 = (bf16[480,256]{1,0:T(8,128)(2,1)S(1)}, bf16[480,256]{1,0:T(8,128)(2,1)S(1)}, u32[]{:S(2)}, u32[]{:S(2)}) collective-permute-start(bf16[480,256]{1,0:T(8,128)(2,1)S(1)} %get-tuple-element.129), channel_id=1, source_target_pairs={{0,16},{8,24},{16,0},{24,8},{1,17},{9,25},{17,1},{25,9},{2,18},{10... | collective-permute-start | bytes 737288 | tf_op jit(solution)/shard_map/ppermute | solution.py:341
  23.0 13.7 %collective-permute-start.2 = (bf16[480,256]{1,0:T(8,128)(2,1)S(1)}, bf16[480,256]{1,0:T(8,128)(2,1)S(1)}, u32[]{:S(2)}, u32[]{:S(2)}) collective-permute-start(bf16[480,256]{1,0:T(8,128)(2,1)S(1)} %get-tuple-element.129), channel_id=1, source_target_pairs={{0,24},{8,16},{16,8},{24,0},{1,25},{9,17},{17,9},{25,1},{2,26},{10... | collective-permute-start | bytes 737288 | tf_op jit(solution)/shard_map/ppermute | solution.py:341
  28.3 15.3 %collective-permute-start.6 = (f32[256,320]{1,0:T(8,128)S(1)}, f32[256,320]{1,0:T(8,128)S(1)}, u32[]{:S(2)}, u32[]{:S(2)}) collective-permute-start(f32[256,320]{1,0:T(8,128)S(1)} %get-tuple-element.136), channel_id=1, source_target_pairs={{0,8},{8,0},{16,24},{24,16},{1,9},{9,1},{17,25},{25,17},{2,10},{10... | collective-permute-start | bytes 983048 | tf_op jit(solution)/shard_map/ppermute | solution.py:341
  29.4 23.1 %collective-permute-start.7 = (f32[256,320]{1,0:T(8,128)S(1)}, f32[256,320]{1,0:T(8,128)S(1)}, u32[]{:S(2)}, u32[]{:S(2)}) collective-permute-start(f32[256,320]{1,0:T(8,128)S(1)} %get-tuple-element.136), channel_id=1, source_target_pairs={{0,16},{8,24},{16,0},{24,8},{1,17},{9,25},{17,1},{25,9},{2,18},{10... | collective-permute-start | bytes 983048 | tf_op jit(solution)/shard_map/ppermute | solution.py:341
  30.8 21.7 %collective-permute-start.8 = (f32[256,320]{1,0:T(8,128)S(1)}, f32[256,320]{1,0:T(8,128)S(1)}, u32[]{:S(2)}, u32[]{:S(2)}) collective-permute-start(f32[256,320]{1,0:T(8,128)S(1)} %get-tuple-element.136), channel_id=1, source_target_pairs={{0,24},{8,16},{16,8},{24,0},{1,25},{9,17},{17,9},{25,1},{2,26},{10... | collective-permute-start | bytes 983048 | tf_op jit(solution)/shard_map/ppermute | solution.py:341
  52.6 20.6 %collective-permute-start.9 = (bf16[256,1024]{1,0:T(8,128)(2,1)S(1)}, bf16[256,1024]{1,0:T(8,128)(2,1)S(1)}, u32[]{:S(2)}, u32[]{:S(2)}) collective-permute-start(bf16[256,1024]{1,0:T(8,128)(2,1)S(1)} %convert_element_type.227), channel_id=1, source_target_pairs={{0,8},{8,0},{16,24},{24,16},{1,9},{9,1},{17,25},{25,17},{2,10},{10... | collective-permute-start | bytes 1572872 | tf_op jit(solution)/shard_map/ppermute | solution.py:341
  53.9 23.9 %collective-permute-start.10 = (bf16[256,1024]{1,0:T(8,128)(2,1)S(1)}, bf16[256,1024]{1,0:T(8,128)(2,1)S(1)}, u32[]{:S(2)}, u32[]{:S(2)}) collective-permute-start(bf16[256,1024]{1,0:T(8,128)(2,1)S(1)} %convert_element_type.227), channel_id=1, source_target_pairs={{0,16},{8,24},{16,0},{24,8},{1,17},{9,25},{17,1},{25,9},{2,18},{10... | collective-permute-start | bytes 1572872 | tf_op jit(solution)/shard_map/ppermute | solution.py:341
  54.7 23.1 %collective-permute-start.11 = (bf16[256,1024]{1,0:T(8,128)(2,1)S(1)}, bf16[256,1024]{1,0:T(8,128)(2,1)S(1)}, u32[]{:S(2)}, u32[]{:S(2)}) collective-permute-start(bf16[256,1024]{1,0:T(8,128)(2,1)S(1)} %convert_element_type.227), channel_id=1, source_target_pairs={{0,24},{8,16},{16,8},{24,0},{1,25},{9,17},{17,9},{25,1},{2,26},{10... | collective-permute-start | bytes 1572872 | tf_op jit(solution)/shard_map/ppermute | solution.py:341
  80.2 115.1 %reduce-scatter.3.cloned.1.call-start = ((), (), s32[]{:S(2)}) async-start(), calls=%async_computation.4 | async-start | bytes 4718592 | tf_op jit(solution)/shard_map/reduce_scatter | solution.py:463
  81.9 15.5 %collective-permute-start.12 = (bf16[3,352,256]{2,1,0:T(8,128)(2,1)}, bf16[3,352,256]{2,1,0:T(8,128)(2,1)}, u32[]{:S(2)}, u32[]{:S(2)}) collective-permute-start(bf16[3,352,256]{2,1,0:T(8,128)(2,1)} %pad_maximum_fusion.3), channel_id=1, source_target_pairs={{0,8},{8,0},{16,24},{24,16},{1,9},{9,1},{17,25},{25,17},{2,10},{10... | collective-permute-start | bytes 1622024 | tf_op jit(solution)/shard_map/ppermute | solution.py:341
  82.5 22.5 %collective-permute-start.13 = (bf16[3,352,256]{2,1,0:T(8,128)(2,1)}, bf16[3,352,256]{2,1,0:T(8,128)(2,1)}, u32[]{:S(2)}, u32[]{:S(2)}) collective-permute-start(bf16[3,352,256]{2,1,0:T(8,128)(2,1)} %pad_maximum_fusion.3), channel_id=1, source_target_pairs={{0,16},{8,24},{16,0},{24,8},{1,17},{9,25},{17,1},{25,9},{2,18},{10... | collective-permute-start | bytes 1622024 | tf_op jit(solution)/shard_map/ppermute | solution.py:341
  83.6 22.6 %collective-permute-start.14 = (bf16[3,352,256]{2,1,0:T(8,128)(2,1)}, bf16[3,352,256]{2,1,0:T(8,128)(2,1)}, u32[]{:S(2)}, u32[]{:S(2)}) collective-permute-start(bf16[3,352,256]{2,1,0:T(8,128)(2,1)} %pad_maximum_fusion.3), channel_id=1, source_target_pairs={{0,24},{8,16},{16,8},{24,0},{1,25},{9,17},{17,9},{25,1},{2,26},{10... | collective-permute-start | bytes 1622024 | tf_op jit(solution)/shard_map/ppermute | solution.py:341
  107.4 11.1 %collective-permute-start.15 = (f32[352,256]{1,0:T(8,128)S(1)}, f32[352,256]{1,0:T(8,128)S(1)}, u32[]{:S(2)}, u32[]{:S(2)}) collective-permute-start(f32[352,256]{1,0:T(8,128)S(1)} %get-tuple-element.118), channel_id=1, source_target_pairs={{0,8},{8,0},{24,16},{1,9},{9,1},{25,17},{2,10},{10,2},{26,18},{3,1... | collective-permute-start | bytes 1081352 | tf_op jit(solution)/shard_map/ppermute | solution.py:460
  110.4 16.9 %collective-permute-start.16 = (f32[352,256]{1,0:T(8,128)S(1)}, f32[352,256]{1,0:T(8,128)S(1)}, u32[]{:S(2)}, u32[]{:S(2)}) collective-permute-start(f32[352,256]{1,0:T(8,128)S(1)} %get-tuple-element.117), channel_id=1, source_target_pairs={{0,16},{16,0},{24,8},{1,17},{17,1},{25,9},{2,18},{18,2},{26,10},{3... | collective-permute-start | bytes 1081352 | tf_op jit(solution)/shard_map/ppermute | solution.py:460
  113.1 14.9 %collective-permute-start.17 = (f32[352,256]{1,0:T(8,128)S(1)}, f32[352,256]{1,0:T(8,128)}, u32[]{:S(2)}, u32[]{:S(2)}) collective-permute-start(f32[352,256]{1,0:T(8,128)S(1)} %get-tuple-element.116), channel_id=1, source_target_pairs={{8,16},{16,8},{24,0},{9,17},{17,9},{25,1},{10,18},{18,10},{26,2},{... | collective-permute-start | bytes 1081352 | tf_op jit(solution)/shard_map/ppermute | solution.py:460
  145.5 127.9 %reduce-scatter.5.cloned.1.call-start = ((), (), s32[]{:S(2)}) async-start(), calls=%async_computation.5 | async-start | bytes 3604480 | tf_op jit(solution)/shard_map/reduce_scatter | solution.py:468
  149.3 13.7 %collective-permute-start.18 = (bf16[4,256,1024]{2,1,0:T(8,128)(2,1)}, bf16[4,256,1024]{2,1,0:T(8,128)(2,1)}, u32[]{:S(2)}, u32[]{:S(2)}) collective-permute-start(bf16[4,256,1024]{2,1,0:T(8,128)(2,1)} %dynamic-slice_bitcast_fusion), channel_id=1, source_target_pairs={{0,1},{1,0},{2,3},{3,2},{4,5},{5,4},{6,7},{7,6},{8,9},{9,8},{10,11... | collective-permute-start | bytes 6291464 | tf_op jit(solution)/shard_map/ppermute | solution.py:364
  167.2 29.2 %copy-start.16 = (f32[256,1024]{1,0:T(8,128)S(1)}, f32[256,1024]{1,0:T(8,128)}, u32[]{:S(2)}) copy-start(f32[256,1024]{1,0:T(8,128)} %copy-done.15) | copy-start | bytes 3145732
  168.4 28.5 %copy-start.39 = (bf16[256,1024]{1,0:T(8,128)(2,1)S(1)}, bf16[256,1024]{1,0:T(8,128)(2,1)}, u32[]{:S(2)}) copy-start(bf16[256,1024]{1,0:T(8,128)(2,1)} %param.15) | copy-start | bytes 1572868
  200.0 11.7 %collective-permute-start.21 = (bf16[4,4,32,1024]{3,2,1,0:T(8,128)(2,1)}, bf16[4,4,32,1024]{3,2,1,0:T(8,128)(2,1)}, u32[]{:S(2)}, u32[]{:S(2)}) collective-permute-start(bf16[4,4,32,1024]{3,2,1,0:T(8,128)(2,1)} %fusion.11), channel_id=1, source_target_pairs={{0,1},{1,0},{2,3},{3,2},{4,5},{5,4},{6,7},{7,6},{8,9},{9,8},{10,11... | collective-permute-start | bytes 3145736 | tf_op jit(solution)/shard_map/ppermute | solution.py:364
  208.2 146.3 %all-reduce.5.cloned.1.call-start = ((), (), s32[]{:S(2)}) async-start(), calls=%async_computation.6 | async-start | bytes 5242880 | tf_op jit(solution)/shard_map/psum | solution.py:500
  208.4 35.9 %collective-permute-start.20 = (bf16[256,1024]{1,0:T(8,128)(2,1)}, bf16[256,1024]{1,0:T(8,128)(2,1)S(1)}, u32[]{:S(2)}, u32[]{:S(2)}) collective-permute-start(bf16[256,1024]{1,0:T(8,128)(2,1)} %get-tuple-element.60), channel_id=1, source_target_pairs={{0,4},{1,5},{2,6},{3,7},{4,0},{5,1},{6,2},{7,3},{8,12},{9,13},{10,... | collective-permute-start | bytes 1572872 | tf_op jit(solution)/shard_map/ppermute | solution.py:368
  208.5 35.8 %collective-permute-start.19 = (bf16[256,1024]{1,0:T(8,128)(2,1)S(1)}, bf16[256,1024]{1,0:T(8,128)(2,1)S(1)}, u32[]{:S(2)}, u32[]{:S(2)}) collective-permute-start(bf16[256,1024]{1,0:T(8,128)(2,1)S(1)} %get-tuple-element.59), channel_id=1, source_target_pairs={{0,2},{1,3},{2,0},{3,1},{4,6},{5,7},{6,4},{7,5},{8,10},{9,11},{10,... | collective-permute-start | bytes 1572872 | tf_op jit(solution)/shard_map/ppermute | solution.py:368
  214.8 29.6 %collective-permute-start.22 = (bf16[128,1024]{1,0:T(8,128)(2,1)S(1)}, bf16[128,1024]{1,0:T(8,128)(2,1)S(1)}, u32[]{:S(2)}, u32[]{:S(2)}) collective-permute-start(bf16[128,1024]{1,0:T(8,128)(2,1)S(1)} %get-tuple-element.93), channel_id=1, source_target_pairs={{0,8},{8,0},{16,24},{24,16},{1,9},{9,1},{17,25},{25,17},{2,10},{10... | collective-permute-start | bytes 786440 | tf_op jit(solution)/shard_map/ppermute | solution.py:355
  215.2 29.2 %collective-permute-start.23 = (bf16[128,1024]{1,0:T(8,128)(2,1)S(1)}, bf16[128,1024]{1,0:T(8,128)(2,1)S(1)}, u32[]{:S(2)}, u32[]{:S(2)}) collective-permute-start(bf16[128,1024]{1,0:T(8,128)(2,1)S(1)} %get-tuple-element.95), channel_id=1, source_target_pairs={{0,16},{8,24},{16,0},{24,8},{1,17},{9,25},{17,1},{25,9},{2,18},{10... | collective-permute-start | bytes 786440 | tf_op jit(solution)/shard_map/ppermute | solution.py:355
  216.7 27.7 %collective-permute-start.24 = (bf16[128,1024]{1,0:T(8,128)(2,1)S(1)}, bf16[128,1024]{1,0:T(8,128)(2,1)S(1)}, u32[]{:S(2)}, u32[]{:S(2)}) collective-permute-start(bf16[128,1024]{1,0:T(8,128)(2,1)S(1)} %get-tuple-element.94), channel_id=1, source_target_pairs={{0,24},{8,16},{16,8},{24,0},{1,25},{9,17},{17,9},{25,1},{2,26},{10... | collective-permute-start | bytes 786440 | tf_op jit(solution)/shard_map/ppermute | solution.py:355
  245.3 6.5 %collective-permute-start.25 = (bf16[32,1024]{1,0:T(8,128)(2,1)S(1)}, bf16[32,1024]{1,0:T(8,128)(2,1)S(1)}, u32[]{:S(2)}, u32[]{:S(2)}) collective-permute-start(bf16[32,1024]{1,0:T(8,128)(2,1)S(1)} %get-tuple-element.121), channel_id=1, source_target_pairs={{0,2},{1,3},{2,0},{3,1},{4,6},{5,7},{6,4},{7,5},{8,10},{9,11},{10,... | collective-permute-start | bytes 196616 | tf_op jit(solution)/shard_map/ppermute | solution.py:368
  245.7 7.6 %collective-permute-start.26 = (bf16[32,1024]{1,0:T(8,128)(2,1)S(1)}, bf16[32,1024]{1,0:T(8,128)(2,1)S(1)}, u32[]{:S(2)}, u32[]{:S(2)}) collective-permute-start(bf16[32,1024]{1,0:T(8,128)(2,1)S(1)} %get-tuple-element.123), channel_id=1, source_target_pairs={{0,4},{1,5},{2,6},{3,7},{4,0},{5,1},{6,2},{7,3},{8,12},{9,13},{10,... | collective-permute-start | bytes 196616 | tf_op jit(solution)/shard_map/ppermute | solution.py:368
  248.7 6.1 %collective-permute-start.27 = (bf16[32,1024]{1,0:T(8,128)(2,1)S(1)}, bf16[32,1024]{1,0:T(8,128)(2,1)S(1)}, u32[]{:S(2)}, u32[]{:S(2)}) collective-permute-start(bf16[32,1024]{1,0:T(8,128)(2,1)S(1)} %get-tuple-element.122), channel_id=1, source_target_pairs={{0,6},{1,7},{2,4},{3,5},{4,2},{5,3},{6,0},{7,1},{8,14},{9,15},{10,... | collective-permute-start | bytes 196616 | tf_op jit(solution)/shard_map/ppermute | solution.py:368
  249.8 12.0 %collective-permute-start.32 = (bf16[256,320]{1,0:T(8,128)(2,1)S(1)}, bf16[256,320]{1,0:T(8,128)(2,1)S(1)}, u32[]{:S(2)}, u32[]{:S(2)}) collective-permute-start(bf16[256,320]{1,0:T(8,128)(2,1)S(1)} %get-tuple-element.99), channel_id=1, source_target_pairs={{0,8},{8,0},{16,24},{24,16},{1,9},{9,1},{17,25},{25,17},{2,10},{10... | collective-permute-start | bytes 491528 | tf_op jit(solution)/shard_map/ppermute | solution.py:355
  250.3 15.0 %collective-permute-start.33 = (bf16[256,320]{1,0:T(8,128)(2,1)S(1)}, bf16[256,320]{1,0:T(8,128)(2,1)S(1)}, u32[]{:S(2)}, u32[]{:S(2)}) collective-permute-start(bf16[256,320]{1,0:T(8,128)(2,1)S(1)} %get-tuple-element.101), channel_id=1, source_target_pairs={{0,16},{8,24},{16,0},{24,8},{1,17},{9,25},{17,1},{25,9},{2,18},{10... | collective-permute-start | bytes 491528 | tf_op jit(solution)/shard_map/ppermute | solution.py:355
  251.8 14.9 %collective-permute-start.34 = (bf16[256,320]{1,0:T(8,128)(2,1)S(1)}, bf16[256,320]{1,0:T(8,128)(2,1)S(1)}, u32[]{:S(2)}, u32[]{:S(2)}) collective-permute-start(bf16[256,320]{1,0:T(8,128)(2,1)S(1)} %get-tuple-element.100), channel_id=1, source_target_pairs={{0,24},{8,16},{16,8},{24,0},{1,25},{9,17},{17,9},{25,1},{2,26},{10... | collective-permute-start | bytes 491528 | tf_op jit(solution)/shard_map/ppermute | solution.py:355
  255.8 17.5 %collective-permute-start.28 = (f32[32,1024]{1,0:T(8,128)S(1)}, f32[32,1024]{1,0:T(8,128)S(1)}, u32[]{:S(2)}, u32[]{:S(2)}) collective-permute-start(f32[32,1024]{1,0:T(8,128)S(1)} %get-tuple-element.89), channel_id=1, source_target_pairs={{16,24},{17,25},{18,26},{19,27},{20,28},{21,29},{22,30},{23,31}} | collective-permute-start | bytes 393224 | tf_op jit(solution)/shard_map/ppermute | solution.py:495
  256.6 16.7 %collective-permute-start.29 = (f32[32,1024]{1,0:T(8,128)S(1)}, f32[32,1024]{1,0:T(8,128)S(1)}, u32[]{:S(2)}, u32[]{:S(2)}) collective-permute-start(f32[32,1024]{1,0:T(8,128)S(1)} %get-tuple-element.89), channel_id=1, source_target_pairs={{8,24},{9,25},{10,26},{11,27},{12,28},{13,29},{14,30},{15,31}} | collective-permute-start | bytes 393224 | tf_op jit(solution)/shard_map/ppermute | solution.py:495
  261.8 11.6 %collective-permute-start.30 = (f32[32,1024]{1,0:T(8,128)S(1)}, f32[32,1024]{1,0:T(8,128)S(1)}, u32[]{:S(2)}, u32[]{:S(2)}) collective-permute-start(f32[32,1024]{1,0:T(8,128)S(1)} %get-tuple-element.89), channel_id=1, source_target_pairs={{0,24},{1,25},{2,26},{3,27},{4,28},{5,29},{6,30},{7,31}} | collective-permute-start | bytes 393224 | tf_op jit(solution)/shard_map/ppermute | solution.py:495
  273.3 5.9 %collective-permute-start.35 = (bf16[4,104,1024]{2,1,0:T(8,128)(2,1)}, bf16[4,104,1024]{2,1,0:T(8,128)(2,1)}, u32[]{:S(2)}, u32[]{:S(2)}) collective-permute-start(bf16[4,104,1024]{2,1,0:T(8,128)(2,1)} %fusion.15), channel_id=1, source_target_pairs={{0,1},{1,0},{2,3},{3,2},{4,5},{5,4},{6,7},{7,6},{8,9},{9,8},{10,11... | collective-permute-start | bytes 2555912 | tf_op jit(solution)/shard_map/ppermute | solution.py:364
  279.1 151.6 %all-gather.9.cloned.1.call-start = ((), (), s32[]{:S(2)}) async-start(), calls=%async_computation.7 | async-start | bytes 3514368 | tf_op jit(solution)/shard_map/all_gather | solution.py:525
  281.3 8.5 %collective-permute-start.36 = (bf16[416,256]{1,0:T(8,128)(2,1)S(1)}, bf16[416,256]{1,0:T(8,128)(2,1)S(1)}, u32[]{:S(2)}, u32[]{:S(2)}) collective-permute-start(bf16[416,256]{1,0:T(8,128)(2,1)S(1)} %get-tuple-element.96), channel_id=1, source_target_pairs={{0,8},{8,0},{16,24},{24,16},{1,9},{9,1},{17,25},{25,17},{2,10},{10... | collective-permute-start | bytes 638984 | tf_op jit(solution)/shard_map/ppermute | solution.py:355
  283.6 11.9 %collective-permute-start.37 = (bf16[416,256]{1,0:T(8,128)(2,1)S(1)}, bf16[416,256]{1,0:T(8,128)(2,1)S(1)}, u32[]{:S(2)}, u32[]{:S(2)}) collective-permute-start(bf16[416,256]{1,0:T(8,128)(2,1)S(1)} %get-tuple-element.98), channel_id=1, source_target_pairs={{0,16},{8,24},{16,0},{24,8},{1,17},{9,25},{17,1},{25,9},{2,18},{10... | collective-permute-start | bytes 638984 | tf_op jit(solution)/shard_map/ppermute | solution.py:355
  284.0 11.5 %collective-permute-start.38 = (bf16[416,256]{1,0:T(8,128)(2,1)S(1)}, bf16[416,256]{1,0:T(8,128)(2,1)S(1)}, u32[]{:S(2)}, u32[]{:S(2)}) collective-permute-start(bf16[416,256]{1,0:T(8,128)(2,1)S(1)} %get-tuple-element.97), channel_id=1, source_target_pairs={{0,24},{8,16},{16,8},{24,0},{1,25},{9,17},{17,9},{25,1},{2,26},{10... | collective-permute-start | bytes 638984 | tf_op jit(solution)/shard_map/ppermute | solution.py:355
  296.7 129.2 %collective-permute-start.42 = (f32[352,256]{1,0:T(8,128)}, f32[352,256]{1,0:T(8,128)}, u32[]{:S(2)}, u32[]{:S(2)}) collective-permute-start(f32[352,256]{1,0:T(8,128)} %get-tuple-element.109), channel_id=1, source_target_pairs={{0,8},{8,0},{16,24},{1,9},{9,1},{17,25},{2,10},{10,2},{18,26},{3,1... | collective-permute-start | bytes 1081352 | tf_op jit(solution)/shard_map/ppermute | solution.py:531
  299.1 10.5 %collective-permute-start.39 = (bf16[104,256]{1,0:T(8,128)(2,1)S(1)}, bf16[104,256]{1,0:T(8,128)(2,1)S(1)}, u32[]{:S(2)}, u32[]{:S(2)}) collective-permute-start(bf16[104,256]{1,0:T(8,128)(2,1)S(1)} %get-tuple-element.124), channel_id=1, source_target_pairs={{0,2},{1,3},{2,0},{3,1},{4,6},{5,7},{6,4},{7,5},{8,10},{9,11},{10,... | collective-permute-start | bytes 159752 | tf_op jit(solution)/shard_map/ppermute | solution.py:368
  300.3 11.3 %collective-permute-start.40 = (bf16[104,256]{1,0:T(8,128)(2,1)S(1)}, bf16[104,256]{1,0:T(8,128)(2,1)S(1)}, u32[]{:S(2)}, u32[]{:S(2)}) collective-permute-start(bf16[104,256]{1,0:T(8,128)(2,1)S(1)} %get-tuple-element.126), channel_id=1, source_target_pairs={{0,4},{1,5},{2,6},{3,7},{4,0},{5,1},{6,2},{7,3},{8,12},{9,13},{10,... | collective-permute-start | bytes 159752 | tf_op jit(solution)/shard_map/ppermute | solution.py:368
  303.9 50.6 %copy-start.44 = (bf16[256,1024]{1,0:T(8,128)(2,1)S(1)}, bf16[256,1024]{1,0:T(8,128)(2,1)}, u32[]{:S(2)}) copy-start(bf16[256,1024]{1,0:T(8,128)(2,1)} %get-tuple-element.70) | copy-start | bytes 1572868
  303.9 7.7 %collective-permute-start.41 = (bf16[104,256]{1,0:T(8,128)(2,1)S(1)}, bf16[104,256]{1,0:T(8,128)(2,1)S(1)}, u32[]{:S(2)}, u32[]{:S(2)}) collective-permute-start(bf16[104,256]{1,0:T(8,128)(2,1)S(1)} %get-tuple-element.125), channel_id=1, source_target_pairs={{0,6},{1,7},{2,4},{3,5},{4,2},{5,3},{6,0},{7,1},{8,14},{9,15},{10,... | collective-permute-start | bytes 159752 | tf_op jit(solution)/shard_map/ppermute | solution.py:368
  305.9 121.8 %collective-permute-start.43 = (f32[352,256]{1,0:T(8,128)}, f32[352,256]{1,0:T(8,128)}, u32[]{:S(2)}, u32[]{:S(2)}) collective-permute-start(f32[352,256]{1,0:T(8,128)} %get-tuple-element.108), channel_id=1, source_target_pairs={{0,16},{8,24},{16,0},{1,17},{9,25},{17,1},{2,18},{10,26},{18,2},{3... | collective-permute-start | bytes 1081352 | tf_op jit(solution)/shard_map/ppermute | solution.py:531
  309.6 166.1 %collective-permute-start.44 = (f32[352,256]{1,0:T(8,128)}, f32[352,256]{1,0:T(8,128)}, u32[]{:S(2)}, u32[]{:S(2)}) collective-permute-start(f32[352,256]{1,0:T(8,128)} %get-tuple-element.107), channel_id=1, source_target_pairs={{0,24},{8,16},{16,8},{1,25},{9,17},{17,9},{2,26},{10,18},{18,10},{... | collective-permute-start | bytes 1081352 | tf_op jit(solution)/shard_map/ppermute | solution.py:531
  312.4 170.0 %all-gather.11.cloned.1.call-start = ((), (), s32[]{:S(2)}) async-start(), calls=%async_computation.8 | async-start | bytes 2359296 | tf_op jit(solution)/shard_map/all_gather | solution.py:546
  354.5 75.0 %collective-permute-start.31 = (bf16[256,1024]{1,0:T(8,128)(2,1)S(1)}, bf16[256,1024]{1,0:T(8,128)(2,1)S(1)}, u32[]{:S(2)}, u32[]{:S(2)}) collective-permute-start(bf16[256,1024]{1,0:T(8,128)(2,1)S(1)} %copy-done.44), channel_id=1, source_target_pairs={{0,6},{1,7},{2,4},{3,5},{4,2},{5,3},{6,0},{7,1},{8,14},{9,15},{10,... | collective-permute-start | bytes 1572872 | tf_op jit(solution)/shard_map/ppermute | solution.py:368
  357.6 71.9 %copy-start.32 = (f32[256,1024]{1,0:T(8,128)S(1)}, f32[256,1024]{1,0:T(8,128)}, u32[]{:S(2)}) copy-start(f32[256,1024]{1,0:T(8,128)} %dynamic-slice_bitcast_fusion.1) | copy-start | bytes 3145732
  357.6 71.9 %copy-start.48 = (bf16[256,1024]{1,0:T(8,128)(2,1)S(1)}, bf16[256,1024]{1,0:T(8,128)(2,1)}, u32[]{:S(2)}) copy-start(bf16[256,1024]{1,0:T(8,128)(2,1)} %copy-done.47) | copy-start | bytes 1572868
  357.6 71.9 %copy-start.50 = (bf16[256,1024]{1,0:T(8,128)(2,1)S(1)}, bf16[256,1024]{1,0:T(8,128)(2,1)}, u32[]{:S(2)}) copy-start(bf16[256,1024]{1,0:T(8,128)(2,1)} %copy-done.49) | copy-start | bytes 1572868
  432.0 8.3 %collective-permute-start.45 = (f32[32,1024]{1,0:T(8,128)S(1)}, f32[32,1024]{1,0:T(8,128)S(1)}, u32[]{:S(2)}, u32[]{:S(2)}) collective-permute-start(f32[32,1024]{1,0:T(8,128)S(1)} %get-tuple-element.115), channel_id=1, source_target_pairs={{24,0},{25,1},{26,2},{27,3},{28,4},{29,5},{30,6},{31,7}} | collective-permute-start | bytes 393224 | tf_op jit(solution)/shard_map/ppermute | solution.py:543
  433.3 7.0 %collective-permute-start.46 = (f32[32,1024]{1,0:T(8,128)S(1)}, f32[32,1024]{1,0:T(8,128)S(1)}, u32[]{:S(2)}, u32[]{:S(2)}) collective-permute-start(f32[32,1024]{1,0:T(8,128)S(1)} %get-tuple-element.114), channel_id=1, source_target_pairs={{24,8},{25,9},{26,10},{27,11},{28,12},{29,13},{30,14},{31,15}} | collective-permute-start | bytes 393224 | tf_op jit(solution)/shard_map/ppermute | solution.py:543
  434.0 6.3 %collective-permute-start.47 = (f32[32,1024]{1,0:T(8,128)S(1)}, f32[32,1024]{1,0:T(8,128)S(1)}, u32[]{:S(2)}, u32[]{:S(2)}) collective-permute-start(f32[32,1024]{1,0:T(8,128)S(1)} %get-tuple-element.113), channel_id=1, source_target_pairs={{24,16},{25,17},{26,18},{27,19},{28,20},{29,21},{30,22},{31,23}} | collective-permute-start | bytes 393224 | tf_op jit(solution)/shard_map/ppermute | solution.py:543
  441.3 32.3 %collective-permute-start.48 = (f32[352,256]{1,0:T(8,128)}, f32[352,256]{1,0:T(8,128)}, u32[]{:S(2)}, u32[]{:S(2)}) collective-permute-start(f32[352,256]{1,0:T(8,128)} %get-tuple-element.112), channel_id=1, source_target_pairs={{0,8},{8,0},{16,24},{1,9},{9,1},{17,25},{2,10},{10,2},{18,26},{3,1... | collective-permute-start | bytes 1081352 | tf_op jit(solution)/shard_map/ppermute | solution.py:531
  444.6 30.1 %collective-permute-start.49 = (f32[352,256]{1,0:T(8,128)}, f32[352,256]{1,0:T(8,128)}, u32[]{:S(2)}, u32[]{:S(2)}) collective-permute-start(f32[352,256]{1,0:T(8,128)} %get-tuple-element.111), channel_id=1, source_target_pairs={{0,16},{8,24},{16,0},{1,17},{9,25},{17,1},{2,18},{10,26},{18,2},{3... | collective-permute-start | bytes 1081352 | tf_op jit(solution)/shard_map/ppermute | solution.py:531
  449.0 26.6 %collective-permute-start.50 = (f32[352,256]{1,0:T(8,128)S(1)}, f32[352,256]{1,0:T(8,128)}, u32[]{:S(2)}, u32[]{:S(2)}) collective-permute-start(f32[352,256]{1,0:T(8,128)S(1)} %get-tuple-element.110), channel_id=1, source_target_pairs={{0,24},{8,16},{16,8},{1,25},{9,17},{17,9},{2,26},{10,18},{18,10},{... | collective-permute-start | bytes 1081352 | tf_op jit(solution)/shard_map/ppermute | solution.py:531
  (52 other events, 283.4 us)
Sparse Core Ops, SparseCore 0:
  11.9 49.8 all-gather.6
  80.3 47.0 all-gather.4
  145.6 49.6 reduce-scatter.2
  208.3 58.3 reduce-scatter.4
  279.2 75.2 all-reduce.4
  357.8 59.4 all-gather.8
  451.9 28.1 all-gather.10

commit v6 on v5

--- a/solution.py
+++ b/solution.py
@@ -492,8 +492,8 @@
     else:
         grad_out = lax.psum_scatter(grad_out, "mp", scatter_dimension=0, tiled=True)
     out_tile = MOMENTUM * lax.dynamic_slice_in_dim(out_mom, mz * out_own, out_own, 0) + grad_out
+    out_tile = after(out_tile, matrix)
     out_rows = place([out_tile] + [lax.ppermute(out_tile, "dp", [(j ^ s, j) for j in range(FFN, n_dp)]) for s in shifts], 0)
-    out_rows = after(out_rows, matrix)
     out_rows = jnp.pad(out_rows, ((0, hidden_own - out_rows.shape[0]), (0, 0)))
     matrix = jnp.where(me < FFN, own_mom + matrix.astype(F32), out_rows)
     gram_part = gram_upper(matrix)

time: 502 us -> 493 us (0.982)
  waiting for transfers between devices: 137 us -> 124 us
  starting transfers between devices: 76.9 us -> 87.5 us
    reduce_scatter x1, waiting for transfers between devices: 26.9 us -> 16.6 us  [body(): lax.psum_scatter(d_second, 'mp', scatter_dimension=0, tiled=True)]
    reduce_scatter x1, starting transfers between devices: 0.57 us -> 10.8 us  [body(): matrix = lax.psum_scatter(grads, 'dp', scatter_dimension=0, tiled=True)]
    ppermute x9, waiting for transfers between devices: 15 us -> 6.14 us  [sum_dp(): total = total + lax.ppermute(block, 'dp', dp_pairs(s)).astype(F32)]
    reduce_scatter x1, waiting for transfers between devices: 0.02 us -> 6.71 us  [body(): matrix = lax.psum_scatter(grads, 'dp', scatter_dimension=0, tiled=True)]
    dynamic_update_slice x31 -> x32, local copies, waits for them, and re-layouts: 23.6 us -> 20.7 us  [place(): out = lax.dynamic_update_slice_in_dim(out, part, (me ^ shift) * step, axis)]
    unnamed x116 -> x122, local copies, waits for them, and re-layouts: 18.4 us -> 19.1 us
  transfers between devices with their start and end apart: 58 -> 58, of which waited for: 17 -> 17; matrix products, arithmetic and copies ran while one was open for 15% -> 15% of each run, Pallas kernels for 28% -> 29%
where the time goes in v6:
time: 493 us; the launch traced here: 484 us
  Pallas kernels  157 us (32%)
  waiting for transfers between devices  124 us (25%)
  starting transfers between devices  87.5 us (18%)
  local copies, waits for them, and re-layouts  60.3 us (12%)
  other arithmetic  31 us (6%)
  between operations  16.6 us (3%)
  matrix products  7.76 us (2%)
    pallas_call x1, Pallas kernels, ns_big(): pl.pallas_call(ns_body, out_shape=jax.ShapeDtypeStruct((w, d), F32), in_s...  68.1 us
    psum x1, waiting for transfers between devices, body(): gram = lax.psum(gram_part, 'mp')  41.3 us
    ppermute x15, waiting for transfers between devices, gather_dp(): lax.ppermute(own, 'dp', dp_pairs(s))  36 us
    pallas_call x1, Pallas kernels, attn_bwd(): pl.pallas_call(functools.partial(attn_bwd_body, *pairs), out_shape=(shape...  25.9 us
    dynamic_update_slice x32, local copies, waits for them, and re-layouts, place(): out = lax.dynamic_update_slice_in_dim(out, part, (me ^ shift) * step, axis)  20.7 us
    ppermute x15, starting transfers between devices, gather_dp(): lax.ppermute(own, 'dp', dp_pairs(s))  20.6 us
    unnamed x122, local copies, waits for them, and re-layouts  19.1 us
    pallas_call x1, Pallas kernels, ns_factor(): pl.pallas_call(ns_factor_body, out_shape=shape(own.shape), in_specs=[VM]...  18.7 us
  transfers between devices with their start and end apart: 58, of which 17 were waited for; matrix products, arithmetic and copies ran while one was open for 15% of the time, Pallas kernels for 29%

profile of v6, /device:TPU:0, one launch (start us, length us, event | category | flops | bytes accessed | tf_op | source)
XLA Modules:
  0.0 483.7 jit_solution(18119022957344929692)
XLA Ops:
  9.2 2.6 fusion.14
  12.8 2.9 collective-permute-start.3
  15.7 1.5 collective-permute-start.4
  19.1 2.0 collective-permute-start
  21.1 1.5 collective-permute-start.1
  30.8 2.0 collective-permute-start.8
  33.5 2.5 collective-permute-done.1
  37.5 1.7 fusion.55.fq_ref
  39.2 4.4 collective-permute-done.6
  43.6 8.9 %collective-permute-done.7 = f32[256,320]{1,0:T(8,128)S(1)} collective-permute-done((f32[256,320]{1,0:T(8,128)S(1)}, f32[256,320]{1,0:T(8,128)S(1)}, u32[]{:S(2)}, u32[]{:S(2)}) %collective-permute-start.7) | collective-permute-done | bytes 327712 | tf_op jit(solution)/shard_map/ppermute | solution.py:341
  54.7 1.4 collective-permute-start.11
  56.1 15.9 %attn_fwd.1 = (bf16[256,1024]{1,0:T(8,128)(2,1)S(1)}, f32[256,16]{1,0:T(8,128)S(1)}, bf16[256,1024]{1,0:T(8,128)(2,1)S(1)}, bf16[1024,1024]{1,0:T(8,128)(2,1)S(1)}, bf16[1024,1024]{1,0:T(8,128)(2,1)S(1)}) custom-call(s32[1]{0:T(128)} %bitcast.base_ref, f32[256,480]{1,0:T(8,128)S(1)} %fusion.55.fq_ref, f32[1024,320]{1,0:T(8,128)S(1)} %constant_dynamic-update-slice_fusion.18.fk_ref), custom_call_target="tpu_custom_call" | custom-call | flops 18400000000 | bytes 1048576 | tf_op jit(solution)/shard_map/attn_fwd/pallas_call | solution.py:87
  74.9 2.9 collective-permute-done.10
  83.6 1.8 collective-permute-start.14
  87.1 10.3 %collective-permute-done.12 = bf16[3,352,256]{2,1,0:T(8,128)(2,1)} collective-permute-done((bf16[3,352,256]{2,1,0:T(8,128)(2,1)}, bf16[3,352,256]{2,1,0:T(8,128)(2,1)}, u32[]{:S(2)}, u32[]{:S(2)}) %collective-permute-start.12) | collective-permute-done | bytes 540704 | tf_op jit(solution)/shard_map/ppermute | solution.py:341
  98.5 6.5 %collective-permute-done.13 = bf16[3,352,256]{2,1,0:T(8,128)(2,1)} collective-permute-done((bf16[3,352,256]{2,1,0:T(8,128)(2,1)}, bf16[3,352,256]{2,1,0:T(8,128)(2,1)}, u32[]{:S(2)}, u32[]{:S(2)}) %collective-permute-start.13) | collective-permute-done | bytes 540704 | tf_op jit(solution)/shard_map/ppermute | solution.py:341
  107.4 3.0 collective-permute-start.15
  110.4 2.7 collective-permute-start.16
  114.4 4.1 collective-permute-done.15
  118.5 8.8 %collective-permute-done.16 = f32[352,256]{1,0:T(8,128)S(1)} collective-permute-done((f32[352,256]{1,0:T(8,128)S(1)}, f32[352,256]{1,0:T(8,128)S(1)}, u32[]{:S(2)}, u32[]{:S(2)}) %collective-permute-start.16) | collective-permute-done | bytes 360480 | tf_op jit(solution)/shard_map/ppermute | solution.py:460
  128.0 17.4 %ffn_tokens.1 = (bf16[2048,1024]{1,0:T(8,128)(2,1)}, bf16[2048,1024]{1,0:T(8,128)(2,1)}, bf16[2048,352]{1,0:T(8,128)(2,1)}, bf16[2048,352]{1,0:T(8,128)(2,1)}, bf16[2048,352]{1,0:T(8,128)(2,1)}) custom-call(bf16[2048,1024]{1,0:T(8,128)(2,1)} %all-gather.5.cloned.1.call-done.x_ref, bf16[2048,1024]{1,0:T(8,128)(2,1)} %all-gather.7.cloned.1.call-done.g_ref, ...), custom_call_target="tpu_custom_call" | custom-call | flops 23000000512 | bytes 1048576 | tf_op jit(solution)/shard_map/ffn_tokens/pallas_call | solution.py:280
  145.5 10.8 %reduce-scatter.5.cloned.1.call-start = ((), (), s32[]{:S(2)}) async-start(), calls=%async_computation.5 | async-start | bytes 3604480 | tf_op jit(solution)/shard_map/reduce_scatter | solution.py:468
  156.3 3.2 dynamic-slice_bitcast_fusion
  159.6 2.2 copy-done.4
  161.8 1.4 copy-done.7
  164.6 8.5 %ffn_grads.1 = bf16[1408,1024]{1,0:T(8,128)(2,1)} custom-call(bf16[2048,352]{1,0:T(8,128)(2,1)S(1)} %copy-done.6, bf16[2048,352]{1,0:T(8,128)(2,1)S(1)} %copy-done.7, bf16[2048,352]{1,0:T(8,128)(2,1)S(1)} %copy-done.8, bf16[2048,1024]{1,0:T(8,128)(2,1)S(1)} %copy-done.4, bf16[2048,1024]{1,0:T(8,128)(2,1)} %all-gather.7.cloned.1.call-done.g_ref), custom_call_target="tpu_custom_call" | custom-call | flops 11500000256 | bytes 1048576 | tf_op jit(solution)/shard_map/ffn_grads/pallas_call | solution.py:300
  173.2 3.2 convert_add_fusion
  178.7 16.6 %reduce-scatter.3.cloned.1.call-done = bf16[256,1024]{1,0:T(8,128)(2,1)} async-done(((bf16[2048,1024]{1,0:T(8,128)(2,1)}), bf16[256,1024]{1,0:T(8,128)(2,1)}) %reduce-scatter.3.cloned.1.call-update) | async-done | bytes 524304 | tf_op jit(solution)/shard_map/reduce_scatter | solution.py:463
  205.9 1.5 collective-permute-start.22
  207.3 1.5 collective-permute-start.23
  209.4 25.9 %attn_bwd.1 = (f32[256,480]{1,0:T(8,128)S(1)}, f32[1024,320]{1,0:T(8,128)S(1)}) custom-call(s32[1]{0:T(128)} %bitcast.base_ref, bf16[256,1024]{1,0:T(8,128)(2,1)S(1)} %copy-done.14, bf16[1024,1024]{1,0:T(8,128)(2,1)S(1)} %copy-done.10, bf16[1024,1024]{1,0:T(8,128)(2,1)S(1)} %copy-done.12, bf16[256,1024]{1,0:T(8,128)(2,1)S(1)} %convolution_convert_fusion.do_ref, ...), custom_call_target="tpu_custom_call" | custom-call | flops 29899999232 | bytes 1048576 | tf_op jit(solution)/shard_map/attn_bwd/pallas_call | solution.py:134
  236.4 2.1 collective-permute-start.25
  238.5 1.8 collective-permute-start.26
  241.7 1.4 collective-permute-start.32
  243.2 1.5 collective-permute-start.33
  247.3 6.7 %reduce-scatter.5.cloned.1.call-done = bf16[352,1024]{1,0:T(8,128)(2,1)} async-done(((bf16[1408,1024]{1,0:T(8,128)(2,1)}), bf16[352,1024]{1,0:T(8,128)(2,1)}) %reduce-scatter.5.cloned.1.call-update) | async-done | bytes 720912 | tf_op jit(solution)/shard_map/reduce_scatter | solution.py:468
  255.5 4.1 collective-permute-start.30
  261.3 1.8 fusion.9
  268.0 2.2 gram_upper.1
  270.3 1.6 copy-done
  271.9 2.0 bitcast_add_fusion.1
  274.1 3.4 collective-permute-start.38
  278.8 3.4 collective-permute-done.36
  282.2 2.7 collective-permute-done.37
  286.1 3.7 collective-permute-start.42
  289.8 2.2 collective-permute-start.39
  292.0 2.3 collective-permute-start.40
  297.6 2.9 collective-permute-start.43
  300.5 2.1 collective-permute-start.44
  304.0 41.3 %all-reduce.5.cloned.1.call-done.g_ref = f32[256,2560]{1,0:T(8,128)} async-done(((f32[256,2560]{1,0:T(8,128)}), f32[256,2560]{1,0:T(8,128)}) %all-reduce.5.cloned.1.call-update) | async-done | bytes 2621456 | tf_op jit(solution)/shard_map/psum | solution.py:500
  346.7 1.7 copy-done.5
  348.5 68.1 %ns_gram.1 = f32[352,1024]{1,0:T(8,128)S(1)} custom-call(f32[256,2560]{1,0:T(8,128)S(1)} %copy-done.5, f32[352,1024]{1,0:T(8,128)S(1)} %pad_select_fusion.y_ref), custom_call_target="tpu_custom_call" | custom-call | flops 81649999872 | bytes 1048576 | tf_op jit(solution)/shard_map/ns_gram/pallas_call | solution.py:198
  416.6 1.9 constant_dynamic-update-slice_fusion.2
  418.5 1.7 constant_dynamic-update-slice_fusion.1
  426.7 2.1 dynamic-slice_bitcast_fusion.3
  428.7 2.2 collective-permute-done.45
  432.0 3.3 collective-permute-start.48
  435.2 4.5 collective-permute-start.49
  439.7 2.0 collective-permute-start.50
  442.5 2.0 copy-done.3
  444.4 18.7 %ns_factor.1 = f32[832,256]{1,0:T(8,128)S(1)} custom-call(f32[4,832,256]{2,1,0:T(8,128)S(1)} %bitcast.191, f32[832,256]{1,0:T(8,128)S(1)} %dynamic-slice_bitcast_fusion.2.own_ref), custom_call_target="tpu_custom_call" | custom-call | flops 25300000768 | bytes 1048576 | tf_op jit(solution)/shard_map/ns_factor/pallas_call | solution.py:260
  466.4 1.9 bitcast_dynamic-update-slice_fusion
  468.3 2.0 slice_bitcast_fusion.1
  473.1 2.5 fusion.13
  (310 shorter events, 83.9 us)
Async XLA Ops:
  7.2 120.8 %all-gather.7.cloned.1.call-start = ((), (), s32[]{:S(2)}) async-start(), calls=%async_computation.3 | async-start | bytes 4718592 | tf_op jit(solution)/shard_map/all_gather | solution.py:443
  11.8 116.2 %all-gather.5.cloned.1.call-start = ((), (), s32[]{:S(2)}) async-start(), calls=%async_computation.2 | async-start | bytes 4718592 | tf_op jit(solution)/shard_map/all_gather | solution.py:461
  12.8 10.2 %collective-permute-start.3 = (bf16[320,256]{1,0:T(8,128)(2,1)}, bf16[320,256]{1,0:T(8,128)(2,1)}, u32[]{:S(2)}, u32[]{:S(2)}) collective-permute-start(bf16[320,256]{1,0:T(8,128)(2,1)} %get-tuple-element.129), channel_id=1, source_target_pairs={{0,8},{8,0},{16,24},{24,16},{1,9},{9,1},{17,25},{25,17},{2,10},{10... | collective-permute-start | bytes 491528 | tf_op jit(solution)/shard_map/ppermute | solution.py:341
  15.7 9.9 %collective-permute-start.4 = (bf16[320,256]{1,0:T(8,128)(2,1)}, bf16[320,256]{1,0:T(8,128)(2,1)}, u32[]{:S(2)}, u32[]{:S(2)}) collective-permute-start(bf16[320,256]{1,0:T(8,128)(2,1)} %get-tuple-element.129), channel_id=1, source_target_pairs={{0,16},{8,24},{16,0},{24,8},{1,17},{9,25},{17,1},{25,9},{2,18},{10... | collective-permute-start | bytes 491528 | tf_op jit(solution)/shard_map/ppermute | solution.py:341
  17.2 9.3 %collective-permute-start.5 = (bf16[320,256]{1,0:T(8,128)(2,1)}, bf16[320,256]{1,0:T(8,128)(2,1)}, u32[]{:S(2)}, u32[]{:S(2)}) collective-permute-start(bf16[320,256]{1,0:T(8,128)(2,1)} %get-tuple-element.129), channel_id=1, source_target_pairs={{0,24},{8,16},{16,8},{24,0},{1,25},{9,17},{17,9},{25,1},{2,26},{10... | collective-permute-start | bytes 491528 | tf_op jit(solution)/shard_map/ppermute | solution.py:341
  19.1 11.7 %collective-permute-start = (bf16[480,256]{1,0:T(8,128)(2,1)S(1)}, bf16[480,256]{1,0:T(8,128)(2,1)S(1)}, u32[]{:S(2)}, u32[]{:S(2)}) collective-permute-start(bf16[480,256]{1,0:T(8,128)(2,1)S(1)} %get-tuple-element.127), channel_id=1, source_target_pairs={{0,8},{8,0},{16,24},{24,16},{1,9},{9,1},{17,25},{25,17},{2,10},{10... | collective-permute-start | bytes 737288 | tf_op jit(solution)/shard_map/ppermute | solution.py:341
  21.1 14.9 %collective-permute-start.1 = (bf16[480,256]{1,0:T(8,128)(2,1)S(1)}, bf16[480,256]{1,0:T(8,128)(2,1)S(1)}, u32[]{:S(2)}, u32[]{:S(2)}) collective-permute-start(bf16[480,256]{1,0:T(8,128)(2,1)S(1)} %get-tuple-element.127), channel_id=1, source_target_pairs={{0,16},{8,24},{16,0},{24,8},{1,17},{9,25},{17,1},{25,9},{2,18},{10... | collective-permute-start | bytes 737288 | tf_op jit(solution)/shard_map/ppermute | solution.py:341
  23.0 13.7 %collective-permute-start.2 = (bf16[480,256]{1,0:T(8,128)(2,1)S(1)}, bf16[480,256]{1,0:T(8,128)(2,1)S(1)}, u32[]{:S(2)}, u32[]{:S(2)}) collective-permute-start(bf16[480,256]{1,0:T(8,128)(2,1)S(1)} %get-tuple-element.127), channel_id=1, source_target_pairs={{0,24},{8,16},{16,8},{24,0},{1,25},{9,17},{17,9},{25,1},{2,26},{10... | collective-permute-start | bytes 737288 | tf_op jit(solution)/shard_map/ppermute | solution.py:341
  28.3 15.3 %collective-permute-start.6 = (f32[256,320]{1,0:T(8,128)S(1)}, f32[256,320]{1,0:T(8,128)S(1)}, u32[]{:S(2)}, u32[]{:S(2)}) collective-permute-start(f32[256,320]{1,0:T(8,128)S(1)} %get-tuple-element.134), channel_id=1, source_target_pairs={{0,8},{8,0},{16,24},{24,16},{1,9},{9,1},{17,25},{25,17},{2,10},{10... | collective-permute-start | bytes 983048 | tf_op jit(solution)/shard_map/ppermute | solution.py:341
  29.4 23.1 %collective-permute-start.7 = (f32[256,320]{1,0:T(8,128)S(1)}, f32[256,320]{1,0:T(8,128)S(1)}, u32[]{:S(2)}, u32[]{:S(2)}) collective-permute-start(f32[256,320]{1,0:T(8,128)S(1)} %get-tuple-element.134), channel_id=1, source_target_pairs={{0,16},{8,24},{16,0},{24,8},{1,17},{9,25},{17,1},{25,9},{2,18},{10... | collective-permute-start | bytes 983048 | tf_op jit(solution)/shard_map/ppermute | solution.py:341
  30.8 21.7 %collective-permute-start.8 = (f32[256,320]{1,0:T(8,128)S(1)}, f32[256,320]{1,0:T(8,128)S(1)}, u32[]{:S(2)}, u32[]{:S(2)}) collective-permute-start(f32[256,320]{1,0:T(8,128)S(1)} %get-tuple-element.134), channel_id=1, source_target_pairs={{0,24},{8,16},{16,8},{24,0},{1,25},{9,17},{17,9},{25,1},{2,26},{10... | collective-permute-start | bytes 983048 | tf_op jit(solution)/shard_map/ppermute | solution.py:341
  52.6 19.5 %copy-start.1 = (f32[1024,320]{1,0:T(8,128)}, f32[1024,320]{1,0:T(8,128)S(1)}, u32[]{:S(2)}) copy-start(f32[1024,320]{1,0:T(8,128)S(1)} %constant_dynamic-update-slice_fusion.18.fk_ref) | copy-start | bytes 3932164
  52.6 20.6 %collective-permute-start.9 = (bf16[256,1024]{1,0:T(8,128)(2,1)S(1)}, bf16[256,1024]{1,0:T(8,128)(2,1)S(1)}, u32[]{:S(2)}, u32[]{:S(2)}) collective-permute-start(bf16[256,1024]{1,0:T(8,128)(2,1)S(1)} %convert_element_type.227), channel_id=1, source_target_pairs={{0,8},{8,0},{16,24},{24,16},{1,9},{9,1},{17,25},{25,17},{2,10},{10... | collective-permute-start | bytes 1572872 | tf_op jit(solution)/shard_map/ppermute | solution.py:341
  53.9 23.9 %collective-permute-start.10 = (bf16[256,1024]{1,0:T(8,128)(2,1)S(1)}, bf16[256,1024]{1,0:T(8,128)(2,1)S(1)}, u32[]{:S(2)}, u32[]{:S(2)}) collective-permute-start(bf16[256,1024]{1,0:T(8,128)(2,1)S(1)} %convert_element_type.227), channel_id=1, source_target_pairs={{0,16},{8,24},{16,0},{24,8},{1,17},{9,25},{17,1},{25,9},{2,18},{10... | collective-permute-start | bytes 1572872 | tf_op jit(solution)/shard_map/ppermute | solution.py:341
  54.7 23.1 %collective-permute-start.11 = (bf16[256,1024]{1,0:T(8,128)(2,1)S(1)}, bf16[256,1024]{1,0:T(8,128)(2,1)S(1)}, u32[]{:S(2)}, u32[]{:S(2)}) collective-permute-start(bf16[256,1024]{1,0:T(8,128)(2,1)S(1)} %convert_element_type.227), channel_id=1, source_target_pairs={{0,24},{8,16},{16,8},{24,0},{1,25},{9,17},{17,9},{25,1},{2,26},{10... | collective-permute-start | bytes 1572872 | tf_op jit(solution)/shard_map/ppermute | solution.py:341
  80.2 115.1 %reduce-scatter.3.cloned.1.call-start = ((), (), s32[]{:S(2)}) async-start(), calls=%async_computation.4 | async-start | bytes 4718592 | tf_op jit(solution)/shard_map/reduce_scatter | solution.py:463
  81.9 15.5 %collective-permute-start.12 = (bf16[3,352,256]{2,1,0:T(8,128)(2,1)}, bf16[3,352,256]{2,1,0:T(8,128)(2,1)}, u32[]{:S(2)}, u32[]{:S(2)}) collective-permute-start(bf16[3,352,256]{2,1,0:T(8,128)(2,1)} %pad_maximum_fusion.3), channel_id=1, source_target_pairs={{0,8},{8,0},{16,24},{24,16},{1,9},{9,1},{17,25},{25,17},{2,10},{10... | collective-permute-start | bytes 1622024 | tf_op jit(solution)/shard_map/ppermute | solution.py:341
  82.5 22.5 %collective-permute-start.13 = (bf16[3,352,256]{2,1,0:T(8,128)(2,1)}, bf16[3,352,256]{2,1,0:T(8,128)(2,1)}, u32[]{:S(2)}, u32[]{:S(2)}) collective-permute-start(bf16[3,352,256]{2,1,0:T(8,128)(2,1)} %pad_maximum_fusion.3), channel_id=1, source_target_pairs={{0,16},{8,24},{16,0},{24,8},{1,17},{9,25},{17,1},{25,9},{2,18},{10... | collective-permute-start | bytes 1622024 | tf_op jit(solution)/shard_map/ppermute | solution.py:341
  83.6 22.6 %collective-permute-start.14 = (bf16[3,352,256]{2,1,0:T(8,128)(2,1)}, bf16[3,352,256]{2,1,0:T(8,128)(2,1)}, u32[]{:S(2)}, u32[]{:S(2)}) collective-permute-start(bf16[3,352,256]{2,1,0:T(8,128)(2,1)} %pad_maximum_fusion.3), channel_id=1, source_target_pairs={{0,24},{8,16},{16,8},{24,0},{1,25},{9,17},{17,9},{25,1},{2,26},{10... | collective-permute-start | bytes 1622024 | tf_op jit(solution)/shard_map/ppermute | solution.py:341
  85.5 21.7 %copy-start.28 = (f32[3,352,256]{2,1,0:T(8,128)}, f32[3,352,256]{2,1,0:T(8,128)S(1)}, u32[]{:S(2)}) copy-start(f32[3,352,256]{2,1,0:T(8,128)S(1)} %pad_maximum_fusion.1) | copy-start | bytes 3244036
  107.4 11.1 %collective-permute-start.15 = (f32[352,256]{1,0:T(8,128)S(1)}, f32[352,256]{1,0:T(8,128)S(1)}, u32[]{:S(2)}, u32[]{:S(2)}) collective-permute-start(f32[352,256]{1,0:T(8,128)S(1)} %get-tuple-element.116), channel_id=1, source_target_pairs={{0,8},{8,0},{24,16},{1,9},{9,1},{25,17},{2,10},{10,2},{26,18},{3,1... | collective-permute-start | bytes 1081352 | tf_op jit(solution)/shard_map/ppermute | solution.py:460
  110.4 16.9 %collective-permute-start.16 = (f32[352,256]{1,0:T(8,128)S(1)}, f32[352,256]{1,0:T(8,128)S(1)}, u32[]{:S(2)}, u32[]{:S(2)}) collective-permute-start(f32[352,256]{1,0:T(8,128)S(1)} %get-tuple-element.115), channel_id=1, source_target_pairs={{0,16},{16,0},{24,8},{1,17},{17,1},{25,9},{2,18},{18,2},{26,10},{3... | collective-permute-start | bytes 1081352 | tf_op jit(solution)/shard_map/ppermute | solution.py:460
  113.1 14.9 %collective-permute-start.17 = (f32[352,256]{1,0:T(8,128)S(1)}, f32[352,256]{1,0:T(8,128)}, u32[]{:S(2)}, u32[]{:S(2)}) collective-permute-start(f32[352,256]{1,0:T(8,128)S(1)} %get-tuple-element.114), channel_id=1, source_target_pairs={{8,16},{16,8},{24,0},{9,17},{17,9},{25,1},{10,18},{18,10},{26,2},{... | collective-permute-start | bytes 1081352 | tf_op jit(solution)/shard_map/ppermute | solution.py:460
  145.5 108.6 %reduce-scatter.5.cloned.1.call-start = ((), (), s32[]{:S(2)}) async-start(), calls=%async_computation.5 | async-start | bytes 3604480 | tf_op jit(solution)/shard_map/reduce_scatter | solution.py:468
  159.5 13.7 %collective-permute-start.18 = (bf16[4,256,1024]{2,1,0:T(8,128)(2,1)}, bf16[4,256,1024]{2,1,0:T(8,128)(2,1)}, u32[]{:S(2)}, u32[]{:S(2)}) collective-permute-start(bf16[4,256,1024]{2,1,0:T(8,128)(2,1)} %dynamic-slice_bitcast_fusion), channel_id=1, source_target_pairs={{0,1},{1,0},{2,3},{3,2},{4,5},{5,4},{6,7},{7,6},{8,9},{9,8},{10,11... | collective-permute-start | bytes 6291464 | tf_op jit(solution)/shard_map/ppermute | solution.py:364
  173.2 172.2 %all-reduce.5.cloned.1.call-start = ((), (), s32[]{:S(2)}) async-start(), calls=%async_computation.6 | async-start | bytes 5242880 | tf_op jit(solution)/shard_map/psum | solution.py:500
  198.8 6.6 %collective-permute-start.21 = (bf16[4,4,32,1024]{3,2,1,0:T(8,128)(2,1)S(1)}, bf16[4,4,32,1024]{3,2,1,0:T(8,128)(2,1)S(1)}, u32[]{:S(2)}, u32[]{:S(2)}) collective-permute-start(bf16[4,4,32,1024]{3,2,1,0:T(8,128)(2,1)S(1)} %fusion.11), channel_id=1, source_target_pairs={{0,1},{1,0},{2,3},{3,2},{4,5},{5,4},{6,7},{7,6},{8,9},{9,8},{10,11... | collective-permute-start | bytes 3145736 | tf_op jit(solution)/shard_map/ppermute | solution.py:364
  203.3 32.0 %collective-permute-start.20 = (bf16[256,1024]{1,0:T(8,128)(2,1)}, bf16[256,1024]{1,0:T(8,128)(2,1)S(1)}, u32[]{:S(2)}, u32[]{:S(2)}) collective-permute-start(bf16[256,1024]{1,0:T(8,128)(2,1)} %get-tuple-element.60), channel_id=1, source_target_pairs={{0,4},{1,5},{2,6},{3,7},{4,0},{5,1},{6,2},{7,3},{8,12},{9,13},{10,... | collective-permute-start | bytes 1572872 | tf_op jit(solution)/shard_map/ppermute | solution.py:368
  204.6 30.9 %collective-permute-start.19 = (bf16[256,1024]{1,0:T(8,128)(2,1)}, bf16[256,1024]{1,0:T(8,128)(2,1)S(1)}, u32[]{:S(2)}, u32[]{:S(2)}) collective-permute-start(bf16[256,1024]{1,0:T(8,128)(2,1)} %get-tuple-element.59), channel_id=1, source_target_pairs={{0,2},{1,3},{2,0},{3,1},{4,6},{5,7},{6,4},{7,5},{8,10},{9,11},{10,... | collective-permute-start | bytes 1572872 | tf_op jit(solution)/shard_map/ppermute | solution.py:368
  205.9 29.6 %collective-permute-start.22 = (bf16[128,1024]{1,0:T(8,128)(2,1)S(1)}, bf16[128,1024]{1,0:T(8,128)(2,1)S(1)}, u32[]{:S(2)}, u32[]{:S(2)}) collective-permute-start(bf16[128,1024]{1,0:T(8,128)(2,1)S(1)} %get-tuple-element.91), channel_id=1, source_target_pairs={{0,8},{8,0},{16,24},{24,16},{1,9},{9,1},{17,25},{25,17},{2,10},{10... | collective-permute-start | bytes 786440 | tf_op jit(solution)/shard_map/ppermute | solution.py:355
  207.3 28.1 %collective-permute-start.23 = (bf16[128,1024]{1,0:T(8,128)(2,1)S(1)}, bf16[128,1024]{1,0:T(8,128)(2,1)S(1)}, u32[]{:S(2)}, u32[]{:S(2)}) collective-permute-start(bf16[128,1024]{1,0:T(8,128)(2,1)S(1)} %get-tuple-element.93), channel_id=1, source_target_pairs={{0,16},{8,24},{16,0},{24,8},{1,17},{9,25},{17,1},{25,9},{2,18},{10... | collective-permute-start | bytes 786440 | tf_op jit(solution)/shard_map/ppermute | solution.py:355
  208.8 26.7 %collective-permute-start.24 = (bf16[128,1024]{1,0:T(8,128)(2,1)S(1)}, bf16[128,1024]{1,0:T(8,128)(2,1)S(1)}, u32[]{:S(2)}, u32[]{:S(2)}) collective-permute-start(bf16[128,1024]{1,0:T(8,128)(2,1)S(1)} %get-tuple-element.92), channel_id=1, source_target_pairs={{0,24},{8,16},{16,8},{24,0},{1,25},{9,17},{17,9},{25,1},{2,26},{10... | collective-permute-start | bytes 786440 | tf_op jit(solution)/shard_map/ppermute | solution.py:355
  236.4 8.2 %collective-permute-start.25 = (bf16[32,1024]{1,0:T(8,128)(2,1)S(1)}, bf16[32,1024]{1,0:T(8,128)(2,1)S(1)}, u32[]{:S(2)}, u32[]{:S(2)}) collective-permute-start(bf16[32,1024]{1,0:T(8,128)(2,1)S(1)} %get-tuple-element.119), channel_id=1, source_target_pairs={{0,2},{1,3},{2,0},{3,1},{4,6},{5,7},{6,4},{7,5},{8,10},{9,11},{10,... | collective-permute-start | bytes 196616 | tf_op jit(solution)/shard_map/ppermute | solution.py:368
  238.5 6.7 %collective-permute-start.26 = (bf16[32,1024]{1,0:T(8,128)(2,1)S(1)}, bf16[32,1024]{1,0:T(8,128)(2,1)S(1)}, u32[]{:S(2)}, u32[]{:S(2)}) collective-permute-start(bf16[32,1024]{1,0:T(8,128)(2,1)S(1)} %get-tuple-element.121), channel_id=1, source_target_pairs={{0,4},{1,5},{2,6},{3,7},{4,0},{5,1},{6,2},{7,3},{8,12},{9,13},{10,... | collective-permute-start | bytes 196616 | tf_op jit(solution)/shard_map/ppermute | solution.py:368
  240.3 6.1 %collective-permute-start.27 = (bf16[32,1024]{1,0:T(8,128)(2,1)S(1)}, bf16[32,1024]{1,0:T(8,128)(2,1)S(1)}, u32[]{:S(2)}, u32[]{:S(2)}) collective-permute-start(bf16[32,1024]{1,0:T(8,128)(2,1)S(1)} %get-tuple-element.120), channel_id=1, source_target_pairs={{0,6},{1,7},{2,4},{3,5},{4,2},{5,3},{6,0},{7,1},{8,14},{9,15},{10,... | collective-permute-start | bytes 196616 | tf_op jit(solution)/shard_map/ppermute | solution.py:368
  241.7 13.7 %collective-permute-start.32 = (bf16[256,320]{1,0:T(8,128)(2,1)}, bf16[256,320]{1,0:T(8,128)(2,1)}, u32[]{:S(2)}, u32[]{:S(2)}) collective-permute-start(bf16[256,320]{1,0:T(8,128)(2,1)} %get-tuple-element.97), channel_id=1, source_target_pairs={{0,8},{8,0},{16,24},{24,16},{1,9},{9,1},{17,25},{25,17},{2,10},{10... | collective-permute-start | bytes 491528 | tf_op jit(solution)/shard_map/ppermute | solution.py:355
  243.2 16.4 %collective-permute-start.33 = (bf16[256,320]{1,0:T(8,128)(2,1)}, bf16[256,320]{1,0:T(8,128)(2,1)}, u32[]{:S(2)}, u32[]{:S(2)}) collective-permute-start(bf16[256,320]{1,0:T(8,128)(2,1)} %get-tuple-element.99), channel_id=1, source_target_pairs={{0,16},{8,24},{16,0},{24,8},{1,17},{9,25},{17,1},{25,9},{2,18},{10... | collective-permute-start | bytes 491528 | tf_op jit(solution)/shard_map/ppermute | solution.py:355
  244.6 15.0 %collective-permute-start.34 = (bf16[256,320]{1,0:T(8,128)(2,1)S(1)}, bf16[256,320]{1,0:T(8,128)(2,1)}, u32[]{:S(2)}, u32[]{:S(2)}) collective-permute-start(bf16[256,320]{1,0:T(8,128)(2,1)S(1)} %get-tuple-element.98), channel_id=1, source_target_pairs={{0,24},{8,16},{16,8},{24,0},{1,25},{9,17},{17,9},{25,1},{2,26},{10... | collective-permute-start | bytes 491528 | tf_op jit(solution)/shard_map/ppermute | solution.py:355
  254.0 11.6 %collective-permute-start.28 = (f32[32,1024]{1,0:T(8,128)S(1)}, f32[32,1024]{1,0:T(8,128)S(1)}, u32[]{:S(2)}, u32[]{:S(2)}) collective-permute-start(f32[32,1024]{1,0:T(8,128)S(1)} %fusion.38), channel_id=1, source_target_pairs={{16,24},{17,25},{18,26},{19,27},{20,28},{21,29},{22,30},{23,31}} | collective-permute-start | bytes 393224 | tf_op jit(solution)/shard_map/ppermute | solution.py:496
  254.7 11.0 %collective-permute-start.29 = (f32[32,1024]{1,0:T(8,128)S(1)}, f32[32,1024]{1,0:T(8,128)S(1)}, u32[]{:S(2)}, u32[]{:S(2)}) collective-permute-start(f32[32,1024]{1,0:T(8,128)S(1)} %fusion.38), channel_id=1, source_target_pairs={{8,24},{9,25},{10,26},{11,27},{12,28},{13,29},{14,30},{15,31}} | collective-permute-start | bytes 393224 | tf_op jit(solution)/shard_map/ppermute | solution.py:496
  255.5 10.3 %collective-permute-start.30 = (f32[32,1024]{1,0:T(8,128)S(1)}, f32[32,1024]{1,0:T(8,128)S(1)}, u32[]{:S(2)}, u32[]{:S(2)}) collective-permute-start(f32[32,1024]{1,0:T(8,128)S(1)} %fusion.38), channel_id=1, source_target_pairs={{0,24},{1,25},{2,26},{3,27},{4,28},{5,29},{6,30},{7,31}} | collective-permute-start | bytes 393224 | tf_op jit(solution)/shard_map/ppermute | solution.py:496
  265.7 6.2 %collective-permute-start.35 = (bf16[4,104,1024]{2,1,0:T(8,128)(2,1)}, bf16[4,104,1024]{2,1,0:T(8,128)(2,1)}, u32[]{:S(2)}, u32[]{:S(2)}) collective-permute-start(bf16[4,104,1024]{2,1,0:T(8,128)(2,1)} %fusion.15), channel_id=1, source_target_pairs={{0,1},{1,0},{2,3},{3,2},{4,5},{5,4},{6,7},{7,6},{8,9},{9,8},{10,11... | collective-permute-start | bytes 2555912 | tf_op jit(solution)/shard_map/ppermute | solution.py:364
  271.8 149.6 %all-gather.9.cloned.1.call-start = ((), (), s32[]{:S(2)}) async-start(), calls=%async_computation.7 | async-start | bytes 3514368 | tf_op jit(solution)/shard_map/all_gather | solution.py:525
  274.0 8.3 %collective-permute-start.36 = (bf16[416,256]{1,0:T(8,128)(2,1)S(1)}, bf16[416,256]{1,0:T(8,128)(2,1)S(1)}, u32[]{:S(2)}, u32[]{:S(2)}) collective-permute-start(bf16[416,256]{1,0:T(8,128)(2,1)S(1)} %get-tuple-element.94), channel_id=1, source_target_pairs={{0,8},{8,0},{16,24},{24,16},{1,9},{9,1},{17,25},{25,17},{2,10},{10... | collective-permute-start | bytes 638984 | tf_op jit(solution)/shard_map/ppermute | solution.py:355
  274.1 10.9 %collective-permute-start.37 = (bf16[416,256]{1,0:T(8,128)(2,1)S(1)}, bf16[416,256]{1,0:T(8,128)(2,1)S(1)}, u32[]{:S(2)}, u32[]{:S(2)}) collective-permute-start(bf16[416,256]{1,0:T(8,128)(2,1)S(1)} %get-tuple-element.96), channel_id=1, source_target_pairs={{0,16},{8,24},{16,0},{24,8},{1,17},{9,25},{17,1},{25,9},{2,18},{10... | collective-permute-start | bytes 638984 | tf_op jit(solution)/shard_map/ppermute | solution.py:355
  274.1 10.8 %collective-permute-start.38 = (bf16[416,256]{1,0:T(8,128)(2,1)S(1)}, bf16[416,256]{1,0:T(8,128)(2,1)S(1)}, u32[]{:S(2)}, u32[]{:S(2)}) collective-permute-start(bf16[416,256]{1,0:T(8,128)(2,1)S(1)} %get-tuple-element.95), channel_id=1, source_target_pairs={{0,24},{8,16},{16,8},{24,0},{1,25},{9,17},{17,9},{25,1},{2,26},{10... | collective-permute-start | bytes 638984 | tf_op jit(solution)/shard_map/ppermute | solution.py:355
  286.1 130.5 %collective-permute-start.42 = (f32[352,256]{1,0:T(8,128)}, f32[352,256]{1,0:T(8,128)}, u32[]{:S(2)}, u32[]{:S(2)}) collective-permute-start(f32[352,256]{1,0:T(8,128)} %get-tuple-element.107), channel_id=1, source_target_pairs={{0,8},{8,0},{16,24},{1,9},{9,1},{17,25},{2,10},{10,2},{18,26},{3,1... | collective-permute-start | bytes 1081352 | tf_op jit(solution)/shard_map/ppermute | solution.py:531
  289.8 10.7 %collective-permute-start.39 = (bf16[104,256]{1,0:T(8,128)(2,1)S(1)}, bf16[104,256]{1,0:T(8,128)(2,1)S(1)}, u32[]{:S(2)}, u32[]{:S(2)}) collective-permute-start(bf16[104,256]{1,0:T(8,128)(2,1)S(1)} %get-tuple-element.122), channel_id=1, source_target_pairs={{0,2},{1,3},{2,0},{3,1},{4,6},{5,7},{6,4},{7,5},{8,10},{9,11},{10,... | collective-permute-start | bytes 159752 | tf_op jit(solution)/shard_map/ppermute | solution.py:368
  292.0 10.6 %collective-permute-start.40 = (bf16[104,256]{1,0:T(8,128)(2,1)S(1)}, bf16[104,256]{1,0:T(8,128)(2,1)S(1)}, u32[]{:S(2)}, u32[]{:S(2)}) collective-permute-start(bf16[104,256]{1,0:T(8,128)(2,1)S(1)} %get-tuple-element.124), channel_id=1, source_target_pairs={{0,4},{1,5},{2,6},{3,7},{4,0},{5,1},{6,2},{7,3},{8,12},{9,13},{10,... | collective-permute-start | bytes 159752 | tf_op jit(solution)/shard_map/ppermute | solution.py:368
  294.3 51.0 %copy-start.48 = (bf16[256,1024]{1,0:T(8,128)(2,1)S(1)}, bf16[256,1024]{1,0:T(8,128)(2,1)}, u32[]{:S(2)}) copy-start(bf16[256,1024]{1,0:T(8,128)(2,1)} %get-tuple-element.70) | copy-start | bytes 1572868
  294.3 9.0 %collective-permute-start.41 = (bf16[104,256]{1,0:T(8,128)(2,1)S(1)}, bf16[104,256]{1,0:T(8,128)(2,1)S(1)}, u32[]{:S(2)}, u32[]{:S(2)}) collective-permute-start(bf16[104,256]{1,0:T(8,128)(2,1)S(1)} %get-tuple-element.123), channel_id=1, source_target_pairs={{0,6},{1,7},{2,4},{3,5},{4,2},{5,3},{6,0},{7,1},{8,14},{9,15},{10,... | collective-permute-start | bytes 159752 | tf_op jit(solution)/shard_map/ppermute | solution.py:368
  297.6 120.9 %collective-permute-start.43 = (f32[352,256]{1,0:T(8,128)}, f32[352,256]{1,0:T(8,128)}, u32[]{:S(2)}, u32[]{:S(2)}) collective-permute-start(f32[352,256]{1,0:T(8,128)} %get-tuple-element.106), channel_id=1, source_target_pairs={{0,16},{8,24},{16,0},{1,17},{9,25},{17,1},{2,18},{10,26},{18,2},{3... | collective-permute-start | bytes 1081352 | tf_op jit(solution)/shard_map/ppermute | solution.py:531
  300.5 165.8 %collective-permute-start.44 = (f32[352,256]{1,0:T(8,128)}, f32[352,256]{1,0:T(8,128)}, u32[]{:S(2)}, u32[]{:S(2)}) collective-permute-start(f32[352,256]{1,0:T(8,128)} %get-tuple-element.105), channel_id=1, source_target_pairs={{0,24},{8,16},{16,8},{1,25},{9,17},{17,9},{2,26},{10,18},{18,10},{... | collective-permute-start | bytes 1081352 | tf_op jit(solution)/shard_map/ppermute | solution.py:531
  304.0 169.1 %all-gather.11.cloned.1.call-start = ((), (), s32[]{:S(2)}) async-start(), calls=%async_computation.8 | async-start | bytes 2359296 | tf_op jit(solution)/shard_map/all_gather | solution.py:546
  345.3 74.9 %collective-permute-start.31 = (bf16[256,1024]{1,0:T(8,128)(2,1)S(1)}, bf16[256,1024]{1,0:T(8,128)(2,1)S(1)}, u32[]{:S(2)}, u32[]{:S(2)}) collective-permute-start(bf16[256,1024]{1,0:T(8,128)(2,1)S(1)} %copy-done.48), channel_id=1, source_target_pairs={{0,6},{1,7},{2,4},{3,5},{4,2},{5,3},{6,0},{7,1},{8,14},{9,15},{10,... | collective-permute-start | bytes 1572872 | tf_op jit(solution)/shard_map/ppermute | solution.py:368
  348.5 71.7 %copy-start.33 = (f32[256,1024]{1,0:T(8,128)S(1)}, f32[256,1024]{1,0:T(8,128)}, u32[]{:S(2)}) copy-start(f32[256,1024]{1,0:T(8,128)} %dynamic-slice_bitcast_fusion.1) | copy-start | bytes 3145732
  348.5 71.7 %copy-start.50 = (bf16[256,1024]{1,0:T(8,128)(2,1)S(1)}, bf16[256,1024]{1,0:T(8,128)(2,1)}, u32[]{:S(2)}) copy-start(bf16[256,1024]{1,0:T(8,128)(2,1)} %copy-done.49) | copy-start | bytes 1572868
  348.5 71.7 %copy-start.52 = (bf16[256,1024]{1,0:T(8,128)(2,1)S(1)}, bf16[256,1024]{1,0:T(8,128)(2,1)}, u32[]{:S(2)}) copy-start(bf16[256,1024]{1,0:T(8,128)(2,1)} %copy-done.51) | copy-start | bytes 1572868
  422.7 8.3 %collective-permute-start.45 = (f32[32,1024]{1,0:T(8,128)S(1)}, f32[32,1024]{1,0:T(8,128)S(1)}, u32[]{:S(2)}, u32[]{:S(2)}) collective-permute-start(f32[32,1024]{1,0:T(8,128)S(1)} %get-tuple-element.113), channel_id=1, source_target_pairs={{24,0},{25,1},{26,2},{27,3},{28,4},{29,5},{30,6},{31,7}} | collective-permute-start | bytes 393224 | tf_op jit(solution)/shard_map/ppermute | solution.py:543
  424.0 7.0 %collective-permute-start.46 = (f32[32,1024]{1,0:T(8,128)S(1)}, f32[32,1024]{1,0:T(8,128)S(1)}, u32[]{:S(2)}, u32[]{:S(2)}) collective-permute-start(f32[32,1024]{1,0:T(8,128)S(1)} %get-tuple-element.112), channel_id=1, source_target_pairs={{24,8},{25,9},{26,10},{27,11},{28,12},{29,13},{30,14},{31,15}} | collective-permute-start | bytes 393224 | tf_op jit(solution)/shard_map/ppermute | solution.py:543
  424.7 6.3 %collective-permute-start.47 = (f32[32,1024]{1,0:T(8,128)S(1)}, f32[32,1024]{1,0:T(8,128)S(1)}, u32[]{:S(2)}, u32[]{:S(2)}) collective-permute-start(f32[32,1024]{1,0:T(8,128)S(1)} %get-tuple-element.111), channel_id=1, source_target_pairs={{24,16},{25,17},{26,18},{27,19},{28,20},{29,21},{30,22},{31,23}} | collective-permute-start | bytes 393224 | tf_op jit(solution)/shard_map/ppermute | solution.py:543
  432.0 32.3 %collective-permute-start.48 = (f32[352,256]{1,0:T(8,128)}, f32[352,256]{1,0:T(8,128)}, u32[]{:S(2)}, u32[]{:S(2)}) collective-permute-start(f32[352,256]{1,0:T(8,128)} %get-tuple-element.110), channel_id=1, source_target_pairs={{0,8},{8,0},{16,24},{1,9},{9,1},{17,25},{2,10},{10,2},{18,26},{3,1... | collective-permute-start | bytes 1081352 | tf_op jit(solution)/shard_map/ppermute | solution.py:531
  435.2 30.1 %collective-permute-start.49 = (f32[352,256]{1,0:T(8,128)}, f32[352,256]{1,0:T(8,128)}, u32[]{:S(2)}, u32[]{:S(2)}) collective-permute-start(f32[352,256]{1,0:T(8,128)} %get-tuple-element.109), channel_id=1, source_target_pairs={{0,16},{8,24},{16,0},{1,17},{9,25},{17,1},{2,18},{10,26},{18,2},{3... | collective-permute-start | bytes 1081352 | tf_op jit(solution)/shard_map/ppermute | solution.py:531
  439.7 26.7 %collective-permute-start.50 = (f32[352,256]{1,0:T(8,128)S(1)}, f32[352,256]{1,0:T(8,128)}, u32[]{:S(2)}, u32[]{:S(2)}) collective-permute-start(f32[352,256]{1,0:T(8,128)S(1)} %get-tuple-element.108), channel_id=1, source_target_pairs={{0,24},{8,16},{16,8},{1,25},{9,17},{17,9},{2,26},{10,18},{18,10},{... | collective-permute-start | bytes 1081352 | tf_op jit(solution)/shard_map/ppermute | solution.py:531
  (55 other events, 275.0 us)
Sparse Core Ops, SparseCore 0:
  11.9 49.8 all-gather.6
  80.3 47.0 all-gather.4
  145.6 49.6 reduce-scatter.2
  198.2 55.7 reduce-scatter.4
  272.0 73.3 all-reduce.4
  348.6 59.4 all-gather.8
  442.6 28.1 all-gather.10

commit v7 on v6

--- a/solution.py
+++ b/solution.py
@@ -524,7 +524,6 @@
     factor_piece = lax.dynamic_slice_in_dim(factor_piece, mz * height, height, 0) + grad_factor
     factor_all = lax.all_gather(factor_piece, ("dp", "mp"), axis=0, tiled=True).reshape(n_dp, n_mp * height, d_own)
     factor_tile = pick(factor_all, me)
-    gain_grad = factor_tile[factor_w.shape[1] : factor_w.shape[1] + 2]
 
     def give_back(whole):
         pieces = [lax.dynamic_slice_in_dim(whole, (me ^ s) * d_own, d_own, 1) for s in range(n_dp)]
@@ -536,13 +535,16 @@
     ortho = after(ortho, factor_all)
     branch += [pass_chip(after(part, gram), 3) for part in last]
     ortho = after(ortho, *branch[3:])
-    block_out = (residual + sum(part.astype(F32) for part in branch)).astype(BF)
     out_ortho = lax.dynamic_slice_in_dim(ortho, me * out_own, out_own, 0)
     for s in shifts:
         piece = lax.dynamic_slice_in_dim(ortho, (me ^ s) * out_own, out_own, 0)
         piece = lax.ppermute(piece, "dp", [(j, j ^ s) for j in range(FFN, n_dp)])
         out_ortho = jnp.where(me ^ s == FFN, piece, out_ortho)
     out_pair = after(jnp.stack([out_tile, out_ortho]), factor_all)
+    branch = [after(part, out_pair) for part in branch]
+    block_out = (residual + sum(part.astype(F32) for part in branch)).astype(BF)
+    factor_tile = after(factor_tile, out_pair)
+    gain_grad = factor_tile[factor_w.shape[1] : factor_w.shape[1] + 2]
     out_both = lax.all_gather(out_pair, "mp", axis=1, tiled=True)
     new_out_mom = out_both[0]
     new_out_w = out_w - LEARN * 0.2 * math.sqrt(D) * out_both[1]

time: 493 us -> 495 us (level)
  no operation moved by 1% of the time
where the time goes in v7:
time: 495 us; the launch traced here: 486 us
  Pallas kernels  157 us (32%)
  waiting for transfers between devices  126 us (25%)
  starting transfers between devices  86.7 us (18%)
  local copies, waits for them, and re-layouts  59.8 us (12%)
  other arithmetic  32.1 us (6%)
  between operations  16.6 us (3%)
  matrix products  7.76 us (2%)
    pallas_call x1, Pallas kernels, ns_big(): pl.pallas_call(ns_body, out_shape=jax.ShapeDtypeStruct((w, d), F32), in_s...  68.1 us
    psum x1, waiting for transfers between devices, body(): gram = lax.psum(gram_part, 'mp')  41.3 us
    ppermute x15, waiting for transfers between devices, gather_dp(): lax.ppermute(own, 'dp', dp_pairs(s))  36 us
    pallas_call x1, Pallas kernels, attn_bwd(): pl.pallas_call(functools.partial(attn_bwd_body, *pairs), out_shape=(shape...  25.9 us
    dynamic_update_slice x32, local copies, waits for them, and re-layouts, place(): out = lax.dynamic_update_slice_in_dim(out, part, (me ^ shift) * step, axis)  20.6 us
    ppermute x15, starting transfers between devices, gather_dp(): lax.ppermute(own, 'dp', dp_pairs(s))  20.6 us
    unnamed x122, local copies, waits for them, and re-layouts  19.9 us
    pallas_call x1, Pallas kernels, ns_factor(): pl.pallas_call(ns_factor_body, out_shape=shape(own.shape), in_specs=[VM]...  18.7 us
  transfers between devices with their start and end apart: 58, of which 17 were waited for; matrix products, arithmetic and copies ran while one was open for 15% of the time, Pallas kernels for 29%

profile of v7, /device:TPU:0, one launch (start us, length us, event | category | flops | bytes accessed | tf_op | source)
XLA Modules:
  0.0 485.8 jit_solution(3887895219252141541)
XLA Ops:
  9.2 2.6 fusion.14
  12.8 2.9 collective-permute-start.3
  15.7 1.5 collective-permute-start.4
  19.1 2.0 collective-permute-start
  21.1 1.5 collective-permute-start.1
  30.8 2.0 collective-permute-start.8
  33.5 2.5 collective-permute-done.1
  37.5 1.7 fusion.54.fq_ref
  39.2 4.4 collective-permute-done.6
  43.6 8.9 %collective-permute-done.7 = f32[256,320]{1,0:T(8,128)S(1)} collective-permute-done((f32[256,320]{1,0:T(8,128)S(1)}, f32[256,320]{1,0:T(8,128)S(1)}, u32[]{:S(2)}, u32[]{:S(2)}) %collective-permute-start.7) | collective-permute-done | bytes 327712 | tf_op jit(solution)/shard_map/ppermute | solution.py:341
  54.7 1.4 collective-permute-start.11
  56.1 15.9 %attn_fwd.1 = (bf16[256,1024]{1,0:T(8,128)(2,1)S(1)}, f32[256,16]{1,0:T(8,128)S(1)}, bf16[256,1024]{1,0:T(8,128)(2,1)S(1)}, bf16[1024,1024]{1,0:T(8,128)(2,1)S(1)}, bf16[1024,1024]{1,0:T(8,128)(2,1)S(1)}) custom-call(s32[1]{0:T(128)} %bitcast.base_ref, f32[256,480]{1,0:T(8,128)S(1)} %fusion.54.fq_ref, f32[1024,320]{1,0:T(8,128)S(1)} %constant_dynamic-update-slice_fusion.18.fk_ref), custom_call_target="tpu_custom_call" | custom-call | flops 18400000000 | bytes 1048576 | tf_op jit(solution)/shard_map/attn_fwd/pallas_call | solution.py:87
  74.9 2.9 collective-permute-done.10
  83.6 1.8 collective-permute-start.14
  87.1 10.3 %collective-permute-done.12 = bf16[3,352,256]{2,1,0:T(8,128)(2,1)} collective-permute-done((bf16[3,352,256]{2,1,0:T(8,128)(2,1)}, bf16[3,352,256]{2,1,0:T(8,128)(2,1)}, u32[]{:S(2)}, u32[]{:S(2)}) %collective-permute-start.12) | collective-permute-done | bytes 540704 | tf_op jit(solution)/shard_map/ppermute | solution.py:341
  98.5 6.5 %collective-permute-done.13 = bf16[3,352,256]{2,1,0:T(8,128)(2,1)} collective-permute-done((bf16[3,352,256]{2,1,0:T(8,128)(2,1)}, bf16[3,352,256]{2,1,0:T(8,128)(2,1)}, u32[]{:S(2)}, u32[]{:S(2)}) %collective-permute-start.13) | collective-permute-done | bytes 540704 | tf_op jit(solution)/shard_map/ppermute | solution.py:341
  107.4 3.0 collective-permute-start.15
  110.4 2.7 collective-permute-start.16
  114.4 4.1 collective-permute-done.15
  118.5 8.8 %collective-permute-done.16 = f32[352,256]{1,0:T(8,128)S(1)} collective-permute-done((f32[352,256]{1,0:T(8,128)S(1)}, f32[352,256]{1,0:T(8,128)S(1)}, u32[]{:S(2)}, u32[]{:S(2)}) %collective-permute-start.16) | collective-permute-done | bytes 360480 | tf_op jit(solution)/shard_map/ppermute | solution.py:460
  128.0 17.4 %ffn_tokens.1 = (bf16[2048,1024]{1,0:T(8,128)(2,1)}, bf16[2048,1024]{1,0:T(8,128)(2,1)}, bf16[2048,352]{1,0:T(8,128)(2,1)}, bf16[2048,352]{1,0:T(8,128)(2,1)}, bf16[2048,352]{1,0:T(8,128)(2,1)}) custom-call(bf16[2048,1024]{1,0:T(8,128)(2,1)} %all-gather.5.cloned.1.call-done.x_ref, bf16[2048,1024]{1,0:T(8,128)(2,1)} %all-gather.7.cloned.1.call-done.g_ref, ...), custom_call_target="tpu_custom_call" | custom-call | flops 23000000512 | bytes 1048576 | tf_op jit(solution)/shard_map/ffn_tokens/pallas_call | solution.py:280
  145.5 10.8 %reduce-scatter.5.cloned.1.call-start = ((), (), s32[]{:S(2)}) async-start(), calls=%async_computation.5 | async-start | bytes 3604480 | tf_op jit(solution)/shard_map/reduce_scatter | solution.py:468
  156.3 3.2 dynamic-slice_bitcast_fusion
  159.6 2.2 copy-done.4
  161.8 1.4 copy-done.7
  164.6 8.5 %ffn_grads.1 = bf16[1408,1024]{1,0:T(8,128)(2,1)} custom-call(bf16[2048,352]{1,0:T(8,128)(2,1)S(1)} %copy-done.6, bf16[2048,352]{1,0:T(8,128)(2,1)S(1)} %copy-done.7, bf16[2048,352]{1,0:T(8,128)(2,1)S(1)} %copy-done.8, bf16[2048,1024]{1,0:T(8,128)(2,1)S(1)} %copy-done.4, bf16[2048,1024]{1,0:T(8,128)(2,1)} %all-gather.7.cloned.1.call-done.g_ref), custom_call_target="tpu_custom_call" | custom-call | flops 11500000256 | bytes 1048576 | tf_op jit(solution)/shard_map/ffn_grads/pallas_call | solution.py:300
  173.2 3.2 convert_add_fusion
  178.7 16.6 %reduce-scatter.3.cloned.1.call-done = bf16[256,1024]{1,0:T(8,128)(2,1)} async-done(((bf16[2048,1024]{1,0:T(8,128)(2,1)}), bf16[256,1024]{1,0:T(8,128)(2,1)}) %reduce-scatter.3.cloned.1.call-update) | async-done | bytes 524304 | tf_op jit(solution)/shard_map/reduce_scatter | solution.py:463
  205.9 1.5 collective-permute-start.22
  207.3 1.5 collective-permute-start.23
  209.4 25.9 %attn_bwd.1 = (f32[256,480]{1,0:T(8,128)S(1)}, f32[1024,320]{1,0:T(8,128)S(1)}) custom-call(s32[1]{0:T(128)} %bitcast.base_ref, bf16[256,1024]{1,0:T(8,128)(2,1)S(1)} %copy-done.14, bf16[1024,1024]{1,0:T(8,128)(2,1)S(1)} %copy-done.10, bf16[1024,1024]{1,0:T(8,128)(2,1)S(1)} %copy-done.12, bf16[256,1024]{1,0:T(8,128)(2,1)S(1)} %convolution_convert_fusion.do_ref, ...), custom_call_target="tpu_custom_call" | custom-call | flops 29899999232 | bytes 1048576 | tf_op jit(solution)/shard_map/attn_bwd/pallas_call | solution.py:134
  236.4 2.1 collective-permute-start.25
  238.5 1.8 collective-permute-start.26
  241.7 1.4 collective-permute-start.31
  243.2 1.5 collective-permute-start.32
  247.3 6.7 %reduce-scatter.5.cloned.1.call-done = bf16[352,1024]{1,0:T(8,128)(2,1)} async-done(((bf16[1408,1024]{1,0:T(8,128)(2,1)}), bf16[352,1024]{1,0:T(8,128)(2,1)}) %reduce-scatter.5.cloned.1.call-update) | async-done | bytes 720912 | tf_op jit(solution)/shard_map/reduce_scatter | solution.py:468
  255.5 4.1 collective-permute-start.30
  261.3 1.8 fusion.6
  268.0 2.2 gram_upper.1
  270.3 1.6 copy-done
  271.9 2.0 bitcast_add_fusion.1
  274.1 3.4 collective-permute-start.37
  278.8 3.4 collective-permute-done.35
  282.2 2.7 collective-permute-done.36
  286.1 3.7 collective-permute-start.41
  289.8 2.2 collective-permute-start.38
  292.0 2.3 collective-permute-start.39
  297.6 2.9 collective-permute-start.42
  300.5 2.1 collective-permute-start.43
  304.0 41.3 %all-reduce.5.cloned.1.call-done.g_ref = f32[256,2560]{1,0:T(8,128)} async-done(((f32[256,2560]{1,0:T(8,128)}), f32[256,2560]{1,0:T(8,128)}) %all-reduce.5.cloned.1.call-update) | async-done | bytes 2621456 | tf_op jit(solution)/shard_map/psum | solution.py:500
  346.7 1.7 copy-done.5
  348.5 68.1 %ns_gram.1 = f32[352,1024]{1,0:T(8,128)S(1)} custom-call(f32[256,2560]{1,0:T(8,128)S(1)} %copy-done.5, f32[352,1024]{1,0:T(8,128)S(1)} %pad_select_fusion.y_ref), custom_call_target="tpu_custom_call" | custom-call | flops 81649999872 | bytes 1048576 | tf_op jit(solution)/shard_map/ns_gram/pallas_call | solution.py:198
  416.6 1.8 constant_dynamic-update-slice_fusion.2
  418.4 1.7 constant_dynamic-update-slice_fusion.1
  424.0 4.4 collective-permute-done.45
  429.4 3.2 collective-permute-start.48
  432.7 3.7 collective-permute-start.49
  436.4 2.0 collective-permute-start.50
  439.2 2.0 copy-done.3
  441.1 18.7 %ns_factor.1 = f32[832,256]{1,0:T(8,128)S(1)} custom-call(f32[4,832,256]{2,1,0:T(8,128)S(1)} %bitcast.184, f32[832,256]{1,0:T(8,128)S(1)} %dynamic-slice_bitcast_fusion.2.own_ref), custom_call_target="tpu_custom_call" | custom-call | flops 25300000768 | bytes 1048576 | tf_op jit(solution)/shard_map/ns_factor/pallas_call | solution.py:260
  461.7 2.3 add_convert_fusion
  468.5 1.9 bitcast_dynamic-update-slice_fusion
  470.3 2.0 slice_bitcast_fusion.2
  475.2 2.5 fusion.13
  (310 shorter events, 84.4 us)
Async XLA Ops:
  7.2 120.8 %all-gather.7.cloned.1.call-start = ((), (), s32[]{:S(2)}) async-start(), calls=%async_computation.3 | async-start | bytes 4718592 | tf_op jit(solution)/shard_map/all_gather | solution.py:443
  11.8 116.2 %all-gather.5.cloned.1.call-start = ((), (), s32[]{:S(2)}) async-start(), calls=%async_computation.2 | async-start | bytes 4718592 | tf_op jit(solution)/shard_map/all_gather | solution.py:461
  12.8 10.2 %collective-permute-start.3 = (bf16[320,256]{1,0:T(8,128)(2,1)}, bf16[320,256]{1,0:T(8,128)(2,1)}, u32[]{:S(2)}, u32[]{:S(2)}) collective-permute-start(bf16[320,256]{1,0:T(8,128)(2,1)} %get-tuple-element.139), channel_id=1, source_target_pairs={{0,8},{8,0},{16,24},{24,16},{1,9},{9,1},{17,25},{25,17},{2,10},{10... | collective-permute-start | bytes 491528 | tf_op jit(solution)/shard_map/ppermute | solution.py:341
  15.7 9.9 %collective-permute-start.4 = (bf16[320,256]{1,0:T(8,128)(2,1)}, bf16[320,256]{1,0:T(8,128)(2,1)}, u32[]{:S(2)}, u32[]{:S(2)}) collective-permute-start(bf16[320,256]{1,0:T(8,128)(2,1)} %get-tuple-element.139), channel_id=1, source_target_pairs={{0,16},{8,24},{16,0},{24,8},{1,17},{9,25},{17,1},{25,9},{2,18},{10... | collective-permute-start | bytes 491528 | tf_op jit(solution)/shard_map/ppermute | solution.py:341
  17.2 9.3 %collective-permute-start.5 = (bf16[320,256]{1,0:T(8,128)(2,1)}, bf16[320,256]{1,0:T(8,128)(2,1)}, u32[]{:S(2)}, u32[]{:S(2)}) collective-permute-start(bf16[320,256]{1,0:T(8,128)(2,1)} %get-tuple-element.139), channel_id=1, source_target_pairs={{0,24},{8,16},{16,8},{24,0},{1,25},{9,17},{17,9},{25,1},{2,26},{10... | collective-permute-start | bytes 491528 | tf_op jit(solution)/shard_map/ppermute | solution.py:341
  19.1 11.7 %collective-permute-start = (bf16[480,256]{1,0:T(8,128)(2,1)S(1)}, bf16[480,256]{1,0:T(8,128)(2,1)S(1)}, u32[]{:S(2)}, u32[]{:S(2)}) collective-permute-start(bf16[480,256]{1,0:T(8,128)(2,1)S(1)} %get-tuple-element.137), channel_id=1, source_target_pairs={{0,8},{8,0},{16,24},{24,16},{1,9},{9,1},{17,25},{25,17},{2,10},{10... | collective-permute-start | bytes 737288 | tf_op jit(solution)/shard_map/ppermute | solution.py:341
  21.1 14.9 %collective-permute-start.1 = (bf16[480,256]{1,0:T(8,128)(2,1)S(1)}, bf16[480,256]{1,0:T(8,128)(2,1)S(1)}, u32[]{:S(2)}, u32[]{:S(2)}) collective-permute-start(bf16[480,256]{1,0:T(8,128)(2,1)S(1)} %get-tuple-element.137), channel_id=1, source_target_pairs={{0,16},{8,24},{16,0},{24,8},{1,17},{9,25},{17,1},{25,9},{2,18},{10... | collective-permute-start | bytes 737288 | tf_op jit(solution)/shard_map/ppermute | solution.py:341
  23.0 13.7 %collective-permute-start.2 = (bf16[480,256]{1,0:T(8,128)(2,1)S(1)}, bf16[480,256]{1,0:T(8,128)(2,1)S(1)}, u32[]{:S(2)}, u32[]{:S(2)}) collective-permute-start(bf16[480,256]{1,0:T(8,128)(2,1)S(1)} %get-tuple-element.137), channel_id=1, source_target_pairs={{0,24},{8,16},{16,8},{24,0},{1,25},{9,17},{17,9},{25,1},{2,26},{10... | collective-permute-start | bytes 737288 | tf_op jit(solution)/shard_map/ppermute | solution.py:341
  28.3 15.3 %collective-permute-start.6 = (f32[256,320]{1,0:T(8,128)S(1)}, f32[256,320]{1,0:T(8,128)S(1)}, u32[]{:S(2)}, u32[]{:S(2)}) collective-permute-start(f32[256,320]{1,0:T(8,128)S(1)} %get-tuple-element.144), channel_id=1, source_target_pairs={{0,8},{8,0},{16,24},{24,16},{1,9},{9,1},{17,25},{25,17},{2,10},{10... | collective-permute-start | bytes 983048 | tf_op jit(solution)/shard_map/ppermute | solution.py:341
  29.4 23.1 %collective-permute-start.7 = (f32[256,320]{1,0:T(8,128)S(1)}, f32[256,320]{1,0:T(8,128)S(1)}, u32[]{:S(2)}, u32[]{:S(2)}) collective-permute-start(f32[256,320]{1,0:T(8,128)S(1)} %get-tuple-element.144), channel_id=1, source_target_pairs={{0,16},{8,24},{16,0},{24,8},{1,17},{9,25},{17,1},{25,9},{2,18},{10... | collective-permute-start | bytes 983048 | tf_op jit(solution)/shard_map/ppermute | solution.py:341
  30.8 21.7 %collective-permute-start.8 = (f32[256,320]{1,0:T(8,128)S(1)}, f32[256,320]{1,0:T(8,128)S(1)}, u32[]{:S(2)}, u32[]{:S(2)}) collective-permute-start(f32[256,320]{1,0:T(8,128)S(1)} %get-tuple-element.144), channel_id=1, source_target_pairs={{0,24},{8,16},{16,8},{24,0},{1,25},{9,17},{17,9},{25,1},{2,26},{10... | collective-permute-start | bytes 983048 | tf_op jit(solution)/shard_map/ppermute | solution.py:341
  52.6 19.5 %copy-start.1 = (f32[1024,320]{1,0:T(8,128)}, f32[1024,320]{1,0:T(8,128)S(1)}, u32[]{:S(2)}) copy-start(f32[1024,320]{1,0:T(8,128)S(1)} %constant_dynamic-update-slice_fusion.18.fk_ref) | copy-start | bytes 3932164
  52.6 20.6 %collective-permute-start.9 = (bf16[256,1024]{1,0:T(8,128)(2,1)S(1)}, bf16[256,1024]{1,0:T(8,128)(2,1)S(1)}, u32[]{:S(2)}, u32[]{:S(2)}) collective-permute-start(bf16[256,1024]{1,0:T(8,128)(2,1)S(1)} %convert_element_type.227), channel_id=1, source_target_pairs={{0,8},{8,0},{16,24},{24,16},{1,9},{9,1},{17,25},{25,17},{2,10},{10... | collective-permute-start | bytes 1572872 | tf_op jit(solution)/shard_map/ppermute | solution.py:341
  53.9 23.9 %collective-permute-start.10 = (bf16[256,1024]{1,0:T(8,128)(2,1)S(1)}, bf16[256,1024]{1,0:T(8,128)(2,1)S(1)}, u32[]{:S(2)}, u32[]{:S(2)}) collective-permute-start(bf16[256,1024]{1,0:T(8,128)(2,1)S(1)} %convert_element_type.227), channel_id=1, source_target_pairs={{0,16},{8,24},{16,0},{24,8},{1,17},{9,25},{17,1},{25,9},{2,18},{10... | collective-permute-start | bytes 1572872 | tf_op jit(solution)/shard_map/ppermute | solution.py:341
  54.7 23.1 %collective-permute-start.11 = (bf16[256,1024]{1,0:T(8,128)(2,1)S(1)}, bf16[256,1024]{1,0:T(8,128)(2,1)S(1)}, u32[]{:S(2)}, u32[]{:S(2)}) collective-permute-start(bf16[256,1024]{1,0:T(8,128)(2,1)S(1)} %convert_element_type.227), channel_id=1, source_target_pairs={{0,24},{8,16},{16,8},{24,0},{1,25},{9,17},{17,9},{25,1},{2,26},{10... | collective-permute-start | bytes 1572872 | tf_op jit(solution)/shard_map/ppermute | solution.py:341
  80.2 115.1 %reduce-scatter.3.cloned.1.call-start = ((), (), s32[]{:S(2)}) async-start(), calls=%async_computation.4 | async-start | bytes 4718592 | tf_op jit(solution)/shard_map/reduce_scatter | solution.py:463
  81.9 15.5 %collective-permute-start.12 = (bf16[3,352,256]{2,1,0:T(8,128)(2,1)}, bf16[3,352,256]{2,1,0:T(8,128)(2,1)}, u32[]{:S(2)}, u32[]{:S(2)}) collective-permute-start(bf16[3,352,256]{2,1,0:T(8,128)(2,1)} %pad_maximum_fusion.3), channel_id=1, source_target_pairs={{0,8},{8,0},{16,24},{24,16},{1,9},{9,1},{17,25},{25,17},{2,10},{10... | collective-permute-start | bytes 1622024 | tf_op jit(solution)/shard_map/ppermute | solution.py:341
  82.5 22.5 %collective-permute-start.13 = (bf16[3,352,256]{2,1,0:T(8,128)(2,1)}, bf16[3,352,256]{2,1,0:T(8,128)(2,1)}, u32[]{:S(2)}, u32[]{:S(2)}) collective-permute-start(bf16[3,352,256]{2,1,0:T(8,128)(2,1)} %pad_maximum_fusion.3), channel_id=1, source_target_pairs={{0,16},{8,24},{16,0},{24,8},{1,17},{9,25},{17,1},{25,9},{2,18},{10... | collective-permute-start | bytes 1622024 | tf_op jit(solution)/shard_map/ppermute | solution.py:341
  83.6 22.6 %collective-permute-start.14 = (bf16[3,352,256]{2,1,0:T(8,128)(2,1)}, bf16[3,352,256]{2,1,0:T(8,128)(2,1)}, u32[]{:S(2)}, u32[]{:S(2)}) collective-permute-start(bf16[3,352,256]{2,1,0:T(8,128)(2,1)} %pad_maximum_fusion.3), channel_id=1, source_target_pairs={{0,24},{8,16},{16,8},{24,0},{1,25},{9,17},{17,9},{25,1},{2,26},{10... | collective-permute-start | bytes 1622024 | tf_op jit(solution)/shard_map/ppermute | solution.py:341
  85.5 21.7 %copy-start.28 = (f32[3,352,256]{2,1,0:T(8,128)}, f32[3,352,256]{2,1,0:T(8,128)S(1)}, u32[]{:S(2)}) copy-start(f32[3,352,256]{2,1,0:T(8,128)S(1)} %pad_maximum_fusion.1) | copy-start | bytes 3244036
  107.4 11.1 %collective-permute-start.15 = (f32[352,256]{1,0:T(8,128)S(1)}, f32[352,256]{1,0:T(8,128)S(1)}, u32[]{:S(2)}, u32[]{:S(2)}) collective-permute-start(f32[352,256]{1,0:T(8,128)S(1)} %get-tuple-element.126), channel_id=1, source_target_pairs={{0,8},{8,0},{24,16},{1,9},{9,1},{25,17},{2,10},{10,2},{26,18},{3,1... | collective-permute-start | bytes 1081352 | tf_op jit(solution)/shard_map/ppermute | solution.py:460
  110.4 16.9 %collective-permute-start.16 = (f32[352,256]{1,0:T(8,128)S(1)}, f32[352,256]{1,0:T(8,128)S(1)}, u32[]{:S(2)}, u32[]{:S(2)}) collective-permute-start(f32[352,256]{1,0:T(8,128)S(1)} %get-tuple-element.125), channel_id=1, source_target_pairs={{0,16},{16,0},{24,8},{1,17},{17,1},{25,9},{2,18},{18,2},{26,10},{3... | collective-permute-start | bytes 1081352 | tf_op jit(solution)/shard_map/ppermute | solution.py:460
  113.1 14.9 %collective-permute-start.17 = (f32[352,256]{1,0:T(8,128)S(1)}, f32[352,256]{1,0:T(8,128)}, u32[]{:S(2)}, u32[]{:S(2)}) collective-permute-start(f32[352,256]{1,0:T(8,128)S(1)} %get-tuple-element.124), channel_id=1, source_target_pairs={{8,16},{16,8},{24,0},{9,17},{17,9},{25,1},{10,18},{18,10},{26,2},{... | collective-permute-start | bytes 1081352 | tf_op jit(solution)/shard_map/ppermute | solution.py:460
  145.5 108.6 %reduce-scatter.5.cloned.1.call-start = ((), (), s32[]{:S(2)}) async-start(), calls=%async_computation.5 | async-start | bytes 3604480 | tf_op jit(solution)/shard_map/reduce_scatter | solution.py:468
  159.5 13.7 %collective-permute-start.18 = (bf16[4,256,1024]{2,1,0:T(8,128)(2,1)}, bf16[4,256,1024]{2,1,0:T(8,128)(2,1)}, u32[]{:S(2)}, u32[]{:S(2)}) collective-permute-start(bf16[4,256,1024]{2,1,0:T(8,128)(2,1)} %dynamic-slice_bitcast_fusion), channel_id=1, source_target_pairs={{0,1},{1,0},{2,3},{3,2},{4,5},{5,4},{6,7},{7,6},{8,9},{9,8},{10,11... | collective-permute-start | bytes 6291464 | tf_op jit(solution)/shard_map/ppermute | solution.py:364
  173.2 172.2 %all-reduce.5.cloned.1.call-start = ((), (), s32[]{:S(2)}) async-start(), calls=%async_computation.6 | async-start | bytes 5242880 | tf_op jit(solution)/shard_map/psum | solution.py:500
  198.8 6.6 %collective-permute-start.19 = (bf16[4,4,32,1024]{3,2,1,0:T(8,128)(2,1)S(1)}, bf16[4,4,32,1024]{3,2,1,0:T(8,128)(2,1)S(1)}, u32[]{:S(2)}, u32[]{:S(2)}) collective-permute-start(bf16[4,4,32,1024]{3,2,1,0:T(8,128)(2,1)S(1)} %fusion.11), channel_id=1, source_target_pairs={{0,1},{1,0},{2,3},{3,2},{4,5},{5,4},{6,7},{7,6},{8,9},{9,8},{10,11... | collective-permute-start | bytes 3145736 | tf_op jit(solution)/shard_map/ppermute | solution.py:364
  203.3 32.0 %collective-permute-start.21 = (bf16[256,1024]{1,0:T(8,128)(2,1)}, bf16[256,1024]{1,0:T(8,128)(2,1)S(1)}, u32[]{:S(2)}, u32[]{:S(2)}) collective-permute-start(bf16[256,1024]{1,0:T(8,128)(2,1)} %get-tuple-element.72), channel_id=1, source_target_pairs={{0,4},{1,5},{2,6},{3,7},{4,0},{5,1},{6,2},{7,3},{8,12},{9,13},{10,... | collective-permute-start | bytes 1572872 | tf_op jit(solution)/shard_map/ppermute | solution.py:368
  204.6 30.9 %collective-permute-start.20 = (bf16[256,1024]{1,0:T(8,128)(2,1)}, bf16[256,1024]{1,0:T(8,128)(2,1)S(1)}, u32[]{:S(2)}, u32[]{:S(2)}) collective-permute-start(bf16[256,1024]{1,0:T(8,128)(2,1)} %get-tuple-element.71), channel_id=1, source_target_pairs={{0,2},{1,3},{2,0},{3,1},{4,6},{5,7},{6,4},{7,5},{8,10},{9,11},{10,... | collective-permute-start | bytes 1572872 | tf_op jit(solution)/shard_map/ppermute | solution.py:368
  205.9 29.6 %collective-permute-start.22 = (bf16[128,1024]{1,0:T(8,128)(2,1)S(1)}, bf16[128,1024]{1,0:T(8,128)(2,1)S(1)}, u32[]{:S(2)}, u32[]{:S(2)}) collective-permute-start(bf16[128,1024]{1,0:T(8,128)(2,1)S(1)} %get-tuple-element.101), channel_id=1, source_target_pairs={{0,8},{8,0},{16,24},{24,16},{1,9},{9,1},{17,25},{25,17},{2,10},{10... | collective-permute-start | bytes 786440 | tf_op jit(solution)/shard_map/ppermute | solution.py:355
  207.3 28.1 %collective-permute-start.23 = (bf16[128,1024]{1,0:T(8,128)(2,1)S(1)}, bf16[128,1024]{1,0:T(8,128)(2,1)S(1)}, u32[]{:S(2)}, u32[]{:S(2)}) collective-permute-start(bf16[128,1024]{1,0:T(8,128)(2,1)S(1)} %get-tuple-element.103), channel_id=1, source_target_pairs={{0,16},{8,24},{16,0},{24,8},{1,17},{9,25},{17,1},{25,9},{2,18},{10... | collective-permute-start | bytes 786440 | tf_op jit(solution)/shard_map/ppermute | solution.py:355
  208.8 26.7 %collective-permute-start.24 = (bf16[128,1024]{1,0:T(8,128)(2,1)S(1)}, bf16[128,1024]{1,0:T(8,128)(2,1)S(1)}, u32[]{:S(2)}, u32[]{:S(2)}) collective-permute-start(bf16[128,1024]{1,0:T(8,128)(2,1)S(1)} %get-tuple-element.102), channel_id=1, source_target_pairs={{0,24},{8,16},{16,8},{24,0},{1,25},{9,17},{17,9},{25,1},{2,26},{10... | collective-permute-start | bytes 786440 | tf_op jit(solution)/shard_map/ppermute | solution.py:355
  236.4 8.2 %collective-permute-start.25 = (bf16[32,1024]{1,0:T(8,128)(2,1)S(1)}, bf16[32,1024]{1,0:T(8,128)(2,1)S(1)}, u32[]{:S(2)}, u32[]{:S(2)}) collective-permute-start(bf16[32,1024]{1,0:T(8,128)(2,1)S(1)} %get-tuple-element.129), channel_id=1, source_target_pairs={{0,2},{1,3},{2,0},{3,1},{4,6},{5,7},{6,4},{7,5},{8,10},{9,11},{10,... | collective-permute-start | bytes 196616 | tf_op jit(solution)/shard_map/ppermute | solution.py:368
  238.5 6.7 %collective-permute-start.26 = (bf16[32,1024]{1,0:T(8,128)(2,1)S(1)}, bf16[32,1024]{1,0:T(8,128)(2,1)S(1)}, u32[]{:S(2)}, u32[]{:S(2)}) collective-permute-start(bf16[32,1024]{1,0:T(8,128)(2,1)S(1)} %get-tuple-element.131), channel_id=1, source_target_pairs={{0,4},{1,5},{2,6},{3,7},{4,0},{5,1},{6,2},{7,3},{8,12},{9,13},{10,... | collective-permute-start | bytes 196616 | tf_op jit(solution)/shard_map/ppermute | solution.py:368
  240.3 6.1 %collective-permute-start.27 = (bf16[32,1024]{1,0:T(8,128)(2,1)S(1)}, bf16[32,1024]{1,0:T(8,128)(2,1)S(1)}, u32[]{:S(2)}, u32[]{:S(2)}) collective-permute-start(bf16[32,1024]{1,0:T(8,128)(2,1)S(1)} %get-tuple-element.130), channel_id=1, source_target_pairs={{0,6},{1,7},{2,4},{3,5},{4,2},{5,3},{6,0},{7,1},{8,14},{9,15},{10,... | collective-permute-start | bytes 196616 | tf_op jit(solution)/shard_map/ppermute | solution.py:368
  241.7 19.1 %copy-start.27 = (bf16[320,1024]{1,0:T(8,128)(2,1)S(1)}, bf16[320,1024]{1,0:T(8,128)(2,1)}, u32[]{:S(2)}) copy-start(bf16[320,1024]{1,0:T(8,128)(2,1)} %copy-done.26) | copy-start | bytes 1966084
  241.7 13.7 %collective-permute-start.31 = (bf16[256,320]{1,0:T(8,128)(2,1)}, bf16[256,320]{1,0:T(8,128)(2,1)}, u32[]{:S(2)}, u32[]{:S(2)}) collective-permute-start(bf16[256,320]{1,0:T(8,128)(2,1)} %get-tuple-element.107), channel_id=1, source_target_pairs={{0,8},{8,0},{16,24},{24,16},{1,9},{9,1},{17,25},{25,17},{2,10},{10... | collective-permute-start | bytes 491528 | tf_op jit(solution)/shard_map/ppermute | solution.py:355
  243.2 16.4 %collective-permute-start.32 = (bf16[256,320]{1,0:T(8,128)(2,1)}, bf16[256,320]{1,0:T(8,128)(2,1)}, u32[]{:S(2)}, u32[]{:S(2)}) collective-permute-start(bf16[256,320]{1,0:T(8,128)(2,1)} %get-tuple-element.109), channel_id=1, source_target_pairs={{0,16},{8,24},{16,0},{24,8},{1,17},{9,25},{17,1},{25,9},{2,18},{10... | collective-permute-start | bytes 491528 | tf_op jit(solution)/shard_map/ppermute | solution.py:355
  244.6 15.0 %collective-permute-start.33 = (bf16[256,320]{1,0:T(8,128)(2,1)S(1)}, bf16[256,320]{1,0:T(8,128)(2,1)}, u32[]{:S(2)}, u32[]{:S(2)}) collective-permute-start(bf16[256,320]{1,0:T(8,128)(2,1)S(1)} %get-tuple-element.108), channel_id=1, source_target_pairs={{0,24},{8,16},{16,8},{24,0},{1,25},{9,17},{17,9},{25,1},{2,26},{10... | collective-permute-start | bytes 491528 | tf_op jit(solution)/shard_map/ppermute | solution.py:355
  254.0 11.6 %collective-permute-start.28 = (f32[32,1024]{1,0:T(8,128)S(1)}, f32[32,1024]{1,0:T(8,128)S(1)}, u32[]{:S(2)}, u32[]{:S(2)}) collective-permute-start(f32[32,1024]{1,0:T(8,128)S(1)} %fusion.38), channel_id=1, source_target_pairs={{16,24},{17,25},{18,26},{19,27},{20,28},{21,29},{22,30},{23,31}} | collective-permute-start | bytes 393224 | tf_op jit(solution)/shard_map/ppermute | solution.py:496
  254.7 11.0 %collective-permute-start.29 = (f32[32,1024]{1,0:T(8,128)S(1)}, f32[32,1024]{1,0:T(8,128)S(1)}, u32[]{:S(2)}, u32[]{:S(2)}) collective-permute-start(f32[32,1024]{1,0:T(8,128)S(1)} %fusion.38), channel_id=1, source_target_pairs={{8,24},{9,25},{10,26},{11,27},{12,28},{13,29},{14,30},{15,31}} | collective-permute-start | bytes 393224 | tf_op jit(solution)/shard_map/ppermute | solution.py:496
  255.5 10.3 %collective-permute-start.30 = (f32[32,1024]{1,0:T(8,128)S(1)}, f32[32,1024]{1,0:T(8,128)S(1)}, u32[]{:S(2)}, u32[]{:S(2)}) collective-permute-start(f32[32,1024]{1,0:T(8,128)S(1)} %fusion.38), channel_id=1, source_target_pairs={{0,24},{1,25},{2,26},{3,27},{4,28},{5,29},{6,30},{7,31}} | collective-permute-start | bytes 393224 | tf_op jit(solution)/shard_map/ppermute | solution.py:496
  265.7 6.2 %collective-permute-start.34 = (bf16[4,104,1024]{2,1,0:T(8,128)(2,1)}, bf16[4,104,1024]{2,1,0:T(8,128)(2,1)}, u32[]{:S(2)}, u32[]{:S(2)}) collective-permute-start(bf16[4,104,1024]{2,1,0:T(8,128)(2,1)} %fusion.15), channel_id=1, source_target_pairs={{0,1},{1,0},{2,3},{3,2},{4,5},{5,4},{6,7},{7,6},{8,9},{9,8},{10,11... | collective-permute-start | bytes 2555912 | tf_op jit(solution)/shard_map/ppermute | solution.py:364
  271.8 148.3 %all-gather.9.cloned.1.call-start = ((), (), s32[]{:S(2)}) async-start(), calls=%async_computation.7 | async-start | bytes 3514368 | tf_op jit(solution)/shard_map/all_gather | solution.py:525
  274.0 8.3 %collective-permute-start.35 = (bf16[416,256]{1,0:T(8,128)(2,1)S(1)}, bf16[416,256]{1,0:T(8,128)(2,1)S(1)}, u32[]{:S(2)}, u32[]{:S(2)}) collective-permute-start(bf16[416,256]{1,0:T(8,128)(2,1)S(1)} %get-tuple-element.104), channel_id=1, source_target_pairs={{0,8},{8,0},{16,24},{24,16},{1,9},{9,1},{17,25},{25,17},{2,10},{10... | collective-permute-start | bytes 638984 | tf_op jit(solution)/shard_map/ppermute | solution.py:355
  274.1 10.9 %collective-permute-start.36 = (bf16[416,256]{1,0:T(8,128)(2,1)S(1)}, bf16[416,256]{1,0:T(8,128)(2,1)S(1)}, u32[]{:S(2)}, u32[]{:S(2)}) collective-permute-start(bf16[416,256]{1,0:T(8,128)(2,1)S(1)} %get-tuple-element.106), channel_id=1, source_target_pairs={{0,16},{8,24},{16,0},{24,8},{1,17},{9,25},{17,1},{25,9},{2,18},{10... | collective-permute-start | bytes 638984 | tf_op jit(solution)/shard_map/ppermute | solution.py:355
  274.1 10.8 %collective-permute-start.37 = (bf16[416,256]{1,0:T(8,128)(2,1)S(1)}, bf16[416,256]{1,0:T(8,128)(2,1)S(1)}, u32[]{:S(2)}, u32[]{:S(2)}) collective-permute-start(bf16[416,256]{1,0:T(8,128)(2,1)S(1)} %get-tuple-element.105), channel_id=1, source_target_pairs={{0,24},{8,16},{16,8},{24,0},{1,25},{9,17},{17,9},{25,1},{2,26},{10... | collective-permute-start | bytes 638984 | tf_op jit(solution)/shard_map/ppermute | solution.py:355
  286.1 130.5 %collective-permute-start.41 = (f32[352,256]{1,0:T(8,128)}, f32[352,256]{1,0:T(8,128)}, u32[]{:S(2)}, u32[]{:S(2)}) collective-permute-start(f32[352,256]{1,0:T(8,128)} %get-tuple-element.117), channel_id=1, source_target_pairs={{0,8},{8,0},{16,24},{1,9},{9,1},{17,25},{2,10},{10,2},{18,26},{3,1... | collective-permute-start | bytes 1081352 | tf_op jit(solution)/shard_map/ppermute | solution.py:530
  289.8 10.7 %collective-permute-start.38 = (bf16[104,256]{1,0:T(8,128)(2,1)S(1)}, bf16[104,256]{1,0:T(8,128)(2,1)S(1)}, u32[]{:S(2)}, u32[]{:S(2)}) collective-permute-start(bf16[104,256]{1,0:T(8,128)(2,1)S(1)} %get-tuple-element.132), channel_id=1, source_target_pairs={{0,2},{1,3},{2,0},{3,1},{4,6},{5,7},{6,4},{7,5},{8,10},{9,11},{10,... | collective-permute-start | bytes 159752 | tf_op jit(solution)/shard_map/ppermute | solution.py:368
  292.0 10.6 %collective-permute-start.39 = (bf16[104,256]{1,0:T(8,128)(2,1)S(1)}, bf16[104,256]{1,0:T(8,128)(2,1)S(1)}, u32[]{:S(2)}, u32[]{:S(2)}) collective-permute-start(bf16[104,256]{1,0:T(8,128)(2,1)S(1)} %get-tuple-element.134), channel_id=1, source_target_pairs={{0,4},{1,5},{2,6},{3,7},{4,0},{5,1},{6,2},{7,3},{8,12},{9,13},{10,... | collective-permute-start | bytes 159752 | tf_op jit(solution)/shard_map/ppermute | solution.py:368
  294.3 51.0 %copy-start.48 = (bf16[256,1024]{1,0:T(8,128)(2,1)S(1)}, bf16[256,1024]{1,0:T(8,128)(2,1)}, u32[]{:S(2)}) copy-start(bf16[256,1024]{1,0:T(8,128)(2,1)} %get-tuple-element.80) | copy-start | bytes 1572868
  294.3 9.0 %collective-permute-start.40 = (bf16[104,256]{1,0:T(8,128)(2,1)S(1)}, bf16[104,256]{1,0:T(8,128)(2,1)S(1)}, u32[]{:S(2)}, u32[]{:S(2)}) collective-permute-start(bf16[104,256]{1,0:T(8,128)(2,1)S(1)} %get-tuple-element.133), channel_id=1, source_target_pairs={{0,6},{1,7},{2,4},{3,5},{4,2},{5,3},{6,0},{7,1},{8,14},{9,15},{10,... | collective-permute-start | bytes 159752 | tf_op jit(solution)/shard_map/ppermute | solution.py:368
  297.6 120.8 %collective-permute-start.42 = (f32[352,256]{1,0:T(8,128)}, f32[352,256]{1,0:T(8,128)}, u32[]{:S(2)}, u32[]{:S(2)}) collective-permute-start(f32[352,256]{1,0:T(8,128)} %get-tuple-element.116), channel_id=1, source_target_pairs={{0,16},{8,24},{16,0},{1,17},{9,25},{17,1},{2,18},{10,26},{18,2},{3... | collective-permute-start | bytes 1081352 | tf_op jit(solution)/shard_map/ppermute | solution.py:530
  300.5 167.9 %collective-permute-start.43 = (f32[352,256]{1,0:T(8,128)}, f32[352,256]{1,0:T(8,128)}, u32[]{:S(2)}, u32[]{:S(2)}) collective-permute-start(f32[352,256]{1,0:T(8,128)} %get-tuple-element.115), channel_id=1, source_target_pairs={{0,24},{8,16},{16,8},{1,25},{9,17},{17,9},{2,26},{10,18},{18,10},{... | collective-permute-start | bytes 1081352 | tf_op jit(solution)/shard_map/ppermute | solution.py:530
  304.0 171.2 %all-gather.11.cloned.1.call-start = ((), (), s32[]{:S(2)}) async-start(), calls=%async_computation.8 | async-start | bytes 2359296 | tf_op jit(solution)/shard_map/all_gather | solution.py:548
  345.3 74.8 %collective-permute-start.44 = (bf16[256,1024]{1,0:T(8,128)(2,1)S(1)}, bf16[256,1024]{1,0:T(8,128)(2,1)}, u32[]{:S(2)}, u32[]{:S(2)}) collective-permute-start(bf16[256,1024]{1,0:T(8,128)(2,1)S(1)} %copy-done.48), channel_id=1, source_target_pairs={{0,6},{1,7},{2,4},{3,5},{4,2},{5,3},{6,0},{7,1},{8,14},{9,15},{10,... | collective-permute-start | bytes 1572872 | tf_op jit(solution)/shard_map/ppermute | solution.py:368
  420.1 8.3 %collective-permute-start.45 = (f32[32,1024]{1,0:T(8,128)S(1)}, f32[32,1024]{1,0:T(8,128)S(1)}, u32[]{:S(2)}, u32[]{:S(2)}) collective-permute-start(f32[32,1024]{1,0:T(8,128)S(1)} %get-tuple-element.123), channel_id=1, source_target_pairs={{24,0},{25,1},{26,2},{27,3},{28,4},{29,5},{30,6},{31,7}} | collective-permute-start | bytes 393224 | tf_op jit(solution)/shard_map/ppermute | solution.py:541
  421.4 7.0 %collective-permute-start.46 = (f32[32,1024]{1,0:T(8,128)S(1)}, f32[32,1024]{1,0:T(8,128)S(1)}, u32[]{:S(2)}, u32[]{:S(2)}) collective-permute-start(f32[32,1024]{1,0:T(8,128)S(1)} %get-tuple-element.122), channel_id=1, source_target_pairs={{24,8},{25,9},{26,10},{27,11},{28,12},{29,13},{30,14},{31,15}} | collective-permute-start | bytes 393224 | tf_op jit(solution)/shard_map/ppermute | solution.py:541
  422.1 6.3 %collective-permute-start.47 = (f32[32,1024]{1,0:T(8,128)S(1)}, f32[32,1024]{1,0:T(8,128)S(1)}, u32[]{:S(2)}, u32[]{:S(2)}) collective-permute-start(f32[32,1024]{1,0:T(8,128)S(1)} %get-tuple-element.121), channel_id=1, source_target_pairs={{24,16},{25,17},{26,18},{27,19},{28,20},{29,21},{30,22},{31,23}} | collective-permute-start | bytes 393224 | tf_op jit(solution)/shard_map/ppermute | solution.py:541
  429.4 36.9 %collective-permute-start.48 = (f32[352,256]{1,0:T(8,128)}, f32[352,256]{1,0:T(8,128)}, u32[]{:S(2)}, u32[]{:S(2)}) collective-permute-start(f32[352,256]{1,0:T(8,128)} %get-tuple-element.120), channel_id=1, source_target_pairs={{0,8},{8,0},{16,24},{1,9},{9,1},{17,25},{2,10},{10,2},{18,26},{3,1... | collective-permute-start | bytes 1081352 | tf_op jit(solution)/shard_map/ppermute | solution.py:530
  432.7 34.7 %collective-permute-start.49 = (f32[352,256]{1,0:T(8,128)}, f32[352,256]{1,0:T(8,128)}, u32[]{:S(2)}, u32[]{:S(2)}) collective-permute-start(f32[352,256]{1,0:T(8,128)} %get-tuple-element.119), channel_id=1, source_target_pairs={{0,16},{8,24},{16,0},{1,17},{9,25},{17,1},{2,18},{10,26},{18,2},{3... | collective-permute-start | bytes 1081352 | tf_op jit(solution)/shard_map/ppermute | solution.py:530
  436.4 32.1 %collective-permute-start.50 = (f32[352,256]{1,0:T(8,128)S(1)}, f32[352,256]{1,0:T(8,128)}, u32[]{:S(2)}, u32[]{:S(2)}) collective-permute-start(f32[352,256]{1,0:T(8,128)S(1)} %get-tuple-element.118), channel_id=1, source_target_pairs={{0,24},{8,16},{16,8},{1,25},{9,17},{17,9},{2,26},{10,18},{18,10},{... | collective-permute-start | bytes 1081352 | tf_op jit(solution)/shard_map/ppermute | solution.py:530
  441.1 19.7 %copy-start.50 = (bf16[256,1024]{1,0:T(8,128)(2,1)S(1)}, bf16[256,1024]{1,0:T(8,128)(2,1)}, u32[]{:S(2)}) copy-start(bf16[256,1024]{1,0:T(8,128)(2,1)} %copy-done.49) | copy-start | bytes 1572868
  441.1 19.7 %copy-start.52 = (bf16[256,1024]{1,0:T(8,128)(2,1)S(1)}, bf16[256,1024]{1,0:T(8,128)(2,1)}, u32[]{:S(2)}) copy-start(bf16[256,1024]{1,0:T(8,128)(2,1)} %copy-done.51) | copy-start | bytes 1572868
  (55 other events, 256.4 us)
Sparse Core Ops, SparseCore 0:
  11.9 49.8 all-gather.6
  80.3 47.0 all-gather.4
  145.6 49.6 reduce-scatter.2
  198.2 55.7 reduce-scatter.4
  272.0 73.3 all-reduce.4
  348.6 59.4 all-gather.8
  439.3 28.3 all-gather.10
